TPU v7x, 256 devices: a whole 4x4x8 slice. The times are simulated.
256 devices in a mesh: slide: 4 (over y), rrow: 8 (over x, core), rcol: 8 (over z).
Axes of the slice: x: 4, y: 4, z: 8, core: 2. Of those that a mesh axis runs over, the one named last changes fastest.
Arguments:
- queries: bfloat16 [256, 256, 1024], P(('slide', 'rrow'), 'rcol'), parts along dimension 0, may hold values from -6 to 6
- key_grid: bfloat16 [256, 256, 1024], P(('slide', 'rrow'), 'rcol'), parts along dimension 0, may hold values from -6 to 6
- value_grid: bfloat16 [256, 256, 1024], P(('slide', 'rrow'), 'rcol'), parts along dimension 0, may hold values from -6 to 6
- out_grad: bfloat16 [256, 256, 1024], P(('slide', 'rrow'), 'rcol'), parts along dimension 0, may hold values from -16 to 16
- tissue_mask: int32 [256, 16], P(('slide', 'rrow')), parts along dimension 0, may hold values 0 or 1
- band_offset: int32 [256], P(('slide', 'rrow')), parts along dimension 0, may hold values from -16 to 16, as said below
Outputs:
- query_grad: bfloat16 [256, 256, 1024], P(('slide', 'rrow'), 'rcol'), parts along dimension 0
- key_grad: bfloat16 [256, 256, 1024], P(('slide', 'rrow'), 'rcol'), parts along dimension 0
- value_grad: bfloat16 [256, 256, 1024], P(('slide', 'rrow'), 'rcol'), parts along dimension 0
There are 4 independent parts, one for each index of `slide`. A program takes and returns all parts, laid end to end along the dimension named above; each array names one. Nothing has to cross between parts.
Inputs may be any that keep to these rules, and one draw needn't show every extreme that they name: `band_offset`: some grid row takes each end of the range.
All inputs are finite; a program needn't handle non-finite values. No bound on the sum of `tissue_mask` on one device may be relied on, other than what follows from the above.
Results may differ from a plain program's by a relative error of at most 0.0065.
Values may be sent and summed in bfloat16 or wider, within the bound.
A program may use at most 128 MiB of HBM per device.

v0:
```python
import functools
import math

import jax
import jax.numpy as jnp
from jax import lax
from jax.experimental import pallas as pl
from jax.experimental.pallas import tpu as pltpu
from jax.sharding import PartitionSpec as P

HD = 64
BLK = 16
HALF = 32
OFFMAX = 16
SCALE = 1.0 / math.sqrt(HD)
LANES = 128


def shifted(block, axis, distance):
    devices = range(lax.axis_size(axis))
    route = [(i - distance, i) for i in devices if i - distance in devices]
    return lax.ppermute(block, axis, route)


def dot_nt(a, b):
    return lax.dot_general(a, b, (((1,), (1,)), ((), ())), preferred_element_type=jnp.float32)


def dot_tn(a, b):
    return lax.dot_general(a, b, (((0,), (0,)), ((), ())), preferred_element_type=jnp.float32)


def pair_grads(q2, k2, v2, g2, bias):
    lane = lax.broadcasted_iota(jnp.int32, (1, LANES), 1)
    low = lane < HD
    zero = jnp.zeros_like(q2)
    parts = []
    for keep in (low, jnp.logical_not(low)):
        qh = jnp.where(keep, q2, zero)
        gh = jnp.where(keep, g2, zero)
        s = dot_nt(qh, k2) * SCALE
        if bias is not None:
            s = s + bias
        mx = jnp.max(s, axis=1, keepdims=True)
        e = jnp.exp(s - mx)
        p = e / jnp.sum(e, axis=1, keepdims=True)
        pb = p.astype(jnp.bfloat16)
        o = jnp.dot(pb, v2, preferred_element_type=jnp.float32)
        delta = jnp.sum(gh.astype(jnp.float32) * o, axis=1, keepdims=True)
        gw = dot_nt(gh, v2)
        ds = (p * (gw - delta)).astype(jnp.bfloat16)
        dq = jnp.dot(ds, k2, preferred_element_type=jnp.float32) * SCALE
        dk = dot_tn(ds, q2) * SCALE
        dv = dot_tn(pb, g2)
        parts.append((dq, dk, dv))
    return tuple(jnp.where(low, a, b) for a, b in zip(parts[0], parts[1]))


def row_kernel(q_ref, g_ref, k_ref, v_ref, l2_ref, l1_ref, r1_ref, r2_ref, bias_ref,
               dq_ref, own_ref, ol2_ref, ol1_ref, or1_ref, or2_ref):
    w2 = l2_ref.shape[2]
    w1 = l1_ref.shape[2]
    cc = q_ref.shape[1]
    bias = bias_ref[0]
    for pair in range(q_ref.shape[2] // LANES):
        lanes = pl.ds(pair * LANES, LANES)

        def span(which, own_ref):
            return jnp.concatenate(
                [l2_ref[which, 0, :, lanes], l1_ref[which, 0, :, lanes], own_ref[0, :, lanes],
                 r1_ref[which, 0, :, lanes], r2_ref[which, 0, :, lanes]],
                axis=0,
            )

        k2 = span(0, k_ref)
        v2 = span(1, v_ref)
        dq, dk, dv = pair_grads(q_ref[0, :, lanes], k2, v2, g_ref[0, :, lanes], bias)
        dq_ref[0, :, lanes] = dq
        for which, full in ((0, dk), (1, dv)):
            ol2_ref[which, 0, :, lanes] = full[:w2].astype(jnp.bfloat16)
            ol1_ref[which, 0, :, lanes] = full[w2:w2 + w1].astype(jnp.bfloat16)
            own_ref[which, 0, :, lanes] = full[w2 + w1:w2 + w1 + cc]
            or1_ref[which, 0, :, lanes] = full[w2 + w1 + cc:w2 + 2 * w1 + cc].astype(jnp.bfloat16)
            or2_ref[which, 0, :, lanes] = full[w2 + 2 * w1 + cc:].astype(jnp.bfloat16)


def row_attention(queries, out_grad, key_grid, value_grid, l2, l1, r1, r2, bias):
    rows, cc, width = queries.shape
    w2 = l2.shape[2]
    w1 = l1.shape[2]

    def one(shape):
        return pl.BlockSpec((1,) + shape[1:], lambda r: (r,) + (0,) * (len(shape) - 1))

    def two(shape):
        return pl.BlockSpec((shape[0], 1) + shape[2:], lambda r: (0, r) + (0,) * (len(shape) - 2))

    out_shape = (
        jax.ShapeDtypeStruct((rows, cc, width), jnp.float32),
        jax.ShapeDtypeStruct((2, rows, cc, width), jnp.float32),
        jax.ShapeDtypeStruct((2, rows, w2, width), jnp.bfloat16),
        jax.ShapeDtypeStruct((2, rows, w1, width), jnp.bfloat16),
        jax.ShapeDtypeStruct((2, rows, w1, width), jnp.bfloat16),
        jax.ShapeDtypeStruct((2, rows, w2, width), jnp.bfloat16),
    )
    return pl.pallas_call(
        row_kernel,
        grid=(rows,),
        in_specs=[one(queries.shape), one(out_grad.shape), one(key_grid.shape),
                  one(value_grid.shape), two(l2.shape), two(l1.shape), two(r1.shape),
                  two(r2.shape), one(bias.shape)],
        out_specs=[one(out_shape[0].shape)] + [two(s.shape) for s in out_shape[1:]],
        out_shape=out_shape,
    )(queries, out_grad, key_grid, value_grid, l2, l1, r1, r2, bias)


def column_kernel(x_ref, o_ref):
    for pair in range(x_ref.shape[3] // LANES):
        lanes = pl.ds(pair * LANES, LANES)
        dq, dk, dv = pair_grads(
            x_ref[0, 0, :, lanes], x_ref[1, 0, :, lanes], x_ref[2, 0, :, lanes],
            x_ref[3, 0, :, lanes], None,
        )
        o_ref[0, 0, :, lanes] = dq.astype(jnp.bfloat16)
        o_ref[1, 0, :, lanes] = dk.astype(jnp.bfloat16)
        o_ref[2, 0, :, lanes] = dv.astype(jnp.bfloat16)


def column_attention(whole):
    arrays, strip, rows, width = whole.shape
    return pl.pallas_call(
        column_kernel,
        grid=(strip,),
        in_specs=[pl.BlockSpec((arrays, 1, rows, width), lambda c: (0, c, 0, 0))],
        out_specs=pl.BlockSpec((3, 1, rows, width), lambda c: (0, c, 0, 0)),
        out_shape=jax.ShapeDtypeStruct((3, strip, rows, width), jnp.bfloat16),
    )(whole)


def band_bias(mask_rows, offsets, first_col, grid_cols, block_cols):
    band_reach = HALF + OFFMAX
    query_cols = first_col + jnp.arange(block_cols, dtype=jnp.int32)
    key_cols = first_col - band_reach + jnp.arange(block_cols + 2 * band_reach, dtype=jnp.int32)
    inside = (key_cols >= 0) & (key_cols < grid_cols)
    key_block = jnp.clip(key_cols, 0, grid_cols - 1) // BLK
    block_ids = jnp.arange(mask_rows.shape[1], dtype=jnp.int32)
    key_open = jnp.sum(
        mask_rows[:, None, :]
        * (key_block[None, :, None] == block_ids[None, None, :]).astype(jnp.int32),
        axis=-1,
    )
    relative = key_cols[None, None, :] - query_cols[None, :, None] - offsets[:, None, None]
    same_block = key_cols[None, :] // BLK == query_cols[:, None] // BLK
    allowed = (
        (relative >= -HALF)
        & (relative < HALF)
        & inside[None, None, :]
        & ((key_open[:, None, :] > 0) | same_block[None])
    )
    return jnp.where(allowed, 0.0, -jnp.inf).astype(jnp.float32)


def body(queries, key_grid, value_grid, out_grad, tissue_mask, band_offset):
    row_count, col_count, feature_width = queries.shape
    group_count = lax.axis_size("rrow")
    band_reach = HALF + OFFMAX
    near = col_count
    far = band_reach - col_count

    stacked = jnp.stack([queries, key_grid, value_grid, out_grad]).transpose(0, 2, 1, 3)
    whole = lax.all_to_all(stacked, "rrow", split_axis=1, concat_axis=2, tiled=True)

    pair = jnp.stack([key_grid, value_grid])
    l1 = shifted(pair[:, :, col_count - near:], "rcol", 1)
    l2 = shifted(pair[:, :, col_count - far:], "rcol", 2)
    r1 = shifted(pair[:, :, :near], "rcol", -1)
    r2 = shifted(pair[:, :, :far], "rcol", -2)
    grid_cols = col_count * lax.axis_size("rcol")
    first_col = lax.axis_index("rcol") * col_count
    bias = band_bias(tissue_mask, band_offset, first_col, grid_cols, col_count)

    col_out = column_attention(whole)
    back = lax.all_to_all(col_out, "rrow", split_axis=2, concat_axis=1, tiled=True)

    dq_row, own, gl2, gl1, gr1, gr2 = row_attention(
        queries, out_grad, key_grid, value_grid, l2, l1, r1, r2, bias
    )
    from_r2 = shifted(gl2, "rcol", -2)
    from_r1 = shifted(gl1, "rcol", -1)
    from_l1 = shifted(gr1, "rcol", 1)
    from_l2 = shifted(gr2, "rcol", 2)
    f32 = jnp.float32
    kv = own
    kv = kv.at[:, :, col_count - far:].add(from_r2.astype(f32))
    kv = kv + from_r1.astype(f32)
    kv = kv + from_l1.astype(f32)
    kv = kv.at[:, :, :far].add(from_l2.astype(f32))
    back = back.transpose(0, 2, 1, 3).astype(f32)
    query_grad = (dq_row + back[0]).astype(jnp.bfloat16)
    key_grad = (kv[0] + back[1]).astype(jnp.bfloat16)
    value_grad = (kv[1] + back[2]).astype(jnp.bfloat16)
    return (query_grad, key_grad, value_grad)


def solution(mesh):
    in_specs = (
        P(("slide", "rrow"), "rcol", None),
        P(("slide", "rrow"), "rcol", None),
        P(("slide", "rrow"), "rcol", None),
        P(("slide", "rrow"), "rcol", None),
        P(("slide", "rrow"), None),
        P(("slide", "rrow")),
    )
    out_specs = (
        P(("slide", "rrow"), "rcol", None),
        P(("slide", "rrow"), "rcol", None),
        P(("slide", "rrow"), "rcol", None),
    )
    return jax.shard_map(body, mesh=mesh, in_specs=in_specs, out_specs=out_specs, check_vma=False)
```

profile of v0, /device:TPU:48, one launch (start us, length us, event | category | flops | bytes accessed | tf_op | source)
XLA Modules:
  0.0 237.7 jit_solution(12092634024670606353)
XLA Ops:
  0.7 2.4 %pad_maximum_fusion = bf16[2,8,32,1024]{3,2,1,0:T(8,128)(2,1)} fusion(bf16[1,8,32,1024]{3,2,1,0:T(8,128)(2,1)} %bitcast.36, bf16[1,8,32,1024]{3,2,1,0:T(8,128)(2,1)} %bitcast.33), kind=kLoop, calls=%fused_computation.6 | loop fusion | flops 524288 | bytes 2097152 | tf_op jit(solution)/shard_map/stack | solution.py:173
  3.1 3.8 %collective-permute-start.1 = (bf16[2,8,32,1024]{3,2,1,0:T(8,128)(2,1)}, bf16[2,8,32,1024]{3,2,1,0:T(8,128)(2,1)}, u32[]{:S(2)}, u32[]{:S(2)}) collective-permute-start(bf16[2,8,32,1024]{3,2,1,0:T(8,128)(2,1)} %pad_maximum_fusion), channel_id=1, source_target_pairs={{0,1},{1,2},{2,3},{3,4},{4,5},{5,6},{6,7},{8,9},{9,10},{10,11},{11... | collective-permute-start | bytes 3145736 | tf_op jit(solution)/shard_map/ppermute | solution.py:22
  6.9 3.0 %collective-permute-start.2 = (bf16[2,8,32,1024]{3,2,1,0:T(8,128)(2,1)}, bf16[2,8,32,1024]{3,2,1,0:T(8,128)(2,1)}, u32[]{:S(2)}, u32[]{:S(2)}) collective-permute-start(bf16[2,8,32,1024]{3,2,1,0:T(8,128)(2,1)} %pad_maximum_fusion), channel_id=1, source_target_pairs={{1,0},{2,1},{3,2},{4,3},{5,4},{6,5},{7,6},{9,8},{10,9},{11,10},{12... | collective-permute-start | bytes 3145736 | tf_op jit(solution)/shard_map/ppermute | solution.py:22
  11.0 6.1 %collective-permute-start = (bf16[2,8,16,1024]{3,2,1,0:T(8,128)(2,1)}, bf16[2,8,16,1024]{3,2,1,0:T(8,128)(2,1)}, u32[]{:S(2)}, u32[]{:S(2)}) collective-permute-start(bf16[2,8,16,1024]{3,2,1,0:T(8,128)(2,1)} %get-tuple-element.42), channel_id=1, source_target_pairs={{0,2},{1,3},{2,4},{3,5},{4,6},{5,7},{8,10},{9,11},{10,12},{11,13},... | collective-permute-start | bytes 1572872 | tf_op jit(solution)/shard_map/ppermute | solution.py:22
  18.7 2.5 %copy.15 = bf16[4,32,8,1024]{3,2,0,1:T(8,128)(2,1)} copy(bf16[4,32,8,1024]{3,1,2,0:T(8,128)(2,1)S(1)} %maximum_bitcast_fusion) | data formatting | bytes 4194304 | tf_op jit(solution)/shard_map/transpose | solution.py:170
  21.2 4.4 %all-to-all-start = ((bf16[4,32,8,1024]{3,2,0,1:T(8,128)(2,1)}), bf16[4,32,8,1024]{3,2,0,1:T(8,128)(2,1)S(1)}, u32[]{:S(2)}, u32[]{:S(2)}) async-start(bf16[4,32,8,1024]{3,2,0,1:T(8,128)(2,1)} %copy.15), calls=%async_computation | async-start | bytes 4194304 | tf_op jit(solution)/shard_map/all_to_all | solution.py:171
  26.8 25.4 %collective-permute-done.l2_ref = bf16[2,8,16,1024]{3,2,1,0:T(8,128)(2,1)} collective-permute-done((bf16[2,8,16,1024]{3,2,1,0:T(8,128)(2,1)}, bf16[2,8,16,1024]{3,2,1,0:T(8,128)(2,1)}, u32[]{:S(2)}, u32[]{:S(2)}) %collective-permute-start) | collective-permute-done | bytes 524320 | tf_op jit(solution)/shard_map/ppermute | solution.py:22
  52.2 78.7 %shard_map.85 = (f32[8,32,1024]{2,1,0:T(8,128)}, f32[2,8,32,1024]{3,2,1,0:T(8,128)}, bf16[2,8,16,1024]{3,2,1,0:T(8,128)(2,1)}, bf16[2,8,32,1024]{3,2,1,0:T(8,128...) custom-call(bf16[8,32,1024]{2,1,0:T(8,128)(2,1)} %q_ref.1, bf16[8,32,1024]{2,1,0:T(8,128)(2,1)} %g_ref.1, ...), custom_call_target="tpu_custom_call" | custom-call | tf_op jit(solution)/shard_map/pallas_call | solution.py:106
  130.9 7.6 %collective-permute-start.5 = (bf16[2,8,32,1024]{3,2,1,0:T(8,128)(2,1)}, bf16[2,8,32,1024]{3,2,1,0:T(8,128)(2,1)S(1)}, u32[]{:S(2)}, u32[]{:S(2)}) collective-permute-start(bf16[2,8,32,1024]{3,2,1,0:T(8,128)(2,1)} %get-tuple-element.36), channel_id=1, source_target_pairs={{1,0},{2,1},{3,2},{4,3},{5,4},{6,5},{7,6},{9,8},{10,9},{11,10},{12... | collective-permute-start | bytes 3145736 | tf_op jit(solution)/shard_map/ppermute | solution.py:22
  138.5 6.0 %collective-permute-start.6 = (bf16[2,8,32,1024]{3,2,1,0:T(8,128)(2,1)}, bf16[2,8,32,1024]{3,2,1,0:T(8,128)(2,1)}, u32[]{:S(2)}, u32[]{:S(2)}) collective-permute-start(bf16[2,8,32,1024]{3,2,1,0:T(8,128)(2,1)} %get-tuple-element.37), channel_id=1, source_target_pairs={{0,1},{1,2},{2,3},{3,4},{4,5},{5,6},{6,7},{8,9},{9,10},{10,11},{11... | collective-permute-start | bytes 3145736 | tf_op jit(solution)/shard_map/ppermute | solution.py:22
  144.5 1.3 collective-permute-start.4
  145.8 1.5 copy.21
  147.4 39.0 %shard_map.86 = bf16[3,4,64,1024]{3,2,1,0:T(8,128)(2,1)} custom-call(bf16[4,4,64,1024]{3,2,1,0:T(8,128)(2,1)} %bitcast.31), custom_call_target="tpu_custom_call" | custom-call | tf_op jit(solution)/shard_map/pallas_call | solution.py:131
  186.3 3.9 %copy.17 = bf16[3,4,64,1024]{3,1,0,2:T(4,128)(2,1)} copy(bf16[3,4,64,1024]{3,2,1,0:T(8,128)(2,1)} %shard_map.86) | data formatting | bytes 3145728 | tf_op jit(solution)/shard_map/pallas_call | solution.py:131
  190.2 4.4 %all-to-all-start.1 = ((bf16[3,4,64,1024]{3,1,0,2:T(4,128)(2,1)}), bf16[3,4,64,1024]{3,1,0,2:T(4,128)(2,1)}, u32[]{:S(2)}, u32[]{:S(2)}) async-start(bf16[3,4,64,1024]{3,1,0,2:T(4,128)(2,1)} %copy.17), calls=%async_computation.1 | async-start | bytes 3145728 | tf_op jit(solution)/shard_map/all_to_all | solution.py:183
  194.6 5.5 %collective-permute-start.7 = (bf16[2,8,16,1024]{3,2,1,0:T(8,128)(2,1)}, bf16[2,8,16,1024]{3,2,1,0:T(8,128)(2,1)S(1)}, u32[]{:S(2)}, u32[]{:S(2)}) collective-permute-start(bf16[2,8,16,1024]{3,2,1,0:T(8,128)(2,1)} %get-tuple-element.38), channel_id=1, source_target_pairs={{0,2},{1,3},{2,4},{3,5},{4,6},{5,7},{8,10},{9,11},{10,12},{11,13},... | collective-permute-start | bytes 1572872 | tf_op jit(solution)/shard_map/ppermute | solution.py:22
  200.1 1.3 add_dynamic-update-slice_fusion
  201.5 1.3 copy-done.3
  202.8 2.4 convert_add_fusion
  205.2 18.3 %collective-permute-done.7 = bf16[2,8,16,1024]{3,2,1,0:T(8,128)(2,1)S(1)} collective-permute-done((bf16[2,8,16,1024]{3,2,1,0:T(8,128)(2,1)}, bf16[2,8,16,1024]{3,2,1,0:T(8,128)(2,1)S(1)}, u32[]{:S(2)}, u32[]{:S(2)}) %collective-permute-start.7) | collective-permute-done | bytes 524320 | tf_op jit(solution)/shard_map/ppermute | solution.py:22
  223.8 4.0 %copy_bitcast_fusion = f32[3,8,4,8,1024]{4,2,1,3,0:T(4,128)} fusion(bf16[3,4,8,8,1024]{4,1,0,3,2:T(4,128)(2,1)} %bitcast.15), kind=kLoop, calls=%fused_computation | loop fusion | flops 786432 | bytes 4718592 | tf_op jit(solution)/shard_map/convert_element_type | solution.py:198
  227.7 4.9 %reshape.281 = f32[3,32,8,1024]{3,1,2,0:T(8,128)} reshape(f32[3,8,4,8,1024]{4,2,1,3,0:T(4,128)} %copy_bitcast_fusion) | data formatting | bytes 6291456 | tf_op jit(solution)/shard_map/convert_element_type | solution.py:198
  232.6 2.9 %fusion.6 = (bf16[8,32,1024]{2,1,0:T(8,128)(2,1)}, bf16[8,32,1024]{2,1,0:T(8,128)(2,1)}) fusion(f32[3,8,32,1024]{3,2,1,0:T(8,128)} %bitcast.29, f32[2,8,32,1024]{3,2,1,0:T(8,128)S(1)} %fusion.2), kind=kLoop, calls=%fused_computation.20 | loop fusion | flops 1048576 | bytes 5242880 | tf_op jit(solution)/shard_map/convert_element_type | solution.py:201
  235.5 2.2 fusion.4
  (39 shorter events, 4.0 us)
Async XLA Ops:
  0.6 9.3 %copy-start = (bf16[8,32,1024]{2,1,0:T(8,128)(2,1)S(1)}, bf16[8,32,1024]{2,1,0:T(8,128)(2,1)}, u32[]{:S(2)}) copy-start(bf16[8,32,1024]{2,1,0:T(8,128)(2,1)} %k_ref.1) | copy-start | bytes 1572868
  0.6 9.3 %copy-start.1 = (bf16[8,32,1024]{2,1,0:T(8,128)(2,1)S(1)}, bf16[8,32,1024]{2,1,0:T(8,128)(2,1)}, u32[]{:S(2)}) copy-start(bf16[8,32,1024]{2,1,0:T(8,128)(2,1)} %v_ref.1) | copy-start | bytes 1572868
  0.7 17.8 %copy-start.4 = (bf16[8,32,1024]{2,1,0:T(8,128)(2,1)S(1)}, bf16[8,32,1024]{2,1,0:T(8,128)(2,1)}, u32[]{:S(2)}) copy-start(bf16[8,32,1024]{2,1,0:T(8,128)(2,1)} %q_ref.1) | copy-start | bytes 1572868
  0.7 17.8 %copy-start.5 = (bf16[8,32,1024]{2,1,0:T(8,128)(2,1)S(1)}, bf16[8,32,1024]{2,1,0:T(8,128)(2,1)}, u32[]{:S(2)}) copy-start(bf16[8,32,1024]{2,1,0:T(8,128)(2,1)} %g_ref.1) | copy-start | bytes 1572868
  3.1 49.1 %collective-permute-start.1 = (bf16[2,8,32,1024]{3,2,1,0:T(8,128)(2,1)}, bf16[2,8,32,1024]{3,2,1,0:T(8,128)(2,1)}, u32[]{:S(2)}, u32[]{:S(2)}) collective-permute-start(bf16[2,8,32,1024]{3,2,1,0:T(8,128)(2,1)} %pad_maximum_fusion), channel_id=1, source_target_pairs={{0,1},{1,2},{2,3},{3,4},{4,5},{5,6},{6,7},{8,9},{9,10},{10,11},{11... | collective-permute-start | bytes 3145736 | tf_op jit(solution)/shard_map/ppermute | solution.py:22
  6.9 45.2 %collective-permute-start.2 = (bf16[2,8,32,1024]{3,2,1,0:T(8,128)(2,1)}, bf16[2,8,32,1024]{3,2,1,0:T(8,128)(2,1)}, u32[]{:S(2)}, u32[]{:S(2)}) collective-permute-start(bf16[2,8,32,1024]{3,2,1,0:T(8,128)(2,1)} %pad_maximum_fusion), channel_id=1, source_target_pairs={{1,0},{2,1},{3,2},{4,3},{5,4},{6,5},{7,6},{9,8},{10,9},{11,10},{12... | collective-permute-start | bytes 3145736 | tf_op jit(solution)/shard_map/ppermute | solution.py:22
  11.0 41.2 %collective-permute-start = (bf16[2,8,16,1024]{3,2,1,0:T(8,128)(2,1)}, bf16[2,8,16,1024]{3,2,1,0:T(8,128)(2,1)}, u32[]{:S(2)}, u32[]{:S(2)}) collective-permute-start(bf16[2,8,16,1024]{3,2,1,0:T(8,128)(2,1)} %get-tuple-element.42), channel_id=1, source_target_pairs={{0,2},{1,3},{2,4},{3,5},{4,6},{5,7},{8,10},{9,11},{10,12},{11,13},... | collective-permute-start | bytes 1572872 | tf_op jit(solution)/shard_map/ppermute | solution.py:22
  17.1 35.0 %collective-permute-start.3 = (bf16[2,8,16,1024]{3,2,1,0:T(8,128)(2,1)}, bf16[2,8,16,1024]{3,2,1,0:T(8,128)(2,1)}, u32[]{:S(2)}, u32[]{:S(2)}) collective-permute-start(bf16[2,8,16,1024]{3,2,1,0:T(8,128)(2,1)} %get-tuple-element.41), channel_id=1, source_target_pairs={{2,0},{3,1},{4,2},{5,3},{6,4},{7,5},{10,8},{11,9},{12,10},{13,11},... | collective-permute-start | bytes 1572872 | tf_op jit(solution)/shard_map/ppermute | solution.py:22
  21.2 4.5 %copy-start.7 = (s32[8,16]{1,0:T(8,128)S(1)}, s32[8,16]{1,0:T(8,128)}, u32[]{:S(2)}) copy-start(s32[8,16]{1,0:T(8,128)} %param.14) | copy-start | bytes 1540
  21.2 4.8 %copy-start.8 = (s32[8]{0:T(128)S(1)}, s32[8]{0:T(128)}, u32[]{:S(2)}) copy-start(s32[8]{0:T(128)} %param.15) | copy-start | bytes 100
  21.2 124.6 %all-to-all-start = ((bf16[4,32,8,1024]{3,2,0,1:T(8,128)(2,1)}), bf16[4,32,8,1024]{3,2,0,1:T(8,128)(2,1)S(1)}, u32[]{:S(2)}, u32[]{:S(2)}) async-start(bf16[4,32,8,1024]{3,2,0,1:T(8,128)(2,1)} %copy.15), calls=%async_computation | async-start | bytes 4194304 | tf_op jit(solution)/shard_map/all_to_all | solution.py:171
  130.9 70.5 %collective-permute-start.5 = (bf16[2,8,32,1024]{3,2,1,0:T(8,128)(2,1)}, bf16[2,8,32,1024]{3,2,1,0:T(8,128)(2,1)S(1)}, u32[]{:S(2)}, u32[]{:S(2)}) collective-permute-start(bf16[2,8,32,1024]{3,2,1,0:T(8,128)(2,1)} %get-tuple-element.36), channel_id=1, source_target_pairs={{1,0},{2,1},{3,2},{4,3},{5,4},{6,5},{7,6},{9,8},{10,9},{11,10},{12... | collective-permute-start | bytes 3145736 | tf_op jit(solution)/shard_map/ppermute | solution.py:22
  138.5 64.3 %collective-permute-start.6 = (bf16[2,8,32,1024]{3,2,1,0:T(8,128)(2,1)}, bf16[2,8,32,1024]{3,2,1,0:T(8,128)(2,1)}, u32[]{:S(2)}, u32[]{:S(2)}) collective-permute-start(bf16[2,8,32,1024]{3,2,1,0:T(8,128)(2,1)} %get-tuple-element.37), channel_id=1, source_target_pairs={{0,1},{1,2},{2,3},{3,4},{4,5},{5,6},{6,7},{8,9},{9,10},{10,11},{11... | collective-permute-start | bytes 3145736 | tf_op jit(solution)/shard_map/ppermute | solution.py:22
  144.5 55.6 %collective-permute-start.4 = (bf16[2,8,16,1024]{3,2,1,0:T(8,128)(2,1)}, bf16[2,8,16,1024]{3,2,1,0:T(8,128)(2,1)}, u32[]{:S(2)}, u32[]{:S(2)}) collective-permute-start(bf16[2,8,16,1024]{3,2,1,0:T(8,128)(2,1)} %get-tuple-element.35), channel_id=1, source_target_pairs={{2,0},{3,1},{4,2},{5,3},{6,4},{7,5},{10,8},{11,9},{12,10},{13,11},... | collective-permute-start | bytes 1572872 | tf_op jit(solution)/shard_map/ppermute | solution.py:22
  190.2 9.9 %copy-start.2 = (f32[2,8,32,1024]{3,2,1,0:T(8,128)S(1)}, f32[2,8,32,1024]{3,2,1,0:T(8,128)}, u32[]{:S(2)}) copy-start(f32[2,8,32,1024]{3,2,1,0:T(8,128)} %get-tuple-element.34) | copy-start | bytes 6291460
  190.2 33.6 %all-to-all-start.1 = ((bf16[3,4,64,1024]{3,1,0,2:T(4,128)(2,1)}), bf16[3,4,64,1024]{3,1,0,2:T(4,128)(2,1)}, u32[]{:S(2)}, u32[]{:S(2)}) async-start(bf16[3,4,64,1024]{3,1,0,2:T(4,128)(2,1)} %copy.17), calls=%async_computation.1 | async-start | bytes 3145728 | tf_op jit(solution)/shard_map/all_to_all | solution.py:183
  194.6 28.9 %collective-permute-start.7 = (bf16[2,8,16,1024]{3,2,1,0:T(8,128)(2,1)}, bf16[2,8,16,1024]{3,2,1,0:T(8,128)(2,1)S(1)}, u32[]{:S(2)}, u32[]{:S(2)}) collective-permute-start(bf16[2,8,16,1024]{3,2,1,0:T(8,128)(2,1)} %get-tuple-element.38), channel_id=1, source_target_pairs={{0,2},{1,3},{2,4},{3,5},{4,6},{5,7},{8,10},{9,11},{10,12},{11,13},... | collective-permute-start | bytes 1572872 | tf_op jit(solution)/shard_map/ppermute | solution.py:22
  201.4 1.4 copy-start.3
  232.6 2.9 %copy-start.6 = (f32[8,32,1024]{2,1,0:T(8,128)S(1)}, f32[8,32,1024]{2,1,0:T(8,128)}, u32[]{:S(2)}) copy-start(f32[8,32,1024]{2,1,0:T(8,128)} %get-tuple-element.33) | copy-start | bytes 3145732
where the time goes:
time: 240 us; the launch traced here: 238 us
  Pallas kernels  118 us (49%)
  waiting for transfers between devices  43.7 us (18%)
  starting transfers between devices  43.4 us (18%)
  other arithmetic  17.7 us (7%)
  local copies, waits for them, and re-layouts  14.2 us (6%)
    pallas_call x1, Pallas kernels, row_attention(): pl.pallas_call(row_kernel, grid=(rows,), in_specs=[one(queries.shape), on...  78.7 us
    ppermute x8, waiting for transfers between devices, shifted(): return lax.ppermute(block, axis, route)  43.7 us
    pallas_call x1, Pallas kernels, column_attention(): pl.pallas_call(column_kernel, grid=(strip,), in_specs=[pl.BlockSpec((arra...  39 us
    ppermute x8, starting transfers between devices, shifted(): return lax.ppermute(block, axis, route)  34.5 us
    convert_element_type x1, local copies, waits for them, and re-layouts, body(): back = back.transpose(0, 2, 1, 3).astype(f32)  4.9 us
  transfers between devices with their start and end apart: 10, of which 2 were waited for; matrix products, arithmetic and copies ran while one was open for 6% of the time, Pallas kernels for 50%

commit v1 on v0

--- a/solution.py
+++ b/solution.py
@@ -30,30 +30,42 @@
     return lax.dot_general(a, b, (((0,), (0,)), ((), ())), preferred_element_type=jnp.float32)
 
 
-def pair_grads(q2, k2, v2, g2, bias):
+def head_stack(x, heads):
+    rows, width = x.shape
+    lane_head = lax.broadcasted_iota(jnp.int32, (heads, 1, width), 2) // HD
+    which = lax.broadcasted_iota(jnp.int32, (heads, 1, width), 0)
+    kept = jnp.where(lane_head == which, x[None], jnp.zeros_like(x)[None])
+    return kept.reshape(heads * rows, width)
+
+
+def block_grads(q, g, k, v, bias):
+    nq, width = q.shape
+    heads = width // HD
+    qm = head_stack(q, heads)
+    gm = head_stack(g, heads)
+    full_bias = jnp.broadcast_to(bias[None], (heads,) + bias.shape).reshape(heads * nq, -1)
+    s = dot_nt(qm, k) * SCALE + full_bias
+    mx = jnp.max(s, axis=1, keepdims=True)
+    e = jnp.exp(s - mx)
+    p = e / jnp.sum(e, axis=1, keepdims=True)
+    pb = p.astype(jnp.bfloat16)
+    gw = dot_nt(gm, v)
+    delta = jnp.sum(pb.astype(jnp.float32) * gw, axis=1, keepdims=True)
+    ds = (p * (gw - delta)).astype(jnp.bfloat16)
+    dk = dot_tn(ds, qm) * SCALE
+    dv = dot_tn(pb, gm)
     lane = lax.broadcasted_iota(jnp.int32, (1, LANES), 1)
     low = lane < HD
-    zero = jnp.zeros_like(q2)
-    parts = []
-    for keep in (low, jnp.logical_not(low)):
-        qh = jnp.where(keep, q2, zero)
-        gh = jnp.where(keep, g2, zero)
-        s = dot_nt(qh, k2) * SCALE
-        if bias is not None:
-            s = s + bias
-        mx = jnp.max(s, axis=1, keepdims=True)
-        e = jnp.exp(s - mx)
-        p = e / jnp.sum(e, axis=1, keepdims=True)
-        pb = p.astype(jnp.bfloat16)
-        o = jnp.dot(pb, v2, preferred_element_type=jnp.float32)
-        delta = jnp.sum(gh.astype(jnp.float32) * o, axis=1, keepdims=True)
-        gw = dot_nt(gh, v2)
-        ds = (p * (gw - delta)).astype(jnp.bfloat16)
-        dq = jnp.dot(ds, k2, preferred_element_type=jnp.float32) * SCALE
-        dk = dot_tn(ds, q2) * SCALE
-        dv = dot_tn(pb, g2)
-        parts.append((dq, dk, dv))
-    return tuple(jnp.where(low, a, b) for a, b in zip(parts[0], parts[1]))
+    tiles = []
+    for pair in range(width // LANES):
+        both = jnp.dot(
+            ds[2 * pair * nq:(2 * pair + 2) * nq],
+            k[:, pair * LANES:(pair + 1) * LANES],
+            preferred_element_type=jnp.float32,
+        )
+        tiles.append(jnp.where(low, both[:nq], both[nq:]) * SCALE)
+    dq = jnp.concatenate(tiles, axis=1)
+    return dq, dk, dv
 
 
 def row_kernel(q_ref, g_ref, k_ref, v_ref, l2_ref, l1_ref, r1_ref, r2_ref, bias_ref,
@@ -61,27 +73,21 @@
     w2 = l2_ref.shape[2]
     w1 = l1_ref.shape[2]
     cc = q_ref.shape[1]
-    bias = bias_ref[0]
-    for pair in range(q_ref.shape[2] // LANES):
-        lanes = pl.ds(pair * LANES, LANES)
-
-        def span(which, own_ref):
-            return jnp.concatenate(
-                [l2_ref[which, 0, :, lanes], l1_ref[which, 0, :, lanes], own_ref[0, :, lanes],
-                 r1_ref[which, 0, :, lanes], r2_ref[which, 0, :, lanes]],
-                axis=0,
-            )
-
-        k2 = span(0, k_ref)
-        v2 = span(1, v_ref)
-        dq, dk, dv = pair_grads(q_ref[0, :, lanes], k2, v2, g_ref[0, :, lanes], bias)
-        dq_ref[0, :, lanes] = dq
-        for which, full in ((0, dk), (1, dv)):
-            ol2_ref[which, 0, :, lanes] = full[:w2].astype(jnp.bfloat16)
-            ol1_ref[which, 0, :, lanes] = full[w2:w2 + w1].astype(jnp.bfloat16)
-            own_ref[which, 0, :, lanes] = full[w2 + w1:w2 + w1 + cc]
-            or1_ref[which, 0, :, lanes] = full[w2 + w1 + cc:w2 + 2 * w1 + cc].astype(jnp.bfloat16)
-            or2_ref[which, 0, :, lanes] = full[w2 + 2 * w1 + cc:].astype(jnp.bfloat16)
+
+    def span(which, own_ref):
+        return jnp.concatenate(
+            [l2_ref[which, 0], l1_ref[which, 0], own_ref[0], r1_ref[which, 0], r2_ref[which, 0]],
+            axis=0,
+        )
+
+    dq, dk, dv = block_grads(q_ref[0], g_ref[0], span(0, k_ref), span(1, v_ref), bias_ref[0])
+    dq_ref[0] = dq
+    for which, full in ((0, dk), (1, dv)):
+        ol2_ref[which, 0] = full[:w2].astype(jnp.bfloat16)
+        ol1_ref[which, 0] = full[w2:w2 + w1].astype(jnp.bfloat16)
+        own_ref[which, 0] = full[w2 + w1:w2 + w1 + cc]
+        or1_ref[which, 0] = full[w2 + w1 + cc:w2 + 2 * w1 + cc].astype(jnp.bfloat16)
+        or2_ref[which, 0] = full[w2 + 2 * w1 + cc:].astype(jnp.bfloat16)
 
 
 def row_attention(queries, out_grad, key_grid, value_grid, l2, l1, r1, r2, bias):
@@ -115,24 +121,29 @@
 
 
 def column_kernel(x_ref, o_ref):
-    for pair in range(x_ref.shape[3] // LANES):
-        lanes = pl.ds(pair * LANES, LANES)
-        dq, dk, dv = pair_grads(
-            x_ref[0, 0, :, lanes], x_ref[1, 0, :, lanes], x_ref[2, 0, :, lanes],
-            x_ref[3, 0, :, lanes], None,
-        )
-        o_ref[0, 0, :, lanes] = dq.astype(jnp.bfloat16)
-        o_ref[1, 0, :, lanes] = dk.astype(jnp.bfloat16)
-        o_ref[2, 0, :, lanes] = dv.astype(jnp.bfloat16)
+    per = x_ref.shape[1]
+    rows = x_ref.shape[2]
+
+    def joined(which):
+        return jnp.concatenate([x_ref[which, c] for c in range(per)], axis=0)
+
+    i = lax.broadcasted_iota(jnp.int32, (per * rows, per * rows), 0) // rows
+    j = lax.broadcasted_iota(jnp.int32, (per * rows, per * rows), 1) // rows
+    bias = jnp.where(i == j, 0.0, -jnp.inf).astype(jnp.float32)
+    grads = block_grads(joined(0), joined(3), joined(1), joined(2), bias)
+    for which, full in enumerate(grads):
+        for c in range(per):
+            o_ref[which, c] = full[c * rows:(c + 1) * rows].astype(jnp.bfloat16)
 
 
 def column_attention(whole):
     arrays, strip, rows, width = whole.shape
+    per = max(1, LANES // rows)
     return pl.pallas_call(
         column_kernel,
-        grid=(strip,),
-        in_specs=[pl.BlockSpec((arrays, 1, rows, width), lambda c: (0, c, 0, 0))],
-        out_specs=pl.BlockSpec((3, 1, rows, width), lambda c: (0, c, 0, 0)),
+        grid=(strip // per,),
+        in_specs=[pl.BlockSpec((arrays, per, rows, width), lambda c: (0, c, 0, 0))],
+        out_specs=pl.BlockSpec((3, per, rows, width), lambda c: (0, c, 0, 0)),
         out_shape=jax.ShapeDtypeStruct((3, strip, rows, width), jnp.bfloat16),
     )(whole)
 

time: 240 us -> 147 us (0.61)
  Pallas kernels: 118 us -> 25.1 us
    pallas_call x1, Pallas kernels: 78.7 us -> 14.2 us  [row_attention(): pl.pallas_call(row_kernel, grid=(rows,), in_specs=[one(queries.shape), on...]
    pallas_call x1, Pallas kernels: 39 us -> 10.9 us  [column_attention(): pl.pallas_call(column_kernel, grid=(strip // per,), in_specs=[pl.BlockSpe...]
  transfers between devices with their start and end apart: 10 -> 10, of which waited for: 2 -> 3; matrix products, arithmetic and copies ran while one was open for 6% -> 10% of each run, Pallas kernels for 50% -> 17%
where the time goes in v1:
time: 147 us; the launch traced here: 145 us
  starting transfers between devices  43.6 us (30%)
  waiting for transfers between devices  43.6 us (30%)
  Pallas kernels  25.1 us (17%)
  other arithmetic  17.7 us (12%)
  local copies, waits for them, and re-layouts  14.2 us (10%)
    ppermute x8, waiting for transfers between devices, shifted(): return lax.ppermute(block, axis, route)  43.6 us
    ppermute x8, starting transfers between devices, shifted(): return lax.ppermute(block, axis, route)  34.7 us
    pallas_call x1, Pallas kernels, row_attention(): pl.pallas_call(row_kernel, grid=(rows,), in_specs=[one(queries.shape), on...  14.2 us
    pallas_call x1, Pallas kernels, column_attention(): pl.pallas_call(column_kernel, grid=(strip // per,), in_specs=[pl.BlockSpe...  10.9 us
    convert_element_type x1, local copies, waits for them, and re-layouts, body(): back = back.transpose(0, 2, 1, 3).astype(f32)  4.9 us
    all_to_all x1, starting transfers between devices, body(): lax.all_to_all(stacked, 'rrow', split_axis=1, concat_axis=2, tiled=True)  4.43 us
    all_to_all x1, starting transfers between devices, body(): lax.all_to_all(col_out, 'rrow', split_axis=2, concat_axis=1, tiled=True)  4.43 us
    convert_element_type x1, other arithmetic, body(): back = back.transpose(0, 2, 1, 3).astype(f32)  3.96 us
  transfers between devices with their start and end apart: 10, of which 3 were waited for; matrix products, arithmetic and copies ran while one was open for 10% of the time, Pallas kernels for 17%

profile of v1, /device:TPU:48, one launch (start us, length us, event | category | flops | bytes accessed | tf_op | source)
XLA Modules:
  0.0 145.1 jit_solution(14086320710407394073)
XLA Ops:
  0.7 2.4 %pad_maximum_fusion = bf16[2,8,32,1024]{3,2,1,0:T(8,128)(2,1)} fusion(bf16[1,8,32,1024]{3,2,1,0:T(8,128)(2,1)} %bitcast.36, bf16[1,8,32,1024]{3,2,1,0:T(8,128)(2,1)} %bitcast.33), kind=kLoop, calls=%fused_computation.6 | loop fusion | flops 524288 | bytes 2097152 | tf_op jit(solution)/shard_map/stack | solution.py:184
  3.1 3.8 %collective-permute-start.1 = (bf16[2,8,32,1024]{3,2,1,0:T(8,128)(2,1)}, bf16[2,8,32,1024]{3,2,1,0:T(8,128)(2,1)}, u32[]{:S(2)}, u32[]{:S(2)}) collective-permute-start(bf16[2,8,32,1024]{3,2,1,0:T(8,128)(2,1)} %pad_maximum_fusion), channel_id=1, source_target_pairs={{0,1},{1,2},{2,3},{3,4},{4,5},{5,6},{6,7},{8,9},{9,10},{10,11},{11... | collective-permute-start | bytes 3145736 | tf_op jit(solution)/shard_map/ppermute | solution.py:22
  6.9 3.0 %collective-permute-start.2 = (bf16[2,8,32,1024]{3,2,1,0:T(8,128)(2,1)}, bf16[2,8,32,1024]{3,2,1,0:T(8,128)(2,1)}, u32[]{:S(2)}, u32[]{:S(2)}) collective-permute-start(bf16[2,8,32,1024]{3,2,1,0:T(8,128)(2,1)} %pad_maximum_fusion), channel_id=1, source_target_pairs={{1,0},{2,1},{3,2},{4,3},{5,4},{6,5},{7,6},{9,8},{10,9},{11,10},{12... | collective-permute-start | bytes 3145736 | tf_op jit(solution)/shard_map/ppermute | solution.py:22
  11.0 6.1 %collective-permute-start = (bf16[2,8,16,1024]{3,2,1,0:T(8,128)(2,1)}, bf16[2,8,16,1024]{3,2,1,0:T(8,128)(2,1)}, u32[]{:S(2)}, u32[]{:S(2)}) collective-permute-start(bf16[2,8,16,1024]{3,2,1,0:T(8,128)(2,1)} %get-tuple-element.42), channel_id=1, source_target_pairs={{0,2},{1,3},{2,4},{3,5},{4,6},{5,7},{8,10},{9,11},{10,12},{11,13},... | collective-permute-start | bytes 1572872 | tf_op jit(solution)/shard_map/ppermute | solution.py:22
  18.7 2.5 %copy.15 = bf16[4,32,8,1024]{3,2,0,1:T(8,128)(2,1)} copy(bf16[4,32,8,1024]{3,1,2,0:T(8,128)(2,1)S(1)} %maximum_bitcast_fusion) | data formatting | bytes 4194304 | tf_op jit(solution)/shard_map/transpose | solution.py:181
  21.2 4.4 %all-to-all-start = ((bf16[4,32,8,1024]{3,2,0,1:T(8,128)(2,1)}), bf16[4,32,8,1024]{3,2,0,1:T(8,128)(2,1)S(1)}, u32[]{:S(2)}, u32[]{:S(2)}) async-start(bf16[4,32,8,1024]{3,2,0,1:T(8,128)(2,1)} %copy.15), calls=%async_computation | async-start | bytes 4194304 | tf_op jit(solution)/shard_map/all_to_all | solution.py:182
  26.8 25.4 %collective-permute-done.l2_ref = bf16[2,8,16,1024]{3,2,1,0:T(8,128)(2,1)} collective-permute-done((bf16[2,8,16,1024]{3,2,1,0:T(8,128)(2,1)}, bf16[2,8,16,1024]{3,2,1,0:T(8,128)(2,1)}, u32[]{:S(2)}, u32[]{:S(2)}) %collective-permute-start) | collective-permute-done | bytes 524320 | tf_op jit(solution)/shard_map/ppermute | solution.py:22
  52.2 14.2 %shard_map.85 = (f32[8,32,1024]{2,1,0:T(8,128)}, f32[2,8,32,1024]{3,2,1,0:T(8,128)}, bf16[2,8,16,1024]{3,2,1,0:T(8,128)(2,1)}, bf16[2,8,32,1024]{3,2,1,0:T(8,128...) custom-call(bf16[8,32,1024]{2,1,0:T(8,128)(2,1)} %q_ref.1, bf16[8,32,1024]{2,1,0:T(8,128)(2,1)} %g_ref.1, ...), custom_call_target="tpu_custom_call" | custom-call | tf_op jit(solution)/shard_map/pallas_call | solution.py:112
  66.4 7.6 %collective-permute-start.5 = (bf16[2,8,32,1024]{3,2,1,0:T(8,128)(2,1)}, bf16[2,8,32,1024]{3,2,1,0:T(8,128)(2,1)S(1)}, u32[]{:S(2)}, u32[]{:S(2)}) collective-permute-start(bf16[2,8,32,1024]{3,2,1,0:T(8,128)(2,1)} %get-tuple-element.36), channel_id=1, source_target_pairs={{1,0},{2,1},{3,2},{4,3},{5,4},{6,5},{7,6},{9,8},{10,9},{11,10},{12... | collective-permute-start | bytes 3145736 | tf_op jit(solution)/shard_map/ppermute | solution.py:22
  74.0 6.0 %collective-permute-start.6 = (bf16[2,8,32,1024]{3,2,1,0:T(8,128)(2,1)}, bf16[2,8,32,1024]{3,2,1,0:T(8,128)(2,1)}, u32[]{:S(2)}, u32[]{:S(2)}) collective-permute-start(bf16[2,8,32,1024]{3,2,1,0:T(8,128)(2,1)} %get-tuple-element.37), channel_id=1, source_target_pairs={{0,1},{1,2},{2,3},{3,4},{4,5},{5,6},{6,7},{8,9},{9,10},{10,11},{11... | collective-permute-start | bytes 3145736 | tf_op jit(solution)/shard_map/ppermute | solution.py:22
  81.3 1.5 %copy.21 = bf16[4,8,4,8,1024]{4,3,1,2,0:T(8,128)(2,1)} copy(bf16[4,8,4,8,1024]{4,3,0,2,1:T(8,128)(2,1)S(1)} %bitcast.32) | data formatting | bytes 4194304 | tf_op jit(solution)/shard_map/all_to_all | solution.py:182
  82.8 10.9 %shard_map.86 = bf16[3,4,64,1024]{3,2,1,0:T(8,128)(2,1)} custom-call(bf16[4,4,64,1024]{3,2,1,0:T(8,128)(2,1)} %bitcast.31), custom_call_target="tpu_custom_call" | custom-call | tf_op jit(solution)/shard_map/pallas_call | solution.py:142
  93.7 3.9 %copy.17 = bf16[3,4,64,1024]{3,1,0,2:T(4,128)(2,1)} copy(bf16[3,4,64,1024]{3,2,1,0:T(8,128)(2,1)} %shard_map.86) | data formatting | bytes 3145728 | tf_op jit(solution)/shard_map/pallas_call | solution.py:142
  97.6 4.4 %all-to-all-start.1 = ((bf16[3,4,64,1024]{3,1,0,2:T(4,128)(2,1)}), bf16[3,4,64,1024]{3,1,0,2:T(4,128)(2,1)}, u32[]{:S(2)}, u32[]{:S(2)}) async-start(bf16[3,4,64,1024]{3,1,0,2:T(4,128)(2,1)} %copy.17), calls=%async_computation.1 | async-start | bytes 3145728 | tf_op jit(solution)/shard_map/all_to_all | solution.py:194
  102.0 5.7 %collective-permute-start.7 = (bf16[2,8,16,1024]{3,2,1,0:T(8,128)(2,1)}, bf16[2,8,16,1024]{3,2,1,0:T(8,128)(2,1)S(1)}, u32[]{:S(2)}, u32[]{:S(2)}) collective-permute-start(bf16[2,8,16,1024]{3,2,1,0:T(8,128)(2,1)} %get-tuple-element.38), channel_id=1, source_target_pairs={{0,2},{1,3},{2,4},{3,5},{4,6},{5,7},{8,10},{9,11},{10,12},{11,13},... | collective-permute-start | bytes 1572872 | tf_op jit(solution)/shard_map/ppermute | solution.py:22
  107.6 16.4 %collective-permute-done.4 = bf16[2,8,16,1024]{3,2,1,0:T(8,128)(2,1)} collective-permute-done((bf16[2,8,16,1024]{3,2,1,0:T(8,128)(2,1)}, bf16[2,8,16,1024]{3,2,1,0:T(8,128)(2,1)}, u32[]{:S(2)}, u32[]{:S(2)}) %collective-permute-start.4) | collective-permute-done | bytes 524320 | tf_op jit(solution)/shard_map/ppermute | solution.py:22
  124.0 1.3 add_dynamic-update-slice_fusion
  125.3 1.3 copy-done.3
  126.7 2.4 %convert_add_fusion = f32[2,8,32,1024]{3,2,1,0:T(8,128)S(1)} fusion(bf16[2,8,32,1024]{3,2,1,0:T(8,128)(2,1)} %collective-permute-done.6, f32[2,8,32,1024]{3,2,1,0:T(8,128)} %copy-done.3, bf16[2,8,32,1024]{3,2,1,0:T(8,128)(2,1)S(1)} %collective-permute-done.5), kind=kLoop, calls=%fused_computation.3 | loop fusion | flops 2097152 | bytes 6291456 | tf_op jit(solution)/shard_map/add | solution.py:207
  129.1 1.8 %collective-permute-done.7 = bf16[2,8,16,1024]{3,2,1,0:T(8,128)(2,1)S(1)} collective-permute-done((bf16[2,8,16,1024]{3,2,1,0:T(8,128)(2,1)}, bf16[2,8,16,1024]{3,2,1,0:T(8,128)(2,1)S(1)}, u32[]{:S(2)}, u32[]{:S(2)}) %collective-permute-start.7) | collective-permute-done | bytes 524320 | tf_op jit(solution)/shard_map/ppermute | solution.py:22
  131.1 4.0 %copy_bitcast_fusion = f32[3,8,4,8,1024]{4,2,1,3,0:T(4,128)} fusion(bf16[3,4,8,8,1024]{4,1,0,3,2:T(4,128)(2,1)} %bitcast.15), kind=kLoop, calls=%fused_computation | loop fusion | flops 786432 | bytes 4718592 | tf_op jit(solution)/shard_map/convert_element_type | solution.py:209
  135.1 4.9 %reshape.281 = f32[3,32,8,1024]{3,1,2,0:T(8,128)} reshape(f32[3,8,4,8,1024]{4,2,1,3,0:T(4,128)} %copy_bitcast_fusion) | data formatting | bytes 6291456 | tf_op jit(solution)/shard_map/convert_element_type | solution.py:209
  140.0 2.9 %fusion.6 = (bf16[8,32,1024]{2,1,0:T(8,128)(2,1)}, bf16[8,32,1024]{2,1,0:T(8,128)(2,1)}) fusion(f32[3,8,32,1024]{3,2,1,0:T(8,128)} %bitcast.29, f32[2,8,32,1024]{3,2,1,0:T(8,128)S(1)} %fusion.2), kind=kLoop, calls=%fused_computation.20 | loop fusion | flops 1048576 | bytes 5242880 | tf_op jit(solution)/shard_map/convert_element_type | solution.py:212
  142.9 2.2 %fusion.4 = bf16[8,32,1024]{2,1,0:T(8,128)(2,1)} fusion(f32[8,32,1024]{2,1,0:T(8,128)S(1)} %copy-done.6, f32[3,8,32,1024]{3,2,1,0:T(8,128)} %bitcast.30), kind=kLoop, calls=%fused_computation.17 | loop fusion | flops 524288 | bytes 2621440 | tf_op jit(solution)/shard_map/convert_element_type | solution.py:210
  (39 shorter events, 5.3 us)
Async XLA Ops:
  0.6 9.3 %copy-start = (bf16[8,32,1024]{2,1,0:T(8,128)(2,1)S(1)}, bf16[8,32,1024]{2,1,0:T(8,128)(2,1)}, u32[]{:S(2)}) copy-start(bf16[8,32,1024]{2,1,0:T(8,128)(2,1)} %k_ref.1) | copy-start | bytes 1572868
  0.6 9.3 %copy-start.1 = (bf16[8,32,1024]{2,1,0:T(8,128)(2,1)S(1)}, bf16[8,32,1024]{2,1,0:T(8,128)(2,1)}, u32[]{:S(2)}) copy-start(bf16[8,32,1024]{2,1,0:T(8,128)(2,1)} %v_ref.1) | copy-start | bytes 1572868
  0.7 17.8 %copy-start.4 = (bf16[8,32,1024]{2,1,0:T(8,128)(2,1)S(1)}, bf16[8,32,1024]{2,1,0:T(8,128)(2,1)}, u32[]{:S(2)}) copy-start(bf16[8,32,1024]{2,1,0:T(8,128)(2,1)} %q_ref.1) | copy-start | bytes 1572868
  0.7 17.8 %copy-start.5 = (bf16[8,32,1024]{2,1,0:T(8,128)(2,1)S(1)}, bf16[8,32,1024]{2,1,0:T(8,128)(2,1)}, u32[]{:S(2)}) copy-start(bf16[8,32,1024]{2,1,0:T(8,128)(2,1)} %g_ref.1) | copy-start | bytes 1572868
  3.1 49.1 %collective-permute-start.1 = (bf16[2,8,32,1024]{3,2,1,0:T(8,128)(2,1)}, bf16[2,8,32,1024]{3,2,1,0:T(8,128)(2,1)}, u32[]{:S(2)}, u32[]{:S(2)}) collective-permute-start(bf16[2,8,32,1024]{3,2,1,0:T(8,128)(2,1)} %pad_maximum_fusion), channel_id=1, source_target_pairs={{0,1},{1,2},{2,3},{3,4},{4,5},{5,6},{6,7},{8,9},{9,10},{10,11},{11... | collective-permute-start | bytes 3145736 | tf_op jit(solution)/shard_map/ppermute | solution.py:22
  6.9 45.2 %collective-permute-start.2 = (bf16[2,8,32,1024]{3,2,1,0:T(8,128)(2,1)}, bf16[2,8,32,1024]{3,2,1,0:T(8,128)(2,1)}, u32[]{:S(2)}, u32[]{:S(2)}) collective-permute-start(bf16[2,8,32,1024]{3,2,1,0:T(8,128)(2,1)} %pad_maximum_fusion), channel_id=1, source_target_pairs={{1,0},{2,1},{3,2},{4,3},{5,4},{6,5},{7,6},{9,8},{10,9},{11,10},{12... | collective-permute-start | bytes 3145736 | tf_op jit(solution)/shard_map/ppermute | solution.py:22
  11.0 41.2 %collective-permute-start = (bf16[2,8,16,1024]{3,2,1,0:T(8,128)(2,1)}, bf16[2,8,16,1024]{3,2,1,0:T(8,128)(2,1)}, u32[]{:S(2)}, u32[]{:S(2)}) collective-permute-start(bf16[2,8,16,1024]{3,2,1,0:T(8,128)(2,1)} %get-tuple-element.42), channel_id=1, source_target_pairs={{0,2},{1,3},{2,4},{3,5},{4,6},{5,7},{8,10},{9,11},{10,12},{11,13},... | collective-permute-start | bytes 1572872 | tf_op jit(solution)/shard_map/ppermute | solution.py:22
  17.1 35.0 %collective-permute-start.3 = (bf16[2,8,16,1024]{3,2,1,0:T(8,128)(2,1)}, bf16[2,8,16,1024]{3,2,1,0:T(8,128)(2,1)}, u32[]{:S(2)}, u32[]{:S(2)}) collective-permute-start(bf16[2,8,16,1024]{3,2,1,0:T(8,128)(2,1)} %get-tuple-element.41), channel_id=1, source_target_pairs={{2,0},{3,1},{4,2},{5,3},{6,4},{7,5},{10,8},{11,9},{12,10},{13,11},... | collective-permute-start | bytes 1572872 | tf_op jit(solution)/shard_map/ppermute | solution.py:22
  21.2 4.5 %copy-start.7 = (s32[8,16]{1,0:T(8,128)S(1)}, s32[8,16]{1,0:T(8,128)}, u32[]{:S(2)}) copy-start(s32[8,16]{1,0:T(8,128)} %param.14) | copy-start | bytes 1540
  21.2 4.8 %copy-start.8 = (s32[8]{0:T(128)S(1)}, s32[8]{0:T(128)}, u32[]{:S(2)}) copy-start(s32[8]{0:T(128)} %param.15) | copy-start | bytes 100
  21.2 60.0 %all-to-all-start = ((bf16[4,32,8,1024]{3,2,0,1:T(8,128)(2,1)}), bf16[4,32,8,1024]{3,2,0,1:T(8,128)(2,1)S(1)}, u32[]{:S(2)}, u32[]{:S(2)}) async-start(bf16[4,32,8,1024]{3,2,0,1:T(8,128)(2,1)} %copy.15), calls=%async_computation | async-start | bytes 4194304 | tf_op jit(solution)/shard_map/all_to_all | solution.py:182
  66.4 58.9 %collective-permute-start.5 = (bf16[2,8,32,1024]{3,2,1,0:T(8,128)(2,1)}, bf16[2,8,32,1024]{3,2,1,0:T(8,128)(2,1)S(1)}, u32[]{:S(2)}, u32[]{:S(2)}) collective-permute-start(bf16[2,8,32,1024]{3,2,1,0:T(8,128)(2,1)} %get-tuple-element.36), channel_id=1, source_target_pairs={{1,0},{2,1},{3,2},{4,3},{5,4},{6,5},{7,6},{9,8},{10,9},{11,10},{12... | collective-permute-start | bytes 3145736 | tf_op jit(solution)/shard_map/ppermute | solution.py:22
  74.0 52.7 %collective-permute-start.6 = (bf16[2,8,32,1024]{3,2,1,0:T(8,128)(2,1)}, bf16[2,8,32,1024]{3,2,1,0:T(8,128)(2,1)}, u32[]{:S(2)}, u32[]{:S(2)}) collective-permute-start(bf16[2,8,32,1024]{3,2,1,0:T(8,128)(2,1)} %get-tuple-element.37), channel_id=1, source_target_pairs={{0,1},{1,2},{2,3},{3,4},{4,5},{5,6},{6,7},{8,9},{9,10},{10,11},{11... | collective-permute-start | bytes 3145736 | tf_op jit(solution)/shard_map/ppermute | solution.py:22
  80.0 44.0 %collective-permute-start.4 = (bf16[2,8,16,1024]{3,2,1,0:T(8,128)(2,1)}, bf16[2,8,16,1024]{3,2,1,0:T(8,128)(2,1)}, u32[]{:S(2)}, u32[]{:S(2)}) collective-permute-start(bf16[2,8,16,1024]{3,2,1,0:T(8,128)(2,1)} %get-tuple-element.35), channel_id=1, source_target_pairs={{2,0},{3,1},{4,2},{5,3},{6,4},{7,5},{10,8},{11,9},{12,10},{13,11},... | collective-permute-start | bytes 1572872 | tf_op jit(solution)/shard_map/ppermute | solution.py:22
  97.6 26.5 %copy-start.2 = (f32[2,8,32,1024]{3,2,1,0:T(8,128)S(1)}, f32[2,8,32,1024]{3,2,1,0:T(8,128)}, u32[]{:S(2)}) copy-start(f32[2,8,32,1024]{3,2,1,0:T(8,128)} %get-tuple-element.34) | copy-start | bytes 6291460
  97.6 33.6 %all-to-all-start.1 = ((bf16[3,4,64,1024]{3,1,0,2:T(4,128)(2,1)}), bf16[3,4,64,1024]{3,1,0,2:T(4,128)(2,1)}, u32[]{:S(2)}, u32[]{:S(2)}) async-start(bf16[3,4,64,1024]{3,1,0,2:T(4,128)(2,1)} %copy.17), calls=%async_computation.1 | async-start | bytes 3145728 | tf_op jit(solution)/shard_map/all_to_all | solution.py:194
  102.0 28.9 %collective-permute-start.7 = (bf16[2,8,16,1024]{3,2,1,0:T(8,128)(2,1)}, bf16[2,8,16,1024]{3,2,1,0:T(8,128)(2,1)S(1)}, u32[]{:S(2)}, u32[]{:S(2)}) collective-permute-start(bf16[2,8,16,1024]{3,2,1,0:T(8,128)(2,1)} %get-tuple-element.38), channel_id=1, source_target_pairs={{0,2},{1,3},{2,4},{3,5},{4,6},{5,7},{8,10},{9,11},{10,12},{11,13},... | collective-permute-start | bytes 1572872 | tf_op jit(solution)/shard_map/ppermute | solution.py:22
  125.3 1.4 copy-start.3
  140.0 2.9 %copy-start.6 = (f32[8,32,1024]{2,1,0:T(8,128)S(1)}, f32[8,32,1024]{2,1,0:T(8,128)}, u32[]{:S(2)}) copy-start(f32[8,32,1024]{2,1,0:T(8,128)} %get-tuple-element.33) | copy-start | bytes 3145732

commit v2 on v1

--- a/solution.py
+++ b/solution.py
@@ -68,64 +68,110 @@
     return dq, dk, dv
 
 
-def row_kernel(q_ref, g_ref, k_ref, v_ref, l2_ref, l1_ref, r1_ref, r2_ref, bias_ref,
-               dq_ref, own_ref, ol2_ref, ol1_ref, or1_ref, or2_ref):
+def fused_row_kernel(q_ref, g_ref, k_ref, v_ref, l2_ref, l1_ref, r1_ref, r2_ref, bias_ref, cb_ref,
+                     qg_ref, kg_ref, vg_ref,
+                     own_s, s_l2, s_l1, s_r1, s_r2, x_r2, x_r1, x_l1, x_l2, send_sem, recv_sem):
+    rows, cc, width = q_ref.shape
     w2 = l2_ref.shape[2]
     w1 = l1_ref.shape[2]
-    cc = q_ref.shape[1]
-
-    def span(which, own_ref):
-        return jnp.concatenate(
-            [l2_ref[which, 0], l1_ref[which, 0], own_ref[0], r1_ref[which, 0], r2_ref[which, 0]],
-            axis=0,
-        )
-
-    dq, dk, dv = block_grads(q_ref[0], g_ref[0], span(0, k_ref), span(1, v_ref), bias_ref[0])
-    dq_ref[0] = dq
-    for which, full in ((0, dk), (1, dv)):
-        ol2_ref[which, 0] = full[:w2].astype(jnp.bfloat16)
-        ol1_ref[which, 0] = full[w2:w2 + w1].astype(jnp.bfloat16)
-        own_ref[which, 0] = full[w2 + w1:w2 + w1 + cc]
-        or1_ref[which, 0] = full[w2 + w1 + cc:w2 + 2 * w1 + cc].astype(jnp.bfloat16)
-        or2_ref[which, 0] = full[w2 + 2 * w1 + cc:].astype(jnp.bfloat16)
-
-
-def row_attention(queries, out_grad, key_grid, value_grid, l2, l1, r1, r2, bias):
+    n = lax.axis_size("rcol")
+    me = lax.axis_index("rcol")
+    here = (lax.axis_index("slide"), lax.axis_index("rrow"))
+
+    def dev(distance):
+        return here + (lax.rem(me + distance + n, n),)
+
+    barrier = pltpu.get_barrier_semaphore()
+    for distance in (-2, -1, 1, 2):
+        pl.semaphore_signal(barrier, 1, device_id=dev(distance), device_id_type=pl.DeviceIdType.MESH)
+    pl.semaphore_wait(barrier, 4)
+
+    routes = ((s_l2, x_r2, -2), (s_l1, x_r1, -1), (s_r1, x_l1, 1), (s_r2, x_l2, 2))
+
+    def row_step(r, carry):
+        def span(which, own_ref):
+            return jnp.concatenate(
+                [l2_ref[which, r], l1_ref[which, r], own_ref[r], r1_ref[which, r],
+                 r2_ref[which, r]],
+                axis=0,
+            )
+
+        dq, dk, dv = block_grads(q_ref[r], g_ref[r], span(0, k_ref), span(1, v_ref), bias_ref[r])
+        qg_ref[r] = (dq + cb_ref[0, r].astype(jnp.float32)).astype(jnp.bfloat16)
+        for which, full in ((0, dk), (1, dv)):
+            s_l2[which, r] = full[:w2].astype(jnp.bfloat16)
+            s_l1[which, r] = full[w2:w2 + w1].astype(jnp.bfloat16)
+            own_s[which, r] = full[w2 + w1:w2 + w1 + cc]
+            s_r1[which, r] = full[w2 + w1 + cc:w2 + 2 * w1 + cc].astype(jnp.bfloat16)
+            s_r2[which, r] = full[w2 + 2 * w1 + cc:].astype(jnp.bfloat16)
+        for slot, (src, dst, distance) in enumerate(routes):
+            pltpu.make_async_remote_copy(
+                src_ref=src.at[:, pl.ds(r, 1)],
+                dst_ref=dst.at[:, pl.ds(r, 1)],
+                send_sem=send_sem.at[slot],
+                recv_sem=recv_sem.at[slot],
+                device_id=dev(distance),
+                device_id_type=pl.DeviceIdType.MESH,
+            ).start()
+        return carry
+
+    lax.fori_loop(0, rows, row_step, 0)
+    for slot, (src, dst, distance) in enumerate(routes):
+        pltpu.make_async_remote_copy(
+            src_ref=src, dst_ref=dst, send_sem=send_sem.at[slot], recv_sem=recv_sem.at[slot],
+            device_id=dev(distance), device_id_type=pl.DeviceIdType.MESH,
+        ).wait()
+    f32 = jnp.float32
+    for which, out_ref in ((0, kg_ref), (1, vg_ref)):
+        total = own_s[which] + x_r1[which].astype(f32) + x_l1[which].astype(f32)
+        total = total + cb_ref[which + 1].astype(f32)
+        low = total[:, :w2] + x_l2[which].astype(f32)
+        high = total[:, cc - w2:] + x_r2[which].astype(f32)
+        out_ref[:, :w2] = low.astype(jnp.bfloat16)
+        out_ref[:, cc - w2:] = high.astype(jnp.bfloat16)
+        if cc > 2 * w2:
+            out_ref[:, w2:cc - w2] = total[:, w2:cc - w2].astype(jnp.bfloat16)
+
+
+def fused_row(queries, out_grad, key_grid, value_grid, l2, l1, r1, r2, bias, col_back):
     rows, cc, width = queries.shape
     w2 = l2.shape[2]
     w1 = l1.shape[2]
-
-    def one(shape):
-        return pl.BlockSpec((1,) + shape[1:], lambda r: (r,) + (0,) * (len(shape) - 1))
-
-    def two(shape):
-        return pl.BlockSpec((shape[0], 1) + shape[2:], lambda r: (0, r) + (0,) * (len(shape) - 2))
-
-    out_shape = (
-        jax.ShapeDtypeStruct((rows, cc, width), jnp.float32),
-        jax.ShapeDtypeStruct((2, rows, cc, width), jnp.float32),
-        jax.ShapeDtypeStruct((2, rows, w2, width), jnp.bfloat16),
-        jax.ShapeDtypeStruct((2, rows, w1, width), jnp.bfloat16),
-        jax.ShapeDtypeStruct((2, rows, w1, width), jnp.bfloat16),
-        jax.ShapeDtypeStruct((2, rows, w2, width), jnp.bfloat16),
-    )
+    vmem = pl.BlockSpec(memory_space=pltpu.VMEM)
+    grads = jax.ShapeDtypeStruct((rows, cc, width), jnp.bfloat16)
+    bf = jnp.bfloat16
     return pl.pallas_call(
-        row_kernel,
-        grid=(rows,),
-        in_specs=[one(queries.shape), one(out_grad.shape), one(key_grid.shape),
-                  one(value_grid.shape), two(l2.shape), two(l1.shape), two(r1.shape),
-                  two(r2.shape), one(bias.shape)],
-        out_specs=[one(out_shape[0].shape)] + [two(s.shape) for s in out_shape[1:]],
-        out_shape=out_shape,
-    )(queries, out_grad, key_grid, value_grid, l2, l1, r1, r2, bias)
-
-
-def column_kernel(x_ref, o_ref):
-    per = x_ref.shape[1]
-    rows = x_ref.shape[2]
+        fused_row_kernel,
+        in_specs=[vmem] * 10,
+        out_specs=[vmem] * 3,
+        out_shape=(grads, grads, grads),
+        scratch_shapes=[
+            pltpu.VMEM((2, rows, cc, width), jnp.float32),
+            pltpu.VMEM((2, rows, w2, width), bf),
+            pltpu.VMEM((2, rows, w1, width), bf),
+            pltpu.VMEM((2, rows, w1, width), bf),
+            pltpu.VMEM((2, rows, w2, width), bf),
+            pltpu.VMEM((2, rows, w2, width), bf),
+            pltpu.VMEM((2, rows, w1, width), bf),
+            pltpu.VMEM((2, rows, w1, width), bf),
+            pltpu.VMEM((2, rows, w2, width), bf),
+            pltpu.SemaphoreType.DMA((4,)),
+            pltpu.SemaphoreType.DMA((4,)),
+        ],
+        compiler_params=pltpu.CompilerParams(
+            collective_id=0, has_side_effects=True, vmem_limit_bytes=60 * 1024 * 1024
+        ),
+    )(queries, out_grad, key_grid, value_grid, l2, l1, r1, r2, bias, col_back)
+
+
+def column_kernel(width, x_ref, o_ref):
+    rows, span_width = x_ref.shape[1], x_ref.shape[2]
+    per = span_width // width
 
     def joined(which):
-        return jnp.concatenate([x_ref[which, c] for c in range(per)], axis=0)
+        return jnp.concatenate(
+            [x_ref[which, :, c * width:(c + 1) * width] for c in range(per)], axis=0
+        )
 
     i = lax.broadcasted_iota(jnp.int32, (per * rows, per * rows), 0) // rows
     j = lax.broadcasted_iota(jnp.int32, (per * rows, per * rows), 1) // rows
@@ -133,18 +179,21 @@
     grads = block_grads(joined(0), joined(3), joined(1), joined(2), bias)
     for which, full in enumerate(grads):
         for c in range(per):
-            o_ref[which, c] = full[c * rows:(c + 1) * rows].astype(jnp.bfloat16)
-
-
-def column_attention(whole):
-    arrays, strip, rows, width = whole.shape
+            o_ref[which, :, c * width:(c + 1) * width] = (
+                full[c * rows:(c + 1) * rows].astype(jnp.bfloat16)
+            )
+
+
+def column_attention(whole, width):
+    arrays, rows, lanes = whole.shape
     per = max(1, LANES // rows)
+    block = per * width
     return pl.pallas_call(
-        column_kernel,
-        grid=(strip // per,),
-        in_specs=[pl.BlockSpec((arrays, per, rows, width), lambda c: (0, c, 0, 0))],
-        out_specs=pl.BlockSpec((3, per, rows, width), lambda c: (0, c, 0, 0)),
-        out_shape=jax.ShapeDtypeStruct((3, strip, rows, width), jnp.bfloat16),
+        functools.partial(column_kernel, width),
+        grid=(lanes // block,),
+        in_specs=[pl.BlockSpec((arrays, rows, block), lambda c: (0, 0, c))],
+        out_specs=pl.BlockSpec((3, rows, block), lambda c: (0, 0, c)),
+        out_shape=jax.ShapeDtypeStruct((3, rows, lanes), jnp.bfloat16),
     )(whole)
 
 
@@ -178,8 +227,10 @@
     near = col_count
     far = band_reach - col_count
 
-    stacked = jnp.stack([queries, key_grid, value_grid, out_grad]).transpose(0, 2, 1, 3)
-    whole = lax.all_to_all(stacked, "rrow", split_axis=1, concat_axis=2, tiled=True)
+    stacked = jnp.stack([queries, key_grid, value_grid, out_grad]).reshape(
+        4, row_count, col_count * feature_width
+    )
+    whole = lax.all_to_all(stacked, "rrow", split_axis=2, concat_axis=1, tiled=True)
 
     pair = jnp.stack([key_grid, value_grid])
     l1 = shifted(pair[:, :, col_count - near:], "rcol", 1)
@@ -190,27 +241,10 @@
     first_col = lax.axis_index("rcol") * col_count
     bias = band_bias(tissue_mask, band_offset, first_col, grid_cols, col_count)
 
-    col_out = column_attention(whole)
-    back = lax.all_to_all(col_out, "rrow", split_axis=2, concat_axis=1, tiled=True)
-
-    dq_row, own, gl2, gl1, gr1, gr2 = row_attention(
-        queries, out_grad, key_grid, value_grid, l2, l1, r1, r2, bias
-    )
-    from_r2 = shifted(gl2, "rcol", -2)
-    from_r1 = shifted(gl1, "rcol", -1)
-    from_l1 = shifted(gr1, "rcol", 1)
-    from_l2 = shifted(gr2, "rcol", 2)
-    f32 = jnp.float32
-    kv = own
-    kv = kv.at[:, :, col_count - far:].add(from_r2.astype(f32))
-    kv = kv + from_r1.astype(f32)
-    kv = kv + from_l1.astype(f32)
-    kv = kv.at[:, :, :far].add(from_l2.astype(f32))
-    back = back.transpose(0, 2, 1, 3).astype(f32)
-    query_grad = (dq_row + back[0]).astype(jnp.bfloat16)
-    key_grad = (kv[0] + back[1]).astype(jnp.bfloat16)
-    value_grad = (kv[1] + back[2]).astype(jnp.bfloat16)
-    return (query_grad, key_grad, value_grad)
+    col_out = column_attention(whole, feature_width)
+    back = lax.all_to_all(col_out, "rrow", split_axis=1, concat_axis=2, tiled=True)
+    back = back.reshape(3, row_count, col_count, feature_width)
+    return fused_row(queries, out_grad, key_grid, value_grid, l2, l1, r1, r2, bias, back)
 
 
 def solution(mesh):

time: 147 us -> 311 us (2.12)
  local copies, waits for them, and re-layouts: 14.2 us -> 174 us
  Pallas kernels: 25.1 us -> 68.8 us
  starting transfers between devices: 43.6 us -> 22.5 us
  other arithmetic: 17.7 us -> 4.99 us
  waiting for transfers between devices: 43.6 us -> 36.6 us
    unnamed x18 -> x19, local copies, waits for them, and re-layouts: 1.38 us -> 86.8 us
    pallas_call x2, Pallas kernels: 25.1 us -> 68.8 us  [the longest x1 58 us: fused_row(): pl.pallas_call(fused_row_kernel, in_specs=[vmem] * 10, out_specs=[vmem] *...]
    ppermute x8 -> x4, waiting for transfers between devices: 43.6 us -> 0.01 us  [shifted(): return lax.ppermute(block, axis, route)]
    all_to_all x1 -> x2, local copies, waits for them, and re-layouts: 1.54 us -> 42.9 us  [the longest x1 40.6 us: body(): lax.all_to_all(stacked, 'rrow', split_axis=2, concat_axis=1, tiled=True)]
    another operation x0 -> x5, local copies, waits for them, and re-layouts: none -> 37 us  [body(): jnp.stack([queries, key_grid, value_grid, out_grad])]
    all_to_all x2, waiting for transfers between devices: 0.01 us -> 36.6 us  [the longest x1 25.8 us: body(): lax.all_to_all(col_out, 'rrow', split_axis=1, concat_axis=2, tiled=True)]
    ppermute x8 -> x4, starting transfers between devices: 34.7 us -> 14.2 us  [shifted(): return lax.ppermute(block, axis, route)]
    convert_element_type x3 -> x0, other arithmetic: 9.01 us -> none  [the longest x1 3.96 us: body(): back = back.transpose(0, 2, 1, 3).astype(f32)]
  transfers between devices with their start and end apart: 10 -> 6, of which waited for: 3 -> 2; matrix products, arithmetic and copies ran while one was open for 10% -> 31% of each run, Pallas kernels for 17% -> 4%
where the time goes in v2:
time: 311 us; the launch traced here: 308 us
  local copies, waits for them, and re-layouts  174 us (56%)
  Pallas kernels  68.8 us (22%)
  waiting for transfers between devices  36.6 us (12%)
  starting transfers between devices  22.5 us (7%)
  other arithmetic  4.99 us (2%)
    unnamed x19, local copies, waits for them, and re-layouts  86.8 us
    pallas_call x1, Pallas kernels, fused_row(): pl.pallas_call(fused_row_kernel, in_specs=[vmem] * 10, out_specs=[vmem] *...  58 us
    all_to_all x1, local copies, waits for them, and re-layouts, body(): lax.all_to_all(stacked, 'rrow', split_axis=2, concat_axis=1, tiled=True)  40.6 us
    another operation x5, local copies, waits for them, and re-layouts, body(): jnp.stack([queries, key_grid, value_grid, out_grad])  37 us
    all_to_all x1, waiting for transfers between devices, body(): lax.all_to_all(col_out, 'rrow', split_axis=1, concat_axis=2, tiled=True)  25.8 us
    ppermute x4, starting transfers between devices, shifted(): return lax.ppermute(block, axis, route)  14.2 us
    pallas_call x1, Pallas kernels, column_attention(): pl.pallas_call(functools.partial(column_kernel, width), grid=(lanes // bl...  10.9 us
    all_to_all x1, waiting for transfers between devices, body(): lax.all_to_all(stacked, 'rrow', split_axis=2, concat_axis=1, tiled=True)  10.8 us
  transfers between devices with their start and end apart: 6, of which 2 were waited for; matrix products, arithmetic and copies ran while one was open for 31% of the time, Pallas kernels for 4%

profile of v2, /device:TPU:48, one launch (start us, length us, event | category | flops | bytes accessed | tf_op | source)
XLA Modules:
  0.0 308.2 jit_solution(16010907599123844813)
XLA Ops:
  0.7 2.2 stack.27
  2.8 2.1 stack.30
  7.0 1.8 pad_maximum_fusion
  8.7 30.6 %copy.21 = bf16[4,8,32768]{1,0,2:T(4,128)(2,1)} copy(bf16[4,8,32768]{2,1,0:T(8,128)(2,1)S(1)} %pad_maximum_fusion) | data formatting | bytes 4194304 | tf_op jit(solution)/shard_map/stack | solution.py:230
  39.4 39.7 %reshape.217 = bf16[8,2,65536]{2,1,0:T(2,128)(2,1)} reshape(bf16[32768,4,8]{2,1,0:T(4,128)(2,1)} %bitcast.14) | data formatting | bytes 4194304
  79.1 4.3 %all-to-all-start = ((bf16[8,2,65536]{2,1,0:T(2,128)(2,1)}), bf16[8,2,65536]{2,1,0:T(2,128)(2,1)S(1)}, u32[]{:S(2)}, u32[]{:S(2)}) async-start(bf16[8,2,65536]{2,1,0:T(2,128)(2,1)} %reshape.217), calls=%async_computation | async-start | bytes 4194304 | tf_op jit(solution)/shard_map/all_to_all | solution.py:233
  83.4 1.1 pad_maximum_fusion.1
  84.5 3.8 %collective-permute-start.1 = (bf16[2,8,32,1024]{3,2,1,0:T(8,128)(2,1)}, bf16[2,8,32,1024]{3,2,1,0:T(8,128)(2,1)}, u32[]{:S(2)}, u32[]{:S(2)}) collective-permute-start(bf16[2,8,32,1024]{3,2,1,0:T(8,128)(2,1)} %pad_maximum_fusion.1), channel_id=1, source_target_pairs={{0,1},{1,2},{2,3},{3,4},{4,5},{5,6},{6,7},{8,9},{9,10},{10,11},{11... | collective-permute-start | bytes 3145736 | tf_op jit(solution)/shard_map/ppermute | solution.py:22
  88.3 3.0 collective-permute-start.2
  91.3 1.1 fusion.1
  92.3 1.3 collective-permute-start.3
  93.6 6.2 %collective-permute-start = (bf16[2,8,16,1024]{3,2,1,0:T(8,128)(2,1)}, bf16[2,8,16,1024]{3,2,1,0:T(8,128)(2,1)S(1)}, u32[]{:S(2)}, u32[]{:S(2)}) collective-permute-start(bf16[2,8,16,1024]{3,2,1,0:T(8,128)(2,1)} %get-tuple-element.4), channel_id=1, source_target_pairs={{0,2},{1,3},{2,4},{3,5},{4,6},{5,7},{8,10},{9,11},{10,12},{11,13},... | collective-permute-start | bytes 1572872 | tf_op jit(solution)/shard_map/ppermute | solution.py:22
  99.8 10.8 %all-to-all-done = bf16[8,2,65536]{2,1,0:T(2,128)(2,1)S(1)} async-done(((bf16[8,2,65536]{2,1,0:T(2,128)(2,1)}), bf16[8,2,65536]{2,1,0:T(2,128)(2,1)S(1)}, u32[]{:S(2)}, u32[]{:S(2)}) %all-to-all-start) | async-done | bytes 2097184 | tf_op jit(solution)/shard_map/all_to_all | solution.py:233
  110.6 41.5 %reshape.218 = bf16[32768,4,8]{2,1,0:T(4,128)(2,1)} reshape(bf16[8,2,65536]{2,1,0:T(2,128)(2,1)S(1)} %all-to-all-done) | data formatting | bytes 4194304
  152.1 40.6 %copy.22 = bf16[4,8,8,4096]{3,1,2,0:T(8,128)(2,1)} copy(bf16[4,8,8,4096]{1,0,3,2:T(4,128)(2,1)} %bitcast.15) | data formatting | bytes 4194304 | tf_op jit(solution)/shard_map/all_to_all | solution.py:233
  192.7 10.9 %shard_map.85 = bf16[3,64,4096]{2,1,0:T(8,128)(2,1)} custom-call(bf16[4,64,4096]{2,1,0:T(8,128)(2,1)} %bitcast.16), custom_call_target="tpu_custom_call" | custom-call | tf_op jit(solution)/shard_map/pallas_call | solution.py:191
  203.6 4.1 %copy.23 = bf16[3,64,4096]{2,0,1:T(4,128)(2,1)} copy(bf16[3,64,4096]{2,1,0:T(8,128)(2,1)} %shard_map.85) | data formatting | bytes 3145728 | tf_op jit(solution)/shard_map/pallas_call | solution.py:191
  207.7 4.0 %all-to-all-start.1 = ((bf16[3,64,4096]{2,0,1:T(4,128)(2,1)}), bf16[3,64,4096]{2,0,1:T(4,128)(2,1)S(1)}, u32[]{:S(2)}, u32[]{:S(2)}) async-start(bf16[3,64,4096]{2,0,1:T(4,128)(2,1)} %copy.23), calls=%async_computation.1 | async-start | bytes 4194304 | tf_op jit(solution)/shard_map/all_to_all | solution.py:245
  212.8 25.8 %all-to-all-done.1 = bf16[3,64,4096]{2,0,1:T(4,128)(2,1)S(1)} async-done(((bf16[3,64,4096]{2,0,1:T(4,128)(2,1)}), bf16[3,64,4096]{2,0,1:T(4,128)(2,1)S(1)}, u32[]{:S(2)}, u32[]{:S(2)}) %all-to-all-start.1) | async-done | bytes 1572896 | tf_op jit(solution)/shard_map/all_to_all | solution.py:245
  238.6 2.3 copy.26
  240.9 3.8 %reshape.216.cb_ref = bf16[3,8,32,1024]{3,2,1,0:T(8,128)(2,1)} reshape(bf16[3,8,8,4096]{3,2,1,0:T(8,128)(2,1)} %bitcast.22) | data formatting | bytes 3145728 | tf_op jit(solution)/shard_map/reshape | solution.py:246
  245.6 58.0 %shard_map.86 = (bf16[8,32,1024]{2,1,0:T(8,128)(2,1)}, bf16[8,32,1024]{2,1,0:T(8,128)(2,1)}, bf16[8,32,1024]{2,1,0:T(8,128)(2,1)}) custom-call(bf16[8,32,1024]{2,1,0:T(8,128)(2,1)} %q_ref.1, bf16[8,32,1024]{2,1,0:T(8,128)(2,1)} %g_ref.1, bf16[8,32,1024]{2,1,0:T(8,128)(2,1)} %k_ref.1, bf16[8,32,1024]{2,1,0:T(8,128)(2,1)} %v_ref.1, ...), custom_call_target="tpu_custom_call" | custom-call | tf_op jit(solution)/shard_map/pallas_call | solution.py:143
  303.6 1.9 copy.30
  305.5 1.9 copy.31
  (31 shorter events, 4.9 us)
Async XLA Ops:
  0.6 4.3 %copy-start = (bf16[8,32,1024]{2,1,0:T(8,128)(2,1)S(1)}, bf16[8,32,1024]{2,1,0:T(8,128)(2,1)}, u32[]{:S(2)}) copy-start(bf16[8,32,1024]{2,1,0:T(8,128)(2,1)} %k_ref.1) | copy-start | bytes 1572868
  0.6 5.3 %copy-start.1 = (bf16[8,32,1024]{2,1,0:T(8,128)(2,1)S(1)}, bf16[8,32,1024]{2,1,0:T(8,128)(2,1)}, u32[]{:S(2)}) copy-start(bf16[8,32,1024]{2,1,0:T(8,128)(2,1)} %v_ref.1) | copy-start | bytes 1572868
  79.1 31.5 %all-to-all-start = ((bf16[8,2,65536]{2,1,0:T(2,128)(2,1)}), bf16[8,2,65536]{2,1,0:T(2,128)(2,1)S(1)}, u32[]{:S(2)}, u32[]{:S(2)}) async-start(bf16[8,2,65536]{2,1,0:T(2,128)(2,1)} %reshape.217), calls=%async_computation | async-start | bytes 4194304 | tf_op jit(solution)/shard_map/all_to_all | solution.py:233
  84.5 160.2 %collective-permute-start.1 = (bf16[2,8,32,1024]{3,2,1,0:T(8,128)(2,1)}, bf16[2,8,32,1024]{3,2,1,0:T(8,128)(2,1)}, u32[]{:S(2)}, u32[]{:S(2)}) collective-permute-start(bf16[2,8,32,1024]{3,2,1,0:T(8,128)(2,1)} %pad_maximum_fusion.1), channel_id=1, source_target_pairs={{0,1},{1,2},{2,3},{3,4},{4,5},{5,6},{6,7},{8,9},{9,10},{10,11},{11... | collective-permute-start | bytes 3145736 | tf_op jit(solution)/shard_map/ppermute | solution.py:22
  88.3 156.4 %collective-permute-start.2 = (bf16[2,8,32,1024]{3,2,1,0:T(8,128)(2,1)}, bf16[2,8,32,1024]{3,2,1,0:T(8,128)(2,1)}, u32[]{:S(2)}, u32[]{:S(2)}) collective-permute-start(bf16[2,8,32,1024]{3,2,1,0:T(8,128)(2,1)} %pad_maximum_fusion.1), channel_id=1, source_target_pairs={{1,0},{2,1},{3,2},{4,3},{5,4},{6,5},{7,6},{9,8},{10,9},{11,10},{12... | collective-permute-start | bytes 3145736 | tf_op jit(solution)/shard_map/ppermute | solution.py:22
  92.3 152.3 %collective-permute-start.3 = (bf16[2,8,16,1024]{3,2,1,0:T(8,128)(2,1)}, bf16[2,8,16,1024]{3,2,1,0:T(8,128)(2,1)S(1)}, u32[]{:S(2)}, u32[]{:S(2)}) collective-permute-start(bf16[2,8,16,1024]{3,2,1,0:T(8,128)(2,1)} %get-tuple-element.3), channel_id=1, source_target_pairs={{2,0},{3,1},{4,2},{5,3},{6,4},{7,5},{10,8},{11,9},{12,10},{13,11},... | collective-permute-start | bytes 1572872 | tf_op jit(solution)/shard_map/ppermute | solution.py:22
  93.6 151.0 %collective-permute-start = (bf16[2,8,16,1024]{3,2,1,0:T(8,128)(2,1)}, bf16[2,8,16,1024]{3,2,1,0:T(8,128)(2,1)S(1)}, u32[]{:S(2)}, u32[]{:S(2)}) collective-permute-start(bf16[2,8,16,1024]{3,2,1,0:T(8,128)(2,1)} %get-tuple-element.4), channel_id=1, source_target_pairs={{0,2},{1,3},{2,4},{3,5},{4,6},{5,7},{8,10},{9,11},{10,12},{11,13},... | collective-permute-start | bytes 1572872 | tf_op jit(solution)/shard_map/ppermute | solution.py:22
  207.7 4.0 %copy-start.5 = (s32[8,16]{1,0:T(8,128)S(1)}, s32[8,16]{1,0:T(8,128)}, u32[]{:S(2)}) copy-start(s32[8,16]{1,0:T(8,128)} %param.10) | copy-start | bytes 1540
  207.7 4.3 %copy-start.6 = (s32[8]{0:T(128)S(1)}, s32[8]{0:T(128)}, u32[]{:S(2)}) copy-start(s32[8]{0:T(128)} %param.11) | copy-start | bytes 100
  207.7 30.9 %all-to-all-start.1 = ((bf16[3,64,4096]{2,0,1:T(4,128)(2,1)}), bf16[3,64,4096]{2,0,1:T(4,128)(2,1)S(1)}, u32[]{:S(2)}, u32[]{:S(2)}) async-start(bf16[3,64,4096]{2,0,1:T(4,128)(2,1)} %copy.23), calls=%async_computation.1 | async-start | bytes 4194304 | tf_op jit(solution)/shard_map/all_to_all | solution.py:245
  244.6 0.8 copy-start.3
  244.6 1.0 copy-start.4
  303.6 3.8 %copy-start.2 = (bf16[8,32,1024]{2,1,0:T(8,128)(2,1)S(1)}, bf16[8,32,1024]{2,1,0:T(8,128)(2,1)}, u32[]{:S(2)}) copy-start(bf16[8,32,1024]{2,1,0:T(8,128)(2,1)} %get-tuple-element.14) | copy-start | bytes 1572868

commit v3 on v2

--- a/solution.py
+++ b/solution.py
@@ -164,14 +164,12 @@
     )(queries, out_grad, key_grid, value_grid, l2, l1, r1, r2, bias, col_back)
 
 
-def column_kernel(width, x_ref, o_ref):
-    rows, span_width = x_ref.shape[1], x_ref.shape[2]
-    per = span_width // width
+def column_kernel(x_ref, o_ref):
+    per = x_ref.shape[1]
+    rows = x_ref.shape[2]
 
     def joined(which):
-        return jnp.concatenate(
-            [x_ref[which, :, c * width:(c + 1) * width] for c in range(per)], axis=0
-        )
+        return jnp.concatenate([x_ref[which, c] for c in range(per)], axis=0)
 
     i = lax.broadcasted_iota(jnp.int32, (per * rows, per * rows), 0) // rows
     j = lax.broadcasted_iota(jnp.int32, (per * rows, per * rows), 1) // rows
@@ -179,21 +177,18 @@
     grads = block_grads(joined(0), joined(3), joined(1), joined(2), bias)
     for which, full in enumerate(grads):
         for c in range(per):
-            o_ref[which, :, c * width:(c + 1) * width] = (
-                full[c * rows:(c + 1) * rows].astype(jnp.bfloat16)
-            )
-
-
-def column_attention(whole, width):
-    arrays, rows, lanes = whole.shape
+            o_ref[which, c] = full[c * rows:(c + 1) * rows].astype(jnp.bfloat16)
+
+
+def column_attention(whole):
+    arrays, strip, rows, width = whole.shape
     per = max(1, LANES // rows)
-    block = per * width
     return pl.pallas_call(
-        functools.partial(column_kernel, width),
-        grid=(lanes // block,),
-        in_specs=[pl.BlockSpec((arrays, rows, block), lambda c: (0, 0, c))],
-        out_specs=pl.BlockSpec((3, rows, block), lambda c: (0, 0, c)),
-        out_shape=jax.ShapeDtypeStruct((3, rows, lanes), jnp.bfloat16),
+        column_kernel,
+        grid=(strip // per,),
+        in_specs=[pl.BlockSpec((arrays, per, rows, width), lambda c: (0, c, 0, 0))],
+        out_specs=pl.BlockSpec((3, per, rows, width), lambda c: (0, c, 0, 0)),
+        out_shape=jax.ShapeDtypeStruct((3, strip, rows, width), jnp.bfloat16),
     )(whole)
 
 
@@ -227,10 +222,8 @@
     near = col_count
     far = band_reach - col_count
 
-    stacked = jnp.stack([queries, key_grid, value_grid, out_grad]).reshape(
-        4, row_count, col_count * feature_width
-    )
-    whole = lax.all_to_all(stacked, "rrow", split_axis=2, concat_axis=1, tiled=True)
+    stacked = jnp.stack([queries, key_grid, value_grid, out_grad]).transpose(0, 2, 1, 3)
+    whole = lax.all_to_all(stacked, "rrow", split_axis=1, concat_axis=2, tiled=True)
 
     pair = jnp.stack([key_grid, value_grid])
     l1 = shifted(pair[:, :, col_count - near:], "rcol", 1)
@@ -241,9 +234,9 @@
     first_col = lax.axis_index("rcol") * col_count
     bias = band_bias(tissue_mask, band_offset, first_col, grid_cols, col_count)
 
-    col_out = column_attention(whole, feature_width)
-    back = lax.all_to_all(col_out, "rrow", split_axis=1, concat_axis=2, tiled=True)
-    back = back.reshape(3, row_count, col_count, feature_width)
+    col_out = column_attention(whole)
+    back = lax.all_to_all(col_out, "rrow", split_axis=2, concat_axis=1, tiled=True)
+    back = back.transpose(0, 2, 1, 3)
     return fused_row(queries, out_grad, key_grid, value_grid, l2, l1, r1, r2, bias, back)
 
 

time: 311 us -> 145 us (0.47)
  local copies, waits for them, and re-layouts: 174 us -> 15.2 us
  waiting for transfers between devices: 36.6 us -> 30.6 us
    unnamed x19 -> x13, local copies, waits for them, and re-layouts: 86.8 us -> 4.61 us
    all_to_all x2 -> x3, local copies, waits for them, and re-layouts: 42.9 us -> 4.27 us  [the longest x2 2.69 us: body(): lax.all_to_all(col_out, 'rrow', split_axis=2, concat_axis=1, tiled=True)]
    another operation x5 -> x0, local copies, waits for them, and re-layouts: 37 us -> none  [body(): jnp.stack([queries, key_grid, value_grid, out_grad])]
    all_to_all x2, waiting for transfers between devices: 36.6 us -> 30.6 us  [the longest x1 20.4 us: body(): lax.all_to_all(col_out, 'rrow', split_axis=2, concat_axis=1, tiled=True)]
    reshape x1 -> x0, local copies, waits for them, and re-layouts: 3.76 us -> none  [body(): back = back.reshape(3, row_count, col_count, feature_width)]
  transfers between devices with their start and end apart: 6 -> 6, of which waited for: 2 -> 2; matrix products, arithmetic and copies ran while one was open for 31% -> 7% of each run, Pallas kernels for 4% -> 8%
where the time goes in v3:
time: 145 us; the launch traced here: 143 us
  Pallas kernels  69 us (48%)
  waiting for transfers between devices  30.6 us (21%)
  starting transfers between devices  23 us (16%)
  local copies, waits for them, and re-layouts  15.2 us (10%)
  other arithmetic  4.97 us (3%)
    pallas_call x1, Pallas kernels, fused_row(): pl.pallas_call(fused_row_kernel, in_specs=[vmem] * 10, out_specs=[vmem] *...  58.1 us
    all_to_all x1, waiting for transfers between devices, body(): lax.all_to_all(col_out, 'rrow', split_axis=2, concat_axis=1, tiled=True)  20.4 us
    ppermute x4, starting transfers between devices, shifted(): return lax.ppermute(block, axis, route)  14.8 us
    pallas_call x1, Pallas kernels, column_attention(): pl.pallas_call(column_kernel, grid=(strip // per,), in_specs=[pl.BlockSpe...  10.9 us
    all_to_all x1, waiting for transfers between devices, body(): lax.all_to_all(stacked, 'rrow', split_axis=1, concat_axis=2, tiled=True)  10.2 us
    unnamed x13, local copies, waits for them, and re-layouts  4.61 us
    all_to_all x1, starting transfers between devices, body(): lax.all_to_all(stacked, 'rrow', split_axis=1, concat_axis=2, tiled=True)  4.43 us
    pallas_call x1, local copies, waits for them, and re-layouts, column_attention(): pl.pallas_call(column_kernel, grid=(strip // per,), in_specs=[pl.BlockSpe...  3.79 us
  transfers between devices with their start and end apart: 6, of which 2 were waited for; matrix products, arithmetic and copies ran while one was open for 7% of the time, Pallas kernels for 8%

profile of v3, /device:TPU:48, one launch (start us, length us, event | category | flops | bytes accessed | tf_op | source)
XLA Modules:
  0.0 143.4 jit_solution(17566274000588851525)
XLA Ops:
  0.6 1.8 %maximum_bitcast_fusion = bf16[4,32,8,1024]{3,1,2,0:T(8,128)(2,1)S(1)} fusion(bf16[1,8,32,1024]{3,2,1,0:T(8,128)(2,1)} %bitcast.31, bf16[1,8,32,1024]{3,2,1,0:T(8,128)(2,1)} %bitcast.24, bf16[1,8,32,1024]{3,2,1,0:T(8,128)(2,1)} %bitcast.21, bf16[1,8,32,1024]{3,2,1,0:T(8,128)(2,1)} %bitcast.30), kind=kLoop, calls=%fused_computation | loop fusion | flops 3145728 | bytes 4194304 | tf_op jit(solution)/shard_map/transpose | solution.py:225
  2.4 2.5 %copy.15 = bf16[4,32,8,1024]{3,2,0,1:T(8,128)(2,1)} copy(bf16[4,32,8,1024]{3,1,2,0:T(8,128)(2,1)S(1)} %maximum_bitcast_fusion) | data formatting | bytes 4194304 | tf_op jit(solution)/shard_map/transpose | solution.py:225
  4.9 4.4 %all-to-all-start = ((bf16[4,32,8,1024]{3,2,0,1:T(8,128)(2,1)}), bf16[4,32,8,1024]{3,2,0,1:T(8,128)(2,1)S(1)}, u32[]{:S(2)}, u32[]{:S(2)}) async-start(bf16[4,32,8,1024]{3,2,0,1:T(8,128)(2,1)} %copy.15), calls=%async_computation | async-start | bytes 4194304 | tf_op jit(solution)/shard_map/all_to_all | solution.py:226
  9.4 1.1 pad_maximum_fusion
  10.4 3.8 %collective-permute-start.1 = (bf16[2,8,32,1024]{3,2,1,0:T(8,128)(2,1)}, bf16[2,8,32,1024]{3,2,1,0:T(8,128)(2,1)}, u32[]{:S(2)}, u32[]{:S(2)}) collective-permute-start(bf16[2,8,32,1024]{3,2,1,0:T(8,128)(2,1)} %pad_maximum_fusion), channel_id=1, source_target_pairs={{0,1},{1,2},{2,3},{3,4},{4,5},{5,6},{6,7},{8,9},{9,10},{10,11},{11... | collective-permute-start | bytes 3145736 | tf_op jit(solution)/shard_map/ppermute | solution.py:22
  14.3 3.0 %collective-permute-start.2 = (bf16[2,8,32,1024]{3,2,1,0:T(8,128)(2,1)}, bf16[2,8,32,1024]{3,2,1,0:T(8,128)(2,1)}, u32[]{:S(2)}, u32[]{:S(2)}) collective-permute-start(bf16[2,8,32,1024]{3,2,1,0:T(8,128)(2,1)} %pad_maximum_fusion), channel_id=1, source_target_pairs={{1,0},{2,1},{3,2},{4,3},{5,4},{6,5},{7,6},{9,8},{10,9},{11,10},{12... | collective-permute-start | bytes 3145736 | tf_op jit(solution)/shard_map/ppermute | solution.py:22
  17.2 1.1 fusion.1
  18.3 1.3 collective-permute-start.3
  19.6 6.8 %collective-permute-start = (bf16[2,8,16,1024]{3,2,1,0:T(8,128)(2,1)}, bf16[2,8,16,1024]{3,2,1,0:T(8,128)(2,1)}, u32[]{:S(2)}, u32[]{:S(2)}) collective-permute-start(bf16[2,8,16,1024]{3,2,1,0:T(8,128)(2,1)} %get-tuple-element.4), channel_id=1, source_target_pairs={{0,2},{1,3},{2,4},{3,5},{4,6},{5,7},{8,10},{9,11},{10,12},{11,13},... | collective-permute-start | bytes 1572872 | tf_op jit(solution)/shard_map/ppermute | solution.py:22
  26.4 10.2 %all-to-all-done = bf16[4,32,8,1024]{3,2,0,1:T(8,128)(2,1)S(1)} async-done(((bf16[4,32,8,1024]{3,2,0,1:T(8,128)(2,1)}), bf16[4,32,8,1024]{3,2,0,1:T(8,128)(2,1)S(1)}, u32[]{:S(2)}, u32[]{:S(2)}) %all-to-all-start) | async-done | bytes 2097184 | tf_op jit(solution)/shard_map/all_to_all | solution.py:226
  36.5 1.6 %copy.21 = bf16[4,8,4,8,1024]{4,3,1,2,0:T(8,128)(2,1)} copy(bf16[4,8,4,8,1024]{4,3,0,2,1:T(8,128)(2,1)S(1)} %bitcast.20) | data formatting | bytes 4194304 | tf_op jit(solution)/shard_map/all_to_all | solution.py:226
  38.1 10.9 %shard_map.85 = bf16[3,4,64,1024]{3,2,1,0:T(8,128)(2,1)} custom-call(bf16[4,4,64,1024]{3,2,1,0:T(8,128)(2,1)} %bitcast.19), custom_call_target="tpu_custom_call" | custom-call | tf_op jit(solution)/shard_map/pallas_call | solution.py:186
  49.0 3.8 %copy.17 = bf16[3,4,64,1024]{3,1,0,2:T(4,128)(2,1)} copy(bf16[3,4,64,1024]{3,2,1,0:T(8,128)(2,1)} %shard_map.85) | data formatting | bytes 3145728 | tf_op jit(solution)/shard_map/pallas_call | solution.py:186
  52.8 3.7 %all-to-all-start.1 = ((bf16[3,4,64,1024]{3,1,0,2:T(4,128)(2,1)}), bf16[3,4,64,1024]{3,1,0,2:T(4,128)(2,1)S(1)}, u32[]{:S(2)}, u32[]{:S(2)}) async-start(bf16[3,4,64,1024]{3,1,0,2:T(4,128)(2,1)} %copy.17), calls=%async_computation.1 | async-start | bytes 3145728 | tf_op jit(solution)/shard_map/all_to_all | solution.py:238
  56.5 0.1 multiply_reduce_fusion
  56.7 0.1 broadcast_compare_fusion
  56.8 0.8 fusion.5.bias_ref
  57.6 20.4 %all-to-all-done.1 = bf16[3,4,64,1024]{3,1,0,2:T(4,128)(2,1)S(1)} async-done(((bf16[3,4,64,1024]{3,1,0,2:T(4,128)(2,1)}), bf16[3,4,64,1024]{3,1,0,2:T(4,128)(2,1)S(1)}, u32[]{:S(2)}, u32[]{:S(2)}) %all-to-all-start.1) | async-done | bytes 1572896 | tf_op jit(solution)/shard_map/all_to_all | solution.py:238
  78.0 0.8 copy.22
  78.8 1.9 %all_to_all.33 = bf16[3,32,8,1024]{3,1,2,0:T(8,128)(2,1)} reshape(bf16[3,8,4,8,1024]{4,2,1,3,0:T(4,128)(2,1)S(1)} %bitcast.28) | data formatting | bytes 3145728 | tf_op jit(solution)/shard_map/all_to_all | solution.py:238
  80.7 58.1 %shard_map.86 = (bf16[8,32,1024]{2,1,0:T(8,128)(2,1)}, bf16[8,32,1024]{2,1,0:T(8,128)(2,1)}, bf16[8,32,1024]{2,1,0:T(8,128)(2,1)}) custom-call(bf16[8,32,1024]{2,1,0:T(8,128)(2,1)} %q_ref.1, bf16[8,32,1024]{2,1,0:T(8,128)(2,1)} %g_ref.1, bf16[8,32,1024]{2,1,0:T(8,128)(2,1)} %k_ref.1, bf16[8,32,1024]{2,1,0:T(8,128)(2,1)} %v_ref.1, ...), custom_call_target="tpu_custom_call" | custom-call | tf_op jit(solution)/shard_map/pallas_call | solution.py:143
  138.8 1.9 %copy.26 = bf16[8,32,1024]{2,1,0:T(8,128)(2,1)} copy(bf16[8,32,1024]{2,1,0:T(8,128)(2,1)} %get-tuple-element.12) | data formatting | bytes 1048576
  140.8 1.9 %copy.27 = bf16[8,32,1024]{2,1,0:T(8,128)(2,1)} copy(bf16[8,32,1024]{2,1,0:T(8,128)(2,1)} %get-tuple-element.13) | data formatting | bytes 1048576
  142.6 0.8 copy.28
  (21 shorter events, 0.2 us)
Async XLA Ops:
  4.9 4.4 %copy-start = (bf16[8,32,1024]{2,1,0:T(8,128)(2,1)S(1)}, bf16[8,32,1024]{2,1,0:T(8,128)(2,1)}, u32[]{:S(2)}) copy-start(bf16[8,32,1024]{2,1,0:T(8,128)(2,1)} %k_ref.1) | copy-start | bytes 1572868
  4.9 4.4 %copy-start.1 = (bf16[8,32,1024]{2,1,0:T(8,128)(2,1)S(1)}, bf16[8,32,1024]{2,1,0:T(8,128)(2,1)}, u32[]{:S(2)}) copy-start(bf16[8,32,1024]{2,1,0:T(8,128)(2,1)} %v_ref.1) | copy-start | bytes 1572868
  4.9 31.6 %all-to-all-start = ((bf16[4,32,8,1024]{3,2,0,1:T(8,128)(2,1)}), bf16[4,32,8,1024]{3,2,0,1:T(8,128)(2,1)S(1)}, u32[]{:S(2)}, u32[]{:S(2)}) async-start(bf16[4,32,8,1024]{3,2,0,1:T(8,128)(2,1)} %copy.15), calls=%async_computation | async-start | bytes 4194304 | tf_op jit(solution)/shard_map/all_to_all | solution.py:226
  10.4 70.3 %collective-permute-start.1 = (bf16[2,8,32,1024]{3,2,1,0:T(8,128)(2,1)}, bf16[2,8,32,1024]{3,2,1,0:T(8,128)(2,1)}, u32[]{:S(2)}, u32[]{:S(2)}) collective-permute-start(bf16[2,8,32,1024]{3,2,1,0:T(8,128)(2,1)} %pad_maximum_fusion), channel_id=1, source_target_pairs={{0,1},{1,2},{2,3},{3,4},{4,5},{5,6},{6,7},{8,9},{9,10},{10,11},{11... | collective-permute-start | bytes 3145736 | tf_op jit(solution)/shard_map/ppermute | solution.py:22
  14.3 66.5 %collective-permute-start.2 = (bf16[2,8,32,1024]{3,2,1,0:T(8,128)(2,1)}, bf16[2,8,32,1024]{3,2,1,0:T(8,128)(2,1)}, u32[]{:S(2)}, u32[]{:S(2)}) collective-permute-start(bf16[2,8,32,1024]{3,2,1,0:T(8,128)(2,1)} %pad_maximum_fusion), channel_id=1, source_target_pairs={{1,0},{2,1},{3,2},{4,3},{5,4},{6,5},{7,6},{9,8},{10,9},{11,10},{12... | collective-permute-start | bytes 3145736 | tf_op jit(solution)/shard_map/ppermute | solution.py:22
  18.3 62.4 %collective-permute-start.3 = (bf16[2,8,16,1024]{3,2,1,0:T(8,128)(2,1)}, bf16[2,8,16,1024]{3,2,1,0:T(8,128)(2,1)}, u32[]{:S(2)}, u32[]{:S(2)}) collective-permute-start(bf16[2,8,16,1024]{3,2,1,0:T(8,128)(2,1)} %get-tuple-element.3), channel_id=1, source_target_pairs={{2,0},{3,1},{4,2},{5,3},{6,4},{7,5},{10,8},{11,9},{12,10},{13,11},... | collective-permute-start | bytes 1572872 | tf_op jit(solution)/shard_map/ppermute | solution.py:22
  19.6 61.1 %collective-permute-start = (bf16[2,8,16,1024]{3,2,1,0:T(8,128)(2,1)}, bf16[2,8,16,1024]{3,2,1,0:T(8,128)(2,1)}, u32[]{:S(2)}, u32[]{:S(2)}) collective-permute-start(bf16[2,8,16,1024]{3,2,1,0:T(8,128)(2,1)} %get-tuple-element.4), channel_id=1, source_target_pairs={{0,2},{1,3},{2,4},{3,5},{4,6},{5,7},{8,10},{9,11},{10,12},{11,13},... | collective-permute-start | bytes 1572872 | tf_op jit(solution)/shard_map/ppermute | solution.py:22
  52.8 3.8 %copy-start.3 = (s32[8,16]{1,0:T(8,128)S(1)}, s32[8,16]{1,0:T(8,128)}, u32[]{:S(2)}) copy-start(s32[8,16]{1,0:T(8,128)} %param.10) | copy-start | bytes 1540
  52.8 4.0 %copy-start.4 = (s32[8]{0:T(128)S(1)}, s32[8]{0:T(128)}, u32[]{:S(2)}) copy-start(s32[8]{0:T(128)} %param.11) | copy-start | bytes 100
  52.8 25.2 %all-to-all-start.1 = ((bf16[3,4,64,1024]{3,1,0,2:T(4,128)(2,1)}), bf16[3,4,64,1024]{3,1,0,2:T(4,128)(2,1)S(1)}, u32[]{:S(2)}, u32[]{:S(2)}) async-start(bf16[3,4,64,1024]{3,1,0,2:T(4,128)(2,1)} %copy.17), calls=%async_computation.1 | async-start | bytes 3145728 | tf_op jit(solution)/shard_map/all_to_all | solution.py:238
  138.8 3.8 %copy-start.2 = (bf16[8,32,1024]{2,1,0:T(8,128)(2,1)S(1)}, bf16[8,32,1024]{2,1,0:T(8,128)(2,1)}, u32[]{:S(2)}) copy-start(bf16[8,32,1024]{2,1,0:T(8,128)(2,1)} %get-tuple-element.14) | copy-start | bytes 1572868

commit v4 on v3

--- a/solution.py
+++ b/solution.py
@@ -227,9 +227,9 @@
 
     pair = jnp.stack([key_grid, value_grid])
     l1 = shifted(pair[:, :, col_count - near:], "rcol", 1)
-    l2 = shifted(pair[:, :, col_count - far:], "rcol", 2)
     r1 = shifted(pair[:, :, :near], "rcol", -1)
-    r2 = shifted(pair[:, :, :far], "rcol", -2)
+    l2 = shifted(l1[:, :, near - far:], "rcol", 1)
+    r2 = shifted(r1[:, :, :far], "rcol", -1)
     grid_cols = col_count * lax.axis_size("rcol")
     first_col = lax.axis_index("rcol") * col_count
     bias = band_bias(tissue_mask, band_offset, first_col, grid_cols, col_count)

time: 145 us -> 145 us (level)
  starting transfers between devices: 23 us -> 19.8 us
  local copies, waits for them, and re-layouts: 15.2 us -> 18 us
    all_to_all x1, waiting for transfers between devices: 10.2 us -> 20.2 us  [body(): lax.all_to_all(stacked, 'rrow', split_axis=1, concat_axis=2, tiled=True)]
    all_to_all x1, waiting for transfers between devices: 20.4 us -> 11.8 us  [body(): lax.all_to_all(col_out, 'rrow', split_axis=2, concat_axis=1, tiled=True)]
    ppermute x4, starting transfers between devices: 14.8 us -> 11.7 us  [shifted(): return lax.ppermute(block, axis, route)]
    slice x0 -> x2, local copies, waits for them, and re-layouts: none -> 2.79 us  [the longest x1 1.89 us: body(): l2 = shifted(l1[:, :, near - far:], 'rcol', 1)]
    unnamed x13 -> x15, local copies, waits for them, and re-layouts: 4.61 us -> 4.61 us
  transfers between devices with their start and end apart: 6 -> 6, of which waited for: 2 -> 2; matrix products, arithmetic and copies ran while one was open for 7% -> 8% of each run, Pallas kernels for 8% -> 8%
where the time goes in v4:
time: 145 us; the launch traced here: 143 us
  Pallas kernels  68.8 us (47%)
  waiting for transfers between devices  32 us (22%)
  starting transfers between devices  19.8 us (14%)
  local copies, waits for them, and re-layouts  18 us (12%)
  other arithmetic  3.94 us (3%)
    pallas_call x1, Pallas kernels, fused_row(): pl.pallas_call(fused_row_kernel, in_specs=[vmem] * 10, out_specs=[vmem] *...  58 us
    all_to_all x1, waiting for transfers between devices, body(): lax.all_to_all(stacked, 'rrow', split_axis=1, concat_axis=2, tiled=True)  20.2 us
    all_to_all x1, waiting for transfers between devices, body(): lax.all_to_all(col_out, 'rrow', split_axis=2, concat_axis=1, tiled=True)  11.8 us
    ppermute x4, starting transfers between devices, shifted(): return lax.ppermute(block, axis, route)  11.7 us
    pallas_call x1, Pallas kernels, column_attention(): pl.pallas_call(column_kernel, grid=(strip // per,), in_specs=[pl.BlockSpe...  10.9 us
    unnamed x15, local copies, waits for them, and re-layouts  4.61 us
    all_to_all x1, starting transfers between devices, body(): lax.all_to_all(stacked, 'rrow', split_axis=1, concat_axis=2, tiled=True)  4.43 us
    pallas_call x1, local copies, waits for them, and re-layouts, column_attention(): pl.pallas_call(column_kernel, grid=(strip // per,), in_specs=[pl.BlockSpe...  3.79 us
  transfers between devices with their start and end apart: 6, of which 2 were waited for; matrix products, arithmetic and copies ran while one was open for 8% of the time, Pallas kernels for 8%

profile of v4, /device:TPU:48, one launch (start us, length us, event | category | flops | bytes accessed | tf_op | source)
XLA Modules:
  0.0 143.3 jit_solution(8077019726618730467)
XLA Ops:
  0.6 1.8 %maximum_bitcast_fusion = bf16[4,32,8,1024]{3,1,2,0:T(8,128)(2,1)S(1)} fusion(bf16[1,8,32,1024]{3,2,1,0:T(8,128)(2,1)} %bitcast.29, bf16[1,8,32,1024]{3,2,1,0:T(8,128)(2,1)} %bitcast.26, bf16[1,8,32,1024]{3,2,1,0:T(8,128)(2,1)} %bitcast.24, bf16[1,8,32,1024]{3,2,1,0:T(8,128)(2,1)} %bitcast.28), kind=kLoop, calls=%fused_computation | loop fusion | flops 3145728 | bytes 4194304 | tf_op jit(solution)/shard_map/transpose | solution.py:225
  2.4 2.5 %copy.15 = bf16[4,32,8,1024]{3,2,0,1:T(8,128)(2,1)} copy(bf16[4,32,8,1024]{3,1,2,0:T(8,128)(2,1)S(1)} %maximum_bitcast_fusion) | data formatting | bytes 4194304 | tf_op jit(solution)/shard_map/transpose | solution.py:225
  4.9 4.4 %all-to-all-start = ((bf16[4,32,8,1024]{3,2,0,1:T(8,128)(2,1)}), bf16[4,32,8,1024]{3,2,0,1:T(8,128)(2,1)S(1)}, u32[]{:S(2)}, u32[]{:S(2)}) async-start(bf16[4,32,8,1024]{3,2,0,1:T(8,128)(2,1)} %copy.15), calls=%async_computation | async-start | bytes 4194304 | tf_op jit(solution)/shard_map/all_to_all | solution.py:226
  9.4 1.1 pad_maximum_fusion
  10.5 2.0 %collective-permute-start.2 = (bf16[2,8,32,1024]{3,2,1,0:T(8,128)(2,1)}, bf16[2,8,32,1024]{3,2,1,0:T(8,128)(2,1)S(1)}, u32[]{:S(2)}, u32[]{:S(2)}) collective-permute-start(bf16[2,8,32,1024]{3,2,1,0:T(8,128)(2,1)} %pad_maximum_fusion), channel_id=1, source_target_pairs={{1,0},{2,1},{3,2},{4,3},{5,4},{6,5},{7,6},{9,8},{10,9},{11,10},{12... | collective-permute-start | bytes 3145736 | tf_op jit(solution)/shard_map/ppermute | solution.py:22
  12.5 3.8 %collective-permute-start = (bf16[2,8,32,1024]{3,2,1,0:T(8,128)(2,1)}, bf16[2,8,32,1024]{3,2,1,0:T(8,128)(2,1)}, u32[]{:S(2)}, u32[]{:S(2)}) collective-permute-start(bf16[2,8,32,1024]{3,2,1,0:T(8,128)(2,1)} %pad_maximum_fusion), channel_id=1, source_target_pairs={{0,1},{1,2},{2,3},{3,4},{4,5},{5,6},{6,7},{8,9},{9,10},{10,11},{11... | collective-permute-start | bytes 3145736 | tf_op jit(solution)/shard_map/ppermute | solution.py:22
  16.4 20.2 %all-to-all-done = bf16[4,32,8,1024]{3,2,0,1:T(8,128)(2,1)S(1)} async-done(((bf16[4,32,8,1024]{3,2,0,1:T(8,128)(2,1)}), bf16[4,32,8,1024]{3,2,0,1:T(8,128)(2,1)S(1)}, u32[]{:S(2)}, u32[]{:S(2)}) %all-to-all-start) | async-done | bytes 2097184 | tf_op jit(solution)/shard_map/all_to_all | solution.py:226
  36.5 1.6 %copy.21 = bf16[4,8,4,8,1024]{4,3,1,2,0:T(8,128)(2,1)} copy(bf16[4,8,4,8,1024]{4,3,0,2,1:T(8,128)(2,1)S(1)} %bitcast.20) | data formatting | bytes 4194304 | tf_op jit(solution)/shard_map/all_to_all | solution.py:226
  38.1 10.9 %shard_map.85 = bf16[3,4,64,1024]{3,2,1,0:T(8,128)(2,1)} custom-call(bf16[4,4,64,1024]{3,2,1,0:T(8,128)(2,1)} %bitcast.19), custom_call_target="tpu_custom_call" | custom-call | tf_op jit(solution)/shard_map/pallas_call | solution.py:186
  49.0 3.8 %copy.17 = bf16[3,4,64,1024]{3,1,0,2:T(4,128)(2,1)} copy(bf16[3,4,64,1024]{3,2,1,0:T(8,128)(2,1)} %shard_map.85) | data formatting | bytes 3145728 | tf_op jit(solution)/shard_map/pallas_call | solution.py:186
  52.8 3.7 %all-to-all-start.1 = ((bf16[3,4,64,1024]{3,1,0,2:T(4,128)(2,1)}), bf16[3,4,64,1024]{3,1,0,2:T(4,128)(2,1)S(1)}, u32[]{:S(2)}, u32[]{:S(2)}) async-start(bf16[3,4,64,1024]{3,1,0,2:T(4,128)(2,1)} %copy.17), calls=%async_computation.1 | async-start | bytes 3145728 | tf_op jit(solution)/shard_map/all_to_all | solution.py:238
  56.5 0.1 multiply_reduce_fusion
  56.7 0.9 slice.9
  57.6 2.0 %collective-permute-start.3 = (bf16[2,8,16,1024]{3,2,1,0:T(8,128)(2,1)}, bf16[2,8,16,1024]{3,2,1,0:T(8,128)(2,1)}, u32[]{:S(2)}, u32[]{:S(2)}) collective-permute-start(bf16[2,8,16,1024]{3,2,1,0:T(8,128)(2,1)} %slice.9), channel_id=1, source_target_pairs={{1,0},{2,1},{3,2},{4,3},{5,4},{6,5},{7,6},{9,8},{10,9},{11,10},{12... | collective-permute-start | bytes 1572872 | tf_op jit(solution)/shard_map/ppermute | solution.py:22
  59.7 1.9 %slice.8 = bf16[2,8,16,1024]{3,2,1,0:T(8,128)(2,1)} slice(bf16[2,8,32,1024]{3,2,1,0:T(8,128)(2,1)} %collective-permute-done.l1_ref), slice={[0:2], [0:8], [16:32], [0:1024]} | slice | bytes 1048576 | tf_op jit(solution)/shard_map/slice | solution.py:231
  61.6 3.8 %collective-permute-start.1 = (bf16[2,8,16,1024]{3,2,1,0:T(8,128)(2,1)}, bf16[2,8,16,1024]{3,2,1,0:T(8,128)(2,1)}, u32[]{:S(2)}, u32[]{:S(2)}) collective-permute-start(bf16[2,8,16,1024]{3,2,1,0:T(8,128)(2,1)} %slice.8), channel_id=1, source_target_pairs={{0,1},{1,2},{2,3},{3,4},{4,5},{5,6},{6,7},{8,9},{9,10},{10,11},{11... | collective-permute-start | bytes 1572872 | tf_op jit(solution)/shard_map/ppermute | solution.py:22
  65.5 0.8 fusion.3.bias_ref
  66.2 11.8 %all-to-all-done.1 = bf16[3,4,64,1024]{3,1,0,2:T(4,128)(2,1)S(1)} async-done(((bf16[3,4,64,1024]{3,1,0,2:T(4,128)(2,1)}), bf16[3,4,64,1024]{3,1,0,2:T(4,128)(2,1)S(1)}, u32[]{:S(2)}, u32[]{:S(2)}) %all-to-all-start.1) | async-done | bytes 1572896 | tf_op jit(solution)/shard_map/all_to_all | solution.py:238
  78.0 0.8 copy.22
  78.8 1.9 %all_to_all.33 = bf16[3,32,8,1024]{3,1,2,0:T(8,128)(2,1)} reshape(bf16[3,8,4,8,1024]{4,2,1,3,0:T(4,128)(2,1)S(1)} %bitcast.22) | data formatting | bytes 3145728 | tf_op jit(solution)/shard_map/all_to_all | solution.py:238
  80.7 58.0 %shard_map.86 = (bf16[8,32,1024]{2,1,0:T(8,128)(2,1)}, bf16[8,32,1024]{2,1,0:T(8,128)(2,1)}, bf16[8,32,1024]{2,1,0:T(8,128)(2,1)}) custom-call(bf16[8,32,1024]{2,1,0:T(8,128)(2,1)} %q_ref.1, bf16[8,32,1024]{2,1,0:T(8,128)(2,1)} %g_ref.1, bf16[8,32,1024]{2,1,0:T(8,128)(2,1)} %k_ref.1, bf16[8,32,1024]{2,1,0:T(8,128)(2,1)} %v_ref.1, ...), custom_call_target="tpu_custom_call" | custom-call | tf_op jit(solution)/shard_map/pallas_call | solution.py:143
  138.7 1.9 %copy.26 = bf16[8,32,1024]{2,1,0:T(8,128)(2,1)} copy(bf16[8,32,1024]{2,1,0:T(8,128)(2,1)} %get-tuple-element.10) | data formatting | bytes 1048576
  140.6 1.9 %copy.27 = bf16[8,32,1024]{2,1,0:T(8,128)(2,1)} copy(bf16[8,32,1024]{2,1,0:T(8,128)(2,1)} %get-tuple-element.11) | data formatting | bytes 1048576
  142.5 0.8 copy.28
  (24 shorter events, 0.2 us)
Async XLA Ops:
  4.9 4.4 %copy-start = (bf16[8,32,1024]{2,1,0:T(8,128)(2,1)S(1)}, bf16[8,32,1024]{2,1,0:T(8,128)(2,1)}, u32[]{:S(2)}) copy-start(bf16[8,32,1024]{2,1,0:T(8,128)(2,1)} %k_ref.1) | copy-start | bytes 1572868
  4.9 4.4 %copy-start.1 = (bf16[8,32,1024]{2,1,0:T(8,128)(2,1)S(1)}, bf16[8,32,1024]{2,1,0:T(8,128)(2,1)}, u32[]{:S(2)}) copy-start(bf16[8,32,1024]{2,1,0:T(8,128)(2,1)} %v_ref.1) | copy-start | bytes 1572868
  4.9 31.6 %all-to-all-start = ((bf16[4,32,8,1024]{3,2,0,1:T(8,128)(2,1)}), bf16[4,32,8,1024]{3,2,0,1:T(8,128)(2,1)S(1)}, u32[]{:S(2)}, u32[]{:S(2)}) async-start(bf16[4,32,8,1024]{3,2,0,1:T(8,128)(2,1)} %copy.15), calls=%async_computation | async-start | bytes 4194304 | tf_op jit(solution)/shard_map/all_to_all | solution.py:226
  10.5 46.3 %collective-permute-start.2 = (bf16[2,8,32,1024]{3,2,1,0:T(8,128)(2,1)}, bf16[2,8,32,1024]{3,2,1,0:T(8,128)(2,1)S(1)}, u32[]{:S(2)}, u32[]{:S(2)}) collective-permute-start(bf16[2,8,32,1024]{3,2,1,0:T(8,128)(2,1)} %pad_maximum_fusion), channel_id=1, source_target_pairs={{1,0},{2,1},{3,2},{4,3},{5,4},{6,5},{7,6},{9,8},{10,9},{11,10},{12... | collective-permute-start | bytes 3145736 | tf_op jit(solution)/shard_map/ppermute | solution.py:22
  12.5 47.2 %collective-permute-start = (bf16[2,8,32,1024]{3,2,1,0:T(8,128)(2,1)}, bf16[2,8,32,1024]{3,2,1,0:T(8,128)(2,1)}, u32[]{:S(2)}, u32[]{:S(2)}) collective-permute-start(bf16[2,8,32,1024]{3,2,1,0:T(8,128)(2,1)} %pad_maximum_fusion), channel_id=1, source_target_pairs={{0,1},{1,2},{2,3},{3,4},{4,5},{5,6},{6,7},{8,9},{9,10},{10,11},{11... | collective-permute-start | bytes 3145736 | tf_op jit(solution)/shard_map/ppermute | solution.py:22
  52.8 3.8 %copy-start.4 = (s32[8,16]{1,0:T(8,128)S(1)}, s32[8,16]{1,0:T(8,128)}, u32[]{:S(2)}) copy-start(s32[8,16]{1,0:T(8,128)} %param.10) | copy-start | bytes 1540
  52.8 12.7 %copy-start.5 = (s32[8]{0:T(128)S(1)}, s32[8]{0:T(128)}, u32[]{:S(2)}) copy-start(s32[8]{0:T(128)} %param.11) | copy-start | bytes 100
  52.8 25.2 %all-to-all-start.1 = ((bf16[3,4,64,1024]{3,1,0,2:T(4,128)(2,1)}), bf16[3,4,64,1024]{3,1,0,2:T(4,128)(2,1)S(1)}, u32[]{:S(2)}, u32[]{:S(2)}) async-start(bf16[3,4,64,1024]{3,1,0,2:T(4,128)(2,1)} %copy.17), calls=%async_computation.1 | async-start | bytes 3145728 | tf_op jit(solution)/shard_map/all_to_all | solution.py:238
  56.7 21.3 %copy-start.2 = (bf16[2,8,32,1024]{3,2,1,0:T(8,128)(2,1)}, bf16[2,8,32,1024]{3,2,1,0:T(8,128)(2,1)S(1)}, u32[]{:S(2)}) copy-start(bf16[2,8,32,1024]{3,2,1,0:T(8,128)(2,1)S(1)} %collective-permute-done.2.r1_ref) | copy-start | bytes 3145732
  57.6 23.1 %collective-permute-start.3 = (bf16[2,8,16,1024]{3,2,1,0:T(8,128)(2,1)}, bf16[2,8,16,1024]{3,2,1,0:T(8,128)(2,1)}, u32[]{:S(2)}, u32[]{:S(2)}) collective-permute-start(bf16[2,8,16,1024]{3,2,1,0:T(8,128)(2,1)} %slice.9), channel_id=1, source_target_pairs={{1,0},{2,1},{3,2},{4,3},{5,4},{6,5},{7,6},{9,8},{10,9},{11,10},{12... | collective-permute-start | bytes 1572872 | tf_op jit(solution)/shard_map/ppermute | solution.py:22
  61.6 19.2 %collective-permute-start.1 = (bf16[2,8,16,1024]{3,2,1,0:T(8,128)(2,1)}, bf16[2,8,16,1024]{3,2,1,0:T(8,128)(2,1)}, u32[]{:S(2)}, u32[]{:S(2)}) collective-permute-start(bf16[2,8,16,1024]{3,2,1,0:T(8,128)(2,1)} %slice.8), channel_id=1, source_target_pairs={{0,1},{1,2},{2,3},{3,4},{4,5},{5,6},{6,7},{8,9},{9,10},{10,11},{11... | collective-permute-start | bytes 1572872 | tf_op jit(solution)/shard_map/ppermute | solution.py:22
  138.7 3.8 %copy-start.3 = (bf16[8,32,1024]{2,1,0:T(8,128)(2,1)S(1)}, bf16[8,32,1024]{2,1,0:T(8,128)(2,1)}, u32[]{:S(2)}) copy-start(bf16[8,32,1024]{2,1,0:T(8,128)(2,1)} %get-tuple-element.12) | copy-start | bytes 1572868

commit v5 on v4

--- a/solution.py
+++ b/solution.py
@@ -68,7 +68,7 @@
     return dq, dk, dv
 
 
-def fused_row_kernel(q_ref, g_ref, k_ref, v_ref, l2_ref, l1_ref, r1_ref, r2_ref, bias_ref, cb_ref,
+def fused_row_kernel(q_ref, g_ref, k_ref, v_ref, l2_ref, l1_ref, r1_ref, r2_ref, bias_ref,
                      qg_ref, kg_ref, vg_ref,
                      own_s, s_l2, s_l1, s_r1, s_r2, x_r2, x_r1, x_l1, x_l2, send_sem, recv_sem):
     rows, cc, width = q_ref.shape
@@ -97,7 +97,7 @@
             )
 
         dq, dk, dv = block_grads(q_ref[r], g_ref[r], span(0, k_ref), span(1, v_ref), bias_ref[r])
-        qg_ref[r] = (dq + cb_ref[0, r].astype(jnp.float32)).astype(jnp.bfloat16)
+        qg_ref[r] = dq
         for which, full in ((0, dk), (1, dv)):
             s_l2[which, r] = full[:w2].astype(jnp.bfloat16)
             s_l1[which, r] = full[w2:w2 + w1].astype(jnp.bfloat16)
@@ -124,25 +124,24 @@
     f32 = jnp.float32
     for which, out_ref in ((0, kg_ref), (1, vg_ref)):
         total = own_s[which] + x_r1[which].astype(f32) + x_l1[which].astype(f32)
-        total = total + cb_ref[which + 1].astype(f32)
         low = total[:, :w2] + x_l2[which].astype(f32)
         high = total[:, cc - w2:] + x_r2[which].astype(f32)
-        out_ref[:, :w2] = low.astype(jnp.bfloat16)
-        out_ref[:, cc - w2:] = high.astype(jnp.bfloat16)
+        out_ref[:, :w2] = low
+        out_ref[:, cc - w2:] = high
         if cc > 2 * w2:
-            out_ref[:, w2:cc - w2] = total[:, w2:cc - w2].astype(jnp.bfloat16)
-
-
-def fused_row(queries, out_grad, key_grid, value_grid, l2, l1, r1, r2, bias, col_back):
+            out_ref[:, w2:cc - w2] = total[:, w2:cc - w2]
+
+
+def fused_row(queries, out_grad, key_grid, value_grid, l2, l1, r1, r2, bias):
     rows, cc, width = queries.shape
     w2 = l2.shape[2]
     w1 = l1.shape[2]
     vmem = pl.BlockSpec(memory_space=pltpu.VMEM)
-    grads = jax.ShapeDtypeStruct((rows, cc, width), jnp.bfloat16)
+    grads = jax.ShapeDtypeStruct((rows, cc, width), jnp.float32)
     bf = jnp.bfloat16
     return pl.pallas_call(
         fused_row_kernel,
-        in_specs=[vmem] * 10,
+        in_specs=[vmem] * 9,
         out_specs=[vmem] * 3,
         out_shape=(grads, grads, grads),
         scratch_shapes=[
@@ -161,7 +160,7 @@
         compiler_params=pltpu.CompilerParams(
             collective_id=0, has_side_effects=True, vmem_limit_bytes=60 * 1024 * 1024
         ),
-    )(queries, out_grad, key_grid, value_grid, l2, l1, r1, r2, bias, col_back)
+    )(queries, out_grad, key_grid, value_grid, l2, l1, r1, r2, bias)
 
 
 def column_kernel(x_ref, o_ref):
@@ -236,8 +235,9 @@
 
     col_out = column_attention(whole)
     back = lax.all_to_all(col_out, "rrow", split_axis=2, concat_axis=1, tiled=True)
-    back = back.transpose(0, 2, 1, 3)
-    return fused_row(queries, out_grad, key_grid, value_grid, l2, l1, r1, r2, bias, back)
+    row_grads = fused_row(queries, out_grad, key_grid, value_grid, l2, l1, r1, r2, bias)
+    back = back.transpose(0, 2, 1, 3).astype(jnp.float32)
+    return tuple((row + col).astype(jnp.bfloat16) for row, col in zip(row_grads, back))
 
 
 def solution(mesh):

time: 145 us -> 146 us (level)
  other arithmetic: 3.94 us -> 10.5 us
  local copies, waits for them, and re-layouts: 18 us -> 12.8 us
    all_to_all x1, waiting for transfers between devices: 11.8 us -> 0.01 us  [body(): lax.all_to_all(col_out, 'rrow', split_axis=2, concat_axis=1, tiled=True)]
    ppermute x4, waiting for transfers between devices: 0.01 us -> 11.4 us  [shifted(): return lax.ppermute(block, axis, route)]
    convert_element_type x0 -> x2, other arithmetic: none -> 6.53 us  [the longest x1 4.21 us: body(): (row + col).astype(jnp.bfloat16)]
    unnamed x15 -> x14, local copies, waits for them, and re-layouts: 4.61 us -> 1.19 us
    all_to_all x2 -> x0, local copies, waits for them, and re-layouts: 2.69 us -> none  [body(): lax.all_to_all(col_out, 'rrow', split_axis=2, concat_axis=1, tiled=True)]
    convert_element_type x0 -> x1, local copies, waits for them, and re-layouts: none -> 2.68 us  [body(): back = back.transpose(0, 2, 1, 3).astype(jnp.float32)]
  transfers between devices with their start and end apart: 6 -> 6, of which waited for: 2 -> 3; matrix products, arithmetic and copies ran while one was open for 8% -> 6% of each run, Pallas kernels for 8% -> 48%
where the time goes in v5:
time: 146 us; the launch traced here: 145 us
  Pallas kernels  69.1 us (47%)
  waiting for transfers between devices  31.7 us (22%)
  starting transfers between devices  19.8 us (14%)
  local copies, waits for them, and re-layouts  12.8 us (9%)
  other arithmetic  10.5 us (7%)
    pallas_call x1, Pallas kernels, fused_row(): pl.pallas_call(fused_row_kernel, in_specs=[vmem] * 9, out_specs=[vmem] *...  58.3 us
    all_to_all x1, waiting for transfers between devices, body(): lax.all_to_all(stacked, 'rrow', split_axis=1, concat_axis=2, tiled=True)  20.2 us
    ppermute x4, starting transfers between devices, shifted(): return lax.ppermute(block, axis, route)  11.7 us
    ppermute x4, waiting for transfers between devices, shifted(): return lax.ppermute(block, axis, route)  11.4 us
    pallas_call x1, Pallas kernels, column_attention(): pl.pallas_call(column_kernel, grid=(strip // per,), in_specs=[pl.BlockSpe...  10.9 us
    all_to_all x1, starting transfers between devices, body(): lax.all_to_all(stacked, 'rrow', split_axis=1, concat_axis=2, tiled=True)  4.43 us
    convert_element_type x1, other arithmetic, body(): (row + col).astype(jnp.bfloat16)  4.21 us
    pallas_call x1, local copies, waits for them, and re-layouts, column_attention(): pl.pallas_call(column_kernel, grid=(strip // per,), in_specs=[pl.BlockSpe...  3.8 us
  transfers between devices with their start and end apart: 6, of which 3 were waited for; matrix products, arithmetic and copies ran while one was open for 6% of the time, Pallas kernels for 48%

profile of v5, /device:TPU:48, one launch (start us, length us, event | category | flops | bytes accessed | tf_op | source)
XLA Modules:
  0.0 144.7 jit_solution(16355177554743517549)
XLA Ops:
  0.6 1.8 %maximum_bitcast_fusion = bf16[4,32,8,1024]{3,1,2,0:T(8,128)(2,1)S(1)} fusion(bf16[1,8,32,1024]{3,2,1,0:T(8,128)(2,1)} %bitcast.46, bf16[1,8,32,1024]{3,2,1,0:T(8,128)(2,1)} %bitcast.43, bf16[1,8,32,1024]{3,2,1,0:T(8,128)(2,1)} %bitcast.41, bf16[1,8,32,1024]{3,2,1,0:T(8,128)(2,1)} %bitcast.45), kind=kLoop, calls=%fused_computation.1 | loop fusion | flops 3145728 | bytes 4194304 | tf_op jit(solution)/shard_map/transpose | solution.py:224
  2.4 2.5 %copy.15 = bf16[4,32,8,1024]{3,2,0,1:T(8,128)(2,1)} copy(bf16[4,32,8,1024]{3,1,2,0:T(8,128)(2,1)S(1)} %maximum_bitcast_fusion) | data formatting | bytes 4194304 | tf_op jit(solution)/shard_map/transpose | solution.py:224
  4.9 4.4 %all-to-all-start = ((bf16[4,32,8,1024]{3,2,0,1:T(8,128)(2,1)}), bf16[4,32,8,1024]{3,2,0,1:T(8,128)(2,1)S(1)}, u32[]{:S(2)}, u32[]{:S(2)}) async-start(bf16[4,32,8,1024]{3,2,0,1:T(8,128)(2,1)} %copy.15), calls=%async_computation | async-start | bytes 4194304 | tf_op jit(solution)/shard_map/all_to_all | solution.py:225
  9.3 1.1 pad_maximum_fusion
  10.4 2.0 %collective-permute-start.2 = (bf16[2,8,32,1024]{3,2,1,0:T(8,128)(2,1)}, bf16[2,8,32,1024]{3,2,1,0:T(8,128)(2,1)S(1)}, u32[]{:S(2)}, u32[]{:S(2)}) collective-permute-start(bf16[2,8,32,1024]{3,2,1,0:T(8,128)(2,1)} %pad_maximum_fusion), channel_id=1, source_target_pairs={{1,0},{2,1},{3,2},{4,3},{5,4},{6,5},{7,6},{9,8},{10,9},{11,10},{12... | collective-permute-start | bytes 3145736 | tf_op jit(solution)/shard_map/ppermute | solution.py:22
  12.4 3.8 %collective-permute-start = (bf16[2,8,32,1024]{3,2,1,0:T(8,128)(2,1)}, bf16[2,8,32,1024]{3,2,1,0:T(8,128)(2,1)}, u32[]{:S(2)}, u32[]{:S(2)}) collective-permute-start(bf16[2,8,32,1024]{3,2,1,0:T(8,128)(2,1)} %pad_maximum_fusion), channel_id=1, source_target_pairs={{0,1},{1,2},{2,3},{3,4},{4,5},{5,6},{6,7},{8,9},{9,10},{10,11},{11... | collective-permute-start | bytes 3145736 | tf_op jit(solution)/shard_map/ppermute | solution.py:22
  16.3 20.2 %all-to-all-done = bf16[4,32,8,1024]{3,2,0,1:T(8,128)(2,1)S(1)} async-done(((bf16[4,32,8,1024]{3,2,0,1:T(8,128)(2,1)}), bf16[4,32,8,1024]{3,2,0,1:T(8,128)(2,1)S(1)}, u32[]{:S(2)}, u32[]{:S(2)}) %all-to-all-start) | async-done | bytes 2097184 | tf_op jit(solution)/shard_map/all_to_all | solution.py:225
  36.5 1.6 %copy.21 = bf16[4,8,4,8,1024]{4,3,1,2,0:T(8,128)(2,1)} copy(bf16[4,8,4,8,1024]{4,3,0,2,1:T(8,128)(2,1)S(1)} %bitcast.39) | data formatting | bytes 4194304 | tf_op jit(solution)/shard_map/all_to_all | solution.py:225
  38.1 10.9 %shard_map.86 = bf16[3,4,64,1024]{3,2,1,0:T(8,128)(2,1)} custom-call(bf16[4,4,64,1024]{3,2,1,0:T(8,128)(2,1)} %bitcast.38), custom_call_target="tpu_custom_call" | custom-call | tf_op jit(solution)/shard_map/pallas_call | solution.py:185
  49.0 3.8 %copy.17 = bf16[3,4,64,1024]{3,1,0,2:T(4,128)(2,1)} copy(bf16[3,4,64,1024]{3,2,1,0:T(8,128)(2,1)} %shard_map.86) | data formatting | bytes 3145728 | tf_op jit(solution)/shard_map/pallas_call | solution.py:185
  52.8 3.7 %all-to-all-start.1 = ((bf16[3,4,64,1024]{3,1,0,2:T(4,128)(2,1)}), bf16[3,4,64,1024]{3,1,0,2:T(4,128)(2,1)S(1)}, u32[]{:S(2)}, u32[]{:S(2)}) async-start(bf16[3,4,64,1024]{3,1,0,2:T(4,128)(2,1)} %copy.17), calls=%async_computation.1 | async-start | bytes 3145728 | tf_op jit(solution)/shard_map/all_to_all | solution.py:237
  56.5 0.1 multiply_reduce_fusion
  56.6 0.1 broadcast_compare_fusion
  56.8 2.0 %collective-permute-start.3 = (bf16[2,8,16,1024]{3,2,1,0:T(8,128)(2,1)S(1)}, bf16[2,8,16,1024]{3,2,1,0:T(8,128)(2,1)S(1)}, u32[]{:S(2)}, u32[]{:S(2)}) collective-permute-start(bf16[2,8,16,1024]{3,2,1,0:T(8,128)(2,1)S(1)} %slice.9), channel_id=1, source_target_pairs={{1,0},{2,1},{3,2},{4,3},{5,4},{6,5},{7,6},{9,8},{10,9},{11,10},{12... | collective-permute-start | bytes 1572872 | tf_op jit(solution)/shard_map/ppermute | solution.py:22
  58.8 1.1 slice.8
  59.9 3.8 %collective-permute-start.1 = (bf16[2,8,16,1024]{3,2,1,0:T(8,128)(2,1)S(1)}, bf16[2,8,16,1024]{3,2,1,0:T(8,128)(2,1)}, u32[]{:S(2)}, u32[]{:S(2)}) collective-permute-start(bf16[2,8,16,1024]{3,2,1,0:T(8,128)(2,1)S(1)} %slice.8), channel_id=1, source_target_pairs={{0,1},{1,2},{2,3},{3,4},{4,5},{5,6},{6,7},{8,9},{9,10},{10,11},{11... | collective-permute-start | bytes 1572872 | tf_op jit(solution)/shard_map/ppermute | solution.py:22
  63.8 0.8 fusion.9.bias_ref
  64.6 8.5 %collective-permute-done.3.r2_ref = bf16[2,8,16,1024]{3,2,1,0:T(8,128)(2,1)S(1)} collective-permute-done((bf16[2,8,16,1024]{3,2,1,0:T(8,128)(2,1)S(1)}, bf16[2,8,16,1024]{3,2,1,0:T(8,128)(2,1)S(1)}, u32[]{:S(2)}, u32[]{:S(2)}) %collective-permute-start.3) | collective-permute-done | bytes 524320 | tf_op jit(solution)/shard_map/ppermute | solution.py:22
  73.1 3.0 %collective-permute-done.1.l2_ref = bf16[2,8,16,1024]{3,2,1,0:T(8,128)(2,1)} collective-permute-done((bf16[2,8,16,1024]{3,2,1,0:T(8,128)(2,1)S(1)}, bf16[2,8,16,1024]{3,2,1,0:T(8,128)(2,1)}, u32[]{:S(2)}, u32[]{:S(2)}) %collective-permute-start.1) | collective-permute-done | bytes 524320 | tf_op jit(solution)/shard_map/ppermute | solution.py:22
  76.0 58.3 %shard_map.85 = (f32[8,32,1024]{2,1,0:T(8,128)}, f32[8,32,1024]{2,1,0:T(8,128)}, f32[8,32,1024]{2,1,0:T(8,128)}) custom-call(bf16[8,32,1024]{2,1,0:T(8,128)(2,1)} %q_ref.1, bf16[8,32,1024]{2,1,0:T(8,128)(2,1)} %g_ref.1, bf16[8,32,1024]{2,1,0:T(8,128)(2,1)} %k_ref.1, bf16[8,32,1024]{2,1,0:T(8,128)(2,1)} %v_ref.1, ...), custom_call_target="tpu_custom_call" | custom-call | tf_op jit(solution)/shard_map/pallas_call | solution.py:142
  134.3 1.2 copy-done
  135.5 2.3 %copy_bitcast_fusion = f32[3,8,4,8,1024]{4,2,1,3,0:T(4,128)S(1)} fusion(bf16[3,4,8,8,1024]{4,1,0,3,2:T(4,128)(2,1)} %bitcast.40), kind=kLoop, calls=%fused_computation | loop fusion | flops 786432 | bytes 4718592 | tf_op jit(solution)/shard_map/convert_element_type | solution.py:239
  137.8 2.7 %reshape.207 = f32[3,32,8,1024]{3,1,2,0:T(8,128)} reshape(f32[3,8,4,8,1024]{4,2,1,3,0:T(4,128)S(1)} %copy_bitcast_fusion) | data formatting | bytes 6291456 | tf_op jit(solution)/shard_map/convert_element_type | solution.py:239
  140.5 4.2 %fusion.1 = (bf16[8,32,1024]{2,1,0:T(8,128)(2,1)}, bf16[8,32,1024]{2,1,0:T(8,128)(2,1)}, bf16[8,32,1024]{2,1,0:T(8,128)(2,1)}) fusion(f32[8,32,1024]{2,1,0:T(8,128)} %get-tuple-element.8, f32[3,8,32,1024]{3,2,1,0:T(8,128)} %bitcast.37, f32[8,32,1024]{2,1,0:T(8,128)} %get-tuple-element.7, f32[8,32,1024]{2,1,0:T(8,128)} %get-tuple-element.6), kind=kLoop, calls=%fused_computation.5 | loop fusion | flops 1572864 | bytes 7864320 | tf_op jit(solution)/shard_map/convert_element_type | solution.py:240
  (24 shorter events, 0.2 us)
Async XLA Ops:
  4.9 4.4 %copy-start.1 = (bf16[8,32,1024]{2,1,0:T(8,128)(2,1)S(1)}, bf16[8,32,1024]{2,1,0:T(8,128)(2,1)}, u32[]{:S(2)}) copy-start(bf16[8,32,1024]{2,1,0:T(8,128)(2,1)} %k_ref.1) | copy-start | bytes 1572868
  4.9 4.4 %copy-start.2 = (bf16[8,32,1024]{2,1,0:T(8,128)(2,1)S(1)}, bf16[8,32,1024]{2,1,0:T(8,128)(2,1)}, u32[]{:S(2)}) copy-start(bf16[8,32,1024]{2,1,0:T(8,128)(2,1)} %v_ref.1) | copy-start | bytes 1572868
  4.9 31.6 %all-to-all-start = ((bf16[4,32,8,1024]{3,2,0,1:T(8,128)(2,1)}), bf16[4,32,8,1024]{3,2,0,1:T(8,128)(2,1)S(1)}, u32[]{:S(2)}, u32[]{:S(2)}) async-start(bf16[4,32,8,1024]{3,2,0,1:T(8,128)(2,1)} %copy.15), calls=%async_computation | async-start | bytes 4194304 | tf_op jit(solution)/shard_map/all_to_all | solution.py:225
  10.4 46.3 %collective-permute-start.2 = (bf16[2,8,32,1024]{3,2,1,0:T(8,128)(2,1)}, bf16[2,8,32,1024]{3,2,1,0:T(8,128)(2,1)S(1)}, u32[]{:S(2)}, u32[]{:S(2)}) collective-permute-start(bf16[2,8,32,1024]{3,2,1,0:T(8,128)(2,1)} %pad_maximum_fusion), channel_id=1, source_target_pairs={{1,0},{2,1},{3,2},{4,3},{5,4},{6,5},{7,6},{9,8},{10,9},{11,10},{12... | collective-permute-start | bytes 3145736 | tf_op jit(solution)/shard_map/ppermute | solution.py:22
  12.4 46.3 %collective-permute-start = (bf16[2,8,32,1024]{3,2,1,0:T(8,128)(2,1)}, bf16[2,8,32,1024]{3,2,1,0:T(8,128)(2,1)}, u32[]{:S(2)}, u32[]{:S(2)}) collective-permute-start(bf16[2,8,32,1024]{3,2,1,0:T(8,128)(2,1)} %pad_maximum_fusion), channel_id=1, source_target_pairs={{0,1},{1,2},{2,3},{3,4},{4,5},{5,6},{6,7},{8,9},{9,10},{10,11},{11... | collective-permute-start | bytes 3145736 | tf_op jit(solution)/shard_map/ppermute | solution.py:22
  52.8 3.8 %copy-start.5 = (s32[8,16]{1,0:T(8,128)S(1)}, s32[8,16]{1,0:T(8,128)}, u32[]{:S(2)}) copy-start(s32[8,16]{1,0:T(8,128)} %param.10) | copy-start | bytes 1540
  52.8 11.1 %copy-start.6 = (s32[8]{0:T(128)S(1)}, s32[8]{0:T(128)}, u32[]{:S(2)}) copy-start(s32[8]{0:T(128)} %param.11) | copy-start | bytes 100
  52.8 81.5 %all-to-all-start.1 = ((bf16[3,4,64,1024]{3,1,0,2:T(4,128)(2,1)}), bf16[3,4,64,1024]{3,1,0,2:T(4,128)(2,1)S(1)}, u32[]{:S(2)}, u32[]{:S(2)}) async-start(bf16[3,4,64,1024]{3,1,0,2:T(4,128)(2,1)} %copy.17), calls=%async_computation.1 | async-start | bytes 3145728 | tf_op jit(solution)/shard_map/all_to_all | solution.py:237
  56.7 19.3 %copy-start.3 = (bf16[2,8,32,1024]{3,2,1,0:T(8,128)(2,1)}, bf16[2,8,32,1024]{3,2,1,0:T(8,128)(2,1)S(1)}, u32[]{:S(2)}) copy-start(bf16[2,8,32,1024]{3,2,1,0:T(8,128)(2,1)S(1)} %collective-permute-done.2.r1_ref) | copy-start | bytes 3145732
  56.8 16.3 %collective-permute-start.3 = (bf16[2,8,16,1024]{3,2,1,0:T(8,128)(2,1)S(1)}, bf16[2,8,16,1024]{3,2,1,0:T(8,128)(2,1)S(1)}, u32[]{:S(2)}, u32[]{:S(2)}) collective-permute-start(bf16[2,8,16,1024]{3,2,1,0:T(8,128)(2,1)S(1)} %slice.9), channel_id=1, source_target_pairs={{1,0},{2,1},{3,2},{4,3},{5,4},{6,5},{7,6},{9,8},{10,9},{11,10},{12... | collective-permute-start | bytes 1572872 | tf_op jit(solution)/shard_map/ppermute | solution.py:22
  59.9 16.1 %collective-permute-start.1 = (bf16[2,8,16,1024]{3,2,1,0:T(8,128)(2,1)S(1)}, bf16[2,8,16,1024]{3,2,1,0:T(8,128)(2,1)}, u32[]{:S(2)}, u32[]{:S(2)}) collective-permute-start(bf16[2,8,16,1024]{3,2,1,0:T(8,128)(2,1)S(1)} %slice.8), channel_id=1, source_target_pairs={{0,1},{1,2},{2,3},{3,4},{4,5},{5,6},{6,7},{8,9},{9,10},{10,11},{11... | collective-permute-start | bytes 1572872 | tf_op jit(solution)/shard_map/ppermute | solution.py:22
  73.1 3.0 %copy-start.4 = (bf16[2,8,16,1024]{3,2,1,0:T(8,128)(2,1)}, bf16[2,8,16,1024]{3,2,1,0:T(8,128)(2,1)S(1)}, u32[]{:S(2)}) copy-start(bf16[2,8,16,1024]{3,2,1,0:T(8,128)(2,1)S(1)} %collective-permute-done.3.r2_ref) | copy-start | bytes 1572868
  134.3 1.2 copy-start

commit v6 on v5

--- a/solution.py
+++ b/solution.py
@@ -70,23 +70,57 @@
 
 def fused_row_kernel(q_ref, g_ref, k_ref, v_ref, l2_ref, l1_ref, r1_ref, r2_ref, bias_ref,
                      qg_ref, kg_ref, vg_ref,
-                     own_s, s_l2, s_l1, s_r1, s_r2, x_r2, x_r1, x_l1, x_l2, send_sem, recv_sem):
+                     own_s, near_l, near_r, s_fl, s_fr, s_nl, s_nr, x_fr, x_fl, x_nr, x_nl,
+                     far_send, far_recv_r, far_recv_l, near_send, near_recv):
     rows, cc, width = q_ref.shape
     w2 = l2_ref.shape[2]
     w1 = l1_ref.shape[2]
     n = lax.axis_size("rcol")
     me = lax.axis_index("rcol")
     here = (lax.axis_index("slide"), lax.axis_index("rrow"))
+    mesh_ids = pl.DeviceIdType.MESH
 
     def dev(distance):
         return here + (lax.rem(me + distance + n, n),)
 
     barrier = pltpu.get_barrier_semaphore()
-    for distance in (-2, -1, 1, 2):
-        pl.semaphore_signal(barrier, 1, device_id=dev(distance), device_id_type=pl.DeviceIdType.MESH)
-    pl.semaphore_wait(barrier, 4)
-
-    routes = ((s_l2, x_r2, -2), (s_l1, x_r1, -1), (s_r1, x_l1, 1), (s_r2, x_l2, 2))
+    for distance in (-1, 1):
+        pl.semaphore_signal(barrier, 1, device_id=dev(distance), device_id_type=mesh_ids)
+    pl.semaphore_wait(barrier, 2)
+
+    def far_copy(r, to_left):
+        if to_left:
+            return pltpu.make_async_remote_copy(
+                src_ref=s_fl.at[:, pl.ds(r, 1)], dst_ref=x_fr.at[:, pl.ds(r, 1)],
+                send_sem=far_send.at[0], recv_sem=far_recv_r.at[r],
+                device_id=dev(-1), device_id_type=mesh_ids)
+        return pltpu.make_async_remote_copy(
+            src_ref=s_fr.at[:, pl.ds(r, 1)], dst_ref=x_fl.at[:, pl.ds(r, 1)],
+            send_sem=far_send.at[1], recv_sem=far_recv_l.at[r],
+            device_id=dev(1), device_id_type=mesh_ids)
+
+    def near_copy(r, to_left, whole=False):
+        rs = slice(None) if whole else pl.ds(r, 1)
+        if to_left:
+            return pltpu.make_async_remote_copy(
+                src_ref=s_nl.at[:, rs], dst_ref=x_nr.at[:, rs],
+                send_sem=near_send.at[0], recv_sem=near_recv.at[0],
+                device_id=dev(-1), device_id_type=mesh_ids)
+        return pltpu.make_async_remote_copy(
+            src_ref=s_nr.at[:, rs], dst_ref=x_nl.at[:, rs],
+            send_sem=near_send.at[1], recv_sem=near_recv.at[1],
+            device_id=dev(1), device_id_type=mesh_ids)
+
+    def send_near(r):
+        far_copy(r, True).wait_recv()
+        far_copy(r, False).wait_recv()
+        f32 = jnp.float32
+        s_nl[:, r, :w1 - w2] = near_l[:, r, :w1 - w2].astype(jnp.bfloat16)
+        s_nl[:, r, w1 - w2:] = (near_l[:, r, w1 - w2:] + x_fr[:, r].astype(f32)).astype(jnp.bfloat16)
+        s_nr[:, r, :w2] = (near_r[:, r, :w2] + x_fl[:, r].astype(f32)).astype(jnp.bfloat16)
+        s_nr[:, r, w2:] = near_r[:, r, w2:].astype(jnp.bfloat16)
+        near_copy(r, True).start()
+        near_copy(r, False).start()
 
     def row_step(r, carry):
         def span(which, own_ref):
@@ -99,37 +133,31 @@
         dq, dk, dv = block_grads(q_ref[r], g_ref[r], span(0, k_ref), span(1, v_ref), bias_ref[r])
         qg_ref[r] = dq
         for which, full in ((0, dk), (1, dv)):
-            s_l2[which, r] = full[:w2].astype(jnp.bfloat16)
-            s_l1[which, r] = full[w2:w2 + w1].astype(jnp.bfloat16)
+            s_fl[which, r] = full[:w2].astype(jnp.bfloat16)
+            near_l[which, r] = full[w2:w2 + w1]
             own_s[which, r] = full[w2 + w1:w2 + w1 + cc]
-            s_r1[which, r] = full[w2 + w1 + cc:w2 + 2 * w1 + cc].astype(jnp.bfloat16)
-            s_r2[which, r] = full[w2 + 2 * w1 + cc:].astype(jnp.bfloat16)
-        for slot, (src, dst, distance) in enumerate(routes):
-            pltpu.make_async_remote_copy(
-                src_ref=src.at[:, pl.ds(r, 1)],
-                dst_ref=dst.at[:, pl.ds(r, 1)],
-                send_sem=send_sem.at[slot],
-                recv_sem=recv_sem.at[slot],
-                device_id=dev(distance),
-                device_id_type=pl.DeviceIdType.MESH,
-            ).start()
+            near_r[which, r] = full[w2 + w1 + cc:w2 + 2 * w1 + cc]
+            s_fr[which, r] = full[w2 + 2 * w1 + cc:].astype(jnp.bfloat16)
+        far_copy(r, True).start()
+        far_copy(r, False).start()
+
+        @pl.when(r > 0)
+        def _():
+            send_near(r - 1)
+
         return carry
 
     lax.fori_loop(0, rows, row_step, 0)
-    for slot, (src, dst, distance) in enumerate(routes):
+    send_near(rows - 1)
+    for src, dst, slot in ((s_fl, x_fr, 0), (s_fr, x_fl, 1)):
         pltpu.make_async_remote_copy(
-            src_ref=src, dst_ref=dst, send_sem=send_sem.at[slot], recv_sem=recv_sem.at[slot],
-            device_id=dev(distance), device_id_type=pl.DeviceIdType.MESH,
-        ).wait()
+            src_ref=src, dst_ref=dst, send_sem=far_send.at[slot], recv_sem=far_recv_r.at[0],
+            device_id=dev(1 - 2 * (1 - slot)), device_id_type=mesh_ids).wait_send()
+    for to_left in (True, False):
+        near_copy(0, to_left, whole=True).wait()
     f32 = jnp.float32
     for which, out_ref in ((0, kg_ref), (1, vg_ref)):
-        total = own_s[which] + x_r1[which].astype(f32) + x_l1[which].astype(f32)
-        low = total[:, :w2] + x_l2[which].astype(f32)
-        high = total[:, cc - w2:] + x_r2[which].astype(f32)
-        out_ref[:, :w2] = low
-        out_ref[:, cc - w2:] = high
-        if cc > 2 * w2:
-            out_ref[:, w2:cc - w2] = total[:, w2:cc - w2]
+        out_ref[...] = own_s[which] + x_nr[which].astype(f32) + x_nl[which].astype(f32)
 
 
 def fused_row(queries, out_grad, key_grid, value_grid, l2, l1, r1, r2, bias):
@@ -139,23 +167,29 @@
     vmem = pl.BlockSpec(memory_space=pltpu.VMEM)
     grads = jax.ShapeDtypeStruct((rows, cc, width), jnp.float32)
     bf = jnp.bfloat16
+    f32 = jnp.float32
     return pl.pallas_call(
         fused_row_kernel,
         in_specs=[vmem] * 9,
         out_specs=[vmem] * 3,
         out_shape=(grads, grads, grads),
         scratch_shapes=[
-            pltpu.VMEM((2, rows, cc, width), jnp.float32),
+            pltpu.VMEM((2, rows, cc, width), f32),
+            pltpu.VMEM((2, rows, w1, width), f32),
+            pltpu.VMEM((2, rows, w1, width), f32),
+            pltpu.VMEM((2, rows, w2, width), bf),
             pltpu.VMEM((2, rows, w2, width), bf),
             pltpu.VMEM((2, rows, w1, width), bf),
             pltpu.VMEM((2, rows, w1, width), bf),
             pltpu.VMEM((2, rows, w2, width), bf),
             pltpu.VMEM((2, rows, w2, width), bf),
-            pltpu.VMEM((2, rows, w1, width), bf),
-            pltpu.VMEM((2, rows, w1, width), bf),
-            pltpu.VMEM((2, rows, w2, width), bf),
-            pltpu.SemaphoreType.DMA((4,)),
-            pltpu.SemaphoreType.DMA((4,)),
+            pltpu.VMEM((2, rows, cc, width), bf),
+            pltpu.VMEM((2, rows, cc, width), bf),
+            pltpu.SemaphoreType.DMA((2,)),
+            pltpu.SemaphoreType.DMA((rows,)),
+            pltpu.SemaphoreType.DMA((rows,)),
+            pltpu.SemaphoreType.DMA((2,)),
+            pltpu.SemaphoreType.DMA((2,)),
         ],
         compiler_params=pltpu.CompilerParams(
             collective_id=0, has_side_effects=True, vmem_limit_bytes=60 * 1024 * 1024

time: 146 us -> 136 us (0.932)
  Pallas kernels: 69.1 us -> 58.2 us
    pallas_call x1, Pallas kernels: 58.3 us -> 47.3 us  [fused_row(): pl.pallas_call(fused_row_kernel, in_specs=[vmem] * 9, out_specs=[vmem] *...]
  transfers between devices with their start and end apart: 6 -> 6, of which waited for: 3 -> 3; matrix products, arithmetic and copies ran while one was open for 6% -> 6% of each run, Pallas kernels for 48% -> 43%
where the time goes in v6:
time: 136 us; the launch traced here: 134 us
  Pallas kernels  58.2 us (43%)
  waiting for transfers between devices  31.7 us (23%)
  starting transfers between devices  19.8 us (15%)
  local copies, waits for them, and re-layouts  12.8 us (9%)
  other arithmetic  10.5 us (8%)
    pallas_call x1, Pallas kernels, fused_row(): pl.pallas_call(fused_row_kernel, in_specs=[vmem] * 9, out_specs=[vmem] *...  47.3 us
    all_to_all x1, waiting for transfers between devices, body(): lax.all_to_all(stacked, 'rrow', split_axis=1, concat_axis=2, tiled=True)  20.2 us
    ppermute x4, starting transfers between devices, shifted(): return lax.ppermute(block, axis, route)  11.7 us
    ppermute x4, waiting for transfers between devices, shifted(): return lax.ppermute(block, axis, route)  11.4 us
    pallas_call x1, Pallas kernels, column_attention(): pl.pallas_call(column_kernel, grid=(strip // per,), in_specs=[pl.BlockSpe...  10.9 us
    all_to_all x1, starting transfers between devices, body(): lax.all_to_all(stacked, 'rrow', split_axis=1, concat_axis=2, tiled=True)  4.43 us
    convert_element_type x1, other arithmetic, body(): (row + col).astype(jnp.bfloat16)  4.21 us
    pallas_call x1, local copies, waits for them, and re-layouts, column_attention(): pl.pallas_call(column_kernel, grid=(strip // per,), in_specs=[pl.BlockSpe...  3.8 us
  transfers between devices with their start and end apart: 6, of which 3 were waited for; matrix products, arithmetic and copies ran while one was open for 6% of the time, Pallas kernels for 43%

profile of v6, /device:TPU:48, one launch (start us, length us, event | category | flops | bytes accessed | tf_op | source)
XLA Modules:
  0.0 133.8 jit_solution(13335361242314149541)
XLA Ops:
  0.6 1.8 %maximum_bitcast_fusion = bf16[4,32,8,1024]{3,1,2,0:T(8,128)(2,1)S(1)} fusion(bf16[1,8,32,1024]{3,2,1,0:T(8,128)(2,1)} %bitcast.46, bf16[1,8,32,1024]{3,2,1,0:T(8,128)(2,1)} %bitcast.43, bf16[1,8,32,1024]{3,2,1,0:T(8,128)(2,1)} %bitcast.41, bf16[1,8,32,1024]{3,2,1,0:T(8,128)(2,1)} %bitcast.45), kind=kLoop, calls=%fused_computation.1 | loop fusion | flops 3145728 | bytes 4194304 | tf_op jit(solution)/shard_map/transpose | solution.py:258
  2.4 2.5 %copy.15 = bf16[4,32,8,1024]{3,2,0,1:T(8,128)(2,1)} copy(bf16[4,32,8,1024]{3,1,2,0:T(8,128)(2,1)S(1)} %maximum_bitcast_fusion) | data formatting | bytes 4194304 | tf_op jit(solution)/shard_map/transpose | solution.py:258
  4.9 4.4 %all-to-all-start = ((bf16[4,32,8,1024]{3,2,0,1:T(8,128)(2,1)}), bf16[4,32,8,1024]{3,2,0,1:T(8,128)(2,1)S(1)}, u32[]{:S(2)}, u32[]{:S(2)}) async-start(bf16[4,32,8,1024]{3,2,0,1:T(8,128)(2,1)} %copy.15), calls=%async_computation | async-start | bytes 4194304 | tf_op jit(solution)/shard_map/all_to_all | solution.py:259
  9.3 1.1 pad_maximum_fusion
  10.4 2.0 %collective-permute-start.2 = (bf16[2,8,32,1024]{3,2,1,0:T(8,128)(2,1)}, bf16[2,8,32,1024]{3,2,1,0:T(8,128)(2,1)S(1)}, u32[]{:S(2)}, u32[]{:S(2)}) collective-permute-start(bf16[2,8,32,1024]{3,2,1,0:T(8,128)(2,1)} %pad_maximum_fusion), channel_id=1, source_target_pairs={{1,0},{2,1},{3,2},{4,3},{5,4},{6,5},{7,6},{9,8},{10,9},{11,10},{12... | collective-permute-start | bytes 3145736 | tf_op jit(solution)/shard_map/ppermute | solution.py:22
  12.4 3.8 %collective-permute-start = (bf16[2,8,32,1024]{3,2,1,0:T(8,128)(2,1)}, bf16[2,8,32,1024]{3,2,1,0:T(8,128)(2,1)}, u32[]{:S(2)}, u32[]{:S(2)}) collective-permute-start(bf16[2,8,32,1024]{3,2,1,0:T(8,128)(2,1)} %pad_maximum_fusion), channel_id=1, source_target_pairs={{0,1},{1,2},{2,3},{3,4},{4,5},{5,6},{6,7},{8,9},{9,10},{10,11},{11... | collective-permute-start | bytes 3145736 | tf_op jit(solution)/shard_map/ppermute | solution.py:22
  16.3 20.2 %all-to-all-done = bf16[4,32,8,1024]{3,2,0,1:T(8,128)(2,1)S(1)} async-done(((bf16[4,32,8,1024]{3,2,0,1:T(8,128)(2,1)}), bf16[4,32,8,1024]{3,2,0,1:T(8,128)(2,1)S(1)}, u32[]{:S(2)}, u32[]{:S(2)}) %all-to-all-start) | async-done | bytes 2097184 | tf_op jit(solution)/shard_map/all_to_all | solution.py:259
  36.5 1.6 %copy.21 = bf16[4,8,4,8,1024]{4,3,1,2,0:T(8,128)(2,1)} copy(bf16[4,8,4,8,1024]{4,3,0,2,1:T(8,128)(2,1)S(1)} %bitcast.39) | data formatting | bytes 4194304 | tf_op jit(solution)/shard_map/all_to_all | solution.py:259
  38.1 10.9 %shard_map.86 = bf16[3,4,64,1024]{3,2,1,0:T(8,128)(2,1)} custom-call(bf16[4,4,64,1024]{3,2,1,0:T(8,128)(2,1)} %bitcast.38), custom_call_target="tpu_custom_call" | custom-call | tf_op jit(solution)/shard_map/pallas_call | solution.py:219
  49.0 3.8 %copy.17 = bf16[3,4,64,1024]{3,1,0,2:T(4,128)(2,1)} copy(bf16[3,4,64,1024]{3,2,1,0:T(8,128)(2,1)} %shard_map.86) | data formatting | bytes 3145728 | tf_op jit(solution)/shard_map/pallas_call | solution.py:219
  52.8 3.7 %all-to-all-start.1 = ((bf16[3,4,64,1024]{3,1,0,2:T(4,128)(2,1)}), bf16[3,4,64,1024]{3,1,0,2:T(4,128)(2,1)S(1)}, u32[]{:S(2)}, u32[]{:S(2)}) async-start(bf16[3,4,64,1024]{3,1,0,2:T(4,128)(2,1)} %copy.17), calls=%async_computation.1 | async-start | bytes 3145728 | tf_op jit(solution)/shard_map/all_to_all | solution.py:271
  56.5 0.1 multiply_reduce_fusion
  56.6 0.1 broadcast_compare_fusion
  56.8 2.0 %collective-permute-start.3 = (bf16[2,8,16,1024]{3,2,1,0:T(8,128)(2,1)S(1)}, bf16[2,8,16,1024]{3,2,1,0:T(8,128)(2,1)S(1)}, u32[]{:S(2)}, u32[]{:S(2)}) collective-permute-start(bf16[2,8,16,1024]{3,2,1,0:T(8,128)(2,1)S(1)} %slice.9), channel_id=1, source_target_pairs={{1,0},{2,1},{3,2},{4,3},{5,4},{6,5},{7,6},{9,8},{10,9},{11,10},{12... | collective-permute-start | bytes 1572872 | tf_op jit(solution)/shard_map/ppermute | solution.py:22
  58.8 1.1 slice.8
  59.9 3.8 %collective-permute-start.1 = (bf16[2,8,16,1024]{3,2,1,0:T(8,128)(2,1)S(1)}, bf16[2,8,16,1024]{3,2,1,0:T(8,128)(2,1)}, u32[]{:S(2)}, u32[]{:S(2)}) collective-permute-start(bf16[2,8,16,1024]{3,2,1,0:T(8,128)(2,1)S(1)} %slice.8), channel_id=1, source_target_pairs={{0,1},{1,2},{2,3},{3,4},{4,5},{5,6},{6,7},{8,9},{9,10},{10,11},{11... | collective-permute-start | bytes 1572872 | tf_op jit(solution)/shard_map/ppermute | solution.py:22
  63.8 0.8 fusion.9.bias_ref
  64.6 8.5 %collective-permute-done.3.r2_ref = bf16[2,8,16,1024]{3,2,1,0:T(8,128)(2,1)S(1)} collective-permute-done((bf16[2,8,16,1024]{3,2,1,0:T(8,128)(2,1)S(1)}, bf16[2,8,16,1024]{3,2,1,0:T(8,128)(2,1)S(1)}, u32[]{:S(2)}, u32[]{:S(2)}) %collective-permute-start.3) | collective-permute-done | bytes 524320 | tf_op jit(solution)/shard_map/ppermute | solution.py:22
  73.1 3.0 %collective-permute-done.1.l2_ref = bf16[2,8,16,1024]{3,2,1,0:T(8,128)(2,1)} collective-permute-done((bf16[2,8,16,1024]{3,2,1,0:T(8,128)(2,1)S(1)}, bf16[2,8,16,1024]{3,2,1,0:T(8,128)(2,1)}, u32[]{:S(2)}, u32[]{:S(2)}) %collective-permute-start.1) | collective-permute-done | bytes 524320 | tf_op jit(solution)/shard_map/ppermute | solution.py:22
  76.0 47.3 %shard_map.85 = (f32[8,32,1024]{2,1,0:T(8,128)}, f32[8,32,1024]{2,1,0:T(8,128)}, f32[8,32,1024]{2,1,0:T(8,128)}) custom-call(bf16[8,32,1024]{2,1,0:T(8,128)(2,1)} %q_ref.1, bf16[8,32,1024]{2,1,0:T(8,128)(2,1)} %g_ref.1, bf16[8,32,1024]{2,1,0:T(8,128)(2,1)} %k_ref.1, bf16[8,32,1024]{2,1,0:T(8,128)(2,1)} %v_ref.1, ...), custom_call_target="tpu_custom_call" | custom-call | tf_op jit(solution)/shard_map/pallas_call | solution.py:171
  123.4 1.2 copy-done
  124.5 2.3 %copy_bitcast_fusion = f32[3,8,4,8,1024]{4,2,1,3,0:T(4,128)S(1)} fusion(bf16[3,4,8,8,1024]{4,1,0,3,2:T(4,128)(2,1)} %bitcast.40), kind=kLoop, calls=%fused_computation | loop fusion | flops 786432 | bytes 4718592 | tf_op jit(solution)/shard_map/convert_element_type | solution.py:273
  126.9 2.7 %reshape.207 = f32[3,32,8,1024]{3,1,2,0:T(8,128)} reshape(f32[3,8,4,8,1024]{4,2,1,3,0:T(4,128)S(1)} %copy_bitcast_fusion) | data formatting | bytes 6291456 | tf_op jit(solution)/shard_map/convert_element_type | solution.py:273
  129.5 4.2 %fusion.1 = (bf16[8,32,1024]{2,1,0:T(8,128)(2,1)}, bf16[8,32,1024]{2,1,0:T(8,128)(2,1)}, bf16[8,32,1024]{2,1,0:T(8,128)(2,1)}) fusion(f32[8,32,1024]{2,1,0:T(8,128)} %get-tuple-element.8, f32[3,8,32,1024]{3,2,1,0:T(8,128)} %bitcast.37, f32[8,32,1024]{2,1,0:T(8,128)} %get-tuple-element.7, f32[8,32,1024]{2,1,0:T(8,128)} %get-tuple-element.6), kind=kLoop, calls=%fused_computation.5 | loop fusion | flops 1572864 | bytes 7864320 | tf_op jit(solution)/shard_map/convert_element_type | solution.py:274
  (24 shorter events, 0.2 us)
Async XLA Ops:
  4.9 4.4 %copy-start.1 = (bf16[8,32,1024]{2,1,0:T(8,128)(2,1)S(1)}, bf16[8,32,1024]{2,1,0:T(8,128)(2,1)}, u32[]{:S(2)}) copy-start(bf16[8,32,1024]{2,1,0:T(8,128)(2,1)} %k_ref.1) | copy-start | bytes 1572868
  4.9 4.4 %copy-start.2 = (bf16[8,32,1024]{2,1,0:T(8,128)(2,1)S(1)}, bf16[8,32,1024]{2,1,0:T(8,128)(2,1)}, u32[]{:S(2)}) copy-start(bf16[8,32,1024]{2,1,0:T(8,128)(2,1)} %v_ref.1) | copy-start | bytes 1572868
  4.9 31.6 %all-to-all-start = ((bf16[4,32,8,1024]{3,2,0,1:T(8,128)(2,1)}), bf16[4,32,8,1024]{3,2,0,1:T(8,128)(2,1)S(1)}, u32[]{:S(2)}, u32[]{:S(2)}) async-start(bf16[4,32,8,1024]{3,2,0,1:T(8,128)(2,1)} %copy.15), calls=%async_computation | async-start | bytes 4194304 | tf_op jit(solution)/shard_map/all_to_all | solution.py:259
  10.4 46.3 %collective-permute-start.2 = (bf16[2,8,32,1024]{3,2,1,0:T(8,128)(2,1)}, bf16[2,8,32,1024]{3,2,1,0:T(8,128)(2,1)S(1)}, u32[]{:S(2)}, u32[]{:S(2)}) collective-permute-start(bf16[2,8,32,1024]{3,2,1,0:T(8,128)(2,1)} %pad_maximum_fusion), channel_id=1, source_target_pairs={{1,0},{2,1},{3,2},{4,3},{5,4},{6,5},{7,6},{9,8},{10,9},{11,10},{12... | collective-permute-start | bytes 3145736 | tf_op jit(solution)/shard_map/ppermute | solution.py:22
  12.4 46.3 %collective-permute-start = (bf16[2,8,32,1024]{3,2,1,0:T(8,128)(2,1)}, bf16[2,8,32,1024]{3,2,1,0:T(8,128)(2,1)}, u32[]{:S(2)}, u32[]{:S(2)}) collective-permute-start(bf16[2,8,32,1024]{3,2,1,0:T(8,128)(2,1)} %pad_maximum_fusion), channel_id=1, source_target_pairs={{0,1},{1,2},{2,3},{3,4},{4,5},{5,6},{6,7},{8,9},{9,10},{10,11},{11... | collective-permute-start | bytes 3145736 | tf_op jit(solution)/shard_map/ppermute | solution.py:22
  52.8 3.8 %copy-start.5 = (s32[8,16]{1,0:T(8,128)S(1)}, s32[8,16]{1,0:T(8,128)}, u32[]{:S(2)}) copy-start(s32[8,16]{1,0:T(8,128)} %param.10) | copy-start | bytes 1540
  52.8 11.1 %copy-start.6 = (s32[8]{0:T(128)S(1)}, s32[8]{0:T(128)}, u32[]{:S(2)}) copy-start(s32[8]{0:T(128)} %param.11) | copy-start | bytes 100
  52.8 70.6 %all-to-all-start.1 = ((bf16[3,4,64,1024]{3,1,0,2:T(4,128)(2,1)}), bf16[3,4,64,1024]{3,1,0,2:T(4,128)(2,1)S(1)}, u32[]{:S(2)}, u32[]{:S(2)}) async-start(bf16[3,4,64,1024]{3,1,0,2:T(4,128)(2,1)} %copy.17), calls=%async_computation.1 | async-start | bytes 3145728 | tf_op jit(solution)/shard_map/all_to_all | solution.py:271
  56.7 19.3 %copy-start.3 = (bf16[2,8,32,1024]{3,2,1,0:T(8,128)(2,1)}, bf16[2,8,32,1024]{3,2,1,0:T(8,128)(2,1)S(1)}, u32[]{:S(2)}) copy-start(bf16[2,8,32,1024]{3,2,1,0:T(8,128)(2,1)S(1)} %collective-permute-done.2.r1_ref) | copy-start | bytes 3145732
  56.8 16.3 %collective-permute-start.3 = (bf16[2,8,16,1024]{3,2,1,0:T(8,128)(2,1)S(1)}, bf16[2,8,16,1024]{3,2,1,0:T(8,128)(2,1)S(1)}, u32[]{:S(2)}, u32[]{:S(2)}) collective-permute-start(bf16[2,8,16,1024]{3,2,1,0:T(8,128)(2,1)S(1)} %slice.9), channel_id=1, source_target_pairs={{1,0},{2,1},{3,2},{4,3},{5,4},{6,5},{7,6},{9,8},{10,9},{11,10},{12... | collective-permute-start | bytes 1572872 | tf_op jit(solution)/shard_map/ppermute | solution.py:22
  59.9 16.1 %collective-permute-start.1 = (bf16[2,8,16,1024]{3,2,1,0:T(8,128)(2,1)S(1)}, bf16[2,8,16,1024]{3,2,1,0:T(8,128)(2,1)}, u32[]{:S(2)}, u32[]{:S(2)}) collective-permute-start(bf16[2,8,16,1024]{3,2,1,0:T(8,128)(2,1)S(1)} %slice.8), channel_id=1, source_target_pairs={{0,1},{1,2},{2,3},{3,4},{4,5},{5,6},{6,7},{8,9},{9,10},{10,11},{11... | collective-permute-start | bytes 1572872 | tf_op jit(solution)/shard_map/ppermute | solution.py:22
  73.1 3.0 %copy-start.4 = (bf16[2,8,16,1024]{3,2,1,0:T(8,128)(2,1)}, bf16[2,8,16,1024]{3,2,1,0:T(8,128)(2,1)S(1)}, u32[]{:S(2)}) copy-start(bf16[2,8,16,1024]{3,2,1,0:T(8,128)(2,1)S(1)} %collective-permute-done.3.r2_ref) | copy-start | bytes 1572868
  123.4 1.2 copy-start

commit v7 on v6

--- a/solution.py
+++ b/solution.py
@@ -197,7 +197,7 @@
     )(queries, out_grad, key_grid, value_grid, l2, l1, r1, r2, bias)
 
 
-def column_kernel(x_ref, o_ref):
+def column_kernel(x_ref, order_ref, o_ref):
     per = x_ref.shape[1]
     rows = x_ref.shape[2]
 
@@ -213,16 +213,19 @@
             o_ref[which, c] = full[c * rows:(c + 1) * rows].astype(jnp.bfloat16)
 
 
-def column_attention(whole):
+def column_attention(whole, order):
     arrays, strip, rows, width = whole.shape
     per = max(1, LANES // rows)
     return pl.pallas_call(
         column_kernel,
         grid=(strip // per,),
-        in_specs=[pl.BlockSpec((arrays, per, rows, width), lambda c: (0, c, 0, 0))],
+        in_specs=[
+            pl.BlockSpec((arrays, per, rows, width), lambda c: (0, c, 0, 0)),
+            pl.BlockSpec(memory_space=pltpu.VMEM),
+        ],
         out_specs=pl.BlockSpec((3, per, rows, width), lambda c: (0, c, 0, 0)),
         out_shape=jax.ShapeDtypeStruct((3, strip, rows, width), jnp.bfloat16),
-    )(whole)
+    )(whole, order)
 
 
 def band_bias(mask_rows, offsets, first_col, grid_cols, block_cols):
@@ -267,7 +270,8 @@
     first_col = lax.axis_index("rcol") * col_count
     bias = band_bias(tissue_mask, band_offset, first_col, grid_cols, col_count)
 
-    col_out = column_attention(whole)
+    order = jnp.concatenate([l2[0, 0, :8, :LANES], r2[0, 0, :8, :LANES]], axis=0)
+    col_out = column_attention(whole, order)
     back = lax.all_to_all(col_out, "rrow", split_axis=2, concat_axis=1, tiled=True)
     row_grads = fused_row(queries, out_grad, key_grid, value_grid, l2, l1, r1, r2, bias)
     back = back.transpose(0, 2, 1, 3).astype(jnp.float32)

time: 136 us -> 134 us (0.985)
  waiting for transfers between devices: 31.7 us -> 25.4 us
  local copies, waits for them, and re-layouts: 12.8 us -> 15.7 us
  Pallas kernels: 58.2 us -> 59.8 us
    all_to_all x1, waiting for transfers between devices: 20.2 us -> 0.01 us  [body(): lax.all_to_all(stacked, 'rrow', split_axis=1, concat_axis=2, tiled=True)]
    ppermute x4, waiting for transfers between devices: 11.4 us -> 25.4 us  [shifted(): return lax.ppermute(block, axis, route)]
    slice x1, local copies, waits for them, and re-layouts: 0.04 us -> 1.88 us  [body(): r2 = shifted(r1[:, :, :far], 'rcol', -1)]
    pallas_call x1, Pallas kernels: 47.3 us -> 49 us  [fused_row(): pl.pallas_call(fused_row_kernel, in_specs=[vmem] * 9, out_specs=[vmem] *...]
    transpose x1, other arithmetic: 1.78 us -> 0.26 us  [body(): jnp.stack([queries, key_grid, value_grid, out_grad]).transpose(0, 2, 1, 3)]
  transfers between devices with their start and end apart: 6 -> 6, of which waited for: 3 -> 3; matrix products, arithmetic and copies ran while one was open for 6% -> 6% of each run, Pallas kernels for 43% -> 37%
where the time goes in v7:
time: 134 us; the launch traced here: 133 us
  Pallas kernels  59.8 us (45%)
  waiting for transfers between devices  25.4 us (19%)
  starting transfers between devices  20.4 us (15%)
  local copies, waits for them, and re-layouts  15.7 us (12%)
  other arithmetic  10.9 us (8%)
    pallas_call x1, Pallas kernels, fused_row(): pl.pallas_call(fused_row_kernel, in_specs=[vmem] * 9, out_specs=[vmem] *...  49 us
    ppermute x4, waiting for transfers between devices, shifted(): return lax.ppermute(block, axis, route)  25.4 us
    ppermute x4, starting transfers between devices, shifted(): return lax.ppermute(block, axis, route)  11.6 us
    pallas_call x1, Pallas kernels, column_attention(): pl.pallas_call(column_kernel, grid=(strip // per,), in_specs=[pl.BlockSpe...  10.8 us
    all_to_all x1, starting transfers between devices, body(): lax.all_to_all(col_out, 'rrow', split_axis=2, concat_axis=1, tiled=True)  4.43 us
    all_to_all x1, starting transfers between devices, body(): lax.all_to_all(stacked, 'rrow', split_axis=1, concat_axis=2, tiled=True)  4.3 us
    convert_element_type x1, other arithmetic, body(): (row + col).astype(jnp.bfloat16)  4.21 us
    pallas_call x1, local copies, waits for them, and re-layouts, column_attention(): pl.pallas_call(column_kernel, grid=(strip // per,), in_specs=[pl.BlockSpe...  3.79 us
  transfers between devices with their start and end apart: 6, of which 3 were waited for; matrix products, arithmetic and copies ran while one was open for 6% of the time, Pallas kernels for 37%

profile of v7, /device:TPU:48, one launch (start us, length us, event | category | flops | bytes accessed | tf_op | source)
XLA Modules:
  0.0 133.0 jit_solution(14005678574737659006)
XLA Ops:
  0.7 2.4 %pad_maximum_fusion = bf16[2,8,32,1024]{3,2,1,0:T(8,128)(2,1)} fusion(bf16[1,8,32,1024]{3,2,1,0:T(8,128)(2,1)} %bitcast.47, bf16[1,8,32,1024]{3,2,1,0:T(8,128)(2,1)} %bitcast.45), kind=kLoop, calls=%fused_computation.12 | loop fusion | flops 524288 | bytes 2097152 | tf_op jit(solution)/shard_map/stack | solution.py:264
  3.1 2.0 %collective-permute-start.2 = (bf16[2,8,32,1024]{3,2,1,0:T(8,128)(2,1)}, bf16[2,8,32,1024]{3,2,1,0:T(8,128)(2,1)}, u32[]{:S(2)}, u32[]{:S(2)}) collective-permute-start(bf16[2,8,32,1024]{3,2,1,0:T(8,128)(2,1)} %pad_maximum_fusion), channel_id=1, source_target_pairs={{1,0},{2,1},{3,2},{4,3},{5,4},{6,5},{7,6},{9,8},{10,9},{11,10},{12... | collective-permute-start | bytes 3145736 | tf_op jit(solution)/shard_map/ppermute | solution.py:22
  5.1 3.8 %collective-permute-start = (bf16[2,8,32,1024]{3,2,1,0:T(8,128)(2,1)}, bf16[2,8,32,1024]{3,2,1,0:T(8,128)(2,1)}, u32[]{:S(2)}, u32[]{:S(2)}) collective-permute-start(bf16[2,8,32,1024]{3,2,1,0:T(8,128)(2,1)} %pad_maximum_fusion), channel_id=1, source_target_pairs={{0,1},{1,2},{2,3},{3,4},{4,5},{5,6},{6,7},{8,9},{9,10},{10,11},{11... | collective-permute-start | bytes 3145736 | tf_op jit(solution)/shard_map/ppermute | solution.py:22
  9.0 0.3 maximum_bitcast_fusion
  9.2 2.5 %copy.15 = bf16[4,32,8,1024]{3,2,0,1:T(8,128)(2,1)} copy(bf16[4,32,8,1024]{3,1,2,0:T(8,128)(2,1)S(1)} %maximum_bitcast_fusion) | data formatting | bytes 4194304 | tf_op jit(solution)/shard_map/transpose | solution.py:261
  11.8 4.3 %all-to-all-start = ((bf16[4,32,8,1024]{3,2,0,1:T(8,128)(2,1)}), bf16[4,32,8,1024]{3,2,0,1:T(8,128)(2,1)S(1)}, u32[]{:S(2)}, u32[]{:S(2)}) async-start(bf16[4,32,8,1024]{3,2,0,1:T(8,128)(2,1)} %copy.15), calls=%async_computation | async-start | bytes 4194304 | tf_op jit(solution)/shard_map/all_to_all | solution.py:262
  16.1 14.3 %collective-permute-done.2.r1_ref = bf16[2,8,32,1024]{3,2,1,0:T(8,128)(2,1)} collective-permute-done((bf16[2,8,32,1024]{3,2,1,0:T(8,128)(2,1)}, bf16[2,8,32,1024]{3,2,1,0:T(8,128)(2,1)}, u32[]{:S(2)}, u32[]{:S(2)}) %collective-permute-start.2) | collective-permute-done | bytes 1048608 | tf_op jit(solution)/shard_map/ppermute | solution.py:22
  30.4 1.9 %slice.17 = bf16[2,8,16,1024]{3,2,1,0:T(8,128)(2,1)} slice(bf16[2,8,32,1024]{3,2,1,0:T(8,128)(2,1)} %collective-permute-done.2.r1_ref), slice={[0:2], [0:8], [0:16], [0:1024]} | slice | bytes 1048576 | tf_op jit(solution)/shard_map/slice | solution.py:268
  32.3 2.0 %collective-permute-start.3 = (bf16[2,8,16,1024]{3,2,1,0:T(8,128)(2,1)}, bf16[2,8,16,1024]{3,2,1,0:T(8,128)(2,1)S(1)}, u32[]{:S(2)}, u32[]{:S(2)}) collective-permute-start(bf16[2,8,16,1024]{3,2,1,0:T(8,128)(2,1)} %slice.17), channel_id=1, source_target_pairs={{1,0},{2,1},{3,2},{4,3},{5,4},{6,5},{7,6},{9,8},{10,9},{11,10},{12... | collective-permute-start | bytes 1572872 | tf_op jit(solution)/shard_map/ppermute | solution.py:22
  34.3 1.9 %slice.16 = bf16[2,8,16,1024]{3,2,1,0:T(8,128)(2,1)} slice(bf16[2,8,32,1024]{3,2,1,0:T(8,128)(2,1)} %collective-permute-done.l1_ref), slice={[0:2], [0:8], [16:32], [0:1024]} | slice | bytes 1048576 | tf_op jit(solution)/shard_map/slice | solution.py:267
  36.2 3.8 %collective-permute-start.1 = (bf16[2,8,16,1024]{3,2,1,0:T(8,128)(2,1)}, bf16[2,8,16,1024]{3,2,1,0:T(8,128)(2,1)S(1)}, u32[]{:S(2)}, u32[]{:S(2)}) collective-permute-start(bf16[2,8,16,1024]{3,2,1,0:T(8,128)(2,1)} %slice.16), channel_id=1, source_target_pairs={{0,1},{1,2},{2,3},{3,4},{4,5},{5,6},{6,7},{8,9},{9,10},{10,11},{11... | collective-permute-start | bytes 1572872 | tf_op jit(solution)/shard_map/ppermute | solution.py:22
  40.0 7.5 %collective-permute-done.3.r2_ref = bf16[2,8,16,1024]{3,2,1,0:T(8,128)(2,1)S(1)} collective-permute-done((bf16[2,8,16,1024]{3,2,1,0:T(8,128)(2,1)}, bf16[2,8,16,1024]{3,2,1,0:T(8,128)(2,1)S(1)}, u32[]{:S(2)}, u32[]{:S(2)}) %collective-permute-start.3) | collective-permute-done | bytes 524320 | tf_op jit(solution)/shard_map/ppermute | solution.py:22
  47.5 3.6 %collective-permute-done.1.l2_ref = bf16[2,8,16,1024]{3,2,1,0:T(8,128)(2,1)S(1)} collective-permute-done((bf16[2,8,16,1024]{3,2,1,0:T(8,128)(2,1)}, bf16[2,8,16,1024]{3,2,1,0:T(8,128)(2,1)S(1)}, u32[]{:S(2)}, u32[]{:S(2)}) %collective-permute-start.1) | collective-permute-done | bytes 524320 | tf_op jit(solution)/shard_map/ppermute | solution.py:22
  51.2 0.6 pad_maximum_fusion.1.order_ref
  51.8 1.6 %copy.21 = bf16[4,8,4,8,1024]{4,3,1,2,0:T(8,128)(2,1)} copy(bf16[4,8,4,8,1024]{4,3,0,2,1:T(8,128)(2,1)S(1)} %bitcast.42) | data formatting | bytes 4194304 | tf_op jit(solution)/shard_map/all_to_all | solution.py:262
  53.4 10.8 %shard_map.86 = bf16[3,4,64,1024]{3,2,1,0:T(8,128)(2,1)} custom-call(bf16[4,4,64,1024]{3,2,1,0:T(8,128)(2,1)} %bitcast.43, bf16[16,128]{1,0:T(8,128)(2,1)} %pad_maximum_fusion.1.order_ref), custom_call_target="tpu_custom_call" | custom-call | tf_op jit(solution)/shard_map/pallas_call | solution.py:219
  64.2 3.8 %copy.17 = bf16[3,4,64,1024]{3,1,0,2:T(4,128)(2,1)} copy(bf16[3,4,64,1024]{3,2,1,0:T(8,128)(2,1)} %shard_map.86) | data formatting | bytes 3145728 | tf_op jit(solution)/shard_map/pallas_call | solution.py:219
  68.0 4.4 %all-to-all-start.1 = ((bf16[3,4,64,1024]{3,1,0,2:T(4,128)(2,1)}), bf16[3,4,64,1024]{3,1,0,2:T(4,128)(2,1)S(1)}, u32[]{:S(2)}, u32[]{:S(2)}) async-start(bf16[3,4,64,1024]{3,1,0,2:T(4,128)(2,1)} %copy.17), calls=%async_computation.1 | async-start | bytes 3145728 | tf_op jit(solution)/shard_map/all_to_all | solution.py:275
  72.8 0.8 fusion.9.bias_ref
  73.5 49.0 %shard_map.85 = (f32[8,32,1024]{2,1,0:T(8,128)}, f32[8,32,1024]{2,1,0:T(8,128)}, f32[8,32,1024]{2,1,0:T(8,128)}) custom-call(bf16[8,32,1024]{2,1,0:T(8,128)(2,1)} %q_ref.1, bf16[8,32,1024]{2,1,0:T(8,128)(2,1)} %g_ref.1, bf16[8,32,1024]{2,1,0:T(8,128)(2,1)} %k_ref.1, bf16[8,32,1024]{2,1,0:T(8,128)(2,1)} %v_ref.1, bf16[2,8,16,1024]{3,2,1,0:T(8,128)(2,1)} %copy-done.6, ...), custom_call_target="tpu_custom_call" | custom-call | tf_op jit(solution)/shard_map/pallas_call | solution.py:171
  122.6 1.2 copy-done
  123.7 2.3 %copy_bitcast_fusion = f32[3,8,4,8,1024]{4,2,1,3,0:T(4,128)S(1)} fusion(bf16[3,4,8,8,1024]{4,1,0,3,2:T(4,128)(2,1)} %bitcast.44), kind=kLoop, calls=%fused_computation | loop fusion | flops 786432 | bytes 4718592 | tf_op jit(solution)/shard_map/convert_element_type | solution.py:277
  126.0 2.8 %reshape.207 = f32[3,32,8,1024]{3,1,2,0:T(8,128)} reshape(f32[3,8,4,8,1024]{4,2,1,3,0:T(4,128)S(1)} %copy_bitcast_fusion) | data formatting | bytes 6291456 | tf_op jit(solution)/shard_map/convert_element_type | solution.py:277
  128.8 4.2 %fusion.1 = (bf16[8,32,1024]{2,1,0:T(8,128)(2,1)}, bf16[8,32,1024]{2,1,0:T(8,128)(2,1)}, bf16[8,32,1024]{2,1,0:T(8,128)(2,1)}) fusion(f32[8,32,1024]{2,1,0:T(8,128)} %get-tuple-element.8, f32[3,8,32,1024]{3,2,1,0:T(8,128)} %bitcast.41, f32[8,32,1024]{2,1,0:T(8,128)} %get-tuple-element.7, f32[8,32,1024]{2,1,0:T(8,128)} %get-tuple-element.6), kind=kLoop, calls=%fused_computation.5 | loop fusion | flops 1572864 | bytes 7864320 | tf_op jit(solution)/shard_map/convert_element_type | solution.py:278
  (31 shorter events, 0.3 us)
Async XLA Ops:
  0.6 8.3 %copy-start.2 = (bf16[8,32,1024]{2,1,0:T(8,128)(2,1)S(1)}, bf16[8,32,1024]{2,1,0:T(8,128)(2,1)}, u32[]{:S(2)}) copy-start(bf16[8,32,1024]{2,1,0:T(8,128)(2,1)} %v_ref.1) | copy-start | bytes 1572868
  0.6 8.3 %copy-start.1 = (bf16[8,32,1024]{2,1,0:T(8,128)(2,1)S(1)}, bf16[8,32,1024]{2,1,0:T(8,128)(2,1)}, u32[]{:S(2)}) copy-start(bf16[8,32,1024]{2,1,0:T(8,128)(2,1)} %k_ref.1) | copy-start | bytes 1572868
  0.7 8.3 %copy-start.3 = (bf16[8,32,1024]{2,1,0:T(8,128)(2,1)S(1)}, bf16[8,32,1024]{2,1,0:T(8,128)(2,1)}, u32[]{:S(2)}) copy-start(bf16[8,32,1024]{2,1,0:T(8,128)(2,1)} %q_ref.1) | copy-start | bytes 1572868
  0.7 8.3 %copy-start.4 = (bf16[8,32,1024]{2,1,0:T(8,128)(2,1)S(1)}, bf16[8,32,1024]{2,1,0:T(8,128)(2,1)}, u32[]{:S(2)}) copy-start(bf16[8,32,1024]{2,1,0:T(8,128)(2,1)} %g_ref.1) | copy-start | bytes 1572868
  3.1 27.3 %collective-permute-start.2 = (bf16[2,8,32,1024]{3,2,1,0:T(8,128)(2,1)}, bf16[2,8,32,1024]{3,2,1,0:T(8,128)(2,1)}, u32[]{:S(2)}, u32[]{:S(2)}) collective-permute-start(bf16[2,8,32,1024]{3,2,1,0:T(8,128)(2,1)} %pad_maximum_fusion), channel_id=1, source_target_pairs={{1,0},{2,1},{3,2},{4,3},{5,4},{6,5},{7,6},{9,8},{10,9},{11,10},{12... | collective-permute-start | bytes 3145736 | tf_op jit(solution)/shard_map/ppermute | solution.py:22
  5.1 29.2 %collective-permute-start = (bf16[2,8,32,1024]{3,2,1,0:T(8,128)(2,1)}, bf16[2,8,32,1024]{3,2,1,0:T(8,128)(2,1)}, u32[]{:S(2)}, u32[]{:S(2)}) collective-permute-start(bf16[2,8,32,1024]{3,2,1,0:T(8,128)(2,1)} %pad_maximum_fusion), channel_id=1, source_target_pairs={{0,1},{1,2},{2,3},{3,4},{4,5},{5,6},{6,7},{8,9},{9,10},{10,11},{11... | collective-permute-start | bytes 3145736 | tf_op jit(solution)/shard_map/ppermute | solution.py:22
  11.8 40.0 %all-to-all-start = ((bf16[4,32,8,1024]{3,2,0,1:T(8,128)(2,1)}), bf16[4,32,8,1024]{3,2,0,1:T(8,128)(2,1)S(1)}, u32[]{:S(2)}, u32[]{:S(2)}) async-start(bf16[4,32,8,1024]{3,2,0,1:T(8,128)(2,1)} %copy.15), calls=%async_computation | async-start | bytes 4194304 | tf_op jit(solution)/shard_map/all_to_all | solution.py:262
  32.3 15.3 %collective-permute-start.3 = (bf16[2,8,16,1024]{3,2,1,0:T(8,128)(2,1)}, bf16[2,8,16,1024]{3,2,1,0:T(8,128)(2,1)S(1)}, u32[]{:S(2)}, u32[]{:S(2)}) collective-permute-start(bf16[2,8,16,1024]{3,2,1,0:T(8,128)(2,1)} %slice.17), channel_id=1, source_target_pairs={{1,0},{2,1},{3,2},{4,3},{5,4},{6,5},{7,6},{9,8},{10,9},{11,10},{12... | collective-permute-start | bytes 1572872 | tf_op jit(solution)/shard_map/ppermute | solution.py:22
  36.2 15.0 %collective-permute-start.1 = (bf16[2,8,16,1024]{3,2,1,0:T(8,128)(2,1)}, bf16[2,8,16,1024]{3,2,1,0:T(8,128)(2,1)S(1)}, u32[]{:S(2)}, u32[]{:S(2)}) collective-permute-start(bf16[2,8,16,1024]{3,2,1,0:T(8,128)(2,1)} %slice.16), channel_id=1, source_target_pairs={{0,1},{1,2},{2,3},{3,4},{4,5},{5,6},{6,7},{8,9},{9,10},{10,11},{11... | collective-permute-start | bytes 1572872 | tf_op jit(solution)/shard_map/ppermute | solution.py:22
  47.5 5.9 %copy-start.5 = (bf16[2,8,16,1024]{3,2,1,0:T(8,128)(2,1)}, bf16[2,8,16,1024]{3,2,1,0:T(8,128)(2,1)S(1)}, u32[]{:S(2)}) copy-start(bf16[2,8,16,1024]{3,2,1,0:T(8,128)(2,1)S(1)} %collective-permute-done.3.r2_ref) | copy-start | bytes 1572868
  51.2 2.2 %copy-start.6 = (bf16[2,8,16,1024]{3,2,1,0:T(8,128)(2,1)}, bf16[2,8,16,1024]{3,2,1,0:T(8,128)(2,1)S(1)}, u32[]{:S(2)}) copy-start(bf16[2,8,16,1024]{3,2,1,0:T(8,128)(2,1)S(1)} %collective-permute-done.1.l2_ref) | copy-start | bytes 1572868
  68.0 4.5 %copy-start.7 = (s32[8,16]{1,0:T(8,128)S(1)}, s32[8,16]{1,0:T(8,128)}, u32[]{:S(2)}) copy-start(s32[8,16]{1,0:T(8,128)} %param.10) | copy-start | bytes 1540
  68.0 4.7 %copy-start.8 = (s32[8]{0:T(128)S(1)}, s32[8]{0:T(128)}, u32[]{:S(2)}) copy-start(s32[8]{0:T(128)} %param.11) | copy-start | bytes 100
  68.0 54.5 %all-to-all-start.1 = ((bf16[3,4,64,1024]{3,1,0,2:T(4,128)(2,1)}), bf16[3,4,64,1024]{3,1,0,2:T(4,128)(2,1)S(1)}, u32[]{:S(2)}, u32[]{:S(2)}) async-start(bf16[3,4,64,1024]{3,1,0,2:T(4,128)(2,1)} %copy.17), calls=%async_computation.1 | async-start | bytes 3145728 | tf_op jit(solution)/shard_map/all_to_all | solution.py:275
  122.5 1.2 copy-start

commit v8 on v6

--- a/solution.py
+++ b/solution.py
@@ -68,12 +68,12 @@
     return dq, dk, dv
 
 
-def fused_row_kernel(q_ref, g_ref, k_ref, v_ref, l2_ref, l1_ref, r1_ref, r2_ref, bias_ref,
+def fused_row_kernel(w2, q_ref, g_ref, k_ref, v_ref, l1_ref, r1_ref, bias_ref,
                      qg_ref, kg_ref, vg_ref,
-                     own_s, near_l, near_r, s_fl, s_fr, s_nl, s_nr, x_fr, x_fl, x_nr, x_nl,
-                     far_send, far_recv_r, far_recv_l, near_send, near_recv):
+                     l2_ref, r2_ref, own_s, near_l, near_r, s_fl, s_fr, s_nl, s_nr, x_fr, x_fl,
+                     x_nr, x_nl, halo_send, halo_recv, far_send, far_recv_r, far_recv_l,
+                     near_send, near_recv):
     rows, cc, width = q_ref.shape
-    w2 = l2_ref.shape[2]
     w1 = l1_ref.shape[2]
     n = lax.axis_size("rcol")
     me = lax.axis_index("rcol")
@@ -87,6 +87,21 @@
     for distance in (-1, 1):
         pl.semaphore_signal(barrier, 1, device_id=dev(distance), device_id_type=mesh_ids)
     pl.semaphore_wait(barrier, 2)
+
+    relays = (
+        pltpu.make_async_remote_copy(
+            src_ref=l1_ref.at[:, :, pl.ds(w1 - w2, w2)], dst_ref=l2_ref,
+            send_sem=halo_send.at[0], recv_sem=halo_recv.at[0],
+            device_id=dev(1), device_id_type=mesh_ids),
+        pltpu.make_async_remote_copy(
+            src_ref=r1_ref.at[:, :, pl.ds(0, w2)], dst_ref=r2_ref,
+            send_sem=halo_send.at[1], recv_sem=halo_recv.at[1],
+            device_id=dev(-1), device_id_type=mesh_ids),
+    )
+    for copy in relays:
+        copy.start()
+    for copy in relays:
+        copy.wait()
 
     def far_copy(r, to_left):
         if to_left:
@@ -160,20 +175,21 @@
         out_ref[...] = own_s[which] + x_nr[which].astype(f32) + x_nl[which].astype(f32)
 
 
-def fused_row(queries, out_grad, key_grid, value_grid, l2, l1, r1, r2, bias):
+def fused_row(queries, out_grad, key_grid, value_grid, l1, r1, bias, w2):
     rows, cc, width = queries.shape
-    w2 = l2.shape[2]
     w1 = l1.shape[2]
     vmem = pl.BlockSpec(memory_space=pltpu.VMEM)
     grads = jax.ShapeDtypeStruct((rows, cc, width), jnp.float32)
     bf = jnp.bfloat16
     f32 = jnp.float32
     return pl.pallas_call(
-        fused_row_kernel,
-        in_specs=[vmem] * 9,
+        functools.partial(fused_row_kernel, w2),
+        in_specs=[vmem] * 7,
         out_specs=[vmem] * 3,
         out_shape=(grads, grads, grads),
         scratch_shapes=[
+            pltpu.VMEM((2, rows, w2, width), bf),
+            pltpu.VMEM((2, rows, w2, width), bf),
             pltpu.VMEM((2, rows, cc, width), f32),
             pltpu.VMEM((2, rows, w1, width), f32),
             pltpu.VMEM((2, rows, w1, width), f32),
@@ -185,6 +201,8 @@
             pltpu.VMEM((2, rows, w2, width), bf),
             pltpu.VMEM((2, rows, cc, width), bf),
             pltpu.VMEM((2, rows, cc, width), bf),
+            pltpu.SemaphoreType.DMA((2,)),
+            pltpu.SemaphoreType.DMA((2,)),
             pltpu.SemaphoreType.DMA((2,)),
             pltpu.SemaphoreType.DMA((rows,)),
             pltpu.SemaphoreType.DMA((rows,)),
@@ -194,7 +212,7 @@
         compiler_params=pltpu.CompilerParams(
             collective_id=0, has_side_effects=True, vmem_limit_bytes=60 * 1024 * 1024
         ),
-    )(queries, out_grad, key_grid, value_grid, l2, l1, r1, r2, bias)
+    )(queries, out_grad, key_grid, value_grid, l1, r1, bias)
 
 
 def column_kernel(x_ref, o_ref):
@@ -261,15 +279,13 @@
     pair = jnp.stack([key_grid, value_grid])
     l1 = shifted(pair[:, :, col_count - near:], "rcol", 1)
     r1 = shifted(pair[:, :, :near], "rcol", -1)
-    l2 = shifted(l1[:, :, near - far:], "rcol", 1)
-    r2 = shifted(r1[:, :, :far], "rcol", -1)
     grid_cols = col_count * lax.axis_size("rcol")
     first_col = lax.axis_index("rcol") * col_count
     bias = band_bias(tissue_mask, band_offset, first_col, grid_cols, col_count)
 
     col_out = column_attention(whole)
     back = lax.all_to_all(col_out, "rrow", split_axis=2, concat_axis=1, tiled=True)
-    row_grads = fused_row(queries, out_grad, key_grid, value_grid, l2, l1, r1, r2, bias)
+    row_grads = fused_row(queries, out_grad, key_grid, value_grid, l1, r1, bias, far)
     back = back.transpose(0, 2, 1, 3).astype(jnp.float32)
     return tuple((row + col).astype(jnp.bfloat16) for row, col in zip(row_grads, back))
 

time: 136 us -> 131 us (0.963)
  Pallas kernels: 58.2 us -> 71.3 us
  waiting for transfers between devices: 31.7 us -> 20.2 us
  starting transfers between devices: 19.8 us -> 14 us
    pallas_call x1, Pallas kernels: 47.3 us -> 60.5 us  [fused_row(): pl.pallas_call(functools.partial(fused_row_kernel, w2), in_specs=[vmem] *...]
    ppermute x4 -> x2, waiting for transfers between devices: 11.4 us -> 0.01 us  [shifted(): return lax.ppermute(block, axis, route)]
    ppermute x4 -> x2, starting transfers between devices: 11.7 us -> 5.83 us  [shifted(): return lax.ppermute(block, axis, route)]
  transfers between devices with their start and end apart: 6 -> 4, of which waited for: 3 -> 1; matrix products, arithmetic and copies ran while one was open for 6% -> 6% of each run, Pallas kernels for 43% -> 55%
where the time goes in v8:
time: 131 us; the launch traced here: 129 us
  Pallas kernels  71.3 us (54%)
  waiting for transfers between devices  20.2 us (15%)
  starting transfers between devices  14 us (11%)
  local copies, waits for them, and re-layouts  12.6 us (10%)
  other arithmetic  10.5 us (8%)
    pallas_call x1, Pallas kernels, fused_row(): pl.pallas_call(functools.partial(fused_row_kernel, w2), in_specs=[vmem] *...  60.5 us
    all_to_all x1, waiting for transfers between devices, body(): lax.all_to_all(stacked, 'rrow', split_axis=1, concat_axis=2, tiled=True)  20.2 us
    pallas_call x1, Pallas kernels, column_attention(): pl.pallas_call(column_kernel, grid=(strip // per,), in_specs=[pl.BlockSpe...  10.8 us
    ppermute x2, starting transfers between devices, shifted(): return lax.ppermute(block, axis, route)  5.83 us
    all_to_all x1, starting transfers between devices, body(): lax.all_to_all(stacked, 'rrow', split_axis=1, concat_axis=2, tiled=True)  4.43 us
    convert_element_type x1, other arithmetic, body(): (row + col).astype(jnp.bfloat16)  4.21 us
    pallas_call x1, local copies, waits for them, and re-layouts, column_attention(): pl.pallas_call(column_kernel, grid=(strip // per,), in_specs=[pl.BlockSpe...  3.78 us
    all_to_all x1, starting transfers between devices, body(): lax.all_to_all(col_out, 'rrow', split_axis=2, concat_axis=1, tiled=True)  3.71 us
  transfers between devices with their start and end apart: 4, of which 1 were waited for; matrix products, arithmetic and copies ran while one was open for 6% of the time, Pallas kernels for 55%

profile of v8, /device:TPU:48, one launch (start us, length us, event | category | flops | bytes accessed | tf_op | source)
XLA Modules:
  0.0 129.4 jit_solution(737327365990306811)
XLA Ops:
  0.6 1.8 %maximum_bitcast_fusion = bf16[4,32,8,1024]{3,1,2,0:T(8,128)(2,1)S(1)} fusion(bf16[1,8,32,1024]{3,2,1,0:T(8,128)(2,1)} %bitcast.46, bf16[1,8,32,1024]{3,2,1,0:T(8,128)(2,1)} %bitcast.43, bf16[1,8,32,1024]{3,2,1,0:T(8,128)(2,1)} %bitcast.41, bf16[1,8,32,1024]{3,2,1,0:T(8,128)(2,1)} %bitcast.45), kind=kLoop, calls=%fused_computation.1 | loop fusion | flops 3145728 | bytes 4194304 | tf_op jit(solution)/shard_map/transpose | solution.py:276
  2.4 2.5 %copy.15 = bf16[4,32,8,1024]{3,2,0,1:T(8,128)(2,1)} copy(bf16[4,32,8,1024]{3,1,2,0:T(8,128)(2,1)S(1)} %maximum_bitcast_fusion) | data formatting | bytes 4194304 | tf_op jit(solution)/shard_map/transpose | solution.py:276
  4.9 4.4 %all-to-all-start = ((bf16[4,32,8,1024]{3,2,0,1:T(8,128)(2,1)}), bf16[4,32,8,1024]{3,2,0,1:T(8,128)(2,1)S(1)}, u32[]{:S(2)}, u32[]{:S(2)}) async-start(bf16[4,32,8,1024]{3,2,0,1:T(8,128)(2,1)} %copy.15), calls=%async_computation | async-start | bytes 4194304 | tf_op jit(solution)/shard_map/all_to_all | solution.py:277
  9.3 1.1 pad_maximum_fusion
  10.4 2.0 %collective-permute-start.1 = (bf16[2,8,32,1024]{3,2,1,0:T(8,128)(2,1)}, bf16[2,8,32,1024]{3,2,1,0:T(8,128)(2,1)S(1)}, u32[]{:S(2)}, u32[]{:S(2)}) collective-permute-start(bf16[2,8,32,1024]{3,2,1,0:T(8,128)(2,1)} %pad_maximum_fusion), channel_id=1, source_target_pairs={{1,0},{2,1},{3,2},{4,3},{5,4},{6,5},{7,6},{9,8},{10,9},{11,10},{12... | collective-permute-start | bytes 3145736 | tf_op jit(solution)/shard_map/ppermute | solution.py:22
  12.4 3.8 %collective-permute-start = (bf16[2,8,32,1024]{3,2,1,0:T(8,128)(2,1)}, bf16[2,8,32,1024]{3,2,1,0:T(8,128)(2,1)}, u32[]{:S(2)}, u32[]{:S(2)}) collective-permute-start(bf16[2,8,32,1024]{3,2,1,0:T(8,128)(2,1)} %pad_maximum_fusion), channel_id=1, source_target_pairs={{0,1},{1,2},{2,3},{3,4},{4,5},{5,6},{6,7},{8,9},{9,10},{10,11},{11... | collective-permute-start | bytes 3145736 | tf_op jit(solution)/shard_map/ppermute | solution.py:22
  16.3 20.2 %all-to-all-done = bf16[4,32,8,1024]{3,2,0,1:T(8,128)(2,1)S(1)} async-done(((bf16[4,32,8,1024]{3,2,0,1:T(8,128)(2,1)}), bf16[4,32,8,1024]{3,2,0,1:T(8,128)(2,1)S(1)}, u32[]{:S(2)}, u32[]{:S(2)}) %all-to-all-start) | async-done | bytes 2097184 | tf_op jit(solution)/shard_map/all_to_all | solution.py:277
  36.5 1.6 %copy.21 = bf16[4,8,4,8,1024]{4,3,1,2,0:T(8,128)(2,1)} copy(bf16[4,8,4,8,1024]{4,3,0,2,1:T(8,128)(2,1)S(1)} %bitcast.39) | data formatting | bytes 4194304 | tf_op jit(solution)/shard_map/all_to_all | solution.py:277
  38.1 10.8 %shard_map.86 = bf16[3,4,64,1024]{3,2,1,0:T(8,128)(2,1)} custom-call(bf16[4,4,64,1024]{3,2,1,0:T(8,128)(2,1)} %bitcast.38), custom_call_target="tpu_custom_call" | custom-call | tf_op jit(solution)/shard_map/pallas_call | solution.py:237
  48.9 3.8 %copy.17 = bf16[3,4,64,1024]{3,1,0,2:T(4,128)(2,1)} copy(bf16[3,4,64,1024]{3,2,1,0:T(8,128)(2,1)} %shard_map.86) | data formatting | bytes 3145728 | tf_op jit(solution)/shard_map/pallas_call | solution.py:237
  52.7 3.7 %all-to-all-start.1 = ((bf16[3,4,64,1024]{3,1,0,2:T(4,128)(2,1)}), bf16[3,4,64,1024]{3,1,0,2:T(4,128)(2,1)S(1)}, u32[]{:S(2)}, u32[]{:S(2)}) async-start(bf16[3,4,64,1024]{3,1,0,2:T(4,128)(2,1)} %copy.17), calls=%async_computation.1 | async-start | bytes 3145728 | tf_op jit(solution)/shard_map/all_to_all | solution.py:287
  56.5 0.1 multiply_reduce_fusion
  56.6 0.1 broadcast_compare_fusion
  56.7 0.1 broadcast_subtract_fusion
  56.8 0.8 fusion.9.bias_ref
  57.5 0.0 collective-permute-done.1.r1_ref
  57.5 0.0 collective-permute-done.l1_ref
  57.5 1.0 copy-done.3
  58.5 60.5 %shard_map.85 = (f32[8,32,1024]{2,1,0:T(8,128)}, f32[8,32,1024]{2,1,0:T(8,128)}, f32[8,32,1024]{2,1,0:T(8,128)}) custom-call(bf16[8,32,1024]{2,1,0:T(8,128)(2,1)} %q_ref.1, bf16[8,32,1024]{2,1,0:T(8,128)(2,1)} %g_ref.1, bf16[8,32,1024]{2,1,0:T(8,128)(2,1)} %k_ref.1, bf16[8,32,1024]{2,1,0:T(8,128)(2,1)} %v_ref.1, ...), custom_call_target="tpu_custom_call" | custom-call | tf_op jit(solution)/shard_map/pallas_call | solution.py:185
  119.0 0.0 all-to-all-done.1
  119.0 1.2 copy-done
  120.1 2.3 %copy_bitcast_fusion = f32[3,8,4,8,1024]{4,2,1,3,0:T(4,128)S(1)} fusion(bf16[3,4,8,8,1024]{4,1,0,3,2:T(4,128)(2,1)} %bitcast.40), kind=kLoop, calls=%fused_computation | loop fusion | flops 786432 | bytes 4718592 | tf_op jit(solution)/shard_map/convert_element_type | solution.py:289
  122.5 2.7 %reshape.207 = f32[3,32,8,1024]{3,1,2,0:T(8,128)} reshape(f32[3,8,4,8,1024]{4,2,1,3,0:T(4,128)S(1)} %copy_bitcast_fusion) | data formatting | bytes 6291456 | tf_op jit(solution)/shard_map/convert_element_type | solution.py:289
  125.2 4.2 %fusion.1 = (bf16[8,32,1024]{2,1,0:T(8,128)(2,1)}, bf16[8,32,1024]{2,1,0:T(8,128)(2,1)}, bf16[8,32,1024]{2,1,0:T(8,128)(2,1)}) fusion(f32[8,32,1024]{2,1,0:T(8,128)} %get-tuple-element.8, f32[3,8,32,1024]{3,2,1,0:T(8,128)} %bitcast.37, f32[8,32,1024]{2,1,0:T(8,128)} %get-tuple-element.7, f32[8,32,1024]{2,1,0:T(8,128)} %get-tuple-element.6), kind=kLoop, calls=%fused_computation.5 | loop fusion | flops 1572864 | bytes 7864320 | tf_op jit(solution)/shard_map/convert_element_type | solution.py:290
  (16 shorter events, 0.1 us)
Async XLA Ops:
  4.9 4.4 %copy-start.1 = (bf16[8,32,1024]{2,1,0:T(8,128)(2,1)S(1)}, bf16[8,32,1024]{2,1,0:T(8,128)(2,1)}, u32[]{:S(2)}) copy-start(bf16[8,32,1024]{2,1,0:T(8,128)(2,1)} %k_ref.1) | copy-start | bytes 1572868
  4.9 4.4 %copy-start.2 = (bf16[8,32,1024]{2,1,0:T(8,128)(2,1)S(1)}, bf16[8,32,1024]{2,1,0:T(8,128)(2,1)}, u32[]{:S(2)}) copy-start(bf16[8,32,1024]{2,1,0:T(8,128)(2,1)} %v_ref.1) | copy-start | bytes 1572868
  4.9 31.6 %all-to-all-start = ((bf16[4,32,8,1024]{3,2,0,1:T(8,128)(2,1)}), bf16[4,32,8,1024]{3,2,0,1:T(8,128)(2,1)S(1)}, u32[]{:S(2)}, u32[]{:S(2)}) async-start(bf16[4,32,8,1024]{3,2,0,1:T(8,128)(2,1)} %copy.15), calls=%async_computation | async-start | bytes 4194304 | tf_op jit(solution)/shard_map/all_to_all | solution.py:277
  10.4 47.1 %collective-permute-start.1 = (bf16[2,8,32,1024]{3,2,1,0:T(8,128)(2,1)}, bf16[2,8,32,1024]{3,2,1,0:T(8,128)(2,1)S(1)}, u32[]{:S(2)}, u32[]{:S(2)}) collective-permute-start(bf16[2,8,32,1024]{3,2,1,0:T(8,128)(2,1)} %pad_maximum_fusion), channel_id=1, source_target_pairs={{1,0},{2,1},{3,2},{4,3},{5,4},{6,5},{7,6},{9,8},{10,9},{11,10},{12... | collective-permute-start | bytes 3145736 | tf_op jit(solution)/shard_map/ppermute | solution.py:22
  12.4 45.1 %collective-permute-start = (bf16[2,8,32,1024]{3,2,1,0:T(8,128)(2,1)}, bf16[2,8,32,1024]{3,2,1,0:T(8,128)(2,1)}, u32[]{:S(2)}, u32[]{:S(2)}) collective-permute-start(bf16[2,8,32,1024]{3,2,1,0:T(8,128)(2,1)} %pad_maximum_fusion), channel_id=1, source_target_pairs={{0,1},{1,2},{2,3},{3,4},{4,5},{5,6},{6,7},{8,9},{9,10},{10,11},{11... | collective-permute-start | bytes 3145736 | tf_op jit(solution)/shard_map/ppermute | solution.py:22
  52.7 3.8 %copy-start.4 = (s32[8,16]{1,0:T(8,128)S(1)}, s32[8,16]{1,0:T(8,128)}, u32[]{:S(2)}) copy-start(s32[8,16]{1,0:T(8,128)} %param.10) | copy-start | bytes 1540
  52.7 4.0 %copy-start.5 = (s32[8]{0:T(128)S(1)}, s32[8]{0:T(128)}, u32[]{:S(2)}) copy-start(s32[8]{0:T(128)} %param.11) | copy-start | bytes 100
  52.7 66.3 %all-to-all-start.1 = ((bf16[3,4,64,1024]{3,1,0,2:T(4,128)(2,1)}), bf16[3,4,64,1024]{3,1,0,2:T(4,128)(2,1)S(1)}, u32[]{:S(2)}, u32[]{:S(2)}) async-start(bf16[3,4,64,1024]{3,1,0,2:T(4,128)(2,1)} %copy.17), calls=%async_computation.1 | async-start | bytes 3145728 | tf_op jit(solution)/shard_map/all_to_all | solution.py:287
  57.5 1.0 copy-start.3
  119.0 1.2 copy-start

commit v9 on v8

--- a/solution.py
+++ b/solution.py
@@ -216,30 +216,42 @@
 
 
 def column_kernel(x_ref, o_ref):
-    per = x_ref.shape[1]
-    rows = x_ref.shape[2]
+    groups, arrays, strip, rows, width = x_ref.shape
+    per = max(1, LANES // (groups * rows))
 
     def joined(which):
-        return jnp.concatenate([x_ref[which, c] for c in range(per)], axis=0)
-
-    i = lax.broadcasted_iota(jnp.int32, (per * rows, per * rows), 0) // rows
-    j = lax.broadcasted_iota(jnp.int32, (per * rows, per * rows), 1) // rows
+        return jnp.concatenate(
+            [x_ref[s, which, c] for c in range(per) for s in range(groups)], axis=0
+        )
+
+    whole_rows = groups * rows
+    i = lax.broadcasted_iota(jnp.int32, (per * whole_rows, per * whole_rows), 0) // whole_rows
+    j = lax.broadcasted_iota(jnp.int32, (per * whole_rows, per * whole_rows), 1) // whole_rows
     bias = jnp.where(i == j, 0.0, -jnp.inf).astype(jnp.float32)
-    grads = block_grads(joined(0), joined(3), joined(1), joined(2), bias)
-    for which, full in enumerate(grads):
-        for c in range(per):
-            o_ref[which, c] = full[c * rows:(c + 1) * rows].astype(jnp.bfloat16)
+    for step in range(strip // per):
+        def pick(which):
+            return jnp.concatenate(
+                [x_ref[s, which, step * per + c] for c in range(per) for s in range(groups)],
+                axis=0,
+            )
+
+        grads = block_grads(pick(0), pick(3), pick(1), pick(2), bias)
+        for which, full in enumerate(grads):
+            low = full.astype(jnp.bfloat16)
+            for c in range(per):
+                for s in range(groups):
+                    start = c * whole_rows + s * rows
+                    o_ref[s, which, step * per + c] = low[start:start + rows]
 
 
 def column_attention(whole):
-    arrays, strip, rows, width = whole.shape
-    per = max(1, LANES // rows)
+    groups, arrays, strip, rows, width = whole.shape
+    vmem = pl.BlockSpec(memory_space=pltpu.VMEM)
     return pl.pallas_call(
         column_kernel,
-        grid=(strip // per,),
-        in_specs=[pl.BlockSpec((arrays, per, rows, width), lambda c: (0, c, 0, 0))],
-        out_specs=pl.BlockSpec((3, per, rows, width), lambda c: (0, c, 0, 0)),
-        out_shape=jax.ShapeDtypeStruct((3, strip, rows, width), jnp.bfloat16),
+        in_specs=[vmem],
+        out_specs=vmem,
+        out_shape=jax.ShapeDtypeStruct((groups, 3, strip, rows, width), jnp.bfloat16),
     )(whole)
 
 
@@ -273,8 +285,13 @@
     near = col_count
     far = band_reach - col_count
 
-    stacked = jnp.stack([queries, key_grid, value_grid, out_grad]).transpose(0, 2, 1, 3)
-    whole = lax.all_to_all(stacked, "rrow", split_axis=1, concat_axis=2, tiled=True)
+    strip = col_count // group_count
+    stacked = (
+        jnp.stack([queries, key_grid, value_grid, out_grad])
+        .reshape(4, row_count, group_count, strip, feature_width)
+        .transpose(2, 0, 3, 1, 4)
+    )
+    whole = lax.all_to_all(stacked, "rrow", split_axis=0, concat_axis=0, tiled=True)
 
     pair = jnp.stack([key_grid, value_grid])
     l1 = shifted(pair[:, :, col_count - near:], "rcol", 1)
@@ -284,9 +301,10 @@
     bias = band_bias(tissue_mask, band_offset, first_col, grid_cols, col_count)
 
     col_out = column_attention(whole)
-    back = lax.all_to_all(col_out, "rrow", split_axis=2, concat_axis=1, tiled=True)
+    back = lax.all_to_all(col_out, "rrow", split_axis=0, concat_axis=0, tiled=True)
     row_grads = fused_row(queries, out_grad, key_grid, value_grid, l1, r1, bias, far)
-    back = back.transpose(0, 2, 1, 3).astype(jnp.float32)
+    back = back.transpose(1, 3, 0, 2, 4).reshape(3, row_count, col_count, feature_width)
+    back = back.astype(jnp.float32)
     return tuple((row + col).astype(jnp.bfloat16) for row, col in zip(row_grads, back))
 
 

time: 131 us -> 124 us (0.947)
  local copies, waits for them, and re-layouts: 12.6 us -> 6.88 us
  other arithmetic: 10.5 us -> 8.33 us
    unnamed x12 -> x22, local copies, waits for them, and re-layouts: 2.14 us -> 6.47 us
    pallas_call x1 -> x0, local copies, waits for them, and re-layouts: 3.78 us -> none  [column_attention(): pl.pallas_call(column_kernel, grid=(strip // per,), in_specs=[pl.BlockSpe...]
    convert_element_type x1 -> x0, local copies, waits for them, and re-layouts: 2.68 us -> none  [body(): back = back.transpose(0, 2, 1, 3).astype(jnp.float32)]
    transpose x1 -> x0, local copies, waits for them, and re-layouts: 2.48 us -> none  [body(): jnp.stack([queries, key_grid, value_grid, out_grad]).transpose(0, 2, 1, 3)]
    convert_element_type x1, other arithmetic: 2.32 us -> 0.38 us  [body(): back = back.astype(jnp.float32)]
    all_to_all x1 -> x0, local copies, waits for them, and re-layouts: 1.57 us -> none  [body(): lax.all_to_all(stacked, 'rrow', split_axis=1, concat_axis=2, tiled=True)]
    convert_element_type x1 -> x3, other arithmetic: 4.21 us -> 4.22 us  [body(): (row + col).astype(jnp.bfloat16)]
  transfers between devices with their start and end apart: 4 -> 4, of which waited for: 1 -> 1; matrix products, arithmetic and copies ran while one was open for 6% -> 2% of each run, Pallas kernels for 55% -> 59%
where the time goes in v9:
time: 124 us; the launch traced here: 122 us
  Pallas kernels  71.7 us (58%)
  waiting for transfers between devices  20.2 us (16%)
  starting transfers between devices  14 us (11%)
  other arithmetic  8.33 us (7%)
  local copies, waits for them, and re-layouts  6.88 us (6%)
    pallas_call x1, Pallas kernels, fused_row(): pl.pallas_call(functools.partial(fused_row_kernel, w2), in_specs=[vmem] *...  60.4 us
    all_to_all x1, waiting for transfers between devices, body(): lax.all_to_all(stacked, 'rrow', split_axis=0, concat_axis=0, tiled=True)  20.2 us
    pallas_call x1, Pallas kernels, column_attention(): pl.pallas_call(column_kernel, in_specs=[vmem], out_specs=vmem, out_shape=...  11.3 us
    unnamed x22, local copies, waits for them, and re-layouts  6.47 us
    ppermute x2, starting transfers between devices, shifted(): return lax.ppermute(block, axis, route)  5.83 us
    all_to_all x1, starting transfers between devices, body(): lax.all_to_all(stacked, 'rrow', split_axis=0, concat_axis=0, tiled=True)  4.3 us
    convert_element_type x3, other arithmetic, body(): (row + col).astype(jnp.bfloat16)  4.22 us
    all_to_all x1, starting transfers between devices, body(): lax.all_to_all(col_out, 'rrow', split_axis=0, concat_axis=0, tiled=True)  3.89 us
  transfers between devices with their start and end apart: 4, of which 1 were waited for; matrix products, arithmetic and copies ran while one was open for 2% of the time, Pallas kernels for 59%

profile of v9, /device:TPU:48, one launch (start us, length us, event | category | flops | bytes accessed | tf_op | source)
XLA Modules:
  0.0 122.0 jit_solution(11142544126566382930)
XLA Ops:
  0.7 1.4 %copy.16 = bf16[8,32,1024]{2,0,1:T(8,128)(2,1)S(1)} copy(bf16[8,32,1024]{2,1,0:T(8,128)(2,1)} %q_ref.1) | data formatting | bytes 1048576 | tf_op args[0]
  2.1 1.3 %copy.19 = bf16[8,32,1024]{2,0,1:T(8,128)(2,1)S(1)} copy(bf16[8,32,1024]{2,1,0:T(8,128)(2,1)} %g_ref.1) | data formatting | bytes 1048576 | tf_op args[3]
  3.4 0.3 copy.17
  3.7 0.3 copy.18
  4.0 1.6 %maximum_bitcast_fusion = bf16[8,4,4,8,1024]{4,3,2,1,0:T(8,128)(2,1)} fusion(bf16[1,8,8,4,1024]{4,1,3,0,2:T(8,128)(2,1)S(1)} %bitcast.19, bf16[1,8,8,4,1024]{4,1,3,0,2:T(8,128)(2,1)S(1)} %bitcast.21, bf16[1,8,8,4,1024]{4,1,3,0,2:T(8,128)(2,1)S(1)} %bitcast.20, bf16[1,8,8,4,1024]{4,1,3,0,2:T(8,128)(2,1)S(1)} %bitcast.18), kind=kLoop, calls=%fused_computation.1 | loop fusion | flops 3145728 | bytes 4194304 | tf_op jit(solution)/shard_map/transpose | solution.py:292
  5.6 4.3 %all-to-all-start = ((bf16[8,4,4,8,1024]{4,3,2,1,0:T(8,128)(2,1)}), bf16[8,4,4,8,1024]{4,3,2,1,0:T(8,128)(2,1)S(1)}, u32[]{:S(2)}, u32[]{:S(2)}) async-start(bf16[8,4,4,8,1024]{4,3,2,1,0:T(8,128)(2,1)} %maximum_bitcast_fusion), calls=%async_computation | async-start | bytes 4194304 | tf_op jit(solution)/shard_map/all_to_all | solution.py:294
  9.9 1.1 pad_maximum_fusion
  11.0 2.0 %collective-permute-start.1 = (bf16[2,8,32,1024]{3,2,1,0:T(8,128)(2,1)}, bf16[2,8,32,1024]{3,2,1,0:T(8,128)(2,1)S(1)}, u32[]{:S(2)}, u32[]{:S(2)}) collective-permute-start(bf16[2,8,32,1024]{3,2,1,0:T(8,128)(2,1)} %pad_maximum_fusion), channel_id=1, source_target_pairs={{1,0},{2,1},{3,2},{4,3},{5,4},{6,5},{7,6},{9,8},{10,9},{11,10},{12... | collective-permute-start | bytes 3145736 | tf_op jit(solution)/shard_map/ppermute | solution.py:22
  13.0 3.8 %collective-permute-start = (bf16[2,8,32,1024]{3,2,1,0:T(8,128)(2,1)}, bf16[2,8,32,1024]{3,2,1,0:T(8,128)(2,1)}, u32[]{:S(2)}, u32[]{:S(2)}) collective-permute-start(bf16[2,8,32,1024]{3,2,1,0:T(8,128)(2,1)} %pad_maximum_fusion), channel_id=1, source_target_pairs={{0,1},{1,2},{2,3},{3,4},{4,5},{5,6},{6,7},{8,9},{9,10},{10,11},{11... | collective-permute-start | bytes 3145736 | tf_op jit(solution)/shard_map/ppermute | solution.py:22
  16.9 20.2 %all-to-all-done.x_ref = bf16[8,4,4,8,1024]{4,3,2,1,0:T(8,128)(2,1)S(1)} async-done(((bf16[8,4,4,8,1024]{4,3,2,1,0:T(8,128)(2,1)}), bf16[8,4,4,8,1024]{4,3,2,1,0:T(8,128)(2,1)S(1)}, u32[]{:S(2)}, u32[]{:S(2)}) %all-to-all-start) | async-done | bytes 2097184 | tf_op jit(solution)/shard_map/all_to_all | solution.py:294
  37.1 1.3 %copy-done = bf16[8,4,4,8,1024]{4,3,2,1,0:T(8,128)(2,1)} copy-done((bf16[8,4,4,8,1024]{4,3,2,1,0:T(8,128)(2,1)}, bf16[8,4,4,8,1024]{4,3,2,1,0:T(8,128)(2,1)S(1)}, u32[]{:S(2)}) %copy-start) | copy-done | bytes 2097176
  38.5 11.3 %shard_map.86 = bf16[8,3,4,8,1024]{4,3,2,1,0:T(8,128)(2,1)} custom-call(bf16[8,4,4,8,1024]{4,3,2,1,0:T(8,128)(2,1)} %copy-done), custom_call_target="tpu_custom_call" | custom-call | tf_op jit(solution)/shard_map/pallas_call | solution.py:250
  49.7 3.9 %all-to-all-start.1 = ((bf16[8,3,4,8,1024]{4,3,2,1,0:T(8,128)(2,1)}), bf16[8,3,4,8,1024]{4,3,2,1,0:T(8,128)(2,1)S(1)}, u32[]{:S(2)}, u32[]{:S(2)}) async-start(bf16[8,3,4,8,1024]{4,3,2,1,0:T(8,128)(2,1)} %shard_map.86), calls=%async_computation.1 | async-start | bytes 3145728 | tf_op jit(solution)/shard_map/all_to_all | solution.py:304
  53.7 0.1 multiply_reduce_fusion
  53.8 0.1 broadcast_compare_fusion
  54.0 0.8 fusion.6.bias_ref
  54.7 1.0 copy-done.6
  55.7 60.4 %shard_map.85 = (f32[8,32,1024]{2,1,0:T(8,128)}, f32[8,32,1024]{2,1,0:T(8,128)}, f32[8,32,1024]{2,1,0:T(8,128)}) custom-call(bf16[8,32,1024]{2,1,0:T(8,128)(2,1)} %q_ref.1, bf16[8,32,1024]{2,1,0:T(8,128)(2,1)} %g_ref.1, bf16[8,32,1024]{2,1,0:T(8,128)(2,1)} %k_ref.1, bf16[8,32,1024]{2,1,0:T(8,128)(2,1)} %v_ref.1, ...), custom_call_target="tpu_custom_call" | custom-call | tf_op jit(solution)/shard_map/pallas_call | solution.py:185
  116.2 0.4 convert_bitcast_fusion
  116.6 0.4 fusion.8
  117.0 0.8 copy-done.5
  117.8 1.4 %fusion.2 = bf16[8,32,1024]{2,1,0:T(8,128)(2,1)} fusion(f32[8,32,1024]{2,1,0:T(8,128)S(1)} %copy-done.5, f32[8,32,1024]{2,0,1:T(8,128)S(1)} %bitcast.17), kind=kLoop, calls=%fused_computation.8 | loop fusion | flops 524288 | bytes 2621440 | tf_op jit(solution)/shard_map/convert_element_type | solution.py:308
  119.2 1.4 %fusion = bf16[8,32,1024]{2,1,0:T(8,128)(2,1)} fusion(f32[8,32,1024]{2,1,0:T(8,128)S(1)} %copy-done.4, f32[8,32,1024]{2,0,1:T(8,128)S(1)} %bitcast.16), kind=kLoop, calls=%fused_computation.4 | loop fusion | flops 524288 | bytes 2621440 | tf_op jit(solution)/shard_map/convert_element_type | solution.py:308
  120.6 1.4 %fusion.1 = bf16[8,32,1024]{2,1,0:T(8,128)(2,1)} fusion(f32[8,32,1024]{2,1,0:T(8,128)S(1)} %copy-done.3, f32[8,32,1024]{2,0,1:T(8,128)S(1)} %bitcast.15), kind=kLoop, calls=%fused_computation.6 | loop fusion | flops 524288 | bytes 2621440 | tf_op jit(solution)/shard_map/convert_element_type | solution.py:308
  (25 shorter events, 0.2 us)
Async XLA Ops:
  0.6 2.8 %copy-start.1 = (bf16[8,32,1024]{2,1,0:T(8,128)(2,1)S(1)}, bf16[8,32,1024]{2,1,0:T(8,128)(2,1)}, u32[]{:S(2)}) copy-start(bf16[8,32,1024]{2,1,0:T(8,128)(2,1)} %k_ref.1) | copy-start | bytes 1572868
  0.6 3.1 %copy-start.2 = (bf16[8,32,1024]{2,1,0:T(8,128)(2,1)S(1)}, bf16[8,32,1024]{2,1,0:T(8,128)(2,1)}, u32[]{:S(2)}) copy-start(bf16[8,32,1024]{2,1,0:T(8,128)(2,1)} %v_ref.1) | copy-start | bytes 1572868
  5.6 31.5 %all-to-all-start = ((bf16[8,4,4,8,1024]{4,3,2,1,0:T(8,128)(2,1)}), bf16[8,4,4,8,1024]{4,3,2,1,0:T(8,128)(2,1)S(1)}, u32[]{:S(2)}, u32[]{:S(2)}) async-start(bf16[8,4,4,8,1024]{4,3,2,1,0:T(8,128)(2,1)} %maximum_bitcast_fusion), calls=%async_computation | async-start | bytes 4194304 | tf_op jit(solution)/shard_map/all_to_all | solution.py:294
  11.0 43.7 %collective-permute-start.1 = (bf16[2,8,32,1024]{3,2,1,0:T(8,128)(2,1)}, bf16[2,8,32,1024]{3,2,1,0:T(8,128)(2,1)S(1)}, u32[]{:S(2)}, u32[]{:S(2)}) collective-permute-start(bf16[2,8,32,1024]{3,2,1,0:T(8,128)(2,1)} %pad_maximum_fusion), channel_id=1, source_target_pairs={{1,0},{2,1},{3,2},{4,3},{5,4},{6,5},{7,6},{9,8},{10,9},{11,10},{12... | collective-permute-start | bytes 3145736 | tf_op jit(solution)/shard_map/ppermute | solution.py:22
  13.0 41.7 %collective-permute-start = (bf16[2,8,32,1024]{3,2,1,0:T(8,128)(2,1)}, bf16[2,8,32,1024]{3,2,1,0:T(8,128)(2,1)}, u32[]{:S(2)}, u32[]{:S(2)}) collective-permute-start(bf16[2,8,32,1024]{3,2,1,0:T(8,128)(2,1)} %pad_maximum_fusion), channel_id=1, source_target_pairs={{0,1},{1,2},{2,3},{3,4},{4,5},{5,6},{6,7},{8,9},{9,10},{10,11},{11... | collective-permute-start | bytes 3145736 | tf_op jit(solution)/shard_map/ppermute | solution.py:22
  37.1 1.3 %copy-start = (bf16[8,4,4,8,1024]{4,3,2,1,0:T(8,128)(2,1)}, bf16[8,4,4,8,1024]{4,3,2,1,0:T(8,128)(2,1)S(1)}, u32[]{:S(2)}) copy-start(bf16[8,4,4,8,1024]{4,3,2,1,0:T(8,128)(2,1)S(1)} %all-to-all-done.x_ref) | copy-start | bytes 6291460
  49.7 3.9 %copy-start.7 = (s32[8,16]{1,0:T(8,128)S(1)}, s32[8,16]{1,0:T(8,128)}, u32[]{:S(2)}) copy-start(s32[8,16]{1,0:T(8,128)} %param.10) | copy-start | bytes 1540
  49.7 4.2 %copy-start.8 = (s32[8]{0:T(128)S(1)}, s32[8]{0:T(128)}, u32[]{:S(2)}) copy-start(s32[8]{0:T(128)} %param.11) | copy-start | bytes 100
  49.7 66.4 %all-to-all-start.1 = ((bf16[8,3,4,8,1024]{4,3,2,1,0:T(8,128)(2,1)}), bf16[8,3,4,8,1024]{4,3,2,1,0:T(8,128)(2,1)S(1)}, u32[]{:S(2)}, u32[]{:S(2)}) async-start(bf16[8,3,4,8,1024]{4,3,2,1,0:T(8,128)(2,1)} %shard_map.86), calls=%async_computation.1 | async-start | bytes 3145728 | tf_op jit(solution)/shard_map/all_to_all | solution.py:304
  54.7 1.0 copy-start.6
  116.5 1.2 %copy-start.5 = (f32[8,32,1024]{2,1,0:T(8,128)S(1)}, f32[8,32,1024]{2,1,0:T(8,128)}, u32[]{:S(2)}) copy-start(f32[8,32,1024]{2,1,0:T(8,128)} %get-tuple-element.6) | copy-start | bytes 3145732
  117.0 2.2 %copy-start.4 = (f32[8,32,1024]{2,1,0:T(8,128)S(1)}, f32[8,32,1024]{2,1,0:T(8,128)}, u32[]{:S(2)}) copy-start(f32[8,32,1024]{2,1,0:T(8,128)} %get-tuple-element.8) | copy-start | bytes 3145732
  117.8 2.8 %copy-start.3 = (f32[8,32,1024]{2,1,0:T(8,128)S(1)}, f32[8,32,1024]{2,1,0:T(8,128)}, u32[]{:S(2)}) copy-start(f32[8,32,1024]{2,1,0:T(8,128)} %get-tuple-element.7) | copy-start | bytes 3145732

commit v10 on v9

--- a/solution.py
+++ b/solution.py
@@ -41,19 +41,28 @@
 def block_grads(q, g, k, v, bias):
     nq, width = q.shape
     heads = width // HD
-    qm = head_stack(q, heads)
-    gm = head_stack(g, heads)
+    group = min(width, 2 * LANES)
+    per_group = group // HD
+    lanes = [slice(t * group, (t + 1) * group) for t in range(width // group)]
+    qm = [head_stack(q[:, part], per_group) for part in lanes]
+    gm = [head_stack(g[:, part], per_group) for part in lanes]
     full_bias = jnp.broadcast_to(bias[None], (heads,) + bias.shape).reshape(heads * nq, -1)
-    s = dot_nt(qm, k) * SCALE + full_bias
+    s = jnp.concatenate([dot_nt(a, k[:, part]) for a, part in zip(qm, lanes)], axis=0)
+    s = s * SCALE + full_bias
     mx = jnp.max(s, axis=1, keepdims=True)
     e = jnp.exp(s - mx)
     p = e / jnp.sum(e, axis=1, keepdims=True)
     pb = p.astype(jnp.bfloat16)
-    gw = dot_nt(gm, v)
+    gw = jnp.concatenate([dot_nt(a, v[:, part]) for a, part in zip(gm, lanes)], axis=0)
     delta = jnp.sum(pb.astype(jnp.float32) * gw, axis=1, keepdims=True)
     ds = (p * (gw - delta)).astype(jnp.bfloat16)
-    dk = dot_tn(ds, qm) * SCALE
-    dv = dot_tn(pb, gm)
+    rows = per_group * nq
+    dk = jnp.concatenate(
+        [dot_tn(ds[t * rows:(t + 1) * rows], a) for t, a in enumerate(qm)], axis=1
+    ) * SCALE
+    dv = jnp.concatenate(
+        [dot_tn(pb[t * rows:(t + 1) * rows], a) for t, a in enumerate(gm)], axis=1
+    )
     lane = lax.broadcasted_iota(jnp.int32, (1, LANES), 1)
     low = lane < HD
     tiles = []

time: 124 us -> 118 us (0.952)
  Pallas kernels: 71.7 us -> 65.9 us
    pallas_call x1, Pallas kernels: 11.3 us -> 5.86 us  [column_attention(): pl.pallas_call(column_kernel, in_specs=[vmem], out_specs=vmem, out_shape=...]
  transfers between devices with their start and end apart: 4 -> 4, of which waited for: 1 -> 1; matrix products, arithmetic and copies ran while one was open for 2% -> 2% of each run, Pallas kernels for 59% -> 57%
where the time goes in v10:
time: 118 us; the launch traced here: 116 us
  Pallas kernels  65.9 us (56%)
  waiting for transfers between devices  20.2 us (17%)
  starting transfers between devices  13.8 us (12%)
  other arithmetic  8.33 us (7%)
  local copies, waits for them, and re-layouts  6.88 us (6%)
    pallas_call x1, Pallas kernels, fused_row(): pl.pallas_call(functools.partial(fused_row_kernel, w2), in_specs=[vmem] *...  60 us
    all_to_all x1, waiting for transfers between devices, body(): lax.all_to_all(stacked, 'rrow', split_axis=0, concat_axis=0, tiled=True)  20.2 us
    unnamed x22, local copies, waits for them, and re-layouts  6.47 us
    pallas_call x1, Pallas kernels, column_attention(): pl.pallas_call(column_kernel, in_specs=[vmem], out_specs=vmem, out_shape=...  5.86 us
    ppermute x2, starting transfers between devices, shifted(): return lax.ppermute(block, axis, route)  5.83 us
    all_to_all x1, starting transfers between devices, body(): lax.all_to_all(stacked, 'rrow', split_axis=0, concat_axis=0, tiled=True)  4.3 us
    convert_element_type x3, other arithmetic, body(): (row + col).astype(jnp.bfloat16)  4.22 us
    all_to_all x1, starting transfers between devices, body(): lax.all_to_all(col_out, 'rrow', split_axis=0, concat_axis=0, tiled=True)  3.71 us
  transfers between devices with their start and end apart: 4, of which 1 were waited for; matrix products, arithmetic and copies ran while one was open for 2% of the time, Pallas kernels for 57%

profile of v10, /device:TPU:48, one launch (start us, length us, event | category | flops | bytes accessed | tf_op | source)
XLA Modules:
  0.0 116.0 jit_solution(11806052802222715489)
XLA Ops:
  0.7 1.4 %copy.16 = bf16[8,32,1024]{2,0,1:T(8,128)(2,1)S(1)} copy(bf16[8,32,1024]{2,1,0:T(8,128)(2,1)} %q_ref.1) | data formatting | bytes 1048576 | tf_op args[0]
  2.1 1.3 %copy.19 = bf16[8,32,1024]{2,0,1:T(8,128)(2,1)S(1)} copy(bf16[8,32,1024]{2,1,0:T(8,128)(2,1)} %g_ref.1) | data formatting | bytes 1048576 | tf_op args[3]
  3.4 0.3 copy.17
  3.7 0.3 copy.18
  4.0 1.6 %maximum_bitcast_fusion = bf16[8,4,4,8,1024]{4,3,2,1,0:T(8,128)(2,1)} fusion(bf16[1,8,8,4,1024]{4,1,3,0,2:T(8,128)(2,1)S(1)} %bitcast.19, bf16[1,8,8,4,1024]{4,1,3,0,2:T(8,128)(2,1)S(1)} %bitcast.21, bf16[1,8,8,4,1024]{4,1,3,0,2:T(8,128)(2,1)S(1)} %bitcast.20, bf16[1,8,8,4,1024]{4,1,3,0,2:T(8,128)(2,1)S(1)} %bitcast.18), kind=kLoop, calls=%fused_computation.1 | loop fusion | flops 3145728 | bytes 4194304 | tf_op jit(solution)/shard_map/transpose | solution.py:301
  5.6 4.3 %all-to-all-start = ((bf16[8,4,4,8,1024]{4,3,2,1,0:T(8,128)(2,1)}), bf16[8,4,4,8,1024]{4,3,2,1,0:T(8,128)(2,1)S(1)}, u32[]{:S(2)}, u32[]{:S(2)}) async-start(bf16[8,4,4,8,1024]{4,3,2,1,0:T(8,128)(2,1)} %maximum_bitcast_fusion), calls=%async_computation | async-start | bytes 4194304 | tf_op jit(solution)/shard_map/all_to_all | solution.py:303
  9.9 1.1 pad_maximum_fusion
  11.0 2.0 %collective-permute-start.1 = (bf16[2,8,32,1024]{3,2,1,0:T(8,128)(2,1)}, bf16[2,8,32,1024]{3,2,1,0:T(8,128)(2,1)S(1)}, u32[]{:S(2)}, u32[]{:S(2)}) collective-permute-start(bf16[2,8,32,1024]{3,2,1,0:T(8,128)(2,1)} %pad_maximum_fusion), channel_id=1, source_target_pairs={{1,0},{2,1},{3,2},{4,3},{5,4},{6,5},{7,6},{9,8},{10,9},{11,10},{12... | collective-permute-start | bytes 3145736 | tf_op jit(solution)/shard_map/ppermute | solution.py:22
  13.0 3.8 %collective-permute-start = (bf16[2,8,32,1024]{3,2,1,0:T(8,128)(2,1)}, bf16[2,8,32,1024]{3,2,1,0:T(8,128)(2,1)}, u32[]{:S(2)}, u32[]{:S(2)}) collective-permute-start(bf16[2,8,32,1024]{3,2,1,0:T(8,128)(2,1)} %pad_maximum_fusion), channel_id=1, source_target_pairs={{0,1},{1,2},{2,3},{3,4},{4,5},{5,6},{6,7},{8,9},{9,10},{10,11},{11... | collective-permute-start | bytes 3145736 | tf_op jit(solution)/shard_map/ppermute | solution.py:22
  16.9 20.2 %all-to-all-done.x_ref = bf16[8,4,4,8,1024]{4,3,2,1,0:T(8,128)(2,1)S(1)} async-done(((bf16[8,4,4,8,1024]{4,3,2,1,0:T(8,128)(2,1)}), bf16[8,4,4,8,1024]{4,3,2,1,0:T(8,128)(2,1)S(1)}, u32[]{:S(2)}, u32[]{:S(2)}) %all-to-all-start) | async-done | bytes 2097184 | tf_op jit(solution)/shard_map/all_to_all | solution.py:303
  37.1 1.3 %copy-done = bf16[8,4,4,8,1024]{4,3,2,1,0:T(8,128)(2,1)} copy-done((bf16[8,4,4,8,1024]{4,3,2,1,0:T(8,128)(2,1)}, bf16[8,4,4,8,1024]{4,3,2,1,0:T(8,128)(2,1)S(1)}, u32[]{:S(2)}) %copy-start) | copy-done | bytes 2097176
  38.5 5.9 %shard_map.86 = bf16[8,3,4,8,1024]{4,3,2,1,0:T(8,128)(2,1)} custom-call(bf16[8,4,4,8,1024]{4,3,2,1,0:T(8,128)(2,1)} %copy-done), custom_call_target="tpu_custom_call" | custom-call | tf_op jit(solution)/shard_map/pallas_call | solution.py:259
  44.3 3.7 %all-to-all-start.1 = ((bf16[8,3,4,8,1024]{4,3,2,1,0:T(8,128)(2,1)}), bf16[8,3,4,8,1024]{4,3,2,1,0:T(8,128)(2,1)S(1)}, u32[]{:S(2)}, u32[]{:S(2)}) async-start(bf16[8,3,4,8,1024]{4,3,2,1,0:T(8,128)(2,1)} %shard_map.86), calls=%async_computation.1 | async-start | bytes 3145728 | tf_op jit(solution)/shard_map/all_to_all | solution.py:313
  48.1 0.1 multiply_reduce_fusion
  48.2 0.1 broadcast_compare_fusion
  48.4 0.8 fusion.6.bias_ref
  49.1 1.0 copy-done.6
  50.1 60.0 %shard_map.85 = (f32[8,32,1024]{2,1,0:T(8,128)}, f32[8,32,1024]{2,1,0:T(8,128)}, f32[8,32,1024]{2,1,0:T(8,128)}) custom-call(bf16[8,32,1024]{2,1,0:T(8,128)(2,1)} %q_ref.1, bf16[8,32,1024]{2,1,0:T(8,128)(2,1)} %g_ref.1, bf16[8,32,1024]{2,1,0:T(8,128)(2,1)} %k_ref.1, bf16[8,32,1024]{2,1,0:T(8,128)(2,1)} %v_ref.1, ...), custom_call_target="tpu_custom_call" | custom-call | tf_op jit(solution)/shard_map/pallas_call | solution.py:194
  110.1 0.4 convert_bitcast_fusion
  110.5 0.4 fusion.8
  110.9 0.8 copy-done.5
  111.8 1.4 %fusion.2 = bf16[8,32,1024]{2,1,0:T(8,128)(2,1)} fusion(f32[8,32,1024]{2,1,0:T(8,128)S(1)} %copy-done.5, f32[8,32,1024]{2,0,1:T(8,128)S(1)} %bitcast.17), kind=kLoop, calls=%fused_computation.8 | loop fusion | flops 524288 | bytes 2621440 | tf_op jit(solution)/shard_map/convert_element_type | solution.py:317
  113.2 1.4 %fusion = bf16[8,32,1024]{2,1,0:T(8,128)(2,1)} fusion(f32[8,32,1024]{2,1,0:T(8,128)S(1)} %copy-done.4, f32[8,32,1024]{2,0,1:T(8,128)S(1)} %bitcast.16), kind=kLoop, calls=%fused_computation.4 | loop fusion | flops 524288 | bytes 2621440 | tf_op jit(solution)/shard_map/convert_element_type | solution.py:317
  114.6 1.4 %fusion.1 = bf16[8,32,1024]{2,1,0:T(8,128)(2,1)} fusion(f32[8,32,1024]{2,1,0:T(8,128)S(1)} %copy-done.3, f32[8,32,1024]{2,0,1:T(8,128)S(1)} %bitcast.15), kind=kLoop, calls=%fused_computation.6 | loop fusion | flops 524288 | bytes 2621440 | tf_op jit(solution)/shard_map/convert_element_type | solution.py:317
  (25 shorter events, 0.2 us)
Async XLA Ops:
  0.6 2.8 %copy-start.1 = (bf16[8,32,1024]{2,1,0:T(8,128)(2,1)S(1)}, bf16[8,32,1024]{2,1,0:T(8,128)(2,1)}, u32[]{:S(2)}) copy-start(bf16[8,32,1024]{2,1,0:T(8,128)(2,1)} %k_ref.1) | copy-start | bytes 1572868
  0.6 3.1 %copy-start.2 = (bf16[8,32,1024]{2,1,0:T(8,128)(2,1)S(1)}, bf16[8,32,1024]{2,1,0:T(8,128)(2,1)}, u32[]{:S(2)}) copy-start(bf16[8,32,1024]{2,1,0:T(8,128)(2,1)} %v_ref.1) | copy-start | bytes 1572868
  5.6 31.5 %all-to-all-start = ((bf16[8,4,4,8,1024]{4,3,2,1,0:T(8,128)(2,1)}), bf16[8,4,4,8,1024]{4,3,2,1,0:T(8,128)(2,1)S(1)}, u32[]{:S(2)}, u32[]{:S(2)}) async-start(bf16[8,4,4,8,1024]{4,3,2,1,0:T(8,128)(2,1)} %maximum_bitcast_fusion), calls=%async_computation | async-start | bytes 4194304 | tf_op jit(solution)/shard_map/all_to_all | solution.py:303
  11.0 38.1 %collective-permute-start.1 = (bf16[2,8,32,1024]{3,2,1,0:T(8,128)(2,1)}, bf16[2,8,32,1024]{3,2,1,0:T(8,128)(2,1)S(1)}, u32[]{:S(2)}, u32[]{:S(2)}) collective-permute-start(bf16[2,8,32,1024]{3,2,1,0:T(8,128)(2,1)} %pad_maximum_fusion), channel_id=1, source_target_pairs={{1,0},{2,1},{3,2},{4,3},{5,4},{6,5},{7,6},{9,8},{10,9},{11,10},{12... | collective-permute-start | bytes 3145736 | tf_op jit(solution)/shard_map/ppermute | solution.py:22
  13.0 36.1 %collective-permute-start = (bf16[2,8,32,1024]{3,2,1,0:T(8,128)(2,1)}, bf16[2,8,32,1024]{3,2,1,0:T(8,128)(2,1)}, u32[]{:S(2)}, u32[]{:S(2)}) collective-permute-start(bf16[2,8,32,1024]{3,2,1,0:T(8,128)(2,1)} %pad_maximum_fusion), channel_id=1, source_target_pairs={{0,1},{1,2},{2,3},{3,4},{4,5},{5,6},{6,7},{8,9},{9,10},{10,11},{11... | collective-permute-start | bytes 3145736 | tf_op jit(solution)/shard_map/ppermute | solution.py:22
  37.1 1.3 %copy-start = (bf16[8,4,4,8,1024]{4,3,2,1,0:T(8,128)(2,1)}, bf16[8,4,4,8,1024]{4,3,2,1,0:T(8,128)(2,1)S(1)}, u32[]{:S(2)}) copy-start(bf16[8,4,4,8,1024]{4,3,2,1,0:T(8,128)(2,1)S(1)} %all-to-all-done.x_ref) | copy-start | bytes 6291460
  44.3 3.8 %copy-start.7 = (s32[8,16]{1,0:T(8,128)S(1)}, s32[8,16]{1,0:T(8,128)}, u32[]{:S(2)}) copy-start(s32[8,16]{1,0:T(8,128)} %param.10) | copy-start | bytes 1540
  44.3 4.0 %copy-start.8 = (s32[8]{0:T(128)S(1)}, s32[8]{0:T(128)}, u32[]{:S(2)}) copy-start(s32[8]{0:T(128)} %param.11) | copy-start | bytes 100
  44.3 65.8 %all-to-all-start.1 = ((bf16[8,3,4,8,1024]{4,3,2,1,0:T(8,128)(2,1)}), bf16[8,3,4,8,1024]{4,3,2,1,0:T(8,128)(2,1)S(1)}, u32[]{:S(2)}, u32[]{:S(2)}) async-start(bf16[8,3,4,8,1024]{4,3,2,1,0:T(8,128)(2,1)} %shard_map.86), calls=%async_computation.1 | async-start | bytes 3145728 | tf_op jit(solution)/shard_map/all_to_all | solution.py:313
  49.1 1.0 copy-start.6
  110.5 1.2 %copy-start.5 = (f32[8,32,1024]{2,1,0:T(8,128)S(1)}, f32[8,32,1024]{2,1,0:T(8,128)}, u32[]{:S(2)}) copy-start(f32[8,32,1024]{2,1,0:T(8,128)} %get-tuple-element.6) | copy-start | bytes 3145732
  110.9 2.2 %copy-start.4 = (f32[8,32,1024]{2,1,0:T(8,128)S(1)}, f32[8,32,1024]{2,1,0:T(8,128)}, u32[]{:S(2)}) copy-start(f32[8,32,1024]{2,1,0:T(8,128)} %get-tuple-element.8) | copy-start | bytes 3145732
  111.7 2.8 %copy-start.3 = (f32[8,32,1024]{2,1,0:T(8,128)S(1)}, f32[8,32,1024]{2,1,0:T(8,128)}, u32[]{:S(2)}) copy-start(f32[8,32,1024]{2,1,0:T(8,128)} %get-tuple-element.7) | copy-start | bytes 3145732

commit v11 on v10

--- a/solution.py
+++ b/solution.py
@@ -77,12 +77,12 @@
     return dq, dk, dv
 
 
-def fused_row_kernel(w2, q_ref, g_ref, k_ref, v_ref, l1_ref, r1_ref, bias_ref,
+def fused_row_kernel(q_ref, g_ref, k_ref, v_ref, l2_ref, l1_ref, r1_ref, r2_ref, bias_ref,
                      qg_ref, kg_ref, vg_ref,
-                     l2_ref, r2_ref, own_s, near_l, near_r, s_fl, s_fr, s_nl, s_nr, x_fr, x_fl,
-                     x_nr, x_nl, halo_send, halo_recv, far_send, far_recv_r, far_recv_l,
-                     near_send, near_recv):
+                     own_s, near_l, near_r, s_fl, s_fr, s_nl, s_nr, x_fr, x_fl,
+                     x_nr, x_nl, far_send, far_recv_r, far_recv_l, near_send, near_recv):
     rows, cc, width = q_ref.shape
+    w2 = l2_ref.shape[2]
     w1 = l1_ref.shape[2]
     n = lax.axis_size("rcol")
     me = lax.axis_index("rcol")
@@ -96,21 +96,6 @@
     for distance in (-1, 1):
         pl.semaphore_signal(barrier, 1, device_id=dev(distance), device_id_type=mesh_ids)
     pl.semaphore_wait(barrier, 2)
-
-    relays = (
-        pltpu.make_async_remote_copy(
-            src_ref=l1_ref.at[:, :, pl.ds(w1 - w2, w2)], dst_ref=l2_ref,
-            send_sem=halo_send.at[0], recv_sem=halo_recv.at[0],
-            device_id=dev(1), device_id_type=mesh_ids),
-        pltpu.make_async_remote_copy(
-            src_ref=r1_ref.at[:, :, pl.ds(0, w2)], dst_ref=r2_ref,
-            send_sem=halo_send.at[1], recv_sem=halo_recv.at[1],
-            device_id=dev(-1), device_id_type=mesh_ids),
-    )
-    for copy in relays:
-        copy.start()
-    for copy in relays:
-        copy.wait()
 
     def far_copy(r, to_left):
         if to_left:
@@ -184,21 +169,20 @@
         out_ref[...] = own_s[which] + x_nr[which].astype(f32) + x_nl[which].astype(f32)
 
 
-def fused_row(queries, out_grad, key_grid, value_grid, l1, r1, bias, w2):
+def fused_row(queries, out_grad, key_grid, value_grid, l2, l1, r1, r2, bias):
     rows, cc, width = queries.shape
+    w2 = l2.shape[2]
     w1 = l1.shape[2]
     vmem = pl.BlockSpec(memory_space=pltpu.VMEM)
     grads = jax.ShapeDtypeStruct((rows, cc, width), jnp.float32)
     bf = jnp.bfloat16
     f32 = jnp.float32
     return pl.pallas_call(
-        functools.partial(fused_row_kernel, w2),
-        in_specs=[vmem] * 7,
+        fused_row_kernel,
+        in_specs=[vmem] * 9,
         out_specs=[vmem] * 3,
         out_shape=(grads, grads, grads),
         scratch_shapes=[
-            pltpu.VMEM((2, rows, w2, width), bf),
-            pltpu.VMEM((2, rows, w2, width), bf),
             pltpu.VMEM((2, rows, cc, width), f32),
             pltpu.VMEM((2, rows, w1, width), f32),
             pltpu.VMEM((2, rows, w1, width), f32),
@@ -211,8 +195,6 @@
             pltpu.VMEM((2, rows, cc, width), bf),
             pltpu.VMEM((2, rows, cc, width), bf),
             pltpu.SemaphoreType.DMA((2,)),
-            pltpu.SemaphoreType.DMA((2,)),
-            pltpu.SemaphoreType.DMA((2,)),
             pltpu.SemaphoreType.DMA((rows,)),
             pltpu.SemaphoreType.DMA((rows,)),
             pltpu.SemaphoreType.DMA((2,)),
@@ -221,7 +203,7 @@
         compiler_params=pltpu.CompilerParams(
             collective_id=0, has_side_effects=True, vmem_limit_bytes=60 * 1024 * 1024
         ),
-    )(queries, out_grad, key_grid, value_grid, l1, r1, bias)
+    )(queries, out_grad, key_grid, value_grid, l2, l1, r1, r2, bias)
 
 
 def column_kernel(x_ref, o_ref):
@@ -305,13 +287,15 @@
     pair = jnp.stack([key_grid, value_grid])
     l1 = shifted(pair[:, :, col_count - near:], "rcol", 1)
     r1 = shifted(pair[:, :, :near], "rcol", -1)
+    l2 = shifted(pair[:, :, col_count - far:], "rcol", 2)
+    r2 = shifted(pair[:, :, :far], "rcol", -2)
     grid_cols = col_count * lax.axis_size("rcol")
     first_col = lax.axis_index("rcol") * col_count
     bias = band_bias(tissue_mask, band_offset, first_col, grid_cols, col_count)
 
     col_out = column_attention(whole)
     back = lax.all_to_all(col_out, "rrow", split_axis=0, concat_axis=0, tiled=True)
-    row_grads = fused_row(queries, out_grad, key_grid, value_grid, l1, r1, bias, far)
+    row_grads = fused_row(queries, out_grad, key_grid, value_grid, l2, l1, r1, r2, bias)
     back = back.transpose(1, 3, 0, 2, 4).reshape(3, row_count, col_count, feature_width)
     back = back.astype(jnp.float32)
     return tuple((row + col).astype(jnp.bfloat16) for row, col in zip(row_grads, back))

time: 118 us -> 119 us (level)
  Pallas kernels: 65.9 us -> 56.1 us
  starting transfers between devices: 13.8 us -> 22.8 us
  waiting for transfers between devices: 20.2 us -> 21.8 us
    ppermute x2 -> x4, waiting for transfers between devices: 0.01 us -> 11.6 us  [shifted(): return lax.ppermute(block, axis, route)]
    all_to_all x1, waiting for transfers between devices: 20.2 us -> 10.2 us  [body(): lax.all_to_all(stacked, 'rrow', split_axis=0, concat_axis=0, tiled=True)]
    pallas_call x1, Pallas kernels: 60 us -> 50.3 us  [fused_row(): pl.pallas_call(fused_row_kernel, in_specs=[vmem] * 9, out_specs=[vmem] *...]
    ppermute x2 -> x4, starting transfers between devices: 5.83 us -> 14.8 us  [shifted(): return lax.ppermute(block, axis, route)]
    unnamed x22 -> x20, local copies, waits for them, and re-layouts: 6.47 us -> 5.51 us
  transfers between devices with their start and end apart: 4 -> 6, of which waited for: 1 -> 3; matrix products, arithmetic and copies ran while one was open for 2% -> 3% of each run, Pallas kernels for 57% -> 48%
where the time goes in v11:
time: 119 us; the launch traced here: 117 us
  Pallas kernels  56.1 us (47%)
  starting transfers between devices  22.8 us (19%)
  waiting for transfers between devices  21.8 us (18%)
  other arithmetic  9.4 us (8%)
  local copies, waits for them, and re-layouts  5.92 us (5%)
    pallas_call x1, Pallas kernels, fused_row(): pl.pallas_call(fused_row_kernel, in_specs=[vmem] * 9, out_specs=[vmem] *...  50.3 us
    ppermute x4, starting transfers between devices, shifted(): return lax.ppermute(block, axis, route)  14.8 us
    ppermute x4, waiting for transfers between devices, shifted(): return lax.ppermute(block, axis, route)  11.6 us
    all_to_all x1, waiting for transfers between devices, body(): lax.all_to_all(stacked, 'rrow', split_axis=0, concat_axis=0, tiled=True)  10.2 us
    pallas_call x1, Pallas kernels, column_attention(): pl.pallas_call(column_kernel, in_specs=[vmem], out_specs=vmem, out_shape=...  5.86 us
    unnamed x20, local copies, waits for them, and re-layouts  5.51 us
    all_to_all x1, starting transfers between devices, body(): lax.all_to_all(stacked, 'rrow', split_axis=0, concat_axis=0, tiled=True)  4.3 us
    convert_element_type x3, other arithmetic, body(): (row + col).astype(jnp.bfloat16)  4.22 us
  transfers between devices with their start and end apart: 6, of which 3 were waited for; matrix products, arithmetic and copies ran while one was open for 3% of the time, Pallas kernels for 48%

profile of v11, /device:TPU:48, one launch (start us, length us, event | category | flops | bytes accessed | tf_op | source)
XLA Modules:
  0.0 116.9 jit_solution(11882850473792225491)
XLA Ops:
  0.7 1.4 %copy.16 = bf16[8,32,1024]{2,0,1:T(8,128)(2,1)S(1)} copy(bf16[8,32,1024]{2,1,0:T(8,128)(2,1)} %q_ref.1) | data formatting | bytes 1048576 | tf_op args[0]
  2.1 1.3 %copy.19 = bf16[8,32,1024]{2,0,1:T(8,128)(2,1)S(1)} copy(bf16[8,32,1024]{2,1,0:T(8,128)(2,1)} %g_ref.1) | data formatting | bytes 1048576 | tf_op args[3]
  4.0 1.6 %maximum_bitcast_fusion = bf16[8,4,4,8,1024]{4,3,2,1,0:T(8,128)(2,1)} fusion(bf16[1,8,8,4,1024]{4,1,3,0,2:T(8,128)(2,1)S(1)} %bitcast.21, bf16[1,8,8,4,1024]{4,1,3,0,2:T(8,128)(2,1)S(1)} %bitcast.23, bf16[1,8,8,4,1024]{4,1,3,0,2:T(8,128)(2,1)S(1)} %bitcast.22, bf16[1,8,8,4,1024]{4,1,3,0,2:T(8,128)(2,1)S(1)} %bitcast.20), kind=kLoop, calls=%fused_computation.1 | loop fusion | flops 3145728 | bytes 4194304 | tf_op jit(solution)/shard_map/transpose | solution.py:283
  5.6 4.3 %all-to-all-start = ((bf16[8,4,4,8,1024]{4,3,2,1,0:T(8,128)(2,1)}), bf16[8,4,4,8,1024]{4,3,2,1,0:T(8,128)(2,1)S(1)}, u32[]{:S(2)}, u32[]{:S(2)}) async-start(bf16[8,4,4,8,1024]{4,3,2,1,0:T(8,128)(2,1)} %maximum_bitcast_fusion), calls=%async_computation | async-start | bytes 4194304 | tf_op jit(solution)/shard_map/all_to_all | solution.py:285
  9.9 1.1 pad_maximum_fusion
  11.0 3.8 %collective-permute-start.1 = (bf16[2,8,32,1024]{3,2,1,0:T(8,128)(2,1)}, bf16[2,8,32,1024]{3,2,1,0:T(8,128)(2,1)}, u32[]{:S(2)}, u32[]{:S(2)}) collective-permute-start(bf16[2,8,32,1024]{3,2,1,0:T(8,128)(2,1)} %pad_maximum_fusion), channel_id=1, source_target_pairs={{0,1},{1,2},{2,3},{3,4},{4,5},{5,6},{6,7},{8,9},{9,10},{10,11},{11... | collective-permute-start | bytes 3145736 | tf_op jit(solution)/shard_map/ppermute | solution.py:22
  14.8 3.0 %collective-permute-start.2 = (bf16[2,8,32,1024]{3,2,1,0:T(8,128)(2,1)}, bf16[2,8,32,1024]{3,2,1,0:T(8,128)(2,1)}, u32[]{:S(2)}, u32[]{:S(2)}) collective-permute-start(bf16[2,8,32,1024]{3,2,1,0:T(8,128)(2,1)} %pad_maximum_fusion), channel_id=1, source_target_pairs={{1,0},{2,1},{3,2},{4,3},{5,4},{6,5},{7,6},{9,8},{10,9},{11,10},{12... | collective-permute-start | bytes 3145736 | tf_op jit(solution)/shard_map/ppermute | solution.py:22
  17.8 1.1 fusion.4
  18.9 1.3 %collective-permute-start.3 = (bf16[2,8,16,1024]{3,2,1,0:T(8,128)(2,1)}, bf16[2,8,16,1024]{3,2,1,0:T(8,128)(2,1)}, u32[]{:S(2)}, u32[]{:S(2)}) collective-permute-start(bf16[2,8,16,1024]{3,2,1,0:T(8,128)(2,1)} %get-tuple-element.12), channel_id=1, source_target_pairs={{2,0},{3,1},{4,2},{5,3},{6,4},{7,5},{10,8},{11,9},{12,10},{13,11},... | collective-permute-start | bytes 1572872 | tf_op jit(solution)/shard_map/ppermute | solution.py:22
  20.2 6.8 %collective-permute-start = (bf16[2,8,16,1024]{3,2,1,0:T(8,128)(2,1)}, bf16[2,8,16,1024]{3,2,1,0:T(8,128)(2,1)}, u32[]{:S(2)}, u32[]{:S(2)}) collective-permute-start(bf16[2,8,16,1024]{3,2,1,0:T(8,128)(2,1)} %get-tuple-element.13), channel_id=1, source_target_pairs={{0,2},{1,3},{2,4},{3,5},{4,6},{5,7},{8,10},{9,11},{10,12},{11,13},... | collective-permute-start | bytes 1572872 | tf_op jit(solution)/shard_map/ppermute | solution.py:22
  26.9 10.2 %all-to-all-done.x_ref = bf16[8,4,4,8,1024]{4,3,2,1,0:T(8,128)(2,1)S(1)} async-done(((bf16[8,4,4,8,1024]{4,3,2,1,0:T(8,128)(2,1)}), bf16[8,4,4,8,1024]{4,3,2,1,0:T(8,128)(2,1)S(1)}, u32[]{:S(2)}, u32[]{:S(2)}) %all-to-all-start) | async-done | bytes 2097184 | tf_op jit(solution)/shard_map/all_to_all | solution.py:285
  37.1 1.3 %copy-done = bf16[8,4,4,8,1024]{4,3,2,1,0:T(8,128)(2,1)} copy-done((bf16[8,4,4,8,1024]{4,3,2,1,0:T(8,128)(2,1)}, bf16[8,4,4,8,1024]{4,3,2,1,0:T(8,128)(2,1)S(1)}, u32[]{:S(2)}) %copy-start) | copy-done | bytes 2097176
  38.5 5.9 %shard_map.86 = bf16[8,3,4,8,1024]{4,3,2,1,0:T(8,128)(2,1)} custom-call(bf16[8,4,4,8,1024]{4,3,2,1,0:T(8,128)(2,1)} %copy-done), custom_call_target="tpu_custom_call" | custom-call | tf_op jit(solution)/shard_map/pallas_call | solution.py:241
  44.3 3.7 %all-to-all-start.1 = ((bf16[8,3,4,8,1024]{4,3,2,1,0:T(8,128)(2,1)}), bf16[8,3,4,8,1024]{4,3,2,1,0:T(8,128)(2,1)S(1)}, u32[]{:S(2)}, u32[]{:S(2)}) async-start(bf16[8,3,4,8,1024]{4,3,2,1,0:T(8,128)(2,1)} %shard_map.86), calls=%async_computation.1 | async-start | bytes 3145728 | tf_op jit(solution)/shard_map/all_to_all | solution.py:297
  48.4 0.8 fusion.8.bias_ref
  49.1 7.5 %collective-permute-done.3.r2_ref = bf16[2,8,16,1024]{3,2,1,0:T(8,128)(2,1)} collective-permute-done((bf16[2,8,16,1024]{3,2,1,0:T(8,128)(2,1)}, bf16[2,8,16,1024]{3,2,1,0:T(8,128)(2,1)}, u32[]{:S(2)}, u32[]{:S(2)}) %collective-permute-start.3) | collective-permute-done | bytes 524320 | tf_op jit(solution)/shard_map/ppermute | solution.py:22
  56.7 4.1 %collective-permute-done.l2_ref = bf16[2,8,16,1024]{3,2,1,0:T(8,128)(2,1)} collective-permute-done((bf16[2,8,16,1024]{3,2,1,0:T(8,128)(2,1)}, bf16[2,8,16,1024]{3,2,1,0:T(8,128)(2,1)}, u32[]{:S(2)}, u32[]{:S(2)}) %collective-permute-start) | collective-permute-done | bytes 524320 | tf_op jit(solution)/shard_map/ppermute | solution.py:22
  60.7 50.3 %shard_map.85 = (f32[8,32,1024]{2,1,0:T(8,128)}, f32[8,32,1024]{2,1,0:T(8,128)}, f32[8,32,1024]{2,1,0:T(8,128)}) custom-call(bf16[8,32,1024]{2,1,0:T(8,128)(2,1)} %q_ref.1, bf16[8,32,1024]{2,1,0:T(8,128)(2,1)} %g_ref.1, bf16[8,32,1024]{2,1,0:T(8,128)(2,1)} %k_ref.1, bf16[8,32,1024]{2,1,0:T(8,128)(2,1)} %v_ref.1, ...), custom_call_target="tpu_custom_call" | custom-call | tf_op jit(solution)/shard_map/pallas_call | solution.py:180
  111.0 0.4 convert_bitcast_fusion
  111.4 0.4 fusion.10
  111.9 0.8 copy-done.5
  112.7 1.4 %fusion.2 = bf16[8,32,1024]{2,1,0:T(8,128)(2,1)} fusion(f32[8,32,1024]{2,1,0:T(8,128)S(1)} %copy-done.5, f32[8,32,1024]{2,0,1:T(8,128)S(1)} %bitcast.19), kind=kLoop, calls=%fused_computation.12 | loop fusion | flops 524288 | bytes 2621440 | tf_op jit(solution)/shard_map/convert_element_type | solution.py:301
  114.1 1.4 %fusion = bf16[8,32,1024]{2,1,0:T(8,128)(2,1)} fusion(f32[8,32,1024]{2,1,0:T(8,128)S(1)} %copy-done.4, f32[8,32,1024]{2,0,1:T(8,128)S(1)} %bitcast.18), kind=kLoop, calls=%fused_computation.8 | loop fusion | flops 524288 | bytes 2621440 | tf_op jit(solution)/shard_map/convert_element_type | solution.py:301
  115.5 1.4 %fusion.1 = bf16[8,32,1024]{2,1,0:T(8,128)(2,1)} fusion(f32[8,32,1024]{2,1,0:T(8,128)S(1)} %copy-done.3, f32[8,32,1024]{2,0,1:T(8,128)S(1)} %bitcast.17), kind=kLoop, calls=%fused_computation.10 | loop fusion | flops 524288 | bytes 2621440 | tf_op jit(solution)/shard_map/convert_element_type | solution.py:301
  (28 shorter events, 0.9 us)
Async XLA Ops:
  0.6 2.8 %copy-start.1 = (bf16[8,32,1024]{2,1,0:T(8,128)(2,1)S(1)}, bf16[8,32,1024]{2,1,0:T(8,128)(2,1)}, u32[]{:S(2)}) copy-start(bf16[8,32,1024]{2,1,0:T(8,128)(2,1)} %k_ref.1) | copy-start | bytes 1572868
  0.6 3.1 %copy-start.2 = (bf16[8,32,1024]{2,1,0:T(8,128)(2,1)S(1)}, bf16[8,32,1024]{2,1,0:T(8,128)(2,1)}, u32[]{:S(2)}) copy-start(bf16[8,32,1024]{2,1,0:T(8,128)(2,1)} %v_ref.1) | copy-start | bytes 1572868
  5.6 31.5 %all-to-all-start = ((bf16[8,4,4,8,1024]{4,3,2,1,0:T(8,128)(2,1)}), bf16[8,4,4,8,1024]{4,3,2,1,0:T(8,128)(2,1)S(1)}, u32[]{:S(2)}, u32[]{:S(2)}) async-start(bf16[8,4,4,8,1024]{4,3,2,1,0:T(8,128)(2,1)} %maximum_bitcast_fusion), calls=%async_computation | async-start | bytes 4194304 | tf_op jit(solution)/shard_map/all_to_all | solution.py:285
  11.0 49.7 %collective-permute-start.1 = (bf16[2,8,32,1024]{3,2,1,0:T(8,128)(2,1)}, bf16[2,8,32,1024]{3,2,1,0:T(8,128)(2,1)}, u32[]{:S(2)}, u32[]{:S(2)}) collective-permute-start(bf16[2,8,32,1024]{3,2,1,0:T(8,128)(2,1)} %pad_maximum_fusion), channel_id=1, source_target_pairs={{0,1},{1,2},{2,3},{3,4},{4,5},{5,6},{6,7},{8,9},{9,10},{10,11},{11... | collective-permute-start | bytes 3145736 | tf_op jit(solution)/shard_map/ppermute | solution.py:22
  14.8 45.9 %collective-permute-start.2 = (bf16[2,8,32,1024]{3,2,1,0:T(8,128)(2,1)}, bf16[2,8,32,1024]{3,2,1,0:T(8,128)(2,1)}, u32[]{:S(2)}, u32[]{:S(2)}) collective-permute-start(bf16[2,8,32,1024]{3,2,1,0:T(8,128)(2,1)} %pad_maximum_fusion), channel_id=1, source_target_pairs={{1,0},{2,1},{3,2},{4,3},{5,4},{6,5},{7,6},{9,8},{10,9},{11,10},{12... | collective-permute-start | bytes 3145736 | tf_op jit(solution)/shard_map/ppermute | solution.py:22
  18.9 37.8 %collective-permute-start.3 = (bf16[2,8,16,1024]{3,2,1,0:T(8,128)(2,1)}, bf16[2,8,16,1024]{3,2,1,0:T(8,128)(2,1)}, u32[]{:S(2)}, u32[]{:S(2)}) collective-permute-start(bf16[2,8,16,1024]{3,2,1,0:T(8,128)(2,1)} %get-tuple-element.12), channel_id=1, source_target_pairs={{2,0},{3,1},{4,2},{5,3},{6,4},{7,5},{10,8},{11,9},{12,10},{13,11},... | collective-permute-start | bytes 1572872 | tf_op jit(solution)/shard_map/ppermute | solution.py:22
  20.2 40.6 %collective-permute-start = (bf16[2,8,16,1024]{3,2,1,0:T(8,128)(2,1)}, bf16[2,8,16,1024]{3,2,1,0:T(8,128)(2,1)}, u32[]{:S(2)}, u32[]{:S(2)}) collective-permute-start(bf16[2,8,16,1024]{3,2,1,0:T(8,128)(2,1)} %get-tuple-element.13), channel_id=1, source_target_pairs={{0,2},{1,3},{2,4},{3,5},{4,6},{5,7},{8,10},{9,11},{10,12},{11,13},... | collective-permute-start | bytes 1572872 | tf_op jit(solution)/shard_map/ppermute | solution.py:22
  37.1 1.3 %copy-start = (bf16[8,4,4,8,1024]{4,3,2,1,0:T(8,128)(2,1)}, bf16[8,4,4,8,1024]{4,3,2,1,0:T(8,128)(2,1)S(1)}, u32[]{:S(2)}) copy-start(bf16[8,4,4,8,1024]{4,3,2,1,0:T(8,128)(2,1)S(1)} %all-to-all-done.x_ref) | copy-start | bytes 6291460
  44.3 3.8 %copy-start.6 = (s32[8,16]{1,0:T(8,128)S(1)}, s32[8,16]{1,0:T(8,128)}, u32[]{:S(2)}) copy-start(s32[8,16]{1,0:T(8,128)} %param.10) | copy-start | bytes 1540
  44.3 4.0 %copy-start.7 = (s32[8]{0:T(128)S(1)}, s32[8]{0:T(128)}, u32[]{:S(2)}) copy-start(s32[8]{0:T(128)} %param.11) | copy-start | bytes 100
  44.3 66.7 %all-to-all-start.1 = ((bf16[8,3,4,8,1024]{4,3,2,1,0:T(8,128)(2,1)}), bf16[8,3,4,8,1024]{4,3,2,1,0:T(8,128)(2,1)S(1)}, u32[]{:S(2)}, u32[]{:S(2)}) async-start(bf16[8,3,4,8,1024]{4,3,2,1,0:T(8,128)(2,1)} %shard_map.86), calls=%async_computation.1 | async-start | bytes 3145728 | tf_op jit(solution)/shard_map/all_to_all | solution.py:297
  111.4 1.2 %copy-start.5 = (f32[8,32,1024]{2,1,0:T(8,128)S(1)}, f32[8,32,1024]{2,1,0:T(8,128)}, u32[]{:S(2)}) copy-start(f32[8,32,1024]{2,1,0:T(8,128)} %get-tuple-element.6) | copy-start | bytes 3145732
  111.9 2.2 %copy-start.4 = (f32[8,32,1024]{2,1,0:T(8,128)S(1)}, f32[8,32,1024]{2,1,0:T(8,128)}, u32[]{:S(2)}) copy-start(f32[8,32,1024]{2,1,0:T(8,128)} %get-tuple-element.8) | copy-start | bytes 3145732
  112.7 2.8 %copy-start.3 = (f32[8,32,1024]{2,1,0:T(8,128)S(1)}, f32[8,32,1024]{2,1,0:T(8,128)}, u32[]{:S(2)}) copy-start(f32[8,32,1024]{2,1,0:T(8,128)} %get-tuple-element.7) | copy-start | bytes 3145732

commit v12 on v10

--- a/solution.py
+++ b/solution.py
@@ -80,7 +80,7 @@
 def fused_row_kernel(w2, q_ref, g_ref, k_ref, v_ref, l1_ref, r1_ref, bias_ref,
                      qg_ref, kg_ref, vg_ref,
                      l2_ref, r2_ref, own_s, near_l, near_r, s_fl, s_fr, s_nl, s_nr, x_fr, x_fl,
-                     x_nr, x_nl, halo_send, halo_recv, far_send, far_recv_r, far_recv_l,
+                     x_nr, x_nl, halo_send, halo_recv_l, halo_recv_r, far_send, far_recv_r, far_recv_l,
                      near_send, near_recv):
     rows, cc, width = q_ref.shape
     w1 = l1_ref.shape[2]
@@ -97,20 +97,22 @@
         pl.semaphore_signal(barrier, 1, device_id=dev(distance), device_id_type=mesh_ids)
     pl.semaphore_wait(barrier, 2)
 
-    relays = (
-        pltpu.make_async_remote_copy(
-            src_ref=l1_ref.at[:, :, pl.ds(w1 - w2, w2)], dst_ref=l2_ref,
-            send_sem=halo_send.at[0], recv_sem=halo_recv.at[0],
-            device_id=dev(1), device_id_type=mesh_ids),
-        pltpu.make_async_remote_copy(
-            src_ref=r1_ref.at[:, :, pl.ds(0, w2)], dst_ref=r2_ref,
-            send_sem=halo_send.at[1], recv_sem=halo_recv.at[1],
-            device_id=dev(-1), device_id_type=mesh_ids),
-    )
-    for copy in relays:
-        copy.start()
-    for copy in relays:
-        copy.wait()
+    def relays(r, whole=False):
+        rs = slice(None) if whole else pl.ds(r, 1)
+        return (
+            pltpu.make_async_remote_copy(
+                src_ref=l1_ref.at[:, rs, pl.ds(w1 - w2, w2)], dst_ref=l2_ref.at[:, rs],
+                send_sem=halo_send.at[0], recv_sem=halo_recv_l.at[r],
+                device_id=dev(1), device_id_type=mesh_ids),
+            pltpu.make_async_remote_copy(
+                src_ref=r1_ref.at[:, rs, pl.ds(0, w2)], dst_ref=r2_ref.at[:, rs],
+                send_sem=halo_send.at[1], recv_sem=halo_recv_r.at[r],
+                device_id=dev(-1), device_id_type=mesh_ids),
+        )
+
+    for r in range(rows):
+        for copy in relays(r):
+            copy.start()
 
     def far_copy(r, to_left):
         if to_left:
@@ -147,6 +149,9 @@
         near_copy(r, False).start()
 
     def row_step(r, carry):
+        for copy in relays(r):
+            copy.wait_recv()
+
         def span(which, own_ref):
             return jnp.concatenate(
                 [l2_ref[which, r], l1_ref[which, r], own_ref[r], r1_ref[which, r],
@@ -173,6 +178,8 @@
 
     lax.fori_loop(0, rows, row_step, 0)
     send_near(rows - 1)
+    for copy in relays(0, whole=True):
+        copy.wait_send()
     for src, dst, slot in ((s_fl, x_fr, 0), (s_fr, x_fl, 1)):
         pltpu.make_async_remote_copy(
             src_ref=src, dst_ref=dst, send_sem=far_send.at[slot], recv_sem=far_recv_r.at[0],
@@ -211,7 +218,8 @@
             pltpu.VMEM((2, rows, cc, width), bf),
             pltpu.VMEM((2, rows, cc, width), bf),
             pltpu.SemaphoreType.DMA((2,)),
-            pltpu.SemaphoreType.DMA((2,)),
+            pltpu.SemaphoreType.DMA((rows,)),
+            pltpu.SemaphoreType.DMA((rows,)),
             pltpu.SemaphoreType.DMA((2,)),
             pltpu.SemaphoreType.DMA((rows,)),
             pltpu.SemaphoreType.DMA((rows,)),

time: 118 us -> 115 us (0.975)
  Pallas kernels: 65.9 us -> 63.3 us
    pallas_call x1, Pallas kernels: 60 us -> 57.4 us  [fused_row(): pl.pallas_call(functools.partial(fused_row_kernel, w2), in_specs=[vmem] *...]
  transfers between devices with their start and end apart: 4 -> 4, of which waited for: 1 -> 1; matrix products, arithmetic and copies ran while one was open for 2% -> 2% of each run, Pallas kernels for 57% -> 56%
where the time goes in v12:
time: 115 us; the launch traced here: 113 us
  Pallas kernels  63.3 us (55%)
  waiting for transfers between devices  20.2 us (18%)
  starting transfers between devices  13.8 us (12%)
  other arithmetic  8.33 us (7%)
  local copies, waits for them, and re-layouts  6.88 us (6%)
    pallas_call x1, Pallas kernels, fused_row(): pl.pallas_call(functools.partial(fused_row_kernel, w2), in_specs=[vmem] *...  57.4 us
    all_to_all x1, waiting for transfers between devices, body(): lax.all_to_all(stacked, 'rrow', split_axis=0, concat_axis=0, tiled=True)  20.2 us
    unnamed x22, local copies, waits for them, and re-layouts  6.47 us
    pallas_call x1, Pallas kernels, column_attention(): pl.pallas_call(column_kernel, in_specs=[vmem], out_specs=vmem, out_shape=...  5.86 us
    ppermute x2, starting transfers between devices, shifted(): return lax.ppermute(block, axis, route)  5.83 us
    all_to_all x1, starting transfers between devices, body(): lax.all_to_all(stacked, 'rrow', split_axis=0, concat_axis=0, tiled=True)  4.3 us
    convert_element_type x3, other arithmetic, body(): (row + col).astype(jnp.bfloat16)  4.22 us
    all_to_all x1, starting transfers between devices, body(): lax.all_to_all(col_out, 'rrow', split_axis=0, concat_axis=0, tiled=True)  3.71 us
  transfers between devices with their start and end apart: 4, of which 1 were waited for; matrix products, arithmetic and copies ran while one was open for 2% of the time, Pallas kernels for 56%

profile of v12, /device:TPU:48, one launch (start us, length us, event | category | flops | bytes accessed | tf_op | source)
XLA Modules:
  0.0 113.4 jit_solution(14827273848323332336)
XLA Ops:
  0.7 1.4 %copy.16 = bf16[8,32,1024]{2,0,1:T(8,128)(2,1)S(1)} copy(bf16[8,32,1024]{2,1,0:T(8,128)(2,1)} %q_ref.1) | data formatting | bytes 1048576 | tf_op args[0]
  2.1 1.3 %copy.19 = bf16[8,32,1024]{2,0,1:T(8,128)(2,1)S(1)} copy(bf16[8,32,1024]{2,1,0:T(8,128)(2,1)} %g_ref.1) | data formatting | bytes 1048576 | tf_op args[3]
  3.4 0.3 copy.17
  3.7 0.3 copy.18
  4.0 1.6 %maximum_bitcast_fusion = bf16[8,4,4,8,1024]{4,3,2,1,0:T(8,128)(2,1)} fusion(bf16[1,8,8,4,1024]{4,1,3,0,2:T(8,128)(2,1)S(1)} %bitcast.19, bf16[1,8,8,4,1024]{4,1,3,0,2:T(8,128)(2,1)S(1)} %bitcast.21, bf16[1,8,8,4,1024]{4,1,3,0,2:T(8,128)(2,1)S(1)} %bitcast.20, bf16[1,8,8,4,1024]{4,1,3,0,2:T(8,128)(2,1)S(1)} %bitcast.18), kind=kLoop, calls=%fused_computation.1 | loop fusion | flops 3145728 | bytes 4194304 | tf_op jit(solution)/shard_map/transpose | solution.py:309
  5.6 4.3 %all-to-all-start = ((bf16[8,4,4,8,1024]{4,3,2,1,0:T(8,128)(2,1)}), bf16[8,4,4,8,1024]{4,3,2,1,0:T(8,128)(2,1)S(1)}, u32[]{:S(2)}, u32[]{:S(2)}) async-start(bf16[8,4,4,8,1024]{4,3,2,1,0:T(8,128)(2,1)} %maximum_bitcast_fusion), calls=%async_computation | async-start | bytes 4194304 | tf_op jit(solution)/shard_map/all_to_all | solution.py:311
  9.9 1.1 pad_maximum_fusion
  11.0 2.0 %collective-permute-start.1 = (bf16[2,8,32,1024]{3,2,1,0:T(8,128)(2,1)}, bf16[2,8,32,1024]{3,2,1,0:T(8,128)(2,1)S(1)}, u32[]{:S(2)}, u32[]{:S(2)}) collective-permute-start(bf16[2,8,32,1024]{3,2,1,0:T(8,128)(2,1)} %pad_maximum_fusion), channel_id=1, source_target_pairs={{1,0},{2,1},{3,2},{4,3},{5,4},{6,5},{7,6},{9,8},{10,9},{11,10},{12... | collective-permute-start | bytes 3145736 | tf_op jit(solution)/shard_map/ppermute | solution.py:22
  13.0 3.8 %collective-permute-start = (bf16[2,8,32,1024]{3,2,1,0:T(8,128)(2,1)}, bf16[2,8,32,1024]{3,2,1,0:T(8,128)(2,1)}, u32[]{:S(2)}, u32[]{:S(2)}) collective-permute-start(bf16[2,8,32,1024]{3,2,1,0:T(8,128)(2,1)} %pad_maximum_fusion), channel_id=1, source_target_pairs={{0,1},{1,2},{2,3},{3,4},{4,5},{5,6},{6,7},{8,9},{9,10},{10,11},{11... | collective-permute-start | bytes 3145736 | tf_op jit(solution)/shard_map/ppermute | solution.py:22
  16.9 20.2 %all-to-all-done.x_ref = bf16[8,4,4,8,1024]{4,3,2,1,0:T(8,128)(2,1)S(1)} async-done(((bf16[8,4,4,8,1024]{4,3,2,1,0:T(8,128)(2,1)}), bf16[8,4,4,8,1024]{4,3,2,1,0:T(8,128)(2,1)S(1)}, u32[]{:S(2)}, u32[]{:S(2)}) %all-to-all-start) | async-done | bytes 2097184 | tf_op jit(solution)/shard_map/all_to_all | solution.py:311
  37.1 1.3 %copy-done = bf16[8,4,4,8,1024]{4,3,2,1,0:T(8,128)(2,1)} copy-done((bf16[8,4,4,8,1024]{4,3,2,1,0:T(8,128)(2,1)}, bf16[8,4,4,8,1024]{4,3,2,1,0:T(8,128)(2,1)S(1)}, u32[]{:S(2)}) %copy-start) | copy-done | bytes 2097176
  38.5 5.9 %shard_map.86 = bf16[8,3,4,8,1024]{4,3,2,1,0:T(8,128)(2,1)} custom-call(bf16[8,4,4,8,1024]{4,3,2,1,0:T(8,128)(2,1)} %copy-done), custom_call_target="tpu_custom_call" | custom-call | tf_op jit(solution)/shard_map/pallas_call | solution.py:267
  44.3 3.7 %all-to-all-start.1 = ((bf16[8,3,4,8,1024]{4,3,2,1,0:T(8,128)(2,1)}), bf16[8,3,4,8,1024]{4,3,2,1,0:T(8,128)(2,1)S(1)}, u32[]{:S(2)}, u32[]{:S(2)}) async-start(bf16[8,3,4,8,1024]{4,3,2,1,0:T(8,128)(2,1)} %shard_map.86), calls=%async_computation.1 | async-start | bytes 3145728 | tf_op jit(solution)/shard_map/all_to_all | solution.py:321
  48.1 0.1 multiply_reduce_fusion
  48.2 0.1 broadcast_compare_fusion
  48.4 0.8 fusion.6.bias_ref
  49.1 1.0 copy-done.6
  50.1 57.4 %shard_map.85 = (f32[8,32,1024]{2,1,0:T(8,128)}, f32[8,32,1024]{2,1,0:T(8,128)}, f32[8,32,1024]{2,1,0:T(8,128)}) custom-call(bf16[8,32,1024]{2,1,0:T(8,128)(2,1)} %q_ref.1, bf16[8,32,1024]{2,1,0:T(8,128)(2,1)} %g_ref.1, bf16[8,32,1024]{2,1,0:T(8,128)(2,1)} %k_ref.1, bf16[8,32,1024]{2,1,0:T(8,128)(2,1)} %v_ref.1, ...), custom_call_target="tpu_custom_call" | custom-call | tf_op jit(solution)/shard_map/pallas_call | solution.py:201
  107.5 0.4 convert_bitcast_fusion
  107.9 0.4 fusion.8
  108.4 0.8 copy-done.5
  109.2 1.4 %fusion.2 = bf16[8,32,1024]{2,1,0:T(8,128)(2,1)} fusion(f32[8,32,1024]{2,1,0:T(8,128)S(1)} %copy-done.5, f32[8,32,1024]{2,0,1:T(8,128)S(1)} %bitcast.17), kind=kLoop, calls=%fused_computation.8 | loop fusion | flops 524288 | bytes 2621440 | tf_op jit(solution)/shard_map/convert_element_type | solution.py:325
  110.6 1.4 %fusion = bf16[8,32,1024]{2,1,0:T(8,128)(2,1)} fusion(f32[8,32,1024]{2,1,0:T(8,128)S(1)} %copy-done.4, f32[8,32,1024]{2,0,1:T(8,128)S(1)} %bitcast.16), kind=kLoop, calls=%fused_computation.4 | loop fusion | flops 524288 | bytes 2621440 | tf_op jit(solution)/shard_map/convert_element_type | solution.py:325
  112.0 1.4 %fusion.1 = bf16[8,32,1024]{2,1,0:T(8,128)(2,1)} fusion(f32[8,32,1024]{2,1,0:T(8,128)S(1)} %copy-done.3, f32[8,32,1024]{2,0,1:T(8,128)S(1)} %bitcast.15), kind=kLoop, calls=%fused_computation.6 | loop fusion | flops 524288 | bytes 2621440 | tf_op jit(solution)/shard_map/convert_element_type | solution.py:325
  (25 shorter events, 0.2 us)
Async XLA Ops:
  0.6 2.8 %copy-start.1 = (bf16[8,32,1024]{2,1,0:T(8,128)(2,1)S(1)}, bf16[8,32,1024]{2,1,0:T(8,128)(2,1)}, u32[]{:S(2)}) copy-start(bf16[8,32,1024]{2,1,0:T(8,128)(2,1)} %k_ref.1) | copy-start | bytes 1572868
  0.6 3.1 %copy-start.2 = (bf16[8,32,1024]{2,1,0:T(8,128)(2,1)S(1)}, bf16[8,32,1024]{2,1,0:T(8,128)(2,1)}, u32[]{:S(2)}) copy-start(bf16[8,32,1024]{2,1,0:T(8,128)(2,1)} %v_ref.1) | copy-start | bytes 1572868
  5.6 31.5 %all-to-all-start = ((bf16[8,4,4,8,1024]{4,3,2,1,0:T(8,128)(2,1)}), bf16[8,4,4,8,1024]{4,3,2,1,0:T(8,128)(2,1)S(1)}, u32[]{:S(2)}, u32[]{:S(2)}) async-start(bf16[8,4,4,8,1024]{4,3,2,1,0:T(8,128)(2,1)} %maximum_bitcast_fusion), calls=%async_computation | async-start | bytes 4194304 | tf_op jit(solution)/shard_map/all_to_all | solution.py:311
  11.0 38.1 %collective-permute-start.1 = (bf16[2,8,32,1024]{3,2,1,0:T(8,128)(2,1)}, bf16[2,8,32,1024]{3,2,1,0:T(8,128)(2,1)S(1)}, u32[]{:S(2)}, u32[]{:S(2)}) collective-permute-start(bf16[2,8,32,1024]{3,2,1,0:T(8,128)(2,1)} %pad_maximum_fusion), channel_id=1, source_target_pairs={{1,0},{2,1},{3,2},{4,3},{5,4},{6,5},{7,6},{9,8},{10,9},{11,10},{12... | collective-permute-start | bytes 3145736 | tf_op jit(solution)/shard_map/ppermute | solution.py:22
  13.0 36.1 %collective-permute-start = (bf16[2,8,32,1024]{3,2,1,0:T(8,128)(2,1)}, bf16[2,8,32,1024]{3,2,1,0:T(8,128)(2,1)}, u32[]{:S(2)}, u32[]{:S(2)}) collective-permute-start(bf16[2,8,32,1024]{3,2,1,0:T(8,128)(2,1)} %pad_maximum_fusion), channel_id=1, source_target_pairs={{0,1},{1,2},{2,3},{3,4},{4,5},{5,6},{6,7},{8,9},{9,10},{10,11},{11... | collective-permute-start | bytes 3145736 | tf_op jit(solution)/shard_map/ppermute | solution.py:22
  37.1 1.3 %copy-start = (bf16[8,4,4,8,1024]{4,3,2,1,0:T(8,128)(2,1)}, bf16[8,4,4,8,1024]{4,3,2,1,0:T(8,128)(2,1)S(1)}, u32[]{:S(2)}) copy-start(bf16[8,4,4,8,1024]{4,3,2,1,0:T(8,128)(2,1)S(1)} %all-to-all-done.x_ref) | copy-start | bytes 6291460
  44.3 3.8 %copy-start.7 = (s32[8,16]{1,0:T(8,128)S(1)}, s32[8,16]{1,0:T(8,128)}, u32[]{:S(2)}) copy-start(s32[8,16]{1,0:T(8,128)} %param.10) | copy-start | bytes 1540
  44.3 4.0 %copy-start.8 = (s32[8]{0:T(128)S(1)}, s32[8]{0:T(128)}, u32[]{:S(2)}) copy-start(s32[8]{0:T(128)} %param.11) | copy-start | bytes 100
  44.3 63.2 %all-to-all-start.1 = ((bf16[8,3,4,8,1024]{4,3,2,1,0:T(8,128)(2,1)}), bf16[8,3,4,8,1024]{4,3,2,1,0:T(8,128)(2,1)S(1)}, u32[]{:S(2)}, u32[]{:S(2)}) async-start(bf16[8,3,4,8,1024]{4,3,2,1,0:T(8,128)(2,1)} %shard_map.86), calls=%async_computation.1 | async-start | bytes 3145728 | tf_op jit(solution)/shard_map/all_to_all | solution.py:321
  49.1 1.0 copy-start.6
  107.9 1.2 %copy-start.5 = (f32[8,32,1024]{2,1,0:T(8,128)S(1)}, f32[8,32,1024]{2,1,0:T(8,128)}, u32[]{:S(2)}) copy-start(f32[8,32,1024]{2,1,0:T(8,128)} %get-tuple-element.6) | copy-start | bytes 3145732
  108.4 2.2 %copy-start.4 = (f32[8,32,1024]{2,1,0:T(8,128)S(1)}, f32[8,32,1024]{2,1,0:T(8,128)}, u32[]{:S(2)}) copy-start(f32[8,32,1024]{2,1,0:T(8,128)} %get-tuple-element.8) | copy-start | bytes 3145732
  109.2 2.8 %copy-start.3 = (f32[8,32,1024]{2,1,0:T(8,128)S(1)}, f32[8,32,1024]{2,1,0:T(8,128)}, u32[]{:S(2)}) copy-start(f32[8,32,1024]{2,1,0:T(8,128)} %get-tuple-element.7) | copy-start | bytes 3145732

commit v13 on v12

--- a/solution.py
+++ b/solution.py
@@ -41,7 +41,7 @@
 def block_grads(q, g, k, v, bias):
     nq, width = q.shape
     heads = width // HD
-    group = min(width, 2 * LANES)
+    group = min(width, LANES)
     per_group = group // HD
     lanes = [slice(t * group, (t + 1) * group) for t in range(width // group)]
     qm = [head_stack(q[:, part], per_group) for part in lanes]

time: 115 us -> 115 us (level)
  no operation moved by 1% of the time
where the time goes in v13:
time: 115 us; the launch traced here: 113 us
  Pallas kernels  63.3 us (55%)
  waiting for transfers between devices  20.2 us (18%)
  starting transfers between devices  13.8 us (12%)
  other arithmetic  8.33 us (7%)
  local copies, waits for them, and re-layouts  6.88 us (6%)
    pallas_call x1, Pallas kernels, fused_row(): pl.pallas_call(functools.partial(fused_row_kernel, w2), in_specs=[vmem] *...  57.4 us
    all_to_all x1, waiting for transfers between devices, body(): lax.all_to_all(stacked, 'rrow', split_axis=0, concat_axis=0, tiled=True)  20.2 us
    unnamed x22, local copies, waits for them, and re-layouts  6.47 us
    pallas_call x1, Pallas kernels, column_attention(): pl.pallas_call(column_kernel, in_specs=[vmem], out_specs=vmem, out_shape=...  5.84 us
    ppermute x2, starting transfers between devices, shifted(): return lax.ppermute(block, axis, route)  5.83 us
    all_to_all x1, starting transfers between devices, body(): lax.all_to_all(stacked, 'rrow', split_axis=0, concat_axis=0, tiled=True)  4.3 us
    convert_element_type x3, other arithmetic, body(): (row + col).astype(jnp.bfloat16)  4.22 us
    all_to_all x1, starting transfers between devices, body(): lax.all_to_all(col_out, 'rrow', split_axis=0, concat_axis=0, tiled=True)  3.71 us
  transfers between devices with their start and end apart: 4, of which 1 were waited for; matrix products, arithmetic and copies ran while one was open for 2% of the time, Pallas kernels for 56%

profile of v13, /device:TPU:48, one launch (start us, length us, event | category | flops | bytes accessed | tf_op | source)
XLA Modules:
  0.0 113.4 jit_solution(1391132003759057187)
XLA Ops:
  0.7 1.4 %copy.16 = bf16[8,32,1024]{2,0,1:T(8,128)(2,1)S(1)} copy(bf16[8,32,1024]{2,1,0:T(8,128)(2,1)} %q_ref.1) | data formatting | bytes 1048576 | tf_op args[0]
  2.1 1.3 %copy.19 = bf16[8,32,1024]{2,0,1:T(8,128)(2,1)S(1)} copy(bf16[8,32,1024]{2,1,0:T(8,128)(2,1)} %g_ref.1) | data formatting | bytes 1048576 | tf_op args[3]
  3.4 0.3 copy.17
  3.7 0.3 copy.18
  4.0 1.6 %maximum_bitcast_fusion = bf16[8,4,4,8,1024]{4,3,2,1,0:T(8,128)(2,1)} fusion(bf16[1,8,8,4,1024]{4,1,3,0,2:T(8,128)(2,1)S(1)} %bitcast.19, bf16[1,8,8,4,1024]{4,1,3,0,2:T(8,128)(2,1)S(1)} %bitcast.21, bf16[1,8,8,4,1024]{4,1,3,0,2:T(8,128)(2,1)S(1)} %bitcast.20, bf16[1,8,8,4,1024]{4,1,3,0,2:T(8,128)(2,1)S(1)} %bitcast.18), kind=kLoop, calls=%fused_computation.1 | loop fusion | flops 3145728 | bytes 4194304 | tf_op jit(solution)/shard_map/transpose | solution.py:309
  5.6 4.3 %all-to-all-start = ((bf16[8,4,4,8,1024]{4,3,2,1,0:T(8,128)(2,1)}), bf16[8,4,4,8,1024]{4,3,2,1,0:T(8,128)(2,1)S(1)}, u32[]{:S(2)}, u32[]{:S(2)}) async-start(bf16[8,4,4,8,1024]{4,3,2,1,0:T(8,128)(2,1)} %maximum_bitcast_fusion), calls=%async_computation | async-start | bytes 4194304 | tf_op jit(solution)/shard_map/all_to_all | solution.py:311
  9.9 1.1 pad_maximum_fusion
  11.0 2.0 %collective-permute-start.1 = (bf16[2,8,32,1024]{3,2,1,0:T(8,128)(2,1)}, bf16[2,8,32,1024]{3,2,1,0:T(8,128)(2,1)S(1)}, u32[]{:S(2)}, u32[]{:S(2)}) collective-permute-start(bf16[2,8,32,1024]{3,2,1,0:T(8,128)(2,1)} %pad_maximum_fusion), channel_id=1, source_target_pairs={{1,0},{2,1},{3,2},{4,3},{5,4},{6,5},{7,6},{9,8},{10,9},{11,10},{12... | collective-permute-start | bytes 3145736 | tf_op jit(solution)/shard_map/ppermute | solution.py:22
  13.0 3.8 %collective-permute-start = (bf16[2,8,32,1024]{3,2,1,0:T(8,128)(2,1)}, bf16[2,8,32,1024]{3,2,1,0:T(8,128)(2,1)}, u32[]{:S(2)}, u32[]{:S(2)}) collective-permute-start(bf16[2,8,32,1024]{3,2,1,0:T(8,128)(2,1)} %pad_maximum_fusion), channel_id=1, source_target_pairs={{0,1},{1,2},{2,3},{3,4},{4,5},{5,6},{6,7},{8,9},{9,10},{10,11},{11... | collective-permute-start | bytes 3145736 | tf_op jit(solution)/shard_map/ppermute | solution.py:22
  16.9 20.2 %all-to-all-done.x_ref = bf16[8,4,4,8,1024]{4,3,2,1,0:T(8,128)(2,1)S(1)} async-done(((bf16[8,4,4,8,1024]{4,3,2,1,0:T(8,128)(2,1)}), bf16[8,4,4,8,1024]{4,3,2,1,0:T(8,128)(2,1)S(1)}, u32[]{:S(2)}, u32[]{:S(2)}) %all-to-all-start) | async-done | bytes 2097184 | tf_op jit(solution)/shard_map/all_to_all | solution.py:311
  37.1 1.3 %copy-done = bf16[8,4,4,8,1024]{4,3,2,1,0:T(8,128)(2,1)} copy-done((bf16[8,4,4,8,1024]{4,3,2,1,0:T(8,128)(2,1)}, bf16[8,4,4,8,1024]{4,3,2,1,0:T(8,128)(2,1)S(1)}, u32[]{:S(2)}) %copy-start) | copy-done | bytes 2097176
  38.5 5.8 %shard_map.86 = bf16[8,3,4,8,1024]{4,3,2,1,0:T(8,128)(2,1)} custom-call(bf16[8,4,4,8,1024]{4,3,2,1,0:T(8,128)(2,1)} %copy-done), custom_call_target="tpu_custom_call" | custom-call | tf_op jit(solution)/shard_map/pallas_call | solution.py:267
  44.3 3.7 %all-to-all-start.1 = ((bf16[8,3,4,8,1024]{4,3,2,1,0:T(8,128)(2,1)}), bf16[8,3,4,8,1024]{4,3,2,1,0:T(8,128)(2,1)S(1)}, u32[]{:S(2)}, u32[]{:S(2)}) async-start(bf16[8,3,4,8,1024]{4,3,2,1,0:T(8,128)(2,1)} %shard_map.86), calls=%async_computation.1 | async-start | bytes 3145728 | tf_op jit(solution)/shard_map/all_to_all | solution.py:321
  48.1 0.1 multiply_reduce_fusion
  48.2 0.1 broadcast_compare_fusion
  48.3 0.8 fusion.6.bias_ref
  49.1 1.0 copy-done.6
  50.1 57.4 %shard_map.85 = (f32[8,32,1024]{2,1,0:T(8,128)}, f32[8,32,1024]{2,1,0:T(8,128)}, f32[8,32,1024]{2,1,0:T(8,128)}) custom-call(bf16[8,32,1024]{2,1,0:T(8,128)(2,1)} %q_ref.1, bf16[8,32,1024]{2,1,0:T(8,128)(2,1)} %g_ref.1, bf16[8,32,1024]{2,1,0:T(8,128)(2,1)} %k_ref.1, bf16[8,32,1024]{2,1,0:T(8,128)(2,1)} %v_ref.1, ...), custom_call_target="tpu_custom_call" | custom-call | tf_op jit(solution)/shard_map/pallas_call | solution.py:201
  107.5 0.4 convert_bitcast_fusion
  107.9 0.4 fusion.8
  108.3 0.8 copy-done.5
  109.1 1.4 %fusion.2 = bf16[8,32,1024]{2,1,0:T(8,128)(2,1)} fusion(f32[8,32,1024]{2,1,0:T(8,128)S(1)} %copy-done.5, f32[8,32,1024]{2,0,1:T(8,128)S(1)} %bitcast.17), kind=kLoop, calls=%fused_computation.8 | loop fusion | flops 524288 | bytes 2621440 | tf_op jit(solution)/shard_map/convert_element_type | solution.py:325
  110.5 1.4 %fusion = bf16[8,32,1024]{2,1,0:T(8,128)(2,1)} fusion(f32[8,32,1024]{2,1,0:T(8,128)S(1)} %copy-done.4, f32[8,32,1024]{2,0,1:T(8,128)S(1)} %bitcast.16), kind=kLoop, calls=%fused_computation.4 | loop fusion | flops 524288 | bytes 2621440 | tf_op jit(solution)/shard_map/convert_element_type | solution.py:325
  112.0 1.4 %fusion.1 = bf16[8,32,1024]{2,1,0:T(8,128)(2,1)} fusion(f32[8,32,1024]{2,1,0:T(8,128)S(1)} %copy-done.3, f32[8,32,1024]{2,0,1:T(8,128)S(1)} %bitcast.15), kind=kLoop, calls=%fused_computation.6 | loop fusion | flops 524288 | bytes 2621440 | tf_op jit(solution)/shard_map/convert_element_type | solution.py:325
  (25 shorter events, 0.2 us)
Async XLA Ops:
  0.6 2.8 %copy-start.1 = (bf16[8,32,1024]{2,1,0:T(8,128)(2,1)S(1)}, bf16[8,32,1024]{2,1,0:T(8,128)(2,1)}, u32[]{:S(2)}) copy-start(bf16[8,32,1024]{2,1,0:T(8,128)(2,1)} %k_ref.1) | copy-start | bytes 1572868
  0.6 3.1 %copy-start.2 = (bf16[8,32,1024]{2,1,0:T(8,128)(2,1)S(1)}, bf16[8,32,1024]{2,1,0:T(8,128)(2,1)}, u32[]{:S(2)}) copy-start(bf16[8,32,1024]{2,1,0:T(8,128)(2,1)} %v_ref.1) | copy-start | bytes 1572868
  5.6 31.5 %all-to-all-start = ((bf16[8,4,4,8,1024]{4,3,2,1,0:T(8,128)(2,1)}), bf16[8,4,4,8,1024]{4,3,2,1,0:T(8,128)(2,1)S(1)}, u32[]{:S(2)}, u32[]{:S(2)}) async-start(bf16[8,4,4,8,1024]{4,3,2,1,0:T(8,128)(2,1)} %maximum_bitcast_fusion), calls=%async_computation | async-start | bytes 4194304 | tf_op jit(solution)/shard_map/all_to_all | solution.py:311
  11.0 38.1 %collective-permute-start.1 = (bf16[2,8,32,1024]{3,2,1,0:T(8,128)(2,1)}, bf16[2,8,32,1024]{3,2,1,0:T(8,128)(2,1)S(1)}, u32[]{:S(2)}, u32[]{:S(2)}) collective-permute-start(bf16[2,8,32,1024]{3,2,1,0:T(8,128)(2,1)} %pad_maximum_fusion), channel_id=1, source_target_pairs={{1,0},{2,1},{3,2},{4,3},{5,4},{6,5},{7,6},{9,8},{10,9},{11,10},{12... | collective-permute-start | bytes 3145736 | tf_op jit(solution)/shard_map/ppermute | solution.py:22
  13.0 36.1 %collective-permute-start = (bf16[2,8,32,1024]{3,2,1,0:T(8,128)(2,1)}, bf16[2,8,32,1024]{3,2,1,0:T(8,128)(2,1)}, u32[]{:S(2)}, u32[]{:S(2)}) collective-permute-start(bf16[2,8,32,1024]{3,2,1,0:T(8,128)(2,1)} %pad_maximum_fusion), channel_id=1, source_target_pairs={{0,1},{1,2},{2,3},{3,4},{4,5},{5,6},{6,7},{8,9},{9,10},{10,11},{11... | collective-permute-start | bytes 3145736 | tf_op jit(solution)/shard_map/ppermute | solution.py:22
  37.1 1.3 %copy-start = (bf16[8,4,4,8,1024]{4,3,2,1,0:T(8,128)(2,1)}, bf16[8,4,4,8,1024]{4,3,2,1,0:T(8,128)(2,1)S(1)}, u32[]{:S(2)}) copy-start(bf16[8,4,4,8,1024]{4,3,2,1,0:T(8,128)(2,1)S(1)} %all-to-all-done.x_ref) | copy-start | bytes 6291460
  44.3 3.8 %copy-start.7 = (s32[8,16]{1,0:T(8,128)S(1)}, s32[8,16]{1,0:T(8,128)}, u32[]{:S(2)}) copy-start(s32[8,16]{1,0:T(8,128)} %param.10) | copy-start | bytes 1540
  44.3 4.0 %copy-start.8 = (s32[8]{0:T(128)S(1)}, s32[8]{0:T(128)}, u32[]{:S(2)}) copy-start(s32[8]{0:T(128)} %param.11) | copy-start | bytes 100
  44.3 63.2 %all-to-all-start.1 = ((bf16[8,3,4,8,1024]{4,3,2,1,0:T(8,128)(2,1)}), bf16[8,3,4,8,1024]{4,3,2,1,0:T(8,128)(2,1)S(1)}, u32[]{:S(2)}, u32[]{:S(2)}) async-start(bf16[8,3,4,8,1024]{4,3,2,1,0:T(8,128)(2,1)} %shard_map.86), calls=%async_computation.1 | async-start | bytes 3145728 | tf_op jit(solution)/shard_map/all_to_all | solution.py:321
  49.1 1.0 copy-start.6
  107.9 1.2 %copy-start.5 = (f32[8,32,1024]{2,1,0:T(8,128)S(1)}, f32[8,32,1024]{2,1,0:T(8,128)}, u32[]{:S(2)}) copy-start(f32[8,32,1024]{2,1,0:T(8,128)} %get-tuple-element.6) | copy-start | bytes 3145732
  108.3 2.2 %copy-start.4 = (f32[8,32,1024]{2,1,0:T(8,128)S(1)}, f32[8,32,1024]{2,1,0:T(8,128)}, u32[]{:S(2)}) copy-start(f32[8,32,1024]{2,1,0:T(8,128)} %get-tuple-element.8) | copy-start | bytes 3145732
  109.1 2.8 %copy-start.3 = (f32[8,32,1024]{2,1,0:T(8,128)S(1)}, f32[8,32,1024]{2,1,0:T(8,128)}, u32[]{:S(2)}) copy-start(f32[8,32,1024]{2,1,0:T(8,128)} %get-tuple-element.7) | copy-start | bytes 3145732

commit v14 on v12

--- a/solution.py
+++ b/solution.py
@@ -78,7 +78,7 @@
 
 
 def fused_row_kernel(w2, q_ref, g_ref, k_ref, v_ref, l1_ref, r1_ref, bias_ref,
-                     qg_ref, kg_ref, vg_ref,
+                     out_ref,
                      l2_ref, r2_ref, own_s, near_l, near_r, s_fl, s_fr, s_nl, s_nr, x_fr, x_fl,
                      x_nr, x_nl, halo_send, halo_recv_l, halo_recv_r, far_send, far_recv_r, far_recv_l,
                      near_send, near_recv):
@@ -160,7 +160,7 @@
             )
 
         dq, dk, dv = block_grads(q_ref[r], g_ref[r], span(0, k_ref), span(1, v_ref), bias_ref[r])
-        qg_ref[r] = dq
+        out_ref[0, r] = dq
         for which, full in ((0, dk), (1, dv)):
             s_fl[which, r] = full[:w2].astype(jnp.bfloat16)
             near_l[which, r] = full[w2:w2 + w1]
@@ -187,22 +187,22 @@
     for to_left in (True, False):
         near_copy(0, to_left, whole=True).wait()
     f32 = jnp.float32
-    for which, out_ref in ((0, kg_ref), (1, vg_ref)):
-        out_ref[...] = own_s[which] + x_nr[which].astype(f32) + x_nl[which].astype(f32)
+    for which in (0, 1):
+        out_ref[which + 1] = own_s[which] + x_nr[which].astype(f32) + x_nl[which].astype(f32)
 
 
 def fused_row(queries, out_grad, key_grid, value_grid, l1, r1, bias, w2):
     rows, cc, width = queries.shape
     w1 = l1.shape[2]
     vmem = pl.BlockSpec(memory_space=pltpu.VMEM)
-    grads = jax.ShapeDtypeStruct((rows, cc, width), jnp.float32)
+    grads = jax.ShapeDtypeStruct((3, rows, cc, width), jnp.float32)
     bf = jnp.bfloat16
     f32 = jnp.float32
     return pl.pallas_call(
         functools.partial(fused_row_kernel, w2),
         in_specs=[vmem] * 7,
-        out_specs=[vmem] * 3,
-        out_shape=(grads, grads, grads),
+        out_specs=vmem,
+        out_shape=grads,
         scratch_shapes=[
             pltpu.VMEM((2, rows, w2, width), bf),
             pltpu.VMEM((2, rows, w2, width), bf),
@@ -322,7 +322,8 @@
     row_grads = fused_row(queries, out_grad, key_grid, value_grid, l1, r1, bias, far)
     back = back.transpose(1, 3, 0, 2, 4).reshape(3, row_count, col_count, feature_width)
     back = back.astype(jnp.float32)
-    return tuple((row + col).astype(jnp.bfloat16) for row, col in zip(row_grads, back))
+    total = (row_grads + back).astype(jnp.bfloat16)
+    return (total[0], total[1], total[2])
 
 
 def solution(mesh):

time: 115 us -> 115 us (level)
  other arithmetic: 8.33 us -> 6.34 us
  local copies, waits for them, and re-layouts: 6.88 us -> 8.72 us
    convert_element_type x3 -> x1, other arithmetic: 4.22 us -> 2.26 us  [body(): total = (row_grads + back).astype(jnp.bfloat16)]
    squeeze x0 -> x1, local copies, waits for them, and re-layouts: none -> 1.17 us  [body(): return (total[0], total[1], total[2])]
    unnamed x22 -> x18, local copies, waits for them, and re-layouts: 6.47 us -> 7.33 us
where the time goes in v14:
time: 115 us; the launch traced here: 113 us
  Pallas kernels  63.5 us (55%)
  waiting for transfers between devices  20.3 us (18%)
  starting transfers between devices  13.8 us (12%)
  local copies, waits for them, and re-layouts  8.72 us (8%)
  other arithmetic  6.34 us (6%)
    pallas_call x1, Pallas kernels, fused_row(): pl.pallas_call(functools.partial(fused_row_kernel, w2), in_specs=[vmem] *...  57.6 us
    all_to_all x1, waiting for transfers between devices, body(): lax.all_to_all(stacked, 'rrow', split_axis=0, concat_axis=0, tiled=True)  20.3 us
    unnamed x18, local copies, waits for them, and re-layouts  7.33 us
    pallas_call x1, Pallas kernels, column_attention(): pl.pallas_call(column_kernel, in_specs=[vmem], out_specs=vmem, out_shape=...  5.86 us
    ppermute x2, starting transfers between devices, shifted(): return lax.ppermute(block, axis, route)  5.83 us
    all_to_all x1, starting transfers between devices, body(): lax.all_to_all(stacked, 'rrow', split_axis=0, concat_axis=0, tiled=True)  4.3 us
    all_to_all x1, starting transfers between devices, body(): lax.all_to_all(col_out, 'rrow', split_axis=0, concat_axis=0, tiled=True)  3.71 us
  transfers between devices with their start and end apart: 4, of which 1 were waited for; matrix products, arithmetic and copies ran while one was open for 2% of the time, Pallas kernels for 56%

profile of v14, /device:TPU:48, one launch (start us, length us, event | category | flops | bytes accessed | tf_op | source)
XLA Modules:
  0.0 113.5 jit_solution(3676484512821897056)
XLA Ops:
  0.7 1.4 %copy.19 = bf16[8,32,1024]{2,0,1:T(8,128)(2,1)S(1)} copy(bf16[8,32,1024]{2,1,0:T(8,128)(2,1)} %q_ref.1) | data formatting | bytes 1048576 | tf_op args[0]
  2.1 1.3 %copy.22 = bf16[8,32,1024]{2,0,1:T(8,128)(2,1)S(1)} copy(bf16[8,32,1024]{2,1,0:T(8,128)(2,1)} %g_ref.1) | data formatting | bytes 1048576 | tf_op args[3]
  3.4 0.3 copy.20
  3.7 0.3 copy.21
  4.0 1.6 %maximum_bitcast_fusion = bf16[8,4,4,8,1024]{4,3,2,1,0:T(8,128)(2,1)} fusion(bf16[1,8,8,4,1024]{4,1,3,0,2:T(8,128)(2,1)S(1)} %bitcast.21, bf16[1,8,8,4,1024]{4,1,3,0,2:T(8,128)(2,1)S(1)} %bitcast.23, bf16[1,8,8,4,1024]{4,1,3,0,2:T(8,128)(2,1)S(1)} %bitcast.22, bf16[1,8,8,4,1024]{4,1,3,0,2:T(8,128)(2,1)S(1)} %bitcast.20), kind=kLoop, calls=%fused_computation.3 | loop fusion | flops 3145728 | bytes 4194304 | tf_op jit(solution)/shard_map/transpose | solution.py:309
  5.6 4.3 %all-to-all-start = ((bf16[8,4,4,8,1024]{4,3,2,1,0:T(8,128)(2,1)}), bf16[8,4,4,8,1024]{4,3,2,1,0:T(8,128)(2,1)S(1)}, u32[]{:S(2)}, u32[]{:S(2)}) async-start(bf16[8,4,4,8,1024]{4,3,2,1,0:T(8,128)(2,1)} %maximum_bitcast_fusion), calls=%async_computation | async-start | bytes 4194304 | tf_op jit(solution)/shard_map/all_to_all | solution.py:311
  9.9 1.1 pad_maximum_fusion
  11.0 2.0 %collective-permute-start.1 = (bf16[2,8,32,1024]{3,2,1,0:T(8,128)(2,1)}, bf16[2,8,32,1024]{3,2,1,0:T(8,128)(2,1)S(1)}, u32[]{:S(2)}, u32[]{:S(2)}) collective-permute-start(bf16[2,8,32,1024]{3,2,1,0:T(8,128)(2,1)} %pad_maximum_fusion), channel_id=1, source_target_pairs={{1,0},{2,1},{3,2},{4,3},{5,4},{6,5},{7,6},{9,8},{10,9},{11,10},{12... | collective-permute-start | bytes 3145736 | tf_op jit(solution)/shard_map/ppermute | solution.py:22
  13.0 3.8 %collective-permute-start = (bf16[2,8,32,1024]{3,2,1,0:T(8,128)(2,1)}, bf16[2,8,32,1024]{3,2,1,0:T(8,128)(2,1)}, u32[]{:S(2)}, u32[]{:S(2)}) collective-permute-start(bf16[2,8,32,1024]{3,2,1,0:T(8,128)(2,1)} %pad_maximum_fusion), channel_id=1, source_target_pairs={{0,1},{1,2},{2,3},{3,4},{4,5},{5,6},{6,7},{8,9},{9,10},{10,11},{11... | collective-permute-start | bytes 3145736 | tf_op jit(solution)/shard_map/ppermute | solution.py:22
  16.9 20.3 %all-to-all-done.x_ref = bf16[8,4,4,8,1024]{4,3,2,1,0:T(8,128)(2,1)S(1)} async-done(((bf16[8,4,4,8,1024]{4,3,2,1,0:T(8,128)(2,1)}), bf16[8,4,4,8,1024]{4,3,2,1,0:T(8,128)(2,1)S(1)}, u32[]{:S(2)}, u32[]{:S(2)}) %all-to-all-start) | async-done | bytes 2097184 | tf_op jit(solution)/shard_map/all_to_all | solution.py:311
  37.1 1.3 %copy-done.1 = bf16[8,4,4,8,1024]{4,3,2,1,0:T(8,128)(2,1)} copy-done((bf16[8,4,4,8,1024]{4,3,2,1,0:T(8,128)(2,1)}, bf16[8,4,4,8,1024]{4,3,2,1,0:T(8,128)(2,1)S(1)}, u32[]{:S(2)}) %copy-start.1) | copy-done | bytes 2097176
  38.5 5.9 %shard_map.86 = bf16[8,3,4,8,1024]{4,3,2,1,0:T(8,128)(2,1)} custom-call(bf16[8,4,4,8,1024]{4,3,2,1,0:T(8,128)(2,1)} %copy-done.1), custom_call_target="tpu_custom_call" | custom-call | tf_op jit(solution)/shard_map/pallas_call | solution.py:267
  44.3 3.7 %all-to-all-start.1 = ((bf16[8,3,4,8,1024]{4,3,2,1,0:T(8,128)(2,1)}), bf16[8,3,4,8,1024]{4,3,2,1,0:T(8,128)(2,1)S(1)}, u32[]{:S(2)}, u32[]{:S(2)}) async-start(bf16[8,3,4,8,1024]{4,3,2,1,0:T(8,128)(2,1)} %shard_map.86), calls=%async_computation.1 | async-start | bytes 3145728 | tf_op jit(solution)/shard_map/all_to_all | solution.py:321
  48.1 0.1 multiply_reduce_fusion
  48.2 0.1 broadcast_compare_fusion
  48.3 0.1 broadcast_subtract_fusion
  48.3 0.8 fusion.4.bias_ref
  49.1 1.0 copy-done.4
  50.1 57.6 %shard_map.85 = f32[3,8,32,1024]{3,2,1,0:T(8,128)} custom-call(bf16[8,32,1024]{2,1,0:T(8,128)(2,1)} %q_ref.1, bf16[8,32,1024]{2,1,0:T(8,128)(2,1)} %g_ref.1, bf16[8,32,1024]{2,1,0:T(8,128)(2,1)} %k_ref.1, bf16[8,32,1024]{2,1,0:T(8,128)(2,1)} %v_ref.1, bf16[2,8,32,1024]{3,2,1,0:T(8,128)(2,1)} %collective-permute-done.l1_ref, ...), custom_call_target="tpu_custom_call" | custom-call | tf_op jit(solution)/shard_map/pallas_call | solution.py:201
  107.8 0.4 convert_bitcast_fusion
  108.2 0.2 copy.23
  108.4 1.7 %copy-done = f32[3,8,32,1024]{3,2,1,0:T(8,128)S(1)} copy-done((f32[3,8,32,1024]{3,2,1,0:T(8,128)S(1)}, f32[3,8,32,1024]{3,2,1,0:T(8,128)}, u32[]{:S(2)}) %copy-start) | copy-done | bytes 3145752
  110.1 2.3 %fusion = bf16[3,8,32,1024]{3,2,1,0:T(8,128)(2,1)S(1)} fusion(f32[3,8,32,1024]{3,2,1,0:T(8,128)S(1)} %copy-done, f32[3,8,32,1024]{3,1,2,0:T(8,128)S(1)} %bitcast.17), kind=kLoop, calls=%fused_computation.1 | loop fusion | flops 1572864 | bytes 7864320 | tf_op jit(solution)/shard_map/convert_element_type | solution.py:325
  112.3 1.2 %slice_bitcast_fusion = (bf16[8,32,1024]{2,1,0:T(8,128)(2,1)}, bf16[8,32,1024]{2,1,0:T(8,128)(2,1)}, bf16[8,32,1024]{2,1,0:T(8,128)(2,1)}) fusion(bf16[3,8,32,1024]{3,2,1,0:T(8,128)(2,1)S(1)} %fusion), kind=kLoop, calls=%fused_computation.5 | loop fusion | bytes 3145728 | tf_op jit(solution)/shard_map/squeeze | solution.py:326
  (20 shorter events, 0.1 us)
Async XLA Ops:
  0.6 2.8 %copy-start.2 = (bf16[8,32,1024]{2,1,0:T(8,128)(2,1)S(1)}, bf16[8,32,1024]{2,1,0:T(8,128)(2,1)}, u32[]{:S(2)}) copy-start(bf16[8,32,1024]{2,1,0:T(8,128)(2,1)} %k_ref.1) | copy-start | bytes 1572868
  0.6 3.1 %copy-start.3 = (bf16[8,32,1024]{2,1,0:T(8,128)(2,1)S(1)}, bf16[8,32,1024]{2,1,0:T(8,128)(2,1)}, u32[]{:S(2)}) copy-start(bf16[8,32,1024]{2,1,0:T(8,128)(2,1)} %v_ref.1) | copy-start | bytes 1572868
  5.6 31.5 %all-to-all-start = ((bf16[8,4,4,8,1024]{4,3,2,1,0:T(8,128)(2,1)}), bf16[8,4,4,8,1024]{4,3,2,1,0:T(8,128)(2,1)S(1)}, u32[]{:S(2)}, u32[]{:S(2)}) async-start(bf16[8,4,4,8,1024]{4,3,2,1,0:T(8,128)(2,1)} %maximum_bitcast_fusion), calls=%async_computation | async-start | bytes 4194304 | tf_op jit(solution)/shard_map/all_to_all | solution.py:311
  11.0 38.1 %collective-permute-start.1 = (bf16[2,8,32,1024]{3,2,1,0:T(8,128)(2,1)}, bf16[2,8,32,1024]{3,2,1,0:T(8,128)(2,1)S(1)}, u32[]{:S(2)}, u32[]{:S(2)}) collective-permute-start(bf16[2,8,32,1024]{3,2,1,0:T(8,128)(2,1)} %pad_maximum_fusion), channel_id=1, source_target_pairs={{1,0},{2,1},{3,2},{4,3},{5,4},{6,5},{7,6},{9,8},{10,9},{11,10},{12... | collective-permute-start | bytes 3145736 | tf_op jit(solution)/shard_map/ppermute | solution.py:22
  13.0 36.1 %collective-permute-start = (bf16[2,8,32,1024]{3,2,1,0:T(8,128)(2,1)}, bf16[2,8,32,1024]{3,2,1,0:T(8,128)(2,1)}, u32[]{:S(2)}, u32[]{:S(2)}) collective-permute-start(bf16[2,8,32,1024]{3,2,1,0:T(8,128)(2,1)} %pad_maximum_fusion), channel_id=1, source_target_pairs={{0,1},{1,2},{2,3},{3,4},{4,5},{5,6},{6,7},{8,9},{9,10},{10,11},{11... | collective-permute-start | bytes 3145736 | tf_op jit(solution)/shard_map/ppermute | solution.py:22
  37.1 1.3 %copy-start.1 = (bf16[8,4,4,8,1024]{4,3,2,1,0:T(8,128)(2,1)}, bf16[8,4,4,8,1024]{4,3,2,1,0:T(8,128)(2,1)S(1)}, u32[]{:S(2)}) copy-start(bf16[8,4,4,8,1024]{4,3,2,1,0:T(8,128)(2,1)S(1)} %all-to-all-done.x_ref) | copy-start | bytes 6291460
  44.3 3.8 %copy-start.5 = (s32[8,16]{1,0:T(8,128)S(1)}, s32[8,16]{1,0:T(8,128)}, u32[]{:S(2)}) copy-start(s32[8,16]{1,0:T(8,128)} %param.10) | copy-start | bytes 1540
  44.3 4.0 %copy-start.6 = (s32[8]{0:T(128)S(1)}, s32[8]{0:T(128)}, u32[]{:S(2)}) copy-start(s32[8]{0:T(128)} %param.11) | copy-start | bytes 100
  44.3 63.4 %all-to-all-start.1 = ((bf16[8,3,4,8,1024]{4,3,2,1,0:T(8,128)(2,1)}), bf16[8,3,4,8,1024]{4,3,2,1,0:T(8,128)(2,1)S(1)}, u32[]{:S(2)}, u32[]{:S(2)}) async-start(bf16[8,3,4,8,1024]{4,3,2,1,0:T(8,128)(2,1)} %shard_map.86), calls=%async_computation.1 | async-start | bytes 3145728 | tf_op jit(solution)/shard_map/all_to_all | solution.py:321
  49.1 1.0 copy-start.4
  108.2 1.9 %copy-start = (f32[3,8,32,1024]{3,2,1,0:T(8,128)S(1)}, f32[3,8,32,1024]{3,2,1,0:T(8,128)}, u32[]{:S(2)}) copy-start(f32[3,8,32,1024]{3,2,1,0:T(8,128)} %shard_map.85) | copy-start | bytes 9437188

commit v15 on v12

--- a/solution.py
+++ b/solution.py
@@ -272,6 +272,25 @@
     )(whole)
 
 
+def regroup_kernel(q_ref, k_ref, v_ref, g_ref, o_ref):
+    groups, arrays, strip, rows, width = o_ref.shape
+    for which, ref in enumerate((q_ref, k_ref, v_ref, g_ref)):
+        for group in range(groups):
+            for c in range(strip):
+                o_ref[group, which, c] = ref[:, group * strip + c, :]
+
+
+def regroup(queries, key_grid, value_grid, out_grad, groups):
+    rows, cols, width = queries.shape
+    vmem = pl.BlockSpec(memory_space=pltpu.VMEM)
+    return pl.pallas_call(
+        regroup_kernel,
+        in_specs=[vmem] * 4,
+        out_specs=vmem,
+        out_shape=jax.ShapeDtypeStruct((groups, 4, cols // groups, rows, width), queries.dtype),
+    )(queries, key_grid, value_grid, out_grad)
+
+
 def band_bias(mask_rows, offsets, first_col, grid_cols, block_cols):
     band_reach = HALF + OFFMAX
     query_cols = first_col + jnp.arange(block_cols, dtype=jnp.int32)
@@ -303,11 +322,7 @@
     far = band_reach - col_count
 
     strip = col_count // group_count
-    stacked = (
-        jnp.stack([queries, key_grid, value_grid, out_grad])
-        .reshape(4, row_count, group_count, strip, feature_width)
-        .transpose(2, 0, 3, 1, 4)
-    )
+    stacked = regroup(queries, key_grid, value_grid, out_grad, group_count)
     whole = lax.all_to_all(stacked, "rrow", split_axis=0, concat_axis=0, tiled=True)
 
     pair = jnp.stack([key_grid, value_grid])

time: 115 us -> 116 us (level)
  Pallas kernels: 63.3 us -> 69.1 us
  local copies, waits for them, and re-layouts: 6.88 us -> 3.53 us
  other arithmetic: 8.33 us -> 6.75 us
    pallas_call x0 -> x1, Pallas kernels: none -> 5.78 us  [regroup(): pl.pallas_call(regroup_kernel, in_specs=[vmem] * 4, out_specs=vmem, out_s...]
    unnamed x22 -> x18, local copies, waits for them, and re-layouts: 6.47 us -> 3.12 us
    transpose x1 -> x0, other arithmetic: 1.59 us -> none  [body(): stacked = jnp.stack([queries, key_grid, value_grid, out_grad]).reshape(4,...]
  transfers between devices with their start and end apart: 4 -> 4, of which waited for: 1 -> 1; matrix products, arithmetic and copies ran while one was open for 2% -> 2% of each run, Pallas kernels for 56% -> 55%
where the time goes in v15:
time: 116 us; the launch traced here: 114 us
  Pallas kernels  69.1 us (60%)
  waiting for transfers between devices  20.2 us (17%)
  starting transfers between devices  14 us (12%)
  other arithmetic  6.75 us (6%)
  local copies, waits for them, and re-layouts  3.53 us (3%)
    pallas_call x1, Pallas kernels, fused_row(): pl.pallas_call(functools.partial(fused_row_kernel, w2), in_specs=[vmem] *...  57.4 us
    all_to_all x1, waiting for transfers between devices, body(): lax.all_to_all(stacked, 'rrow', split_axis=0, concat_axis=0, tiled=True)  20.2 us
    pallas_call x1, Pallas kernels, column_attention(): pl.pallas_call(column_kernel, in_specs=[vmem], out_specs=vmem, out_shape=...  5.87 us
    ppermute x2, starting transfers between devices, shifted(): return lax.ppermute(block, axis, route)  5.83 us
    pallas_call x1, Pallas kernels, regroup(): pl.pallas_call(regroup_kernel, in_specs=[vmem] * 4, out_specs=vmem, out_s...  5.78 us
    all_to_all x1, starting transfers between devices, body(): lax.all_to_all(stacked, 'rrow', split_axis=0, concat_axis=0, tiled=True)  4.43 us
    convert_element_type x3, other arithmetic, body(): (row + col).astype(jnp.bfloat16)  4.22 us
    all_to_all x1, starting transfers between devices, body(): lax.all_to_all(col_out, 'rrow', split_axis=0, concat_axis=0, tiled=True)  3.71 us
  transfers between devices with their start and end apart: 4, of which 1 were waited for; matrix products, arithmetic and copies ran while one was open for 2% of the time, Pallas kernels for 55%

profile of v15, /device:TPU:48, one launch (start us, length us, event | category | flops | bytes accessed | tf_op | source)
XLA Modules:
  0.0 114.3 jit_solution(10433776458322731342)
XLA Ops:
  0.6 5.8 %shard_map.86 = bf16[8,4,4,8,1024]{4,3,2,1,0:T(8,128)(2,1)} custom-call(bf16[8,32,1024]{2,1,0:T(8,128)(2,1)} %q_ref.3, bf16[8,32,1024]{2,1,0:T(8,128)(2,1)} %k_ref.3, bf16[8,32,1024]{2,1,0:T(8,128)(2,1)} %v_ref.3, bf16[8,32,1024]{2,1,0:T(8,128)(2,1)} %g_ref.3), custom_call_target="tpu_custom_call" | custom-call | tf_op jit(solution)/shard_map/pallas_call | solution.py:286
  6.4 4.4 %all-to-all-start = ((bf16[8,4,4,8,1024]{4,3,2,1,0:T(8,128)(2,1)}), bf16[8,4,4,8,1024]{4,3,2,1,0:T(8,128)(2,1)S(1)}, u32[]{:S(2)}, u32[]{:S(2)}) async-start(bf16[8,4,4,8,1024]{4,3,2,1,0:T(8,128)(2,1)} %shard_map.86), calls=%async_computation | async-start | bytes 4194304 | tf_op jit(solution)/shard_map/all_to_all | solution.py:326
  10.9 1.1 pad_maximum_fusion
  11.9 2.0 %collective-permute-start.1 = (bf16[2,8,32,1024]{3,2,1,0:T(8,128)(2,1)}, bf16[2,8,32,1024]{3,2,1,0:T(8,128)(2,1)S(1)}, u32[]{:S(2)}, u32[]{:S(2)}) collective-permute-start(bf16[2,8,32,1024]{3,2,1,0:T(8,128)(2,1)} %pad_maximum_fusion), channel_id=1, source_target_pairs={{1,0},{2,1},{3,2},{4,3},{5,4},{6,5},{7,6},{9,8},{10,9},{11,10},{12... | collective-permute-start | bytes 3145736 | tf_op jit(solution)/shard_map/ppermute | solution.py:22
  14.0 3.8 %collective-permute-start = (bf16[2,8,32,1024]{3,2,1,0:T(8,128)(2,1)}, bf16[2,8,32,1024]{3,2,1,0:T(8,128)(2,1)}, u32[]{:S(2)}, u32[]{:S(2)}) collective-permute-start(bf16[2,8,32,1024]{3,2,1,0:T(8,128)(2,1)} %pad_maximum_fusion), channel_id=1, source_target_pairs={{0,1},{1,2},{2,3},{3,4},{4,5},{5,6},{6,7},{8,9},{9,10},{10,11},{11... | collective-permute-start | bytes 3145736 | tf_op jit(solution)/shard_map/ppermute | solution.py:22
  17.8 20.2 %all-to-all-done.x_ref = bf16[8,4,4,8,1024]{4,3,2,1,0:T(8,128)(2,1)S(1)} async-done(((bf16[8,4,4,8,1024]{4,3,2,1,0:T(8,128)(2,1)}), bf16[8,4,4,8,1024]{4,3,2,1,0:T(8,128)(2,1)S(1)}, u32[]{:S(2)}, u32[]{:S(2)}) %all-to-all-start) | async-done | bytes 2097184 | tf_op jit(solution)/shard_map/all_to_all | solution.py:326
  38.0 1.3 %copy-done = bf16[8,4,4,8,1024]{4,3,2,1,0:T(8,128)(2,1)} copy-done((bf16[8,4,4,8,1024]{4,3,2,1,0:T(8,128)(2,1)}, bf16[8,4,4,8,1024]{4,3,2,1,0:T(8,128)(2,1)S(1)}, u32[]{:S(2)}) %copy-start) | copy-done | bytes 2097176
  39.4 5.9 %shard_map.87 = bf16[8,3,4,8,1024]{4,3,2,1,0:T(8,128)(2,1)} custom-call(bf16[8,4,4,8,1024]{4,3,2,1,0:T(8,128)(2,1)} %copy-done), custom_call_target="tpu_custom_call" | custom-call | tf_op jit(solution)/shard_map/pallas_call | solution.py:267
  45.2 3.7 %all-to-all-start.1 = ((bf16[8,3,4,8,1024]{4,3,2,1,0:T(8,128)(2,1)}), bf16[8,3,4,8,1024]{4,3,2,1,0:T(8,128)(2,1)S(1)}, u32[]{:S(2)}, u32[]{:S(2)}) async-start(bf16[8,3,4,8,1024]{4,3,2,1,0:T(8,128)(2,1)} %shard_map.87), calls=%async_computation.1 | async-start | bytes 3145728 | tf_op jit(solution)/shard_map/all_to_all | solution.py:336
  49.0 0.1 multiply_reduce_fusion
  49.1 0.1 broadcast_compare_fusion
  49.2 0.1 broadcast_subtract_fusion
  49.3 0.8 fusion.6.bias_ref
  50.0 0.0 collective-permute-done.1.r1_ref
  50.0 0.0 collective-permute-done.l1_ref
  50.1 1.0 copy-done.6
  51.0 57.4 %shard_map.85 = (f32[8,32,1024]{2,1,0:T(8,128)}, f32[8,32,1024]{2,1,0:T(8,128)}, f32[8,32,1024]{2,1,0:T(8,128)}) custom-call(bf16[8,32,1024]{2,1,0:T(8,128)(2,1)} %q_ref.3, bf16[8,32,1024]{2,1,0:T(8,128)(2,1)} %g_ref.3, bf16[8,32,1024]{2,1,0:T(8,128)(2,1)} %k_ref.3, bf16[8,32,1024]{2,1,0:T(8,128)(2,1)} %v_ref.3, ...), custom_call_target="tpu_custom_call" | custom-call | tf_op jit(solution)/shard_map/pallas_call | solution.py:201
  108.4 0.0 all-to-all-done.1
  108.5 0.4 convert_bitcast_fusion
  108.9 0.4 fusion.8
  109.3 0.8 copy-done.5
  110.1 1.4 %fusion.2 = bf16[8,32,1024]{2,1,0:T(8,128)(2,1)} fusion(f32[8,32,1024]{2,1,0:T(8,128)S(1)} %copy-done.5, f32[8,32,1024]{2,0,1:T(8,128)S(1)} %bitcast.11), kind=kLoop, calls=%fused_computation.7 | loop fusion | flops 524288 | bytes 2621440 | tf_op jit(solution)/shard_map/convert_element_type | solution.py:340
  111.5 1.4 %fusion = bf16[8,32,1024]{2,1,0:T(8,128)(2,1)} fusion(f32[8,32,1024]{2,1,0:T(8,128)S(1)} %copy-done.4, f32[8,32,1024]{2,0,1:T(8,128)S(1)} %bitcast.10), kind=kLoop, calls=%fused_computation.3 | loop fusion | flops 524288 | bytes 2621440 | tf_op jit(solution)/shard_map/convert_element_type | solution.py:340
  112.9 1.4 %fusion.1 = bf16[8,32,1024]{2,1,0:T(8,128)(2,1)} fusion(f32[8,32,1024]{2,1,0:T(8,128)S(1)} %copy-done.3, f32[8,32,1024]{2,0,1:T(8,128)S(1)} %bitcast.9), kind=kLoop, calls=%fused_computation.5 | loop fusion | flops 524288 | bytes 2621440 | tf_op jit(solution)/shard_map/convert_element_type | solution.py:340
  (21 shorter events, 0.1 us)
Async XLA Ops:
  6.4 4.4 %copy-start.1 = (bf16[8,32,1024]{2,1,0:T(8,128)(2,1)S(1)}, bf16[8,32,1024]{2,1,0:T(8,128)(2,1)}, u32[]{:S(2)}) copy-start(bf16[8,32,1024]{2,1,0:T(8,128)(2,1)} %k_ref.3) | copy-start | bytes 1572868
  6.4 4.4 %copy-start.2 = (bf16[8,32,1024]{2,1,0:T(8,128)(2,1)S(1)}, bf16[8,32,1024]{2,1,0:T(8,128)(2,1)}, u32[]{:S(2)}) copy-start(bf16[8,32,1024]{2,1,0:T(8,128)(2,1)} %v_ref.3) | copy-start | bytes 1572868
  6.4 31.6 %all-to-all-start = ((bf16[8,4,4,8,1024]{4,3,2,1,0:T(8,128)(2,1)}), bf16[8,4,4,8,1024]{4,3,2,1,0:T(8,128)(2,1)S(1)}, u32[]{:S(2)}, u32[]{:S(2)}) async-start(bf16[8,4,4,8,1024]{4,3,2,1,0:T(8,128)(2,1)} %shard_map.86), calls=%async_computation | async-start | bytes 4194304 | tf_op jit(solution)/shard_map/all_to_all | solution.py:326
  11.9 38.1 %collective-permute-start.1 = (bf16[2,8,32,1024]{3,2,1,0:T(8,128)(2,1)}, bf16[2,8,32,1024]{3,2,1,0:T(8,128)(2,1)S(1)}, u32[]{:S(2)}, u32[]{:S(2)}) collective-permute-start(bf16[2,8,32,1024]{3,2,1,0:T(8,128)(2,1)} %pad_maximum_fusion), channel_id=1, source_target_pairs={{1,0},{2,1},{3,2},{4,3},{5,4},{6,5},{7,6},{9,8},{10,9},{11,10},{12... | collective-permute-start | bytes 3145736 | tf_op jit(solution)/shard_map/ppermute | solution.py:22
  14.0 36.1 %collective-permute-start = (bf16[2,8,32,1024]{3,2,1,0:T(8,128)(2,1)}, bf16[2,8,32,1024]{3,2,1,0:T(8,128)(2,1)}, u32[]{:S(2)}, u32[]{:S(2)}) collective-permute-start(bf16[2,8,32,1024]{3,2,1,0:T(8,128)(2,1)} %pad_maximum_fusion), channel_id=1, source_target_pairs={{0,1},{1,2},{2,3},{3,4},{4,5},{5,6},{6,7},{8,9},{9,10},{10,11},{11... | collective-permute-start | bytes 3145736 | tf_op jit(solution)/shard_map/ppermute | solution.py:22
  38.0 1.3 %copy-start = (bf16[8,4,4,8,1024]{4,3,2,1,0:T(8,128)(2,1)}, bf16[8,4,4,8,1024]{4,3,2,1,0:T(8,128)(2,1)S(1)}, u32[]{:S(2)}) copy-start(bf16[8,4,4,8,1024]{4,3,2,1,0:T(8,128)(2,1)S(1)} %all-to-all-done.x_ref) | copy-start | bytes 6291460
  45.2 3.8 %copy-start.7 = (s32[8,16]{1,0:T(8,128)S(1)}, s32[8,16]{1,0:T(8,128)}, u32[]{:S(2)}) copy-start(s32[8,16]{1,0:T(8,128)} %param.10) | copy-start | bytes 1540
  45.2 4.0 %copy-start.8 = (s32[8]{0:T(128)S(1)}, s32[8]{0:T(128)}, u32[]{:S(2)}) copy-start(s32[8]{0:T(128)} %param.11) | copy-start | bytes 100
  45.2 63.2 %all-to-all-start.1 = ((bf16[8,3,4,8,1024]{4,3,2,1,0:T(8,128)(2,1)}), bf16[8,3,4,8,1024]{4,3,2,1,0:T(8,128)(2,1)S(1)}, u32[]{:S(2)}, u32[]{:S(2)}) async-start(bf16[8,3,4,8,1024]{4,3,2,1,0:T(8,128)(2,1)} %shard_map.87), calls=%async_computation.1 | async-start | bytes 3145728 | tf_op jit(solution)/shard_map/all_to_all | solution.py:336
  50.0 1.0 copy-start.6
  108.8 1.2 %copy-start.5 = (f32[8,32,1024]{2,1,0:T(8,128)S(1)}, f32[8,32,1024]{2,1,0:T(8,128)}, u32[]{:S(2)}) copy-start(f32[8,32,1024]{2,1,0:T(8,128)} %get-tuple-element.6) | copy-start | bytes 3145732
  109.3 2.2 %copy-start.4 = (f32[8,32,1024]{2,1,0:T(8,128)S(1)}, f32[8,32,1024]{2,1,0:T(8,128)}, u32[]{:S(2)}) copy-start(f32[8,32,1024]{2,1,0:T(8,128)} %get-tuple-element.8) | copy-start | bytes 3145732
  110.1 2.8 %copy-start.3 = (f32[8,32,1024]{2,1,0:T(8,128)S(1)}, f32[8,32,1024]{2,1,0:T(8,128)}, u32[]{:S(2)}) copy-start(f32[8,32,1024]{2,1,0:T(8,128)} %get-tuple-element.7) | copy-start | bytes 3145732

commit v16 on v12

--- a/solution.py
+++ b/solution.py
@@ -170,14 +170,10 @@
         far_copy(r, True).start()
         far_copy(r, False).start()
 
-        @pl.when(r > 0)
-        def _():
-            send_near(r - 1)
-
+        send_near(r)
         return carry
 
     lax.fori_loop(0, rows, row_step, 0)
-    send_near(rows - 1)
     for copy in relays(0, whole=True):
         copy.wait_send()
     for src, dst, slot in ((s_fl, x_fr, 0), (s_fr, x_fl, 1)):

time: 115 us -> 129 us (1.12)
  Pallas kernels: 63.3 us -> 78.2 us
    pallas_call x1, Pallas kernels: 57.4 us -> 72.4 us  [fused_row(): pl.pallas_call(functools.partial(fused_row_kernel, w2), in_specs=[vmem] *...]
  transfers between devices with their start and end apart: 4 -> 4, of which waited for: 1 -> 1; matrix products, arithmetic and copies ran while one was open for 2% -> 2% of each run, Pallas kernels for 56% -> 61%
where the time goes in v16:
time: 129 us; the launch traced here: 128 us
  Pallas kernels  78.2 us (61%)
  waiting for transfers between devices  20.2 us (16%)
  starting transfers between devices  13.8 us (11%)
  other arithmetic  8.33 us (6%)
  local copies, waits for them, and re-layouts  6.88 us (5%)
    pallas_call x1, Pallas kernels, fused_row(): pl.pallas_call(functools.partial(fused_row_kernel, w2), in_specs=[vmem] *...  72.4 us
    all_to_all x1, waiting for transfers between devices, body(): lax.all_to_all(stacked, 'rrow', split_axis=0, concat_axis=0, tiled=True)  20.2 us
    unnamed x22, local copies, waits for them, and re-layouts  6.47 us
    pallas_call x1, Pallas kernels, column_attention(): pl.pallas_call(column_kernel, in_specs=[vmem], out_specs=vmem, out_shape=...  5.86 us
    ppermute x2, starting transfers between devices, shifted(): return lax.ppermute(block, axis, route)  5.83 us
    all_to_all x1, starting transfers between devices, body(): lax.all_to_all(stacked, 'rrow', split_axis=0, concat_axis=0, tiled=True)  4.3 us
    convert_element_type x3, other arithmetic, body(): (row + col).astype(jnp.bfloat16)  4.22 us
    all_to_all x1, starting transfers between devices, body(): lax.all_to_all(col_out, 'rrow', split_axis=0, concat_axis=0, tiled=True)  3.71 us
  transfers between devices with their start and end apart: 4, of which 1 were waited for; matrix products, arithmetic and copies ran while one was open for 2% of the time, Pallas kernels for 61%

profile of v16, /device:TPU:48, one launch (start us, length us, event | category | flops | bytes accessed | tf_op | source)
XLA Modules:
  0.0 128.3 jit_solution(11778142074734390030)
XLA Ops:
  0.7 1.4 %copy.16 = bf16[8,32,1024]{2,0,1:T(8,128)(2,1)S(1)} copy(bf16[8,32,1024]{2,1,0:T(8,128)(2,1)} %q_ref.1) | data formatting | bytes 1048576 | tf_op args[0]
  2.1 1.3 %copy.19 = bf16[8,32,1024]{2,0,1:T(8,128)(2,1)S(1)} copy(bf16[8,32,1024]{2,1,0:T(8,128)(2,1)} %g_ref.1) | data formatting | bytes 1048576 | tf_op args[3]
  3.4 0.3 copy.17
  3.7 0.3 copy.18
  4.0 1.6 %maximum_bitcast_fusion = bf16[8,4,4,8,1024]{4,3,2,1,0:T(8,128)(2,1)} fusion(bf16[1,8,8,4,1024]{4,1,3,0,2:T(8,128)(2,1)S(1)} %bitcast.19, bf16[1,8,8,4,1024]{4,1,3,0,2:T(8,128)(2,1)S(1)} %bitcast.21, bf16[1,8,8,4,1024]{4,1,3,0,2:T(8,128)(2,1)S(1)} %bitcast.20, bf16[1,8,8,4,1024]{4,1,3,0,2:T(8,128)(2,1)S(1)} %bitcast.18), kind=kLoop, calls=%fused_computation.1 | loop fusion | flops 3145728 | bytes 4194304 | tf_op jit(solution)/shard_map/transpose | solution.py:305
  5.6 4.3 %all-to-all-start = ((bf16[8,4,4,8,1024]{4,3,2,1,0:T(8,128)(2,1)}), bf16[8,4,4,8,1024]{4,3,2,1,0:T(8,128)(2,1)S(1)}, u32[]{:S(2)}, u32[]{:S(2)}) async-start(bf16[8,4,4,8,1024]{4,3,2,1,0:T(8,128)(2,1)} %maximum_bitcast_fusion), calls=%async_computation | async-start | bytes 4194304 | tf_op jit(solution)/shard_map/all_to_all | solution.py:307
  9.9 1.1 pad_maximum_fusion
  11.0 2.0 %collective-permute-start.1 = (bf16[2,8,32,1024]{3,2,1,0:T(8,128)(2,1)}, bf16[2,8,32,1024]{3,2,1,0:T(8,128)(2,1)S(1)}, u32[]{:S(2)}, u32[]{:S(2)}) collective-permute-start(bf16[2,8,32,1024]{3,2,1,0:T(8,128)(2,1)} %pad_maximum_fusion), channel_id=1, source_target_pairs={{1,0},{2,1},{3,2},{4,3},{5,4},{6,5},{7,6},{9,8},{10,9},{11,10},{12... | collective-permute-start | bytes 3145736 | tf_op jit(solution)/shard_map/ppermute | solution.py:22
  13.0 3.8 %collective-permute-start = (bf16[2,8,32,1024]{3,2,1,0:T(8,128)(2,1)}, bf16[2,8,32,1024]{3,2,1,0:T(8,128)(2,1)}, u32[]{:S(2)}, u32[]{:S(2)}) collective-permute-start(bf16[2,8,32,1024]{3,2,1,0:T(8,128)(2,1)} %pad_maximum_fusion), channel_id=1, source_target_pairs={{0,1},{1,2},{2,3},{3,4},{4,5},{5,6},{6,7},{8,9},{9,10},{10,11},{11... | collective-permute-start | bytes 3145736 | tf_op jit(solution)/shard_map/ppermute | solution.py:22
  16.9 20.2 %all-to-all-done.x_ref = bf16[8,4,4,8,1024]{4,3,2,1,0:T(8,128)(2,1)S(1)} async-done(((bf16[8,4,4,8,1024]{4,3,2,1,0:T(8,128)(2,1)}), bf16[8,4,4,8,1024]{4,3,2,1,0:T(8,128)(2,1)S(1)}, u32[]{:S(2)}, u32[]{:S(2)}) %all-to-all-start) | async-done | bytes 2097184 | tf_op jit(solution)/shard_map/all_to_all | solution.py:307
  37.1 1.3 %copy-done = bf16[8,4,4,8,1024]{4,3,2,1,0:T(8,128)(2,1)} copy-done((bf16[8,4,4,8,1024]{4,3,2,1,0:T(8,128)(2,1)}, bf16[8,4,4,8,1024]{4,3,2,1,0:T(8,128)(2,1)S(1)}, u32[]{:S(2)}) %copy-start) | copy-done | bytes 2097176
  38.5 5.9 %shard_map.86 = bf16[8,3,4,8,1024]{4,3,2,1,0:T(8,128)(2,1)} custom-call(bf16[8,4,4,8,1024]{4,3,2,1,0:T(8,128)(2,1)} %copy-done), custom_call_target="tpu_custom_call" | custom-call | tf_op jit(solution)/shard_map/pallas_call | solution.py:263
  44.3 3.7 %all-to-all-start.1 = ((bf16[8,3,4,8,1024]{4,3,2,1,0:T(8,128)(2,1)}), bf16[8,3,4,8,1024]{4,3,2,1,0:T(8,128)(2,1)S(1)}, u32[]{:S(2)}, u32[]{:S(2)}) async-start(bf16[8,3,4,8,1024]{4,3,2,1,0:T(8,128)(2,1)} %shard_map.86), calls=%async_computation.1 | async-start | bytes 3145728 | tf_op jit(solution)/shard_map/all_to_all | solution.py:317
  48.1 0.1 multiply_reduce_fusion
  48.2 0.1 broadcast_compare_fusion
  48.4 0.8 fusion.6.bias_ref
  49.1 1.0 copy-done.6
  50.1 72.4 %shard_map.85 = (f32[8,32,1024]{2,1,0:T(8,128)}, f32[8,32,1024]{2,1,0:T(8,128)}, f32[8,32,1024]{2,1,0:T(8,128)}) custom-call(bf16[8,32,1024]{2,1,0:T(8,128)(2,1)} %q_ref.1, bf16[8,32,1024]{2,1,0:T(8,128)(2,1)} %g_ref.1, bf16[8,32,1024]{2,1,0:T(8,128)(2,1)} %k_ref.1, bf16[8,32,1024]{2,1,0:T(8,128)(2,1)} %v_ref.1, ...), custom_call_target="tpu_custom_call" | custom-call | tf_op jit(solution)/shard_map/pallas_call | solution.py:197
  122.5 0.4 convert_bitcast_fusion
  122.9 0.4 fusion.8
  123.3 0.8 copy-done.5
  124.1 1.4 %fusion.2 = bf16[8,32,1024]{2,1,0:T(8,128)(2,1)} fusion(f32[8,32,1024]{2,1,0:T(8,128)S(1)} %copy-done.5, f32[8,32,1024]{2,0,1:T(8,128)S(1)} %bitcast.17), kind=kLoop, calls=%fused_computation.8 | loop fusion | flops 524288 | bytes 2621440 | tf_op jit(solution)/shard_map/convert_element_type | solution.py:321
  125.5 1.4 %fusion = bf16[8,32,1024]{2,1,0:T(8,128)(2,1)} fusion(f32[8,32,1024]{2,1,0:T(8,128)S(1)} %copy-done.4, f32[8,32,1024]{2,0,1:T(8,128)S(1)} %bitcast.16), kind=kLoop, calls=%fused_computation.4 | loop fusion | flops 524288 | bytes 2621440 | tf_op jit(solution)/shard_map/convert_element_type | solution.py:321
  126.9 1.4 %fusion.1 = bf16[8,32,1024]{2,1,0:T(8,128)(2,1)} fusion(f32[8,32,1024]{2,1,0:T(8,128)S(1)} %copy-done.3, f32[8,32,1024]{2,0,1:T(8,128)S(1)} %bitcast.15), kind=kLoop, calls=%fused_computation.6 | loop fusion | flops 524288 | bytes 2621440 | tf_op jit(solution)/shard_map/convert_element_type | solution.py:321
  (25 shorter events, 0.2 us)
Async XLA Ops:
  0.6 2.8 %copy-start.1 = (bf16[8,32,1024]{2,1,0:T(8,128)(2,1)S(1)}, bf16[8,32,1024]{2,1,0:T(8,128)(2,1)}, u32[]{:S(2)}) copy-start(bf16[8,32,1024]{2,1,0:T(8,128)(2,1)} %k_ref.1) | copy-start | bytes 1572868
  0.6 3.1 %copy-start.2 = (bf16[8,32,1024]{2,1,0:T(8,128)(2,1)S(1)}, bf16[8,32,1024]{2,1,0:T(8,128)(2,1)}, u32[]{:S(2)}) copy-start(bf16[8,32,1024]{2,1,0:T(8,128)(2,1)} %v_ref.1) | copy-start | bytes 1572868
  5.6 31.5 %all-to-all-start = ((bf16[8,4,4,8,1024]{4,3,2,1,0:T(8,128)(2,1)}), bf16[8,4,4,8,1024]{4,3,2,1,0:T(8,128)(2,1)S(1)}, u32[]{:S(2)}, u32[]{:S(2)}) async-start(bf16[8,4,4,8,1024]{4,3,2,1,0:T(8,128)(2,1)} %maximum_bitcast_fusion), calls=%async_computation | async-start | bytes 4194304 | tf_op jit(solution)/shard_map/all_to_all | solution.py:307
  11.0 38.1 %collective-permute-start.1 = (bf16[2,8,32,1024]{3,2,1,0:T(8,128)(2,1)}, bf16[2,8,32,1024]{3,2,1,0:T(8,128)(2,1)S(1)}, u32[]{:S(2)}, u32[]{:S(2)}) collective-permute-start(bf16[2,8,32,1024]{3,2,1,0:T(8,128)(2,1)} %pad_maximum_fusion), channel_id=1, source_target_pairs={{1,0},{2,1},{3,2},{4,3},{5,4},{6,5},{7,6},{9,8},{10,9},{11,10},{12... | collective-permute-start | bytes 3145736 | tf_op jit(solution)/shard_map/ppermute | solution.py:22
  13.0 36.1 %collective-permute-start = (bf16[2,8,32,1024]{3,2,1,0:T(8,128)(2,1)}, bf16[2,8,32,1024]{3,2,1,0:T(8,128)(2,1)}, u32[]{:S(2)}, u32[]{:S(2)}) collective-permute-start(bf16[2,8,32,1024]{3,2,1,0:T(8,128)(2,1)} %pad_maximum_fusion), channel_id=1, source_target_pairs={{0,1},{1,2},{2,3},{3,4},{4,5},{5,6},{6,7},{8,9},{9,10},{10,11},{11... | collective-permute-start | bytes 3145736 | tf_op jit(solution)/shard_map/ppermute | solution.py:22
  37.1 1.3 %copy-start = (bf16[8,4,4,8,1024]{4,3,2,1,0:T(8,128)(2,1)}, bf16[8,4,4,8,1024]{4,3,2,1,0:T(8,128)(2,1)S(1)}, u32[]{:S(2)}) copy-start(bf16[8,4,4,8,1024]{4,3,2,1,0:T(8,128)(2,1)S(1)} %all-to-all-done.x_ref) | copy-start | bytes 6291460
  44.3 3.8 %copy-start.7 = (s32[8,16]{1,0:T(8,128)S(1)}, s32[8,16]{1,0:T(8,128)}, u32[]{:S(2)}) copy-start(s32[8,16]{1,0:T(8,128)} %param.10) | copy-start | bytes 1540
  44.3 4.0 %copy-start.8 = (s32[8]{0:T(128)S(1)}, s32[8]{0:T(128)}, u32[]{:S(2)}) copy-start(s32[8]{0:T(128)} %param.11) | copy-start | bytes 100
  44.3 78.1 %all-to-all-start.1 = ((bf16[8,3,4,8,1024]{4,3,2,1,0:T(8,128)(2,1)}), bf16[8,3,4,8,1024]{4,3,2,1,0:T(8,128)(2,1)S(1)}, u32[]{:S(2)}, u32[]{:S(2)}) async-start(bf16[8,3,4,8,1024]{4,3,2,1,0:T(8,128)(2,1)} %shard_map.86), calls=%async_computation.1 | async-start | bytes 3145728 | tf_op jit(solution)/shard_map/all_to_all | solution.py:317
  49.1 1.0 copy-start.6
  122.9 1.2 copy-start.5
  123.3 2.2 %copy-start.4 = (f32[8,32,1024]{2,1,0:T(8,128)S(1)}, f32[8,32,1024]{2,1,0:T(8,128)}, u32[]{:S(2)}) copy-start(f32[8,32,1024]{2,1,0:T(8,128)} %get-tuple-element.8) | copy-start | bytes 3145732
  124.1 2.8 %copy-start.3 = (f32[8,32,1024]{2,1,0:T(8,128)S(1)}, f32[8,32,1024]{2,1,0:T(8,128)}, u32[]{:S(2)}) copy-start(f32[8,32,1024]{2,1,0:T(8,128)} %get-tuple-element.7) | copy-start | bytes 3145732

commit v17 on v12

--- a/solution.py
+++ b/solution.py
@@ -170,13 +170,14 @@
         far_copy(r, True).start()
         far_copy(r, False).start()
 
-        @pl.when(r > 0)
+        @pl.when(r > 1)
         def _():
-            send_near(r - 1)
+            send_near(r - 2)
 
         return carry
 
     lax.fori_loop(0, rows, row_step, 0)
+    send_near(rows - 2)
     send_near(rows - 1)
     for copy in relays(0, whole=True):
         copy.wait_send()

time: 115 us -> 114 us (level)
  Pallas kernels: 63.3 us -> 62 us
    pallas_call x1, Pallas kernels: 57.4 us -> 56.1 us  [fused_row(): pl.pallas_call(functools.partial(fused_row_kernel, w2), in_specs=[vmem] *...]
  transfers between devices with their start and end apart: 4 -> 4, of which waited for: 1 -> 1; matrix products, arithmetic and copies ran while one was open for 2% -> 2% of each run, Pallas kernels for 56% -> 55%
where the time goes in v17:
time: 114 us; the launch traced here: 112 us
  Pallas kernels  62 us (54%)
  waiting for transfers between devices  20.2 us (18%)
  starting transfers between devices  13.8 us (12%)
  other arithmetic  8.33 us (7%)
  local copies, waits for them, and re-layouts  6.88 us (6%)
    pallas_call x1, Pallas kernels, fused_row(): pl.pallas_call(functools.partial(fused_row_kernel, w2), in_specs=[vmem] *...  56.1 us
    all_to_all x1, waiting for transfers between devices, body(): lax.all_to_all(stacked, 'rrow', split_axis=0, concat_axis=0, tiled=True)  20.2 us
    unnamed x22, local copies, waits for them, and re-layouts  6.47 us
    pallas_call x1, Pallas kernels, column_attention(): pl.pallas_call(column_kernel, in_specs=[vmem], out_specs=vmem, out_shape=...  5.86 us
    ppermute x2, starting transfers between devices, shifted(): return lax.ppermute(block, axis, route)  5.83 us
    all_to_all x1, starting transfers between devices, body(): lax.all_to_all(stacked, 'rrow', split_axis=0, concat_axis=0, tiled=True)  4.3 us
    convert_element_type x3, other arithmetic, body(): (row + col).astype(jnp.bfloat16)  4.22 us
    all_to_all x1, starting transfers between devices, body(): lax.all_to_all(col_out, 'rrow', split_axis=0, concat_axis=0, tiled=True)  3.71 us
  transfers between devices with their start and end apart: 4, of which 1 were waited for; matrix products, arithmetic and copies ran while one was open for 2% of the time, Pallas kernels for 55%

profile of v17, /device:TPU:48, one launch (start us, length us, event | category | flops | bytes accessed | tf_op | source)
XLA Modules:
  0.0 112.1 jit_solution(549698622206717731)
XLA Ops:
  0.7 1.4 %copy.16 = bf16[8,32,1024]{2,0,1:T(8,128)(2,1)S(1)} copy(bf16[8,32,1024]{2,1,0:T(8,128)(2,1)} %q_ref.1) | data formatting | bytes 1048576 | tf_op args[0]
  2.1 1.3 %copy.19 = bf16[8,32,1024]{2,0,1:T(8,128)(2,1)S(1)} copy(bf16[8,32,1024]{2,1,0:T(8,128)(2,1)} %g_ref.1) | data formatting | bytes 1048576 | tf_op args[3]
  3.4 0.3 copy.17
  3.7 0.3 copy.18
  4.0 1.6 %maximum_bitcast_fusion = bf16[8,4,4,8,1024]{4,3,2,1,0:T(8,128)(2,1)} fusion(bf16[1,8,8,4,1024]{4,1,3,0,2:T(8,128)(2,1)S(1)} %bitcast.19, bf16[1,8,8,4,1024]{4,1,3,0,2:T(8,128)(2,1)S(1)} %bitcast.21, bf16[1,8,8,4,1024]{4,1,3,0,2:T(8,128)(2,1)S(1)} %bitcast.20, bf16[1,8,8,4,1024]{4,1,3,0,2:T(8,128)(2,1)S(1)} %bitcast.18), kind=kLoop, calls=%fused_computation.1 | loop fusion | flops 3145728 | bytes 4194304 | tf_op jit(solution)/shard_map/transpose | solution.py:310
  5.6 4.3 %all-to-all-start = ((bf16[8,4,4,8,1024]{4,3,2,1,0:T(8,128)(2,1)}), bf16[8,4,4,8,1024]{4,3,2,1,0:T(8,128)(2,1)S(1)}, u32[]{:S(2)}, u32[]{:S(2)}) async-start(bf16[8,4,4,8,1024]{4,3,2,1,0:T(8,128)(2,1)} %maximum_bitcast_fusion), calls=%async_computation | async-start | bytes 4194304 | tf_op jit(solution)/shard_map/all_to_all | solution.py:312
  9.9 1.1 pad_maximum_fusion
  11.0 2.0 %collective-permute-start.1 = (bf16[2,8,32,1024]{3,2,1,0:T(8,128)(2,1)}, bf16[2,8,32,1024]{3,2,1,0:T(8,128)(2,1)S(1)}, u32[]{:S(2)}, u32[]{:S(2)}) collective-permute-start(bf16[2,8,32,1024]{3,2,1,0:T(8,128)(2,1)} %pad_maximum_fusion), channel_id=1, source_target_pairs={{1,0},{2,1},{3,2},{4,3},{5,4},{6,5},{7,6},{9,8},{10,9},{11,10},{12... | collective-permute-start | bytes 3145736 | tf_op jit(solution)/shard_map/ppermute | solution.py:22
  13.0 3.8 %collective-permute-start = (bf16[2,8,32,1024]{3,2,1,0:T(8,128)(2,1)}, bf16[2,8,32,1024]{3,2,1,0:T(8,128)(2,1)}, u32[]{:S(2)}, u32[]{:S(2)}) collective-permute-start(bf16[2,8,32,1024]{3,2,1,0:T(8,128)(2,1)} %pad_maximum_fusion), channel_id=1, source_target_pairs={{0,1},{1,2},{2,3},{3,4},{4,5},{5,6},{6,7},{8,9},{9,10},{10,11},{11... | collective-permute-start | bytes 3145736 | tf_op jit(solution)/shard_map/ppermute | solution.py:22
  16.9 20.2 %all-to-all-done.x_ref = bf16[8,4,4,8,1024]{4,3,2,1,0:T(8,128)(2,1)S(1)} async-done(((bf16[8,4,4,8,1024]{4,3,2,1,0:T(8,128)(2,1)}), bf16[8,4,4,8,1024]{4,3,2,1,0:T(8,128)(2,1)S(1)}, u32[]{:S(2)}, u32[]{:S(2)}) %all-to-all-start) | async-done | bytes 2097184 | tf_op jit(solution)/shard_map/all_to_all | solution.py:312
  37.1 1.3 %copy-done = bf16[8,4,4,8,1024]{4,3,2,1,0:T(8,128)(2,1)} copy-done((bf16[8,4,4,8,1024]{4,3,2,1,0:T(8,128)(2,1)}, bf16[8,4,4,8,1024]{4,3,2,1,0:T(8,128)(2,1)S(1)}, u32[]{:S(2)}) %copy-start) | copy-done | bytes 2097176
  38.5 5.9 %shard_map.86 = bf16[8,3,4,8,1024]{4,3,2,1,0:T(8,128)(2,1)} custom-call(bf16[8,4,4,8,1024]{4,3,2,1,0:T(8,128)(2,1)} %copy-done), custom_call_target="tpu_custom_call" | custom-call | tf_op jit(solution)/shard_map/pallas_call | solution.py:268
  44.3 3.7 %all-to-all-start.1 = ((bf16[8,3,4,8,1024]{4,3,2,1,0:T(8,128)(2,1)}), bf16[8,3,4,8,1024]{4,3,2,1,0:T(8,128)(2,1)S(1)}, u32[]{:S(2)}, u32[]{:S(2)}) async-start(bf16[8,3,4,8,1024]{4,3,2,1,0:T(8,128)(2,1)} %shard_map.86), calls=%async_computation.1 | async-start | bytes 3145728 | tf_op jit(solution)/shard_map/all_to_all | solution.py:322
  48.1 0.1 multiply_reduce_fusion
  48.2 0.1 broadcast_compare_fusion
  48.4 0.8 fusion.6.bias_ref
  49.1 1.0 copy-done.6
  50.1 56.1 %shard_map.85 = (f32[8,32,1024]{2,1,0:T(8,128)}, f32[8,32,1024]{2,1,0:T(8,128)}, f32[8,32,1024]{2,1,0:T(8,128)}) custom-call(bf16[8,32,1024]{2,1,0:T(8,128)(2,1)} %q_ref.1, bf16[8,32,1024]{2,1,0:T(8,128)(2,1)} %g_ref.1, bf16[8,32,1024]{2,1,0:T(8,128)(2,1)} %k_ref.1, bf16[8,32,1024]{2,1,0:T(8,128)(2,1)} %v_ref.1, ...), custom_call_target="tpu_custom_call" | custom-call | tf_op jit(solution)/shard_map/pallas_call | solution.py:202
  106.2 0.4 convert_bitcast_fusion
  106.6 0.4 fusion.8
  107.1 0.8 copy-done.5
  107.9 1.4 %fusion.2 = bf16[8,32,1024]{2,1,0:T(8,128)(2,1)} fusion(f32[8,32,1024]{2,1,0:T(8,128)S(1)} %copy-done.5, f32[8,32,1024]{2,0,1:T(8,128)S(1)} %bitcast.17), kind=kLoop, calls=%fused_computation.8 | loop fusion | flops 524288 | bytes 2621440 | tf_op jit(solution)/shard_map/convert_element_type | solution.py:326
  109.3 1.4 %fusion = bf16[8,32,1024]{2,1,0:T(8,128)(2,1)} fusion(f32[8,32,1024]{2,1,0:T(8,128)S(1)} %copy-done.4, f32[8,32,1024]{2,0,1:T(8,128)S(1)} %bitcast.16), kind=kLoop, calls=%fused_computation.4 | loop fusion | flops 524288 | bytes 2621440 | tf_op jit(solution)/shard_map/convert_element_type | solution.py:326
  110.7 1.4 %fusion.1 = bf16[8,32,1024]{2,1,0:T(8,128)(2,1)} fusion(f32[8,32,1024]{2,1,0:T(8,128)S(1)} %copy-done.3, f32[8,32,1024]{2,0,1:T(8,128)S(1)} %bitcast.15), kind=kLoop, calls=%fused_computation.6 | loop fusion | flops 524288 | bytes 2621440 | tf_op jit(solution)/shard_map/convert_element_type | solution.py:326
  (25 shorter events, 0.2 us)
Async XLA Ops:
  0.6 2.8 %copy-start.1 = (bf16[8,32,1024]{2,1,0:T(8,128)(2,1)S(1)}, bf16[8,32,1024]{2,1,0:T(8,128)(2,1)}, u32[]{:S(2)}) copy-start(bf16[8,32,1024]{2,1,0:T(8,128)(2,1)} %k_ref.1) | copy-start | bytes 1572868
  0.6 3.1 %copy-start.2 = (bf16[8,32,1024]{2,1,0:T(8,128)(2,1)S(1)}, bf16[8,32,1024]{2,1,0:T(8,128)(2,1)}, u32[]{:S(2)}) copy-start(bf16[8,32,1024]{2,1,0:T(8,128)(2,1)} %v_ref.1) | copy-start | bytes 1572868
  5.6 31.5 %all-to-all-start = ((bf16[8,4,4,8,1024]{4,3,2,1,0:T(8,128)(2,1)}), bf16[8,4,4,8,1024]{4,3,2,1,0:T(8,128)(2,1)S(1)}, u32[]{:S(2)}, u32[]{:S(2)}) async-start(bf16[8,4,4,8,1024]{4,3,2,1,0:T(8,128)(2,1)} %maximum_bitcast_fusion), calls=%async_computation | async-start | bytes 4194304 | tf_op jit(solution)/shard_map/all_to_all | solution.py:312
  11.0 38.1 %collective-permute-start.1 = (bf16[2,8,32,1024]{3,2,1,0:T(8,128)(2,1)}, bf16[2,8,32,1024]{3,2,1,0:T(8,128)(2,1)S(1)}, u32[]{:S(2)}, u32[]{:S(2)}) collective-permute-start(bf16[2,8,32,1024]{3,2,1,0:T(8,128)(2,1)} %pad_maximum_fusion), channel_id=1, source_target_pairs={{1,0},{2,1},{3,2},{4,3},{5,4},{6,5},{7,6},{9,8},{10,9},{11,10},{12... | collective-permute-start | bytes 3145736 | tf_op jit(solution)/shard_map/ppermute | solution.py:22
  13.0 36.1 %collective-permute-start = (bf16[2,8,32,1024]{3,2,1,0:T(8,128)(2,1)}, bf16[2,8,32,1024]{3,2,1,0:T(8,128)(2,1)}, u32[]{:S(2)}, u32[]{:S(2)}) collective-permute-start(bf16[2,8,32,1024]{3,2,1,0:T(8,128)(2,1)} %pad_maximum_fusion), channel_id=1, source_target_pairs={{0,1},{1,2},{2,3},{3,4},{4,5},{5,6},{6,7},{8,9},{9,10},{10,11},{11... | collective-permute-start | bytes 3145736 | tf_op jit(solution)/shard_map/ppermute | solution.py:22
  37.1 1.3 %copy-start = (bf16[8,4,4,8,1024]{4,3,2,1,0:T(8,128)(2,1)}, bf16[8,4,4,8,1024]{4,3,2,1,0:T(8,128)(2,1)S(1)}, u32[]{:S(2)}) copy-start(bf16[8,4,4,8,1024]{4,3,2,1,0:T(8,128)(2,1)S(1)} %all-to-all-done.x_ref) | copy-start | bytes 6291460
  44.3 3.8 %copy-start.7 = (s32[8,16]{1,0:T(8,128)S(1)}, s32[8,16]{1,0:T(8,128)}, u32[]{:S(2)}) copy-start(s32[8,16]{1,0:T(8,128)} %param.10) | copy-start | bytes 1540
  44.3 4.0 %copy-start.8 = (s32[8]{0:T(128)S(1)}, s32[8]{0:T(128)}, u32[]{:S(2)}) copy-start(s32[8]{0:T(128)} %param.11) | copy-start | bytes 100
  44.3 61.9 %all-to-all-start.1 = ((bf16[8,3,4,8,1024]{4,3,2,1,0:T(8,128)(2,1)}), bf16[8,3,4,8,1024]{4,3,2,1,0:T(8,128)(2,1)S(1)}, u32[]{:S(2)}, u32[]{:S(2)}) async-start(bf16[8,3,4,8,1024]{4,3,2,1,0:T(8,128)(2,1)} %shard_map.86), calls=%async_computation.1 | async-start | bytes 3145728 | tf_op jit(solution)/shard_map/all_to_all | solution.py:322
  49.1 1.0 copy-start.6
  106.6 1.2 %copy-start.5 = (f32[8,32,1024]{2,1,0:T(8,128)S(1)}, f32[8,32,1024]{2,1,0:T(8,128)}, u32[]{:S(2)}) copy-start(f32[8,32,1024]{2,1,0:T(8,128)} %get-tuple-element.6) | copy-start | bytes 3145732
  107.1 2.2 %copy-start.4 = (f32[8,32,1024]{2,1,0:T(8,128)S(1)}, f32[8,32,1024]{2,1,0:T(8,128)}, u32[]{:S(2)}) copy-start(f32[8,32,1024]{2,1,0:T(8,128)} %get-tuple-element.8) | copy-start | bytes 3145732
  107.9 2.8 %copy-start.3 = (f32[8,32,1024]{2,1,0:T(8,128)S(1)}, f32[8,32,1024]{2,1,0:T(8,128)}, u32[]{:S(2)}) copy-start(f32[8,32,1024]{2,1,0:T(8,128)} %get-tuple-element.7) | copy-start | bytes 3145732

commit v18 on v17

--- a/solution.py
+++ b/solution.py
@@ -170,13 +170,14 @@
         far_copy(r, True).start()
         far_copy(r, False).start()
 
-        @pl.when(r > 1)
+        @pl.when(r > 2)
         def _():
-            send_near(r - 2)
+            send_near(r - 3)
 
         return carry
 
     lax.fori_loop(0, rows, row_step, 0)
+    send_near(rows - 3)
     send_near(rows - 2)
     send_near(rows - 1)
     for copy in relays(0, whole=True):

time: 114 us -> 114 us (level)
  no operation moved by 1% of the time
where the time goes in v18:
time: 114 us; the launch traced here: 112 us
  Pallas kernels  62 us (54%)
  waiting for transfers between devices  20.2 us (18%)
  starting transfers between devices  13.8 us (12%)
  other arithmetic  8.33 us (7%)
  local copies, waits for them, and re-layouts  6.88 us (6%)
    pallas_call x1, Pallas kernels, fused_row(): pl.pallas_call(functools.partial(fused_row_kernel, w2), in_specs=[vmem] *...  56.1 us
    all_to_all x1, waiting for transfers between devices, body(): lax.all_to_all(stacked, 'rrow', split_axis=0, concat_axis=0, tiled=True)  20.2 us
    unnamed x22, local copies, waits for them, and re-layouts  6.47 us
    pallas_call x1, Pallas kernels, column_attention(): pl.pallas_call(column_kernel, in_specs=[vmem], out_specs=vmem, out_shape=...  5.86 us
    ppermute x2, starting transfers between devices, shifted(): return lax.ppermute(block, axis, route)  5.83 us
    all_to_all x1, starting transfers between devices, body(): lax.all_to_all(stacked, 'rrow', split_axis=0, concat_axis=0, tiled=True)  4.3 us
    convert_element_type x3, other arithmetic, body(): (row + col).astype(jnp.bfloat16)  4.22 us
    all_to_all x1, starting transfers between devices, body(): lax.all_to_all(col_out, 'rrow', split_axis=0, concat_axis=0, tiled=True)  3.71 us
  transfers between devices with their start and end apart: 4, of which 1 were waited for; matrix products, arithmetic and copies ran while one was open for 2% of the time, Pallas kernels for 55%

profile of v18, /device:TPU:48, one launch (start us, length us, event | category | flops | bytes accessed | tf_op | source)
XLA Modules:
  0.0 112.1 jit_solution(1532147574643874238)
XLA Ops:
  0.7 1.4 %copy.16 = bf16[8,32,1024]{2,0,1:T(8,128)(2,1)S(1)} copy(bf16[8,32,1024]{2,1,0:T(8,128)(2,1)} %q_ref.1) | data formatting | bytes 1048576 | tf_op args[0]
  2.1 1.3 %copy.19 = bf16[8,32,1024]{2,0,1:T(8,128)(2,1)S(1)} copy(bf16[8,32,1024]{2,1,0:T(8,128)(2,1)} %g_ref.1) | data formatting | bytes 1048576 | tf_op args[3]
  3.4 0.3 copy.17
  3.7 0.3 copy.18
  4.0 1.6 %maximum_bitcast_fusion = bf16[8,4,4,8,1024]{4,3,2,1,0:T(8,128)(2,1)} fusion(bf16[1,8,8,4,1024]{4,1,3,0,2:T(8,128)(2,1)S(1)} %bitcast.19, bf16[1,8,8,4,1024]{4,1,3,0,2:T(8,128)(2,1)S(1)} %bitcast.21, bf16[1,8,8,4,1024]{4,1,3,0,2:T(8,128)(2,1)S(1)} %bitcast.20, bf16[1,8,8,4,1024]{4,1,3,0,2:T(8,128)(2,1)S(1)} %bitcast.18), kind=kLoop, calls=%fused_computation.1 | loop fusion | flops 3145728 | bytes 4194304 | tf_op jit(solution)/shard_map/transpose | solution.py:311
  5.6 4.3 %all-to-all-start = ((bf16[8,4,4,8,1024]{4,3,2,1,0:T(8,128)(2,1)}), bf16[8,4,4,8,1024]{4,3,2,1,0:T(8,128)(2,1)S(1)}, u32[]{:S(2)}, u32[]{:S(2)}) async-start(bf16[8,4,4,8,1024]{4,3,2,1,0:T(8,128)(2,1)} %maximum_bitcast_fusion), calls=%async_computation | async-start | bytes 4194304 | tf_op jit(solution)/shard_map/all_to_all | solution.py:313
  9.9 1.1 pad_maximum_fusion
  11.0 2.0 %collective-permute-start.1 = (bf16[2,8,32,1024]{3,2,1,0:T(8,128)(2,1)}, bf16[2,8,32,1024]{3,2,1,0:T(8,128)(2,1)S(1)}, u32[]{:S(2)}, u32[]{:S(2)}) collective-permute-start(bf16[2,8,32,1024]{3,2,1,0:T(8,128)(2,1)} %pad_maximum_fusion), channel_id=1, source_target_pairs={{1,0},{2,1},{3,2},{4,3},{5,4},{6,5},{7,6},{9,8},{10,9},{11,10},{12... | collective-permute-start | bytes 3145736 | tf_op jit(solution)/shard_map/ppermute | solution.py:22
  13.0 3.8 %collective-permute-start = (bf16[2,8,32,1024]{3,2,1,0:T(8,128)(2,1)}, bf16[2,8,32,1024]{3,2,1,0:T(8,128)(2,1)}, u32[]{:S(2)}, u32[]{:S(2)}) collective-permute-start(bf16[2,8,32,1024]{3,2,1,0:T(8,128)(2,1)} %pad_maximum_fusion), channel_id=1, source_target_pairs={{0,1},{1,2},{2,3},{3,4},{4,5},{5,6},{6,7},{8,9},{9,10},{10,11},{11... | collective-permute-start | bytes 3145736 | tf_op jit(solution)/shard_map/ppermute | solution.py:22
  16.9 20.2 %all-to-all-done.x_ref = bf16[8,4,4,8,1024]{4,3,2,1,0:T(8,128)(2,1)S(1)} async-done(((bf16[8,4,4,8,1024]{4,3,2,1,0:T(8,128)(2,1)}), bf16[8,4,4,8,1024]{4,3,2,1,0:T(8,128)(2,1)S(1)}, u32[]{:S(2)}, u32[]{:S(2)}) %all-to-all-start) | async-done | bytes 2097184 | tf_op jit(solution)/shard_map/all_to_all | solution.py:313
  37.1 1.3 %copy-done = bf16[8,4,4,8,1024]{4,3,2,1,0:T(8,128)(2,1)} copy-done((bf16[8,4,4,8,1024]{4,3,2,1,0:T(8,128)(2,1)}, bf16[8,4,4,8,1024]{4,3,2,1,0:T(8,128)(2,1)S(1)}, u32[]{:S(2)}) %copy-start) | copy-done | bytes 2097176
  38.5 5.9 %shard_map.86 = bf16[8,3,4,8,1024]{4,3,2,1,0:T(8,128)(2,1)} custom-call(bf16[8,4,4,8,1024]{4,3,2,1,0:T(8,128)(2,1)} %copy-done), custom_call_target="tpu_custom_call" | custom-call | tf_op jit(solution)/shard_map/pallas_call | solution.py:269
  44.3 3.7 %all-to-all-start.1 = ((bf16[8,3,4,8,1024]{4,3,2,1,0:T(8,128)(2,1)}), bf16[8,3,4,8,1024]{4,3,2,1,0:T(8,128)(2,1)S(1)}, u32[]{:S(2)}, u32[]{:S(2)}) async-start(bf16[8,3,4,8,1024]{4,3,2,1,0:T(8,128)(2,1)} %shard_map.86), calls=%async_computation.1 | async-start | bytes 3145728 | tf_op jit(solution)/shard_map/all_to_all | solution.py:323
  48.1 0.1 multiply_reduce_fusion
  48.2 0.1 broadcast_compare_fusion
  48.4 0.8 fusion.6.bias_ref
  49.1 1.0 copy-done.6
  50.1 56.1 %shard_map.85 = (f32[8,32,1024]{2,1,0:T(8,128)}, f32[8,32,1024]{2,1,0:T(8,128)}, f32[8,32,1024]{2,1,0:T(8,128)}) custom-call(bf16[8,32,1024]{2,1,0:T(8,128)(2,1)} %q_ref.1, bf16[8,32,1024]{2,1,0:T(8,128)(2,1)} %g_ref.1, bf16[8,32,1024]{2,1,0:T(8,128)(2,1)} %k_ref.1, bf16[8,32,1024]{2,1,0:T(8,128)(2,1)} %v_ref.1, ...), custom_call_target="tpu_custom_call" | custom-call | tf_op jit(solution)/shard_map/pallas_call | solution.py:203
  106.2 0.4 convert_bitcast_fusion
  106.6 0.4 fusion.8
  107.1 0.8 copy-done.5
  107.9 1.4 %fusion.2 = bf16[8,32,1024]{2,1,0:T(8,128)(2,1)} fusion(f32[8,32,1024]{2,1,0:T(8,128)S(1)} %copy-done.5, f32[8,32,1024]{2,0,1:T(8,128)S(1)} %bitcast.17), kind=kLoop, calls=%fused_computation.8 | loop fusion | flops 524288 | bytes 2621440 | tf_op jit(solution)/shard_map/convert_element_type | solution.py:327
  109.3 1.4 %fusion = bf16[8,32,1024]{2,1,0:T(8,128)(2,1)} fusion(f32[8,32,1024]{2,1,0:T(8,128)S(1)} %copy-done.4, f32[8,32,1024]{2,0,1:T(8,128)S(1)} %bitcast.16), kind=kLoop, calls=%fused_computation.4 | loop fusion | flops 524288 | bytes 2621440 | tf_op jit(solution)/shard_map/convert_element_type | solution.py:327
  110.7 1.4 %fusion.1 = bf16[8,32,1024]{2,1,0:T(8,128)(2,1)} fusion(f32[8,32,1024]{2,1,0:T(8,128)S(1)} %copy-done.3, f32[8,32,1024]{2,0,1:T(8,128)S(1)} %bitcast.15), kind=kLoop, calls=%fused_computation.6 | loop fusion | flops 524288 | bytes 2621440 | tf_op jit(solution)/shard_map/convert_element_type | solution.py:327
  (25 shorter events, 0.2 us)
Async XLA Ops:
  0.6 2.8 %copy-start.1 = (bf16[8,32,1024]{2,1,0:T(8,128)(2,1)S(1)}, bf16[8,32,1024]{2,1,0:T(8,128)(2,1)}, u32[]{:S(2)}) copy-start(bf16[8,32,1024]{2,1,0:T(8,128)(2,1)} %k_ref.1) | copy-start | bytes 1572868
  0.6 3.1 %copy-start.2 = (bf16[8,32,1024]{2,1,0:T(8,128)(2,1)S(1)}, bf16[8,32,1024]{2,1,0:T(8,128)(2,1)}, u32[]{:S(2)}) copy-start(bf16[8,32,1024]{2,1,0:T(8,128)(2,1)} %v_ref.1) | copy-start | bytes 1572868
  5.6 31.5 %all-to-all-start = ((bf16[8,4,4,8,1024]{4,3,2,1,0:T(8,128)(2,1)}), bf16[8,4,4,8,1024]{4,3,2,1,0:T(8,128)(2,1)S(1)}, u32[]{:S(2)}, u32[]{:S(2)}) async-start(bf16[8,4,4,8,1024]{4,3,2,1,0:T(8,128)(2,1)} %maximum_bitcast_fusion), calls=%async_computation | async-start | bytes 4194304 | tf_op jit(solution)/shard_map/all_to_all | solution.py:313
  11.0 38.1 %collective-permute-start.1 = (bf16[2,8,32,1024]{3,2,1,0:T(8,128)(2,1)}, bf16[2,8,32,1024]{3,2,1,0:T(8,128)(2,1)S(1)}, u32[]{:S(2)}, u32[]{:S(2)}) collective-permute-start(bf16[2,8,32,1024]{3,2,1,0:T(8,128)(2,1)} %pad_maximum_fusion), channel_id=1, source_target_pairs={{1,0},{2,1},{3,2},{4,3},{5,4},{6,5},{7,6},{9,8},{10,9},{11,10},{12... | collective-permute-start | bytes 3145736 | tf_op jit(solution)/shard_map/ppermute | solution.py:22
  13.0 36.1 %collective-permute-start = (bf16[2,8,32,1024]{3,2,1,0:T(8,128)(2,1)}, bf16[2,8,32,1024]{3,2,1,0:T(8,128)(2,1)}, u32[]{:S(2)}, u32[]{:S(2)}) collective-permute-start(bf16[2,8,32,1024]{3,2,1,0:T(8,128)(2,1)} %pad_maximum_fusion), channel_id=1, source_target_pairs={{0,1},{1,2},{2,3},{3,4},{4,5},{5,6},{6,7},{8,9},{9,10},{10,11},{11... | collective-permute-start | bytes 3145736 | tf_op jit(solution)/shard_map/ppermute | solution.py:22
  37.1 1.3 %copy-start = (bf16[8,4,4,8,1024]{4,3,2,1,0:T(8,128)(2,1)}, bf16[8,4,4,8,1024]{4,3,2,1,0:T(8,128)(2,1)S(1)}, u32[]{:S(2)}) copy-start(bf16[8,4,4,8,1024]{4,3,2,1,0:T(8,128)(2,1)S(1)} %all-to-all-done.x_ref) | copy-start | bytes 6291460
  44.3 3.8 %copy-start.7 = (s32[8,16]{1,0:T(8,128)S(1)}, s32[8,16]{1,0:T(8,128)}, u32[]{:S(2)}) copy-start(s32[8,16]{1,0:T(8,128)} %param.10) | copy-start | bytes 1540
  44.3 4.0 %copy-start.8 = (s32[8]{0:T(128)S(1)}, s32[8]{0:T(128)}, u32[]{:S(2)}) copy-start(s32[8]{0:T(128)} %param.11) | copy-start | bytes 100
  44.3 61.9 %all-to-all-start.1 = ((bf16[8,3,4,8,1024]{4,3,2,1,0:T(8,128)(2,1)}), bf16[8,3,4,8,1024]{4,3,2,1,0:T(8,128)(2,1)S(1)}, u32[]{:S(2)}, u32[]{:S(2)}) async-start(bf16[8,3,4,8,1024]{4,3,2,1,0:T(8,128)(2,1)} %shard_map.86), calls=%async_computation.1 | async-start | bytes 3145728 | tf_op jit(solution)/shard_map/all_to_all | solution.py:323
  49.1 1.0 copy-start.6
  106.6 1.2 %copy-start.5 = (f32[8,32,1024]{2,1,0:T(8,128)S(1)}, f32[8,32,1024]{2,1,0:T(8,128)}, u32[]{:S(2)}) copy-start(f32[8,32,1024]{2,1,0:T(8,128)} %get-tuple-element.6) | copy-start | bytes 3145732
  107.1 2.2 %copy-start.4 = (f32[8,32,1024]{2,1,0:T(8,128)S(1)}, f32[8,32,1024]{2,1,0:T(8,128)}, u32[]{:S(2)}) copy-start(f32[8,32,1024]{2,1,0:T(8,128)} %get-tuple-element.8) | copy-start | bytes 3145732
  107.9 2.8 %copy-start.3 = (f32[8,32,1024]{2,1,0:T(8,128)S(1)}, f32[8,32,1024]{2,1,0:T(8,128)}, u32[]{:S(2)}) copy-start(f32[8,32,1024]{2,1,0:T(8,128)} %get-tuple-element.7) | copy-start | bytes 3145732

commit v19 on v17

--- a/solution.py
+++ b/solution.py
@@ -233,7 +233,7 @@
     )(queries, out_grad, key_grid, value_grid, l1, r1, bias)
 
 
-def column_kernel(x_ref, o_ref):
+def column_kernel(x_ref, order_ref, o_ref):
     groups, arrays, strip, rows, width = x_ref.shape
     per = max(1, LANES // (groups * rows))
 
@@ -262,15 +262,15 @@
                     o_ref[s, which, step * per + c] = low[start:start + rows]
 
 
-def column_attention(whole):
+def column_attention(whole, order):
     groups, arrays, strip, rows, width = whole.shape
     vmem = pl.BlockSpec(memory_space=pltpu.VMEM)
     return pl.pallas_call(
         column_kernel,
-        in_specs=[vmem],
+        in_specs=[vmem, vmem],
         out_specs=vmem,
         out_shape=jax.ShapeDtypeStruct((groups, 3, strip, rows, width), jnp.bfloat16),
-    )(whole)
+    )(whole, order)
 
 
 def band_bias(mask_rows, offsets, first_col, grid_cols, block_cols):
@@ -318,7 +318,7 @@
     first_col = lax.axis_index("rcol") * col_count
     bias = band_bias(tissue_mask, band_offset, first_col, grid_cols, col_count)
 
-    col_out = column_attention(whole)
+    col_out = column_attention(whole, bias[:, :8, :])
     back = lax.all_to_all(col_out, "rrow", split_axis=0, concat_axis=0, tiled=True)
     row_grads = fused_row(queries, out_grad, key_grid, value_grid, l1, r1, bias, far)
     back = back.transpose(1, 3, 0, 2, 4).reshape(3, row_count, col_count, feature_width)

time: 114 us -> 141 us (1.24)
  waiting for transfers between devices: 20.2 us -> 49.6 us
  other arithmetic: 8.33 us -> 6.71 us
    ppermute x2, waiting for transfers between devices: 0.01 us -> 23.5 us  [shifted(): return lax.ppermute(block, axis, route)]
    all_to_all x1, waiting for transfers between devices: 20.2 us -> 26.1 us  [body(): lax.all_to_all(stacked, 'rrow', split_axis=0, concat_axis=0, tiled=True)]
    unnamed x22 -> x24, local copies, waits for them, and re-layouts: 6.47 us -> 5.53 us
  transfers between devices with their start and end apart: 4 -> 4, of which waited for: 1 -> 3; matrix products, arithmetic and copies ran while one was open for 2% -> 1% of each run, Pallas kernels for 55% -> 40%
where the time goes in v19:
time: 141 us; the launch traced here: 139 us
  Pallas kernels  61.7 us (44%)
  waiting for transfers between devices  49.6 us (35%)
  starting transfers between devices  13.9 us (10%)
  other arithmetic  6.71 us (5%)
  local copies, waits for them, and re-layouts  6.58 us (5%)
    pallas_call x1, Pallas kernels, fused_row(): pl.pallas_call(functools.partial(fused_row_kernel, w2), in_specs=[vmem] *...  55.9 us
    all_to_all x1, waiting for transfers between devices, body(): lax.all_to_all(stacked, 'rrow', split_axis=0, concat_axis=0, tiled=True)  26.1 us
    ppermute x2, waiting for transfers between devices, shifted(): return lax.ppermute(block, axis, route)  23.5 us
    pallas_call x1, Pallas kernels, column_attention(): pl.pallas_call(column_kernel, in_specs=[vmem, vmem], out_specs=vmem, out_...  5.87 us
    ppermute x2, starting transfers between devices, shifted(): return lax.ppermute(block, axis, route)  5.84 us
    unnamed x24, local copies, waits for them, and re-layouts  5.53 us
    all_to_all x1, starting transfers between devices, body(): lax.all_to_all(stacked, 'rrow', split_axis=0, concat_axis=0, tiled=True)  4.43 us
    convert_element_type x3, other arithmetic, body(): (row + col).astype(jnp.bfloat16)  4.22 us
  transfers between devices with their start and end apart: 4, of which 3 were waited for; matrix products, arithmetic and copies ran while one was open for 1% of the time, Pallas kernels for 40%

profile of v19, /device:TPU:48, one launch (start us, length us, event | category | flops | bytes accessed | tf_op | source)
XLA Modules:
  0.0 139.3 jit_solution(17517680401288109186)
XLA Ops:
  0.7 1.4 %copy.16 = bf16[8,32,1024]{2,0,1:T(8,128)(2,1)S(1)} copy(bf16[8,32,1024]{2,1,0:T(8,128)(2,1)} %q_ref.1) | data formatting | bytes 1048576 | tf_op args[0]
  2.1 1.3 copy.19
  3.4 0.3 copy.17
  3.7 0.3 copy.18
  4.0 1.6 %maximum_bitcast_fusion = bf16[8,4,4,8,1024]{4,3,2,1,0:T(8,128)(2,1)} fusion(bf16[1,8,8,4,1024]{4,1,3,0,2:T(8,128)(2,1)S(1)} %bitcast.19, bf16[1,8,8,4,1024]{4,1,3,0,2:T(8,128)(2,1)S(1)} %bitcast.21, bf16[1,8,8,4,1024]{4,1,3,0,2:T(8,128)(2,1)S(1)} %bitcast.20, bf16[1,8,8,4,1024]{4,1,3,0,2:T(8,128)(2,1)S(1)} %bitcast.18), kind=kLoop, calls=%fused_computation.1 | loop fusion | flops 3145728 | bytes 4194304 | tf_op jit(solution)/shard_map/transpose | solution.py:310
  5.6 4.4 %all-to-all-start = ((bf16[8,4,4,8,1024]{4,3,2,1,0:T(8,128)(2,1)}), bf16[8,4,4,8,1024]{4,3,2,1,0:T(8,128)(2,1)S(1)}, u32[]{:S(2)}, u32[]{:S(2)}) async-start(bf16[8,4,4,8,1024]{4,3,2,1,0:T(8,128)(2,1)} %maximum_bitcast_fusion), calls=%async_computation | async-start | bytes 4194304 | tf_op jit(solution)/shard_map/all_to_all | solution.py:312
  10.4 0.1 fusion.6.bias_ref
  10.5 0.6 slice.7.order_ref
  11.2 26.1 %all-to-all-done.x_ref = bf16[8,4,4,8,1024]{4,3,2,1,0:T(8,128)(2,1)S(1)} async-done(((bf16[8,4,4,8,1024]{4,3,2,1,0:T(8,128)(2,1)}), bf16[8,4,4,8,1024]{4,3,2,1,0:T(8,128)(2,1)S(1)}, u32[]{:S(2)}, u32[]{:S(2)}) %all-to-all-start) | async-done | bytes 2097184 | tf_op jit(solution)/shard_map/all_to_all | solution.py:312
  37.3 1.3 copy-done
  38.6 5.9 %shard_map.86 = bf16[8,3,4,8,1024]{4,3,2,1,0:T(8,128)(2,1)} custom-call(bf16[8,4,4,8,1024]{4,3,2,1,0:T(8,128)(2,1)} %copy-done, f32[8,8,128]{2,1,0:T(8,128)} %slice.7.order_ref), custom_call_target="tpu_custom_call" | custom-call | tf_op jit(solution)/shard_map/pallas_call | solution.py:268
  44.5 3.6 %all-to-all-start.1 = ((bf16[8,3,4,8,1024]{4,3,2,1,0:T(8,128)(2,1)}), bf16[8,3,4,8,1024]{4,3,2,1,0:T(8,128)(2,1)S(1)}, u32[]{:S(2)}, u32[]{:S(2)}) async-start(bf16[8,3,4,8,1024]{4,3,2,1,0:T(8,128)(2,1)} %shard_map.86), calls=%async_computation.1 | async-start | bytes 3145728 | tf_op jit(solution)/shard_map/all_to_all | solution.py:322
  48.1 0.1 pad_maximum_fusion
  48.2 2.0 %collective-permute-start.1 = (bf16[2,8,32,1024]{3,2,1,0:T(8,128)(2,1)S(1)}, bf16[2,8,32,1024]{3,2,1,0:T(8,128)(2,1)S(1)}, u32[]{:S(2)}, u32[]{:S(2)}) collective-permute-start(bf16[2,8,32,1024]{3,2,1,0:T(8,128)(2,1)S(1)} %pad_maximum_fusion), channel_id=1, source_target_pairs={{1,0},{2,1},{3,2},{4,3},{5,4},{6,5},{7,6},{9,8},{10,9},{11,10},{12... | collective-permute-start | bytes 3145736 | tf_op jit(solution)/shard_map/ppermute | solution.py:22
  50.2 3.8 %collective-permute-start = (bf16[2,8,32,1024]{3,2,1,0:T(8,128)(2,1)S(1)}, bf16[2,8,32,1024]{3,2,1,0:T(8,128)(2,1)}, u32[]{:S(2)}, u32[]{:S(2)}) collective-permute-start(bf16[2,8,32,1024]{3,2,1,0:T(8,128)(2,1)S(1)} %pad_maximum_fusion), channel_id=1, source_target_pairs={{0,1},{1,2},{2,3},{3,4},{4,5},{5,6},{6,7},{8,9},{9,10},{10,11},{11... | collective-permute-start | bytes 3145736 | tf_op jit(solution)/shard_map/ppermute | solution.py:22
  54.0 21.7 %collective-permute-done.1.r1_ref = bf16[2,8,32,1024]{3,2,1,0:T(8,128)(2,1)S(1)} collective-permute-done((bf16[2,8,32,1024]{3,2,1,0:T(8,128)(2,1)S(1)}, bf16[2,8,32,1024]{3,2,1,0:T(8,128)(2,1)S(1)}, u32[]{:S(2)}, u32[]{:S(2)}) %collective-permute-start.1) | collective-permute-done | bytes 1048608 | tf_op jit(solution)/shard_map/ppermute | solution.py:22
  75.7 1.9 %collective-permute-done.l1_ref = bf16[2,8,32,1024]{3,2,1,0:T(8,128)(2,1)} collective-permute-done((bf16[2,8,32,1024]{3,2,1,0:T(8,128)(2,1)S(1)}, bf16[2,8,32,1024]{3,2,1,0:T(8,128)(2,1)}, u32[]{:S(2)}, u32[]{:S(2)}) %collective-permute-start) | collective-permute-done | bytes 1048608 | tf_op jit(solution)/shard_map/ppermute | solution.py:22
  77.6 55.9 %shard_map.85 = (f32[8,32,1024]{2,1,0:T(8,128)}, f32[8,32,1024]{2,1,0:T(8,128)}, f32[8,32,1024]{2,1,0:T(8,128)}) custom-call(bf16[8,32,1024]{2,1,0:T(8,128)(2,1)} %q_ref.1, bf16[8,32,1024]{2,1,0:T(8,128)(2,1)} %g_ref.1, bf16[8,32,1024]{2,1,0:T(8,128)(2,1)} %k_ref.1, bf16[8,32,1024]{2,1,0:T(8,128)(2,1)} %v_ref.1, ...), custom_call_target="tpu_custom_call" | custom-call | tf_op jit(solution)/shard_map/pallas_call | solution.py:202
  133.5 0.4 convert_bitcast_fusion
  133.9 0.4 fusion.8
  134.3 0.8 copy-done.5
  135.1 1.4 %fusion.2 = bf16[8,32,1024]{2,1,0:T(8,128)(2,1)} fusion(f32[8,32,1024]{2,1,0:T(8,128)S(1)} %copy-done.5, f32[8,32,1024]{2,0,1:T(8,128)S(1)} %bitcast.17), kind=kLoop, calls=%fused_computation.8 | loop fusion | flops 524288 | bytes 2621440 | tf_op jit(solution)/shard_map/convert_element_type | solution.py:326
  136.5 1.4 %fusion = bf16[8,32,1024]{2,1,0:T(8,128)(2,1)} fusion(f32[8,32,1024]{2,1,0:T(8,128)S(1)} %copy-done.4, f32[8,32,1024]{2,0,1:T(8,128)S(1)} %bitcast.16), kind=kLoop, calls=%fused_computation.4 | loop fusion | flops 524288 | bytes 2621440 | tf_op jit(solution)/shard_map/convert_element_type | solution.py:326
  137.9 1.4 %fusion.1 = bf16[8,32,1024]{2,1,0:T(8,128)(2,1)} fusion(f32[8,32,1024]{2,1,0:T(8,128)S(1)} %copy-done.3, f32[8,32,1024]{2,0,1:T(8,128)S(1)} %bitcast.15), kind=kLoop, calls=%fused_computation.6 | loop fusion | flops 524288 | bytes 2621440 | tf_op jit(solution)/shard_map/convert_element_type | solution.py:326
  (28 shorter events, 0.3 us)
Async XLA Ops:
  0.6 2.8 %copy-start.1 = (bf16[8,32,1024]{2,1,0:T(8,128)(2,1)S(1)}, bf16[8,32,1024]{2,1,0:T(8,128)(2,1)}, u32[]{:S(2)}) copy-start(bf16[8,32,1024]{2,1,0:T(8,128)(2,1)} %k_ref.1) | copy-start | bytes 1572868
  0.6 3.1 %copy-start.2 = (bf16[8,32,1024]{2,1,0:T(8,128)(2,1)S(1)}, bf16[8,32,1024]{2,1,0:T(8,128)(2,1)}, u32[]{:S(2)}) copy-start(bf16[8,32,1024]{2,1,0:T(8,128)(2,1)} %v_ref.1) | copy-start | bytes 1572868
  5.6 4.5 %copy-start.8 = (s32[8,16]{1,0:T(8,128)S(1)}, s32[8,16]{1,0:T(8,128)}, u32[]{:S(2)}) copy-start(s32[8,16]{1,0:T(8,128)} %param.10) | copy-start | bytes 1540
  5.6 4.8 %copy-start.9 = (s32[8]{0:T(128)S(1)}, s32[8]{0:T(128)}, u32[]{:S(2)}) copy-start(s32[8]{0:T(128)} %param.11) | copy-start | bytes 100
  5.6 31.6 %all-to-all-start = ((bf16[8,4,4,8,1024]{4,3,2,1,0:T(8,128)(2,1)}), bf16[8,4,4,8,1024]{4,3,2,1,0:T(8,128)(2,1)S(1)}, u32[]{:S(2)}, u32[]{:S(2)}) async-start(bf16[8,4,4,8,1024]{4,3,2,1,0:T(8,128)(2,1)} %maximum_bitcast_fusion), calls=%async_computation | async-start | bytes 4194304 | tf_op jit(solution)/shard_map/all_to_all | solution.py:312
  10.5 67.0 %copy-start.7 = (f32[8,32,128]{2,1,0:T(8,128)}, f32[8,32,128]{2,1,0:T(8,128)S(1)}, u32[]{:S(2)}) copy-start(f32[8,32,128]{2,1,0:T(8,128)S(1)} %fusion.6.bias_ref) | copy-start | bytes 393220
  37.3 1.3 copy-start
  44.5 89.0 %all-to-all-start.1 = ((bf16[8,3,4,8,1024]{4,3,2,1,0:T(8,128)(2,1)}), bf16[8,3,4,8,1024]{4,3,2,1,0:T(8,128)(2,1)S(1)}, u32[]{:S(2)}, u32[]{:S(2)}) async-start(bf16[8,3,4,8,1024]{4,3,2,1,0:T(8,128)(2,1)} %shard_map.86), calls=%async_computation.1 | async-start | bytes 3145728 | tf_op jit(solution)/shard_map/all_to_all | solution.py:322
  48.2 27.5 %collective-permute-start.1 = (bf16[2,8,32,1024]{3,2,1,0:T(8,128)(2,1)S(1)}, bf16[2,8,32,1024]{3,2,1,0:T(8,128)(2,1)S(1)}, u32[]{:S(2)}, u32[]{:S(2)}) collective-permute-start(bf16[2,8,32,1024]{3,2,1,0:T(8,128)(2,1)S(1)} %pad_maximum_fusion), channel_id=1, source_target_pairs={{1,0},{2,1},{3,2},{4,3},{5,4},{6,5},{7,6},{9,8},{10,9},{11,10},{12... | collective-permute-start | bytes 3145736 | tf_op jit(solution)/shard_map/ppermute | solution.py:22
  50.2 27.4 %collective-permute-start = (bf16[2,8,32,1024]{3,2,1,0:T(8,128)(2,1)S(1)}, bf16[2,8,32,1024]{3,2,1,0:T(8,128)(2,1)}, u32[]{:S(2)}, u32[]{:S(2)}) collective-permute-start(bf16[2,8,32,1024]{3,2,1,0:T(8,128)(2,1)S(1)} %pad_maximum_fusion), channel_id=1, source_target_pairs={{0,1},{1,2},{2,3},{3,4},{4,5},{5,6},{6,7},{8,9},{9,10},{10,11},{11... | collective-permute-start | bytes 3145736 | tf_op jit(solution)/shard_map/ppermute | solution.py:22
  75.7 1.9 %copy-start.6 = (bf16[2,8,32,1024]{3,2,1,0:T(8,128)(2,1)}, bf16[2,8,32,1024]{3,2,1,0:T(8,128)(2,1)S(1)}, u32[]{:S(2)}) copy-start(bf16[2,8,32,1024]{3,2,1,0:T(8,128)(2,1)S(1)} %collective-permute-done.1.r1_ref) | copy-start | bytes 3145732
  133.9 1.2 copy-start.5
  134.3 2.2 %copy-start.4 = (f32[8,32,1024]{2,1,0:T(8,128)S(1)}, f32[8,32,1024]{2,1,0:T(8,128)}, u32[]{:S(2)}) copy-start(f32[8,32,1024]{2,1,0:T(8,128)} %get-tuple-element.8) | copy-start | bytes 3145732
  135.1 2.8 %copy-start.3 = (f32[8,32,1024]{2,1,0:T(8,128)S(1)}, f32[8,32,1024]{2,1,0:T(8,128)}, u32[]{:S(2)}) copy-start(f32[8,32,1024]{2,1,0:T(8,128)} %get-tuple-element.7) | copy-start | bytes 3145732
